TPU v7x, 32 devices: a whole 2x2x4 slice. The times are simulated.
32 devices in a mesh: seq: 4 (over z), dp: 8 (over y, x, core).
Axes of the slice: x: 2, y: 2, z: 4, core: 2. Of those that a mesh axis runs over, the one named last changes fastest.
Arguments:
- hidden_in: bfloat16 [16, 2048, 1024], P('dp', 'seq'), may hold values from -6 to 6
- mixer_weights: float32 [1, 5, 1024, 1024], P(None, None, 'dp'), may hold values from -0.1875 to 0.1875
- channel_in_weights: float32 [1, 2, 1024, 2816], P(None, None, 'dp'), may hold values from -0.1875 to 0.1875
- channel_out_weights: float32 [1, 2816, 1024], P(None, 'dp'), may hold values from -0.109375 to 0.109375
- decay_rates: float32 [1, 8], replicated, may hold values from 0 to 0.034, as said below
- doc_lengths: int32 [16, 4], P('dp'), may hold values from 1 to 1024, 2048 in all within a row
- out_cotangent: bfloat16 [16, 2048, 1024], P('dp', 'seq'), may hold values from -6 to 6
Outputs:
- block_output: bfloat16 [16, 2048, 1024], P('dp', 'seq')
- input_gradient: float32 [16, 2048, 1024], P('dp', 'seq')
- mixer_gradient: float32 [1, 5, 1024, 1024], P(None, None, 'dp')
- channel_in_gradient: float32 [1, 2, 1024, 2816], P(None, None, 'dp')
- channel_out_gradient: float32 [1, 2816, 1024], P(None, 'dp')
Inputs may be any that keep to these rules, and one draw needn't show every extreme that they name: `decay_rates`: positive decay rates. `doc_lengths`: each row's 4 lengths add up to 2048.
All inputs are finite; a program needn't handle non-finite values.
Results may differ from a plain program's by a relative error of at most 0.02.
Values may be sent and summed in bfloat16 or wider, within the bound.
No kernel may reach another device: no remote copies, remote signals or barrier semaphores. Data moves between devices by JAX's collectives and lax.ppermute only.
A program may use at most 256 MiB of HBM per device.

v0:
```python
import jax
import jax.numpy as jnp
from jax import lax
from jax.sharding import PartitionSpec as P

EPS = 1e-06
FULL_PRECISION = lax.Precision.HIGHEST


def passed_along(value, axis, steps):
    count = lax.axis_size(axis)
    leading, last = (max(0, -steps), min(count, count - steps))
    return lax.ppermute(value, axis, [(source, source + steps) for source in range(leading, last)])


def product(left, right):
    return jnp.dot(left, right, preferred_element_type=jnp.float32)


def rms_norm(value_rows):
    factor = lax.rsqrt(jnp.mean(value_rows * value_rows, axis=-1, keepdims=True) + EPS)
    return (value_rows * factor, factor)


def norm_back(value_rows, factor, upstream):
    features = value_rows.shape[-1]
    inner_sum = jnp.sum(upstream * value_rows, axis=-1, keepdims=True)
    return factor * upstream - factor * factor * factor / features * value_rows * inner_sum


def swish_slope(value_rows):
    sigmoid_part = jax.nn.sigmoid(value_rows)
    return sigmoid_part * (1.0 + value_rows * (1.0 - sigmoid_part))


def doc_index(doc_ends, places):
    compare = places[None, :, None] >= doc_ends[:, None, :]
    return jnp.sum(compare.astype(jnp.int32), axis=-1, dtype=jnp.int32)


def decay_tables(rates, doc_ends, start, count):
    float_kind = rates.dtype
    offsets = jnp.arange(count, dtype=jnp.int32)
    start = jnp.asarray(start, dtype=jnp.int32)
    doc_here = doc_index(doc_ends, start + offsets)
    before_place = jnp.full((1,), -1, dtype=jnp.int32) + start
    doc_before = doc_index(doc_ends, before_place)[:, 0]
    doc_last = doc_here[:, count - 1]
    distance = jnp.maximum(offsets[:, None] - offsets[None, :], 0).astype(float_kind)
    causal = offsets[:, None] >= offsets[None, :]
    linked = causal[None] & (doc_here[:, :, None] == doc_here[:, None, :])
    intra_vals = jnp.exp(-rates[None, :, None, None] * distance[None, None])
    intra = jnp.where(linked[:, None], intra_vals, jnp.zeros_like(intra_vals))
    ahead = (offsets + 1).astype(float_kind)
    behind = (count - 1 - offsets).astype(float_kind)
    entry_vals = jnp.exp(-rates[None, None, :] * ahead[None, :, None])
    entry = jnp.where(
        (doc_here == doc_before[:, None])[:, :, None], entry_vals, jnp.zeros_like(entry_vals)
    )
    leaving_vals = jnp.exp(-rates[None, None, :] * behind[None, :, None])
    leaving = jnp.where(
        (doc_here == doc_last[:, None])[:, :, None], leaving_vals, jnp.zeros_like(leaving_vals)
    )
    length_value = jnp.asarray(count, dtype=float_kind)
    passing_vals = jnp.exp(-rates * length_value)[None, :] + jnp.zeros(
        (doc_last.shape[0], 1), float_kind
    )
    passing = jnp.where(
        (doc_last == doc_before)[:, None], passing_vals, jnp.zeros_like(passing_vals)
    )
    return (intra, entry, leaving, passing)


def block_out(per_head_queries, per_head_keys, per_head_values, tables, state_in):
    scores = (
        jnp.einsum("rthd,rshd->rhts", per_head_queries, per_head_keys, precision=FULL_PRECISION)
        * tables[0]
    )
    local_part = jnp.einsum("rhts,rshe->rthe", scores, per_head_values, precision=FULL_PRECISION)
    carried = (
        jnp.einsum("rthd,rhde->rthe", per_head_queries, state_in, precision=FULL_PRECISION)
        * tables[1][..., None]
    )
    return local_part + carried


def block_state(per_head_keys, per_head_values, tables):
    return jnp.einsum(
        "rshd,rshe->rhde",
        per_head_keys * tables[2][..., None],
        per_head_values,
        precision=FULL_PRECISION,
    )


def block_back(
    per_head_queries, per_head_keys, per_head_values, upstream, tables, state_in, state_grad
):
    intra, entry, leaving, passing = tables
    scores = (
        jnp.einsum("rthd,rshd->rhts", per_head_queries, per_head_keys, precision=FULL_PRECISION)
        * intra
    )
    score_grad = (
        jnp.einsum("rthe,rshe->rhts", upstream, per_head_values, precision=FULL_PRECISION) * intra
    )
    query_grad = jnp.einsum("rhts,rshd->rthd", score_grad, per_head_keys, precision=FULL_PRECISION)
    query_grad = (
        query_grad
        + jnp.einsum("rthe,rhde->rthd", upstream, state_in, precision=FULL_PRECISION)
        * entry[..., None]
    )
    key_grad = jnp.einsum("rhts,rthd->rshd", score_grad, per_head_queries, precision=FULL_PRECISION)
    key_grad = (
        key_grad
        + jnp.einsum("rshe,rhde->rshd", per_head_values, state_grad, precision=FULL_PRECISION)
        * leaving[..., None]
    )
    value_grad = jnp.einsum("rhts,rthe->rshe", scores, upstream, precision=FULL_PRECISION)
    value_grad = (
        value_grad
        + jnp.einsum("rshd,rhde->rshe", per_head_keys, state_grad, precision=FULL_PRECISION)
        * leaving[..., None]
    )
    return (query_grad, key_grad, value_grad)


def carry_forward(passing, local_state):

    def step_forward(turn_index, incoming):
        outgoing = passing[..., None, None] * incoming + local_state
        return passed_along(outgoing.astype(jnp.bfloat16), "seq", 1).astype(outgoing.dtype)

    return lax.fori_loop(0, lax.axis_size("seq") - 1, step_forward, jnp.zeros_like(local_state))


def carry_backward(passing, local_grad):

    def retreat(turn_index, incoming):
        outgoing = passing[..., None, None] * incoming + local_grad
        return passed_along(outgoing.astype(jnp.bfloat16), "seq", -1).astype(outgoing.dtype)

    return lax.fori_loop(0, lax.axis_size("seq") - 1, retreat, jnp.zeros_like(local_grad))


def reduce_grads(terms):
    pieces = (
        lax.psum_scatter(
            terms[0].astype(jnp.bfloat16), "dp", scatter_dimension=1, tiled=True
        ).astype(jnp.float32),
        lax.psum_scatter(
            terms[1].astype(jnp.bfloat16), "dp", scatter_dimension=0, tiled=True
        ).astype(jnp.float32),
        lax.psum_scatter(
            terms[2].astype(jnp.bfloat16), "dp", scatter_dimension=1, tiled=True
        ).astype(jnp.float32),
        lax.psum_scatter(
            terms[3].astype(jnp.bfloat16), "dp", scatter_dimension=0, tiled=True
        ).astype(jnp.float32),
    )
    return (
        lax.psum(pieces[0].astype(jnp.bfloat16), "seq").astype(jnp.float32),
        lax.psum(pieces[1].astype(jnp.bfloat16), "seq").astype(jnp.float32),
        lax.psum(pieces[2].astype(jnp.bfloat16), "seq").astype(jnp.float32),
        lax.psum(pieces[3].astype(jnp.bfloat16), "seq").astype(jnp.float32),
    )


def local(
    hidden_in,
    mixer_weights,
    channel_in_weights,
    channel_out_weights,
    decay_rates,
    doc_lengths,
    out_cotangent,
):
    rows, tokens, features = hidden_in.shape
    layers = mixer_weights.shape[0]
    heads = decay_rates.shape[1]
    head_dim = features // heads
    count = rows * tokens
    head_shape = (rows, tokens, heads, head_dim)
    start = lax.axis_index("seq") * jnp.asarray(tokens, dtype=jnp.int32)
    doc_ends = jnp.cumsum(doc_lengths, axis=1, dtype=jnp.int32)
    resid = hidden_in.astype(jnp.float32).reshape(count, features)
    layer_index = 0
    gathered = (
        mixer_weights[layer_index].astype(jnp.bfloat16),
        channel_in_weights[layer_index].astype(jnp.bfloat16),
        channel_out_weights[layer_index].astype(jnp.bfloat16),
    )
    mixer_full = lax.all_gather(gathered[0], "dp", axis=1, tiled=True)
    channel_full = lax.all_gather(gathered[1], "dp", axis=1, tiled=True)
    down_full = lax.all_gather(gathered[2], "dp", axis=0, tiled=True)
    normed, factor_in = rms_norm(resid)
    normed_low = normed.astype(jnp.bfloat16)
    projected = jnp.einsum(
        "nd,kde->kne", normed_low, mixer_full[:4], preferred_element_type=jnp.float32
    )
    query_pre = projected[0]
    key_pre = projected[1]
    value_pre = projected[2]
    gate_pre = projected[3]
    per_head_queries = (query_pre * jax.nn.sigmoid(query_pre)).reshape(head_shape)
    per_head_keys = (key_pre * jax.nn.sigmoid(key_pre)).reshape(head_shape)
    per_head_values = value_pre.reshape(head_shape)
    tables = decay_tables(decay_rates[layer_index], doc_ends, start, tokens)
    local_state = block_state(per_head_keys, per_head_values, tables)
    state_in = carry_forward(tables[3], local_state)
    mixed = block_out(per_head_queries, per_head_keys, per_head_values, tables, state_in).reshape(
        count, features
    )
    mixed_norm, factor_mix = rms_norm(mixed)
    gated = (mixed_norm * gate_pre).astype(jnp.bfloat16)
    after_mixer = resid + product(gated, mixer_full[4])
    normed_two, factor_two = rms_norm(after_mixer)
    normed_two_low = normed_two.astype(jnp.bfloat16)
    pair = jnp.einsum(
        "nd,kdf->knf", normed_two_low, channel_full, preferred_element_type=jnp.float32
    )
    glu = (pair[0] * pair[1]).astype(jnp.bfloat16)
    saved = [
        (
            mixer_full,
            channel_full,
            down_full,
            resid,
            factor_in,
            normed_low,
            query_pre,
            key_pre,
            gate_pre,
            per_head_queries,
            per_head_keys,
            per_head_values,
            tables,
            state_in,
            mixed,
            mixed_norm,
            factor_mix,
            gated,
            after_mixer,
            factor_two,
            normed_two_low,
            pair,
            glu,
        )
    ]
    resid = after_mixer + product(glu, down_full)
    block_output = resid.astype(jnp.bfloat16).reshape(rows, tokens, features)
    upstream = out_cotangent.astype(jnp.float32).reshape(count, features)
    mixer_list = []
    channel_list = []
    down_list = []
    for layer_index in reversed(range(layers)):
        (
            mixer_full,
            channel_full,
            down_full,
            resid_in,
            factor_in,
            normed_low,
            query_pre,
            key_pre,
            gate_pre,
            per_head_queries,
            per_head_keys,
            per_head_values,
            tables,
            state_in,
            mixed,
            mixed_norm,
            factor_mix,
            gated,
            after_mixer,
            factor_two,
            normed_two_low,
            pair,
            glu,
        ) = saved[layer_index]
        branch_low = upstream.astype(jnp.bfloat16)
        down_term = jnp.einsum("nf,nd->fd", glu, branch_low, preferred_element_type=jnp.float32)
        glu_grad = (
            jnp.einsum("nd,fd->nf", branch_low, down_full, preferred_element_type=jnp.float32)
            .astype(jnp.bfloat16)
            .astype(jnp.float32)
        )
        pair_grad = jnp.stack([glu_grad * pair[1], glu_grad * pair[0]]).astype(jnp.bfloat16)
        channel_term = jnp.einsum(
            "nd,knf->kdf", normed_two_low, pair_grad, preferred_element_type=jnp.float32
        )
        two_grad = jnp.einsum(
            "knf,kdf->nd", pair_grad, channel_full, preferred_element_type=jnp.float32
        )
        upstream_mid = upstream + norm_back(after_mixer, factor_two, two_grad)
        mixer_low = upstream_mid.astype(jnp.bfloat16)
        out_term = jnp.einsum("nd,ne->de", gated, mixer_low, preferred_element_type=jnp.float32)
        gated_grad = (
            jnp.einsum("ne,de->nd", mixer_low, mixer_full[4], preferred_element_type=jnp.float32)
            .astype(jnp.bfloat16)
            .astype(jnp.float32)
        )
        gate_grad = gated_grad * mixed_norm
        mixed_grad = norm_back(mixed, factor_mix, gated_grad * gate_pre).reshape(head_shape)
        local_grad = jnp.einsum(
            "rthd,rthe->rhde",
            per_head_queries * tables[1][..., None],
            mixed_grad,
            precision=FULL_PRECISION,
        )
        state_grad = carry_backward(tables[3], local_grad)
        query_grad, key_grad, value_grad = block_back(
            per_head_queries,
            per_head_keys,
            per_head_values,
            mixed_grad,
            tables,
            state_in,
            state_grad,
        )
        proj_grad = jnp.stack(
            [
                query_grad.reshape(count, features) * swish_slope(query_pre),
                key_grad.reshape(count, features) * swish_slope(key_pre),
                value_grad.reshape(count, features),
                gate_grad,
            ]
        ).astype(jnp.bfloat16)
        four_term = jnp.einsum(
            "nd,kne->kde", normed_low, proj_grad, preferred_element_type=jnp.float32
        )
        one_grad = jnp.einsum(
            "kne,kde->nd", proj_grad, mixer_full[:4], preferred_element_type=jnp.float32
        )
        upstream = upstream_mid + norm_back(resid_in, factor_in, one_grad)
        summed = reduce_grads((four_term, out_term, channel_term, down_term))
        mixer_list.append(jnp.concatenate([summed[0], summed[1][None]], axis=0))
        channel_list.append(summed[2])
        down_list.append(summed[3])
    mixer_gradient = jnp.stack(mixer_list[::-1])
    channel_in_gradient = jnp.stack(channel_list[::-1])
    channel_out_gradient = jnp.stack(down_list[::-1])
    input_gradient = upstream.reshape(rows, tokens, features)
    return (block_output, input_gradient, mixer_gradient, channel_in_gradient, channel_out_gradient)


def solution(mesh):
    in_specs = (
        P("dp", "seq", None),
        P(None, None, "dp", None),
        P(None, None, "dp", None),
        P(None, "dp", None),
        P(),
        P("dp", None),
        P("dp", "seq", None),
    )
    out_specs = (
        P("dp", "seq", None),
        P("dp", "seq", None),
        P(None, None, "dp", None),
        P(None, None, "dp", None),
        P(None, "dp", None),
    )
    return jax.shard_map(local, mesh=mesh, in_specs=in_specs, out_specs=out_specs, check_vma=False)
```

profile of v0, /device:TPU:0, one launch (start us, length us, event | category | flops | bytes accessed | tf_op | source)
XLA Modules:
  0.0 966.9 jit_solution(12912789637610193381)
XLA Ops:
  10.1 3.2 convert_element_type.150
  20.7 5.8 multiply_exponential_fusion
  26.6 51.9 %all-gather.7.cloned.1.call-done = bf16[1,5,1024,1024]{2,3,1,0:T(8,128)(2,1)} async-done(((bf16[1,5,128,1024]{2,3,1,0:T(8,128)(2,1)}), bf16[1,5,1024,1024]{2,3,1,0:T(8,128)(2,1)}) %all-gather.7.cloned.1.call-update) | async-done | bytes 10485776 | tf_op jit(solution)/shard_map/all_gather | solution.py:193
  78.5 16.3 %convolution_bitcast_fusion = f32[4,1024,1024]{1,2,0:T(8,128)} fusion(bf16[1,5,1024,1024]{2,3,1,0:T(8,128)(2,1)} %all-gather.7.cloned.1.call-done, bf16[1024,1024]{1,0:T(8,128)(2,1)} %fusion.65), kind=kOutput, calls=%fused_computation.30 | convolution fusion | flops 8589934592 | bytes 27262976 | tf_op jit(solution)/shard_map/nd,kde->kne/dot_general | solution.py:198
  94.7 10.2 %fusion.120 = (f32[1,1024,1024]{1,2,0:T(8,128)}, f32[1,1024,1024]{1,2,0:T(8,128)}, f32[1,1024,1024]{1,2,0:T(8,128)}) fusion(f32[4,1024,1024]{1,2,0:T(8,128)} %convolution_bitcast_fusion), kind=kLoop, calls=%fused_computation.166 | loop fusion | bytes 25165824 | tf_op jit(solution)/shard_map/slice | solution.py:201
  104.9 6.6 reshape_squeeze.3
  111.5 7.4 copy.119
  118.9 6.6 squeeze.13
  125.5 6.8 squeeze.12
  132.2 8.6 fusion.69
  140.8 48.7 %while.22 = (s32[]{:T(128)}, f32[2,8,128,128]{3,2,1,0:T(8,128)S(1)}, f32[2,8,128,128]{3,2,1,0:T(8,128)S(1)}, f32[8]{0:T(128)S(1)}, pred[2]{0:T(512)(128)(4,1)S(1)}, /*index=5*/s32[]{:T(128)}, s32[]{:T(128)}) while((s32[]{:T(128)}, f32[2,8,128,128]{3,2,1,0:T(8,128)S(1)}, f32[2,8,128,128]{3,2,1,0:T(8,128)S(1)}, f32[8]{0:T(128)S(1)}, ...), condition=%wide.region_5.6_spmd.clone, body=%wide.region_4.5_spmd.clone.sunk | while | flops 1310739 | bytes 6291745 | solution.py:134
  141.9 3.4 collective-permute-start
  145.3 11.9 %collective-permute-done = bf16[2,8,128,128]{3,2,1,0:T(8,128)(2,1)S(1)} collective-permute-done((bf16[2,8,128,128]{3,2,1,0:T(8,128)(2,1)}, bf16[2,8,128,128]{3,2,1,0:T(8,128)(2,1)S(1)}, u32[]{:S(2)}, u32[]{:S(2)}) %collective-permute-start) | collective-permute-done | bytes 524320 | tf_op jit(solution)/shard_map/while/body/eval_jaxpr/ppermute | solution.py:13
  158.4 4.3 collective-permute-start
  162.7 11.1 %collective-permute-done = bf16[2,8,128,128]{3,2,1,0:T(8,128)(2,1)S(1)} collective-permute-done((bf16[2,8,128,128]{3,2,1,0:T(8,128)(2,1)}, bf16[2,8,128,128]{3,2,1,0:T(8,128)(2,1)S(1)}, u32[]{:S(2)}, u32[]{:S(2)}) %collective-permute-start) | collective-permute-done | bytes 524320 | tf_op jit(solution)/shard_map/while/body/eval_jaxpr/ppermute | solution.py:13
  174.9 4.3 collective-permute-start
  179.2 10.1 %collective-permute-done = bf16[2,8,128,128]{3,2,1,0:T(8,128)(2,1)S(1)} collective-permute-done((bf16[2,8,128,128]{3,2,1,0:T(8,128)(2,1)}, bf16[2,8,128,128]{3,2,1,0:T(8,128)(2,1)S(1)}, u32[]{:S(2)}, u32[]{:S(2)}) %collective-permute-start) | collective-permute-done | bytes 524320 | tf_op jit(solution)/shard_map/while/body/eval_jaxpr/ppermute | solution.py:13
  189.6 9.2 fusion.119
  198.8 17.2 %fusion.118 = f32[2,8,512,512]{3,2,1,0:T(8,128)} fusion(f32[2,512,8,128]{1,0,3,2:T(2,128)S(1)} %copy-done.14, f32[2,512,8,128]{1,0,3,2:T(2,128)S(1)} %copy-done.13), kind=kOutput, calls=%fused_computation.164 | convolution fusion | flops 6450839552 | bytes 25165824 | tf_op jit(solution)/shard_map/rthd,rshd->rhts/dot_general | solution.py:76
  216.0 23.7 %multiply_reduce_fusion.2 = (f32[2,512]{1,0:T(2,128)S(1)}, f32[2,512,8,128]{1,3,2,0:T(8,128)}) fusion(f32[2,512,8]{1,2,0:T(8,128)S(1)} %get-tuple-element.166, f32[2,8,128,512]{3,2,1,0:T(8,128)} %fusion.119, f32[2,512,8,128]{3,1,2,0:T(8,128)} %copy.119, f32[2,8,512,512]{3,2,1,0:T(8,128)} %fusion.118, f32[8,512,512]{2,1,0:T(8,128)} %multiply_exponential_fusion, ...), kind=kOutput, calls=%fused_computation.99 | convolution fusion | flops 6455032832 | bytes 38309888 | tf_op jit(solution)/shard_map/rhts,rshe->rthe/dot_general | solution.py:79
  239.7 7.5 copy.123
  247.3 6.6 reshape.339
  253.9 5.4 copy.159
  259.4 7.6 multiply_reduce_fusion.1
  267.0 20.9 %fusion.19 = f32[2,1024,2816]{2,1,0:T(8,128)} fusion(bf16[1,2,1024,2816]{3,2,1,0:T(8,128)(2,1)} %all-gather.9.cloned.1.call-done, f32[1024,1024]{1,0:T(8,128)} %get-tuple-element.159, f32[1024]{0:T(1024)S(1)} %get-tuple-element.149), kind=kOutput, calls=%fused_computation.29 | convolution fusion | flops 11813257216 | bytes 38801408 | tf_op jit(solution)/shard_map/nd,kdf->knf/dot_general | solution.py:219
  287.9 14.9 %fusion.41 = (bf16[1,1024,2816]{2,1,0:T(8,128)(2,1)}, bf16[1,1024,2816]{2,1,0:T(8,128)(2,1)}) fusion(f32[2,1024,2816]{2,1,0:T(8,128)} %fusion.19, bf16[1024,1024]{1,0:T(8,128)(2,1)S(1)} %bitcast.231, bf16[1,2816,1024]{2,1,0:T(8,128)(2,1)} %all-gather.11.cloned.1.call-done), kind=kOutput, calls=%fused_computation.52 | convolution fusion | flops 5922881536 | bytes 42467328 | tf_op jit(solution)/shard_map/nd,fd->nf/dot_general | solution.py:285
  302.9 20.3 %fusion.62 = (f32[1024]{0:T(1024)S(1)}, f32[1024,1024,1]{1,0,2:T(8,128)}) fusion(f32[1024,1024]{1,0:T(8,128)} %get-tuple-element.159, bf16[1,2,1024,2816]{3,2,1,0:T(8,128)(2,1)} %all-gather.9.cloned.1.call-done, bf16[1,1024,2816]{2,1,0:T(8,128)(2,1)} %get-tuple-element.140, bf16[1,1024,2816]{2,1,0:T(8,128)(2,1)} %get-tuple-element.139), kind=kOutput, calls=%fused_computation.79 | convolution fusion | flops 11819023360 | bytes 31461376 | tf_op jit(solution)/shard_map/knf,kdf->nd/dot_general | solution.py:293
  323.1 4.7 fusion.61
  327.9 7.2 multiply_reduce_fusion
  335.1 6.3 multiply_subtract_fusion
  341.4 6.6 reshape.344
  348.0 19.9 %fusion.8 = f32[2,8,128,512]{3,2,1,0:T(8,128)} fusion(f32[2,8,512,512]{3,2,1,0:T(8,128)} %fusion.118, f32[8,512,512]{2,1,0:T(8,128)} %multiply_exponential_fusion, pred[2,512,512]{2,1,0:T(8,128)(4,1)S(1)} %compare_and_fusion, f32[2,512,8,128]{1,0,3,2:T(2,128)} %reshape.344), kind=kOutput, calls=%fused_computation.12 | convolution fusion | flops 6450839552 | bytes 34078720 | tf_op jit(solution)/shard_map/rhts,rthe->rshe/dot_general | solution.py:119
  367.9 8.9 fusion.67
  376.8 16.0 %fusion.74 = f32[2,8,512,512]{3,2,1,0:T(8,128)} fusion(f32[2,512,8,128]{3,1,2,0:T(8,128)S(1)} %copy-done.5, f32[2,512,8,128]{1,0,3,2:T(2,128)S(1)} %copy-done.6), kind=kOutput, calls=%fused_computation.107 | convolution fusion | flops 6442450944 | bytes 25165824 | tf_op jit(solution)/shard_map/rthe,rshe->rhts/dot_general | solution.py:105
  392.8 5.9 fusion.98
  398.8 43.1 %while.23 = (s32[]{:T(128)}, f32[2,8,128,128]{3,2,1,0:T(8,128)S(1)}, f32[2,8,128,128]{3,2,1,0:T(8,128)S(1)}, f32[8]{0:T(128)S(1)}, pred[2]{0:T(512)(128)(4,1)S(1)}, /*index=5*/s32[]{:T(128)}, s32[]{:T(128)}) while((s32[]{:T(128)}, f32[2,8,128,128]{3,2,1,0:T(8,128)S(1)}, f32[2,8,128,128]{3,2,1,0:T(8,128)S(1)}, f32[8]{0:T(128)S(1)}, ...), condition=%wide.region_11.12_spmd.clone, body=%wide.region_10.11_spmd.clone.sunk | while | flops 1310739 | bytes 6291745 | solution.py:143
  401.1 13.0 %collective-permute-done.1 = bf16[2,8,128,128]{3,2,1,0:T(8,128)(2,1)S(1)} collective-permute-done((bf16[2,8,128,128]{3,2,1,0:T(8,128)(2,1)}, bf16[2,8,128,128]{3,2,1,0:T(8,128)(2,1)S(1)}, u32[]{:S(2)}, u32[]{:S(2)}) %collective-permute-start.1) | collective-permute-done | bytes 524320 | tf_op jit(solution)/shard_map/while/body/eval_jaxpr/ppermute | solution.py:13
  416.6 11.7 %collective-permute-done.1 = bf16[2,8,128,128]{3,2,1,0:T(8,128)(2,1)S(1)} collective-permute-done((bf16[2,8,128,128]{3,2,1,0:T(8,128)(2,1)}, bf16[2,8,128,128]{3,2,1,0:T(8,128)(2,1)S(1)}, u32[]{:S(2)}, u32[]{:S(2)}) %collective-permute-start.1) | collective-permute-done | bytes 524320 | tf_op jit(solution)/shard_map/while/body/eval_jaxpr/ppermute | solution.py:13
  430.7 10.8 %collective-permute-done.1 = bf16[2,8,128,128]{3,2,1,0:T(8,128)(2,1)S(1)} collective-permute-done((bf16[2,8,128,128]{3,2,1,0:T(8,128)(2,1)}, bf16[2,8,128,128]{3,2,1,0:T(8,128)(2,1)S(1)}, u32[]{:S(2)}, u32[]{:S(2)}) %collective-permute-start.1) | collective-permute-done | bytes 524320 | tf_op jit(solution)/shard_map/while/body/eval_jaxpr/ppermute | solution.py:13
  441.9 8.1 fusion.123
  450.0 4.9 fusion.56
  459.8 28.1 %fusion.11 = f32[2,8,128,512]{3,2,1,0:T(8,128)} fusion(f32[2,8,512,512]{3,2,1,0:T(8,128)} %fusion.74, f32[8,512,512]{2,1,0:T(8,128)} %multiply_exponential_fusion, pred[2,512,512]{2,1,0:T(8,128)(4,1)S(1)} %compare_and_fusion, f32[2,512,8,128]{1,0,3,2:T(2,128)} %squeeze.13), kind=kOutput, calls=%fused_computation.15 | convolution fusion | flops 6455033856 | bytes 34078720 | tf_op jit(solution)/shard_map/rhts,rshd->rthd/dot_general | solution.py:107
  487.8 8.5 fusion.58
  496.3 5.3 copy.128
  501.6 6.6 reshape.345
  508.2 21.7 %fusion.57 = f32[2,512,8,128]{1,3,2,0:T(8,128)} fusion(f32[2,8,128,512]{3,2,1,0:T(8,128)} %fusion.123, f32[2,8,512,512]{3,2,1,0:T(8,128)} %fusion.74, f32[8,512,512]{2,1,0:T(8,128)} %multiply_exponential_fusion, pred[2,512,512]{2,1,0:T(8,128)(4,1)S(1)} %compare_and_fusion, f32[2,512,8]{1,2,0:T(8,128)S(1)} %copy-done.28, f32[2,512,8,128]{1,0,3,2:T(2,128)} %squeeze.12), kind=kOutput, calls=%fused_computation.70 | convolution fusion | flops 6457131008 | bytes 38305792 | tf_op jit(solution)/shard_map/rhts,rthd->rshd/dot_general | solution.py:113
  529.9 7.5 copy.131
  537.4 6.6 reshape.346
  544.1 8.3 multiply_convert_fusion.2
  554.5 11.0 %convert_bitcast_fusion.1 = bf16[4,1024,1024]{1,2,0:T(8,128)(2,1)} fusion(bf16[1024,1024]{1,0:T(8,128)(2,1)S(1)} %copy-done.22, bf16[1,1024,1024]{1,2,0:T(8,128)(2,1)S(1)} %copy-done.19, bf16[1,1024,1024]{1,2,0:T(8,128)(2,1)S(1)} %copy-done.23, bf16[1,1024,1024]{1,2,0:T(8,128)(2,1)S(1)} %get-tuple-element.142, bf16[1,1024,1024]{1,2,0:T(8,128)(2,1)S(1)} %get-tuple-element.141), kind=kOutput, calls=%fused_computation.33 | convolution fusion | flops 8606711808 | bytes 18874368 | tf_op jit(solution)/shard_map/nd,kne->kde/dot_general | solution.py:330
  565.5 15.0 %copy.151 = bf16[4,1024,1024]{2,0,1:T(4,128)(2,1)} copy(bf16[4,1024,1024]{1,2,0:T(8,128)(2,1)} %convert_bitcast_fusion.1) | data formatting | bytes 16777216
  580.5 12.3 %copy.160 = bf16[128,8,4,1024]{3,1,2,0:T(8,128)(2,1)} copy(bf16[128,8,4,1024]{3,2,1,0:T(4,128)(2,1)} %bitcast.226) | data formatting | bytes 16777216
  592.8 19.1 %convert_bitcast_fusion = bf16[2,1024,2816]{1,2,0:T(8,128)(2,1)} fusion(bf16[1,1024,2816]{2,1,0:T(8,128)(2,1)} %get-tuple-element.140, bf16[1,1024,2816]{2,1,0:T(8,128)(2,1)} %get-tuple-element.139, f32[1024,1024]{1,0:T(8,128)} %get-tuple-element.159, f32[1024]{0:T(1024)S(1)} %get-tuple-element.149), kind=kOutput, calls=%fused_computation.28 | convolution fusion | flops 11824791552 | bytes 27267072 | tf_op jit(solution)/shard_map/nd,knf->kdf/dot_general | solution.py:290
  611.9 29.1 %copy.155 = bf16[2,1024,2816]{2,0,1:T(2,128)(2,1)} copy(bf16[2,1024,2816]{1,2,0:T(8,128)(2,1)} %convert_bitcast_fusion) | data formatting | bytes 23068672
  641.0 11.4 %copy.161 = bf16[128,8,2,2816]{3,1,2,0:T(8,128)(2,1)} copy(bf16[128,8,2,2816]{3,2,1,0:T(2,128)(2,1)} %bitcast.223) | data formatting | bytes 23068672
  654.0 15.9 %fusion.45 = bf16[2816,1024]{1,0:T(8,128)(2,1)} fusion(bf16[1024,1024]{1,0:T(8,128)(2,1)S(1)} %bitcast.232, f32[2,1024,2816]{2,1,0:T(8,128)} %fusion.19), kind=kOutput, calls=%fused_computation.56 | convolution fusion | flops 5914230784 | bytes 30932992 | tf_op jit(solution)/shard_map/nf,nd->fd/dot_general | solution.py:283
  676.2 76.9 %reduce-scatter.17.cloned.1.call-done = bf16[128,5632]{1,0:T(8,128)(2,1)} async-done(((bf16[1024,5632]{1,0:T(8,128)(2,1)}), bf16[128,5632]{1,0:T(8,128)(2,1)}) %reduce-scatter.17.cloned.1.call-update) | async-done | bytes 1441808
  753.1 3.4 reshape.364
  756.5 3.1 copy.156
  759.6 56.0 %reduce-scatter.11.cloned.1.call-done = bf16[352,1024]{1,0:T(8,128)(2,1)} async-done(((bf16[2816,1024]{1,0:T(8,128)(2,1)}), bf16[352,1024]{1,0:T(8,128)(2,1)}) %reduce-scatter.11.cloned.1.call-update) | async-done | bytes 720912 | tf_op jit(solution)/shard_map/reduce_scatter | solution.py:157
  815.7 15.1 %fusion.54 = (f32[1024]{0:T(1024)S(1)}, f32[1024,1024,1]{1,0,2:T(8,128)S(1)}) fusion(bf16[2,512,1024]{2,1,0:T(8,128)(2,1)S(1)} %copy-done.12, bf16[1,5,1024,1024]{2,3,1,0:T(8,128)(2,1)} %all-gather.7.cloned.1.call-done, bf16[1,1024,1024]{1,2,0:T(8,128)(2,1)} %get-tuple-element.147, bf16[1,1024,1024]{1,2,0:T(8,128)(2,1)} %stack_reshape.4, ...), kind=kOutput, calls=%fused_computation.65 | convolution fusion | flops 8605662208 | bytes 23072768 | tf_op jit(solution)/shard_map/kne,kde->nd/dot_general | solution.py:333
  834.4 13.7 %add_convert_fusion = bf16[1024,1024]{1,0:T(8,128)(2,1)} fusion(f32[1024,1024]{1,0:T(8,128)S(1)} %copy-done.17, bf16[1,2816,1024]{2,1,0:T(8,128)(2,1)} %all-gather.11.cloned.1.call-done, f32[2,1024,2816]{2,1,0:T(8,128)} %fusion.19), kind=kOutput, calls=%fused_computation.95 | convolution fusion | flops 5913444352 | bytes 35127296 | tf_op jit(solution)/shard_map/dot_general | solution.py:17
  848.1 103.7 %all-reduce.3.cloned.1.call-done = (bf16[1,2,128,2816]{2,3,1,0:T(8,128)(2,1)}, bf16[1,128,1024]{1,2,0:T(8,128)(2,1)}, bf16[4,128,1024]{1,2,0:T(8,128)(2,1)}, bf16[1,352,1024]{2,1,0:T(8,128)(2,1)}) async-done(((bf16[1,2,128,2816]{2,3,1,0:T(8,128)(2,1)}, bf16[1,128,1024]{1,2,0:T(8,128)(2,1)}, bf16[4,128,1024]{1,2,0:T(8,128)(2,1)}, bf16[1,352,1024]{2,1,0:T(8,128)(2,1)}), (bf16[1,2,128,2816]{2,3,1,0:T(8,128)(2,1)}, ...) | async-done | bytes 3473424 | tf_op jit(solution)/shard_map/psum | solution.py:164
  955.4 3.0 copy.141
  (153 shorter events, 44.4 us)
Async XLA Ops:
  7.2 71.3 %all-gather.7.cloned.1.call-start = ((), (), s32[]{:S(2)}) async-start(), calls=%async_computation.5 | async-start | bytes 11796480 | tf_op jit(solution)/shard_map/all_gather | solution.py:193
  10.0 7.0 copy-start.10
  10.0 256.9 %all-gather.9.cloned.1.call-start = ((), (), s32[]{:S(2)}) async-start(), calls=%async_computation.6 | async-start | bytes 12976128 | tf_op jit(solution)/shard_map/all_gather | solution.py:194
  13.3 274.6 %all-gather.11.cloned.1.call-start = ((), (), s32[]{:S(2)}) async-start(), calls=%async_computation.7 | async-start | bytes 6488064 | tf_op jit(solution)/shard_map/all_gather | solution.py:195
  15.7 3.6 copy-start.36
  15.7 3.6 copy-start.35
  15.7 654.9 %reduce-scatter.15.cloned.1.call-start = ((), (), s32[]{:S(2)}) async-start(), calls=%async_computation.9 | async-start | bytes 2359296
  17.5 1.7 copy-start.29
  26.6 105.7 %copy-start.27 = (f32[2,512,8]{1,2,0:T(8,128)}, f32[2,512,8]{1,2,0:T(8,128)S(1)}, u32[]{:S(2)}) copy-start(f32[2,512,8]{1,2,0:T(8,128)S(1)} %get-tuple-element.167) | copy-start | bytes 98308
  141.9 15.3 %collective-permute-start = (bf16[2,8,128,128]{3,2,1,0:T(8,128)(2,1)}, bf16[2,8,128,128]{3,2,1,0:T(8,128)(2,1)S(1)}, u32[]{:S(2)}, u32[]{:S(2)}) collective-permute-start(bf16[2,8,128,128]{3,2,1,0:T(8,128)(2,1)} %fusion.136), channel_id=1, source_target_pairs={{0,8},{8,16},{16,24},{1,9},{9,17},{17,25},{2,10},{10,18},{18,26},{... | collective-permute-start | bytes 1572872 | tf_op jit(solution)/shard_map/while/body/eval_jaxpr/ppermute | solution.py:13
  158.4 15.4 %collective-permute-start = (bf16[2,8,128,128]{3,2,1,0:T(8,128)(2,1)}, bf16[2,8,128,128]{3,2,1,0:T(8,128)(2,1)S(1)}, u32[]{:S(2)}, u32[]{:S(2)}) collective-permute-start(bf16[2,8,128,128]{3,2,1,0:T(8,128)(2,1)} %fusion.136), channel_id=1, source_target_pairs={{0,8},{8,16},{16,24},{1,9},{9,17},{17,25},{2,10},{10,18},{18,26},{... | collective-permute-start | bytes 1572872 | tf_op jit(solution)/shard_map/while/body/eval_jaxpr/ppermute | solution.py:13
  174.9 14.5 %collective-permute-start = (bf16[2,8,128,128]{3,2,1,0:T(8,128)(2,1)}, bf16[2,8,128,128]{3,2,1,0:T(8,128)(2,1)S(1)}, u32[]{:S(2)}, u32[]{:S(2)}) collective-permute-start(bf16[2,8,128,128]{3,2,1,0:T(8,128)(2,1)} %fusion.136), channel_id=1, source_target_pairs={{0,8},{8,16},{16,24},{1,9},{9,17},{17,25},{2,10},{10,18},{18,26},{... | collective-permute-start | bytes 1572872 | tf_op jit(solution)/shard_map/while/body/eval_jaxpr/ppermute | solution.py:13
  189.5 9.2 copy-start.8
  189.5 9.2 copy-start.31
  189.5 9.2 copy-start.33
  189.5 9.2 copy-start.13
  189.5 9.2 copy-start.14
  253.9 5.5 copy-start.11
  253.9 5.5 copy-start.16
  267.0 20.9 %copy-start.24 = (bf16[2,512,1024]{2,1,0:T(8,128)(2,1)S(1)}, bf16[2,512,1024]{2,1,0:T(8,128)(2,1)}, u32[]{:S(2)}) copy-start(bf16[2,512,1024]{2,1,0:T(8,128)(2,1)} %param.17) | copy-start | bytes 6291460
  323.1 4.7 copy-start
  327.8 7.2 copy-start.2
  367.9 8.9 copy-start.5
  367.9 8.9 copy-start.6
  376.8 16.0 %copy-start.1 = (f32[128,8,2,512]{3,1,2,0:T(8,128)S(1)}, f32[128,8,2,512]{3,1,2,0:T(8,128)}, u32[]{:S(2)}) copy-start(f32[128,8,2,512]{3,1,2,0:T(8,128)} %copy.159) | copy-start | bytes 12582916
  376.8 16.0 %copy-start.3 = (f32[1024,1024]{1,0:T(8,128)S(1)}, f32[1024,1024]{1,0:T(8,128)}, u32[]{:S(2)}) copy-start(f32[1024,1024]{1,0:T(8,128)} %copy-done.2) | copy-start | bytes 12582916
  392.8 5.9 copy-start.7
  392.8 5.9 copy-start.32
  392.8 5.9 copy-start.34
  399.8 14.3 %collective-permute-start.1 = (bf16[2,8,128,128]{3,2,1,0:T(8,128)(2,1)}, bf16[2,8,128,128]{3,2,1,0:T(8,128)(2,1)S(1)}, u32[]{:S(2)}, u32[]{:S(2)}) collective-permute-start(bf16[2,8,128,128]{3,2,1,0:T(8,128)(2,1)} %fusion.137), channel_id=1, source_target_pairs={{8,0},{16,8},{24,16},{9,1},{17,9},{25,17},{10,2},{18,10},{26,18},{... | collective-permute-start | bytes 1572872 | tf_op jit(solution)/shard_map/while/body/eval_jaxpr/ppermute | solution.py:13
  415.3 13.0 %collective-permute-start.1 = (bf16[2,8,128,128]{3,2,1,0:T(8,128)(2,1)}, bf16[2,8,128,128]{3,2,1,0:T(8,128)(2,1)S(1)}, u32[]{:S(2)}, u32[]{:S(2)}) collective-permute-start(bf16[2,8,128,128]{3,2,1,0:T(8,128)(2,1)} %fusion.137), channel_id=1, source_target_pairs={{8,0},{16,8},{24,16},{9,1},{17,9},{25,17},{10,2},{18,10},{26,18},{... | collective-permute-start | bytes 1572872 | tf_op jit(solution)/shard_map/while/body/eval_jaxpr/ppermute | solution.py:13
  429.5 12.1 %collective-permute-start.1 = (bf16[2,8,128,128]{3,2,1,0:T(8,128)(2,1)}, bf16[2,8,128,128]{3,2,1,0:T(8,128)(2,1)S(1)}, u32[]{:S(2)}, u32[]{:S(2)}) collective-permute-start(bf16[2,8,128,128]{3,2,1,0:T(8,128)(2,1)} %fusion.137), channel_id=1, source_target_pairs={{8,0},{16,8},{24,16},{9,1},{17,9},{25,17},{10,2},{18,10},{26,18},{... | collective-permute-start | bytes 1572872 | tf_op jit(solution)/shard_map/while/body/eval_jaxpr/ppermute | solution.py:13
  441.9 8.1 copy-start.15
  441.9 8.1 copy-start.18
  441.9 8.1 copy-start.28
  459.8 28.1 %copy-start.9 = (f32[2,8,128,128]{3,2,1,0:T(8,128)S(1)}, f32[2,8,128,128]{3,2,1,0:T(8,128)}, u32[]{:S(2)}) copy-start(f32[2,8,128,128]{3,2,1,0:T(8,128)} %copy-done.8) | copy-start | bytes 3145732
  544.0 10.4 %copy-start.19 = (bf16[1,1024,1024]{1,2,0:T(8,128)(2,1)S(1)}, bf16[1,1024,1024]{1,2,0:T(8,128)(2,1)}, u32[]{:S(2)}) copy-start(bf16[1,1024,1024]{1,2,0:T(8,128)(2,1)} %get-tuple-element.147) | copy-start | bytes 6291460
  544.0 128.4 %reduce-scatter.13.cloned.1.call-start = ((), (), s32[]{:S(2)}) async-start(), calls=%async_computation.8 | async-start | bytes 9437184
  544.1 10.4 %copy-start.22 = (bf16[1024,1024]{1,0:T(8,128)(2,1)S(1)}, bf16[1024,1024]{1,0:T(8,128)(2,1)}, u32[]{:S(2)}) copy-start(bf16[1024,1024]{1,0:T(8,128)(2,1)} %fusion.65) | copy-start | bytes 6291460
  544.1 10.4 %copy-start.23 = (bf16[1,1024,1024]{1,2,0:T(8,128)(2,1)S(1)}, bf16[1,1024,1024]{1,2,0:T(8,128)(2,1)}, u32[]{:S(2)}) copy-start(bf16[1,1024,1024]{1,2,0:T(8,128)(2,1)} %stack_reshape.4) | copy-start | bytes 6291460
  552.4 1.4 copy-start.20
  552.4 2.0 copy-start.21
  592.7 160.4 %reduce-scatter.17.cloned.1.call-start = ((), (), s32[]{:S(2)}) async-start(), calls=%async_computation.10 | async-start | bytes 12976128
  652.4 1.6 copy-start.25
  652.4 163.2 %reduce-scatter.11.cloned.1.call-start = ((), (), s32[]{:S(2)}) async-start(), calls=%async_computation.4 | async-start | bytes 6488064 | tf_op jit(solution)/shard_map/reduce_scatter | solution.py:157
  669.9 0.7 copy-start.30
  670.0 281.8 %all-reduce.3.cloned.1.call-start = ((), (), s32[]{:S(2)}) async-start(), calls=%async_computation.11 | async-start | bytes 6946816 | tf_op jit(solution)/shard_map/psum | solution.py:164
  676.2 139.5 %copy-start.12 = (bf16[2,512,1024]{2,1,0:T(8,128)(2,1)S(1)}, bf16[2,512,1024]{2,1,0:T(8,128)(2,1)}, u32[]{:S(2)}) copy-start(bf16[2,512,1024]{2,1,0:T(8,128)(2,1)} %param.11) | copy-start | bytes 6291460
  815.7 15.1 %copy-start.4 = (f32[1024,1024]{1,0:T(8,128)S(1)}, f32[1024,1024]{1,0:T(8,128)}, u32[]{:S(2)}) copy-start(f32[1024,1024]{1,0:T(8,128)} %copy-done.2) | copy-start | bytes 12582916
  830.9 3.5 copy-start.17
  953.3 5.1 copy-start.26
Sparse Core Ops, SparseCore 0:
  10.4 67.9 all-gather.6
  80.9 67.6 all-gather.8
  150.5 43.3 all-gather.10
  544.1 40.0 reduce-scatter.14
  592.9 70.0 reduce-scatter.12
  666.3 86.8 reduce-scatter.16
  756.6 59.0 reduce-scatter.10
  819.1 132.6 all-reduce.2
where the time goes:
time: 978 us; the launch traced here: 967 us
  waiting for transfers between devices  357 us (37%)
  matrix products  343 us (35%)
  local copies, waits for them, and re-layouts  187 us (19%)
  other arithmetic  47.8 us (5%)
  starting transfers between devices  16.2 us (2%)
  between operations  15.2 us (2%)
    psum x1, waiting for transfers between devices, reduce_grads(): lax.psum(pieces[2].astype(jnp.bfloat16), 'seq').astype(jnp.float32)  104 us
    unnamed x89, local copies, waits for them, and re-layouts  98 us
    unnamed x11, waiting for transfers between devices  77.1 us
    ppermute x6, waiting for transfers between devices, passed_along(): lax.ppermute(value, axis, [(source, source + steps) for source in range(l...  68.6 us
    reduce_scatter x1, waiting for transfers between devices, reduce_grads(): lax.psum_scatter(terms[3].astype(jnp.bfloat16), 'dp', scatter_dimension=0...  56 us
    all_gather x1, waiting for transfers between devices, local(): mixer_full = lax.all_gather(gathered[0], 'dp', axis=1, tiled=True)  51.9 us
    dot_general x1, matrix products, block_back(): jnp.einsum('rhts,rshd->rthd', score_grad, per_head_keys, precision=FULL_P...  28.1 us
    dot_general x1, matrix products, block_out(): jnp.einsum('rhts,rshe->rthe', scores, per_head_values, precision=FULL_PRE...  23.7 us
  transfers between devices with their start and end apart: 14, of which 10 were waited for; matrix products, arithmetic and copies ran while one was open for 36% of the time, Pallas kernels for 0%

commit v1 on v0

v1 whole, which is shorter than its diff:
```python
import functools

import jax
import jax.numpy as jnp
from jax import lax
from jax.experimental import pallas as pl
from jax.experimental.pallas import tpu as pltpu
from jax.sharding import PartitionSpec as P

EPS = 1e-06
LONGEST_DOC = 1024
LOW = jnp.bfloat16
WIDE = jnp.float32
VMEM_BYTES = 60 * 1024 * 1024


def dot(left, right, left_dim, right_dim):
    return lax.dot_general(
        left, right, (((left_dim,), (right_dim,)), ((), ())), preferred_element_type=WIDE
    )


def swish(value_rows):
    return value_rows * jax.nn.sigmoid(value_rows)


def swish_slope(value_rows):
    gate = jax.nn.sigmoid(value_rows)
    return gate * (1.0 + value_rows * (1.0 - gate))


def doc_bounds(lengths_ref, row, docs, start, count):
    last = start + count - 1
    end = jnp.int32(0)
    last_from = jnp.int32(0)
    entry_to = jnp.int32(0)
    found = jnp.int32(0)
    for index in range(docs):
        end = end + lengths_ref[row, index]
        last_from = jnp.where(end <= last, end, last_from)
        ends_later = end > start - 1
        entry_to = jnp.where(ends_later & (found == 0), end, entry_to)
        found = jnp.where(ends_later, 1, found)
    return last_from - start, entry_to - start


def doc_starts(lengths_ref, row, docs, start, places):
    end = jnp.int32(0)
    begin = jnp.full(places.shape, -start, jnp.int32)
    for index in range(docs):
        end = end + lengths_ref[row, index]
        begin = jnp.where(places >= end - start, end - start, begin)
    return begin


def state_kernel(docs, start_ref, rates_ref, lengths_ref, keys_ref, values_ref, state_ref):
    count, head_dim = keys_ref.shape[1], state_ref.shape[-1]
    last_from, _ = doc_bounds(lengths_ref, pl.program_id(0), docs, start_ref[0], count)
    places = lax.broadcasted_iota(jnp.int32, (count, 1), 0)
    for head in range(state_ref.shape[1]):
        span = slice(head * head_dim, (head + 1) * head_dim)
        leaving = jnp.where(
            places >= last_from,
            jnp.exp(-rates_ref[head] * (count - 1 - places).astype(WIDE)),
            0.0,
        )
        keys = (swish(keys_ref[0, :, span].astype(WIDE)) * leaving).astype(LOW)
        state_ref[0, head] = dot(keys, values_ref[0, :, span], 0, 0).astype(LOW)


def mixing_kernel(
    docs, tile, start_ref, rates_ref, lengths_ref, q_ref, k_ref, v_ref, out_ref, mask_ref
):
    count, features = q_ref.shape[1], q_ref.shape[2]
    heads = rates_ref.shape[0]
    head_dim = features // heads
    places = lax.broadcasted_iota(jnp.int32, (count, 1), 0)
    begin = doc_starts(lengths_ref, pl.program_id(0), docs, start_ref[0], places)
    across = lax.broadcasted_iota(jnp.int32, (count, count), 1)
    mask_ref[...] = ((across <= places) & (across >= begin)).astype(WIDE)
    centred = (places - count // 2).astype(WIDE)
    for head in range(heads):
        span = slice(head * head_dim, (head + 1) * head_dim)
        rate = rates_ref[head]
        queries = (swish(q_ref[0, :, span].astype(WIDE)) * jnp.exp(-rate * centred)).astype(LOW)
        keys = (swish(k_ref[0, :, span].astype(WIDE)) * jnp.exp(rate * centred)).astype(LOW)
        values = v_ref[0, :, span]
        for first in range(0, count, tile):
            upto = first + tile
            scores = dot(queries[first:upto], keys[:upto], 1, 1) * mask_ref[first:upto, :upto]
            out_ref[0, first:upto, span] = dot(scores.astype(LOW), values[:upto], 1, 0).astype(
                out_ref.dtype
            )


def finish_kernel(
    docs,
    start_ref,
    rates_ref,
    lengths_ref,
    q_ref,
    u_ref,
    part_ref,
    state_ref,
    mixed_ref,
    gated_ref,
    whole_ref,
):
    count, features = q_ref.shape[1], q_ref.shape[2]
    heads = rates_ref.shape[0]
    head_dim = features // heads
    _, entry_to = doc_bounds(lengths_ref, pl.program_id(0), docs, start_ref[0], count)
    places = lax.broadcasted_iota(jnp.int32, (count, 1), 0)
    for head in range(heads):
        span = slice(head * head_dim, (head + 1) * head_dim)
        entry = jnp.where(
            places < entry_to, jnp.exp(-rates_ref[head] * (places + 1).astype(WIDE)), 0.0
        )
        queries = (swish(q_ref[0, :, span].astype(WIDE)) * entry).astype(LOW)
        whole_ref[:, span] = part_ref[0, :, span].astype(WIDE) + dot(
            queries, state_ref[0, head], 1, 0
        )
    mixed = whole_ref[...]
    factor = lax.rsqrt(jnp.mean(mixed * mixed, axis=-1, keepdims=True) + EPS)
    mixed_ref[0] = mixed.astype(LOW)
    gated_ref[0] = (mixed * factor * u_ref[0].astype(WIDE)).astype(LOW)


def back_gate_kernel(
    docs,
    start_ref,
    rates_ref,
    lengths_ref,
    q_ref,
    u_ref,
    mixed_ref,
    dgated_ref,
    dmixed_ref,
    du_ref,
    grad_ref,
):
    count, features = q_ref.shape[1], q_ref.shape[2]
    heads = rates_ref.shape[0]
    head_dim = features // heads
    mixed = mixed_ref[0].astype(WIDE)
    factor = lax.rsqrt(jnp.mean(mixed * mixed, axis=-1, keepdims=True) + EPS)
    dgated = dgated_ref[0].astype(WIDE)
    du_ref[0] = (dgated * mixed * factor).astype(LOW)
    upstream = dgated * u_ref[0].astype(WIDE)
    inner = jnp.sum(upstream * mixed, axis=-1, keepdims=True)
    dmixed_ref[0] = (
        factor * upstream - (factor * factor * factor / features * inner) * mixed
    ).astype(LOW)
    _, entry_to = doc_bounds(lengths_ref, pl.program_id(0), docs, start_ref[0], count)
    places = lax.broadcasted_iota(jnp.int32, (count, 1), 0)
    for head in range(heads):
        span = slice(head * head_dim, (head + 1) * head_dim)
        entry = jnp.where(
            places < entry_to, jnp.exp(-rates_ref[head] * (places + 1).astype(WIDE)), 0.0
        )
        queries = (swish(q_ref[0, :, span].astype(WIDE)) * entry).astype(LOW)
        grad_ref[0, head] = dot(queries, dmixed_ref[0, :, span], 0, 0).astype(LOW)


def back_mixing_kernel(
    docs,
    tile,
    start_ref,
    rates_ref,
    lengths_ref,
    q_ref,
    k_ref,
    v_ref,
    dmixed_ref,
    state_ref,
    dq_ref,
    dk_ref,
    dv_ref,
    mask_ref,
    turned_ref,
):
    count, features = q_ref.shape[1], q_ref.shape[2]
    heads = rates_ref.shape[0]
    head_dim = features // heads
    row = pl.program_id(0)
    start = start_ref[0]
    _, entry_to = doc_bounds(lengths_ref, row, docs, start, count)
    places = lax.broadcasted_iota(jnp.int32, (count, 1), 0)
    begin = doc_starts(lengths_ref, row, docs, start, places)
    across = lax.broadcasted_iota(jnp.int32, (count, count), 1)
    mask_ref[...] = ((across <= places) & (across >= begin)).astype(WIDE)
    flat = lax.broadcasted_iota(jnp.int32, (1, count), 1)
    begin = doc_starts(lengths_ref, row, docs, start, flat)
    down = lax.broadcasted_iota(jnp.int32, (count, count), 0)
    turned_ref[...] = ((down <= flat) & (down >= begin)).astype(WIDE)
    centred = (places - count // 2).astype(WIDE)
    for head in range(heads):
        span = slice(head * head_dim, (head + 1) * head_dim)
        rate = rates_ref[head]
        query_decay, key_decay = jnp.exp(-rate * centred), jnp.exp(rate * centred)
        entry = jnp.where(places < entry_to, jnp.exp(-rate * (places + 1).astype(WIDE)), 0.0)
        query_pre = q_ref[0, :, span].astype(WIDE)
        queries = (swish(query_pre) * query_decay).astype(LOW)
        keys = (swish(k_ref[0, :, span].astype(WIDE)) * key_decay).astype(LOW)
        values = v_ref[0, :, span]
        upstream = dmixed_ref[0, :, span]
        slope = swish_slope(query_pre)
        for first in range(0, count, tile):
            upto = first + tile
            grads = dot(upstream[first:upto], values[:upto], 1, 1) * mask_ref[first:upto, :upto]
            dq = dot(grads.astype(LOW), keys[:upto], 1, 0) * query_decay[first:upto]
            carried = dot(upstream[first:upto], state_ref[0, head], 1, 1) * entry[first:upto]
            dq_ref[0, first:upto, span] = ((dq + carried) * slope[first:upto]).astype(LOW)
            turned = turned_ref[first:upto, first:]
            grads = dot(values[first:upto], upstream[first:], 1, 1) * turned
            dk = dot(grads.astype(LOW), queries[first:], 1, 0) * key_decay[first:upto]
            dk_ref[0, first:upto, span] = dk.astype(LOW)
            scores = dot(keys[first:upto], queries[first:], 1, 1) * turned
            dv_ref[0, first:upto, span] = dot(scores.astype(LOW), upstream[first:], 1, 0).astype(LOW)


def back_finish_kernel(
    docs,
    start_ref,
    rates_ref,
    lengths_ref,
    k_ref,
    v_ref,
    dk_part_ref,
    dv_part_ref,
    grad_ref,
    dk_ref,
    dv_ref,
):
    count, features = k_ref.shape[1], k_ref.shape[2]
    heads = rates_ref.shape[0]
    head_dim = features // heads
    last_from, _ = doc_bounds(lengths_ref, pl.program_id(0), docs, start_ref[0], count)
    places = lax.broadcasted_iota(jnp.int32, (count, 1), 0)
    for head in range(heads):
        span = slice(head * head_dim, (head + 1) * head_dim)
        leaving = jnp.where(
            places >= last_from,
            jnp.exp(-rates_ref[head] * (count - 1 - places).astype(WIDE)),
            0.0,
        )
        key_pre = k_ref[0, :, span].astype(WIDE)
        grad = grad_ref[0, head]
        dk = dot(v_ref[0, :, span], grad, 1, 1) * leaving + dk_part_ref[0, :, span].astype(WIDE)
        dk_ref[0, :, span] = (dk * swish_slope(key_pre)).astype(LOW)
        keys = (swish(key_pre) * leaving).astype(LOW)
        dv = dot(keys, grad, 1, 0) + dv_part_ref[0, :, span].astype(WIDE)
        dv_ref[0, :, span] = dv.astype(LOW)


def row_call(kernel, scalars, inputs, outputs, scratch, flops):
    rows = inputs[0].shape[0]

    def spec(array):
        rest = len(array.shape) - 1
        return pl.BlockSpec((1, *array.shape[1:]), lambda i, *_: (i,) + (0,) * rest)

    size = sum(a.size * a.dtype.itemsize for a in inputs)
    size += sum(o.size * o.dtype.itemsize for o in outputs)
    return pl.pallas_call(
        kernel,
        out_shape=outputs,
        grid_spec=pltpu.PrefetchScalarGridSpec(
            num_scalar_prefetch=len(scalars),
            grid=(rows,),
            in_specs=[spec(a) for a in inputs],
            out_specs=[spec(o) for o in outputs],
            scratch_shapes=scratch,
        ),
        compiler_params=pltpu.CompilerParams(vmem_limit_bytes=VMEM_BYTES),
        cost_estimate=pl.CostEstimate(flops=flops, bytes_accessed=size, transcendentals=0),
    )(*scalars, *inputs)


def passed_along(value, steps):
    count = lax.axis_size("seq")
    leading, last = max(0, -steps), min(count, count - steps)
    return lax.ppermute(value, "seq", [(source, source + steps) for source in range(leading, last)])


def carried(local_state, passing, tokens, steps):
    hops = min((LONGEST_DOC - 2) // tokens + 1, lax.axis_size("seq") - 1)
    message, total = local_state, jnp.zeros(local_state.shape, WIDE)
    for hop in range(hops):
        received = passed_along(message, steps)
        total = total + received.astype(WIDE)
        message = (passing[..., None, None] * received.astype(WIDE)).astype(LOW)
    return total.astype(LOW)


def place_kernel(order_ref, *refs):
    count = len(refs) - 4
    pieces, out_ref, whole_ref, in_sem, out_sem = refs[:count], *refs[count:]
    rows = pieces[0].shape[1]

    def into(index):
        at = pl.ds(pl.multiple_of(order_ref[index] * rows, rows), rows)
        return pltpu.make_async_copy(pieces[index], whole_ref.at[:, at, :], in_sem.at[index])

    def out(index):
        at = pl.ds(pl.multiple_of(order_ref[index] * rows, rows), rows)
        return pltpu.make_async_copy(
            whole_ref.at[:, at, :], out_ref.at[:, at, :], out_sem.at[index]
        )

    for index in range(count):
        into(index).start()
    for index in range(count):
        into(index).wait()
        out(index).start()
    for index in range(count):
        out(index).wait()


def placed(pieces, order):
    count, (layers, rows, columns) = len(pieces), pieces[0].shape
    shape = (layers, count * rows, columns)
    size = count * pieces[0].size * pieces[0].dtype.itemsize
    return pl.pallas_call(
        place_kernel,
        out_shape=jax.ShapeDtypeStruct(shape, pieces[0].dtype),
        grid_spec=pltpu.PrefetchScalarGridSpec(
            num_scalar_prefetch=1,
            grid=(),
            in_specs=[pl.BlockSpec(memory_space=pl.ANY)] * count,
            out_specs=pl.BlockSpec(memory_space=pl.ANY),
            scratch_shapes=[
                pltpu.VMEM(shape, pieces[0].dtype),
                pltpu.SemaphoreType.DMA((count,)),
                pltpu.SemaphoreType.DMA((count,)),
            ],
        ),
        compiler_params=pltpu.CompilerParams(vmem_limit_bytes=VMEM_BYTES),
        cost_estimate=pl.CostEstimate(flops=0, bytes_accessed=2 * size, transcendentals=0),
    )(order, *pieces)


def side_steps(device):
    return (2, 4) if device % 2 == 0 else (4, 2)


def moved(value, kind):
    count = lax.axis_size("dp")
    if kind == "core":
        pairs = [(device, device ^ 1) for device in range(count)]
    else:
        pairs = [(device, device ^ side_steps(device)[kind]) for device in range(count)]
    return lax.ppermute(value, "dp", pairs)


def block_order():
    device = lax.axis_index("dp")
    table = []
    for index in range(8):
        row = []
        for mine in (index, index ^ 1):
            first, second = side_steps(mine)
            row += [mine, mine ^ first, mine ^ second, mine ^ first ^ second]
        table.append(row)
    return jnp.asarray(table, jnp.int32)[device]


def gathered(piece):
    if lax.axis_size("dp") != 8:
        return lax.all_gather(piece, "dp", axis=1, tiled=True)
    first = moved(piece, 0)
    second = moved(piece, 1)
    across = moved(first, 1)
    mine = [piece, first, second, across]
    other = [moved(part, "core") for part in mine]
    return placed(mine + other, block_order())


def order_kernel(order_ref, in_ref, out_ref):
    out_ref[...] = in_ref[...]


def ordered(value, order):
    count, (tokens, features) = order.shape[0], value.shape
    width = features // count
    return pl.pallas_call(
        order_kernel,
        out_shape=jax.ShapeDtypeStruct(value.shape, value.dtype),
        grid_spec=pltpu.PrefetchScalarGridSpec(
            num_scalar_prefetch=1,
            grid=(count,),
            in_specs=[pl.BlockSpec((tokens, width), lambda i, order: (0, order[i]))],
            out_specs=pl.BlockSpec((tokens, width), lambda i, order: (0, i)),
        ),
        cost_estimate=pl.CostEstimate(
            flops=0, bytes_accessed=2 * value.size * 2, transcendentals=0
        ),
    )(order, value)


def over_seq(value):
    count = lax.axis_size("seq")
    if count % 2:
        return lax.psum(value, "seq")
    place = lax.axis_index("seq")
    total = value
    half = count // 2
    for step in range(half - 1):
        pairs = [(step, step + 1), (count - 1 - step, count - 2 - step)]
        total = (total.astype(WIDE) + lax.ppermute(total, "seq", pairs).astype(WIDE)).astype(LOW)
    pairs = [(half - 1, half), (half, half - 1)]
    total = (total.astype(WIDE) + lax.ppermute(total, "seq", pairs).astype(WIDE)).astype(LOW)
    for step in reversed(range(half - 1)):
        pairs = [(step + 1, step), (count - 2 - step, count - 1 - step)]
        received = lax.ppermute(total, "seq", pairs)
        outside = (place == step) | (place == count - 1 - step)
        total = jnp.where(outside, received, total)
    return total


def weight_gradient(left, right):
    return jnp.einsum("nd,nf->df", left, right, preferred_element_type=WIDE)


def kept_blocks(left_ordered, right):
    half = left_ordered.shape[1] // 2
    received = moved(weight_gradient(left_ordered[:, half:], right).astype(LOW), "core")
    kept = (weight_gradient(left_ordered[:, :half], right) + received.astype(WIDE)).astype(LOW)
    return kept.reshape(4, half // 4, right.shape[1])


def kept_blocks_of_rows(term, order):
    term = term.reshape(8, -1, term.shape[-1])
    blocks = [lax.dynamic_index_in_dim(term, order[i], 0, keepdims=False) for i in range(8)]
    received = moved(jnp.stack(blocks[4:]).astype(LOW), "core")
    return [
        (blocks[i].astype(WIDE) + received[i].astype(WIDE)).astype(LOW) for i in range(4)
    ]


def scattered(members):
    own, first, second, across = (jnp.stack([m[i] for m in members]) for i in range(4))
    from_across = moved(across, 0)
    from_first = moved(first, 0)
    second = (second.astype(WIDE) + from_across.astype(WIDE)).astype(LOW)
    from_second = moved(second, 1)
    own = own.astype(WIDE) + from_first.astype(WIDE) + from_second.astype(WIDE)
    return over_seq(own.astype(LOW)).astype(WIDE)


def scattered_plainly(members):
    part = lax.psum_scatter(
        jnp.stack(members).astype(LOW), "dp", scatter_dimension=1, tiled=True
    )
    return over_seq(part).astype(WIDE)


def product(left, right):
    return jnp.dot(left, right, preferred_element_type=WIDE)


def norm_factor(value_rows):
    return lax.rsqrt(jnp.mean(value_rows * value_rows, axis=-1, keepdims=True) + EPS)


def norm_back(value_rows, factor, upstream):
    features = value_rows.shape[-1]
    inner_sum = jnp.sum(upstream * value_rows, axis=-1, keepdims=True)
    return factor * upstream - factor * factor * factor / features * value_rows * inner_sum


def local(
    hidden_in,
    mixer_weights,
    channel_in_weights,
    channel_out_weights,
    decay_rates,
    doc_lengths,
    out_cotangent,
):
    rows, tokens, features = hidden_in.shape
    heads = decay_rates.shape[1]
    head_dim = features // heads
    docs = doc_lengths.shape[1]
    count = rows * tokens
    tile = min(256, tokens)
    rates = decay_rates[0]
    start = lax.axis_index("seq") * jnp.asarray(tokens, jnp.int32)
    scalars = (start[None], rates, doc_lengths)
    ends = jnp.cumsum(doc_lengths, axis=1, dtype=jnp.int32)
    doc_before = jnp.sum((ends <= start - 1).astype(jnp.int32), axis=1)
    doc_last = jnp.sum((ends <= start + tokens - 1).astype(jnp.int32), axis=1)
    passing = jnp.where(
        (doc_before == doc_last)[:, None], jnp.exp(-rates * tokens)[None, :], 0.0
    )
    by_row = (rows, tokens, features)
    activation = jax.ShapeDtypeStruct(by_row, LOW)
    states = jax.ShapeDtypeStruct((rows, heads, head_dim, head_dim), LOW)

    by_hand = lax.axis_size("dp") == 8
    order = block_order() if by_hand else None
    scatter = scattered if by_hand else scattered_plainly

    def members(left, rights):
        if not by_hand:
            return [weight_gradient(left, right) for right in rights]
        left = ordered(left, order)
        return [kept_blocks(left, right) for right in rights]

    def gradients(left, rights):
        return scatter(members(left, rights))

    mixer = mixer_weights[0].astype(LOW)
    key_value = gathered(mixer[1:3])
    query_gate = gathered(jnp.stack([mixer[0], mixer[3]]))
    out_proj = gathered(mixer[4:5])[0]
    channel = gathered(channel_in_weights[0].astype(LOW))
    down = gathered(channel_out_weights.astype(LOW))[0]

    resid = hidden_in.astype(WIDE).reshape(count, features)
    factor_in = norm_factor(resid)
    normed = (resid * factor_in).astype(LOW)
    keys = product(normed, key_value[0]).astype(LOW).reshape(by_row)
    values = product(normed, key_value[1]).astype(LOW).reshape(by_row)
    local_state = row_call(
        functools.partial(state_kernel, docs), scalars, [keys, values], [states], [], 2 * count * features * head_dim
    )[0]
    state_in = carried(local_state, passing, tokens, 1)
    queries = product(normed, query_gate[0]).astype(LOW).reshape(by_row)
    gates = product(normed, query_gate[1]).astype(LOW).reshape(by_row)
    square = [pltpu.VMEM((tokens, tokens), WIDE)]
    part = row_call(
        functools.partial(mixing_kernel, docs, tile),
        scalars,
        [queries, keys, values],
        [activation],
        square,
        4 * count * features * tokens,
    )[0]
    mixed, gated = row_call(
        functools.partial(finish_kernel, docs),
        scalars,
        [queries, gates, part, state_in],
        [activation, activation],
        [pltpu.VMEM((tokens, features), WIDE)],
        2 * count * features * head_dim,
    )
    gated_rows = gated.reshape(count, features)
    after_mixer = resid + product(gated_rows, out_proj)
    factor_two = norm_factor(after_mixer)
    normed_two = (after_mixer * factor_two).astype(LOW)
    first = product(normed_two, channel[0]).astype(LOW)
    second = product(normed_two, channel[1]).astype(LOW)
    glu = (first.astype(WIDE) * second.astype(WIDE)).astype(LOW)
    block_output = (after_mixer + product(glu, down)).astype(LOW).reshape(by_row)

    branch = out_cotangent.reshape(count, features)
    glu_grad = jnp.einsum("nd,fd->nf", branch, down, preferred_element_type=WIDE)
    first_grad = (glu_grad * second.astype(WIDE)).astype(LOW)
    second_grad = (glu_grad * first.astype(WIDE)).astype(LOW)
    down_term = jnp.einsum("nf,nd->fd", glu, branch, preferred_element_type=WIDE)
    if by_hand:
        down_gradient = scattered([kept_blocks_of_rows(down_term.astype(LOW), order)])
    else:
        down_gradient = scattered_plainly([down_term])
    two_grad = jnp.einsum("nf,df->nd", first_grad, channel[0], preferred_element_type=WIDE)
    two_grad += jnp.einsum("nf,df->nd", second_grad, channel[1], preferred_element_type=WIDE)
    channel_gradient = gradients(normed_two, (first_grad, second_grad))
    upstream_mid = branch.astype(WIDE) + norm_back(after_mixer, factor_two, two_grad)
    middle = upstream_mid.astype(LOW)
    gated_grad = jnp.einsum("ne,de->nd", middle, out_proj, preferred_element_type=WIDE).astype(LOW)
    out_members = members(gated_rows, (middle,))
    mixed_grad, gate_grad, local_grad = row_call(
        functools.partial(back_gate_kernel, docs),
        scalars,
        [queries, gates, mixed, gated_grad.reshape(by_row)],
        [activation, activation, states],
        [],
        2 * count * features * head_dim,
    )
    state_grad = carried(local_grad, passing, tokens, -1)
    query_grad, key_part, value_part = row_call(
        functools.partial(back_mixing_kernel, docs, tile),
        scalars,
        [queries, keys, values, mixed_grad, state_in],
        [activation, activation, activation],
        square * 2,
        12 * count * features * tokens,
    )
    key_grad, value_grad = row_call(
        functools.partial(back_finish_kernel, docs),
        scalars,
        [keys, values, key_part, value_part, state_grad],
        [activation, activation],
        [],
        4 * count * features * head_dim,
    )
    grads = [
        g.reshape(count, features) for g in (query_grad, key_grad, value_grad, gate_grad)
    ]
    weights = (query_gate[0], key_value[0], key_value[1], query_gate[1])
    one_grad = sum(
        jnp.einsum("ne,de->nd", g, w, preferred_element_type=WIDE) for g, w in zip(grads, weights)
    )
    upstream = upstream_mid + norm_back(resid, factor_in, one_grad)
    outer = scatter(members(normed, grads[3:]) + out_members)
    inner = scatter(members(normed, grads[:3]))
    mixer_gradient = jnp.concatenate([inner, outer])
    return (
        block_output,
        upstream.reshape(by_row),
        mixer_gradient[None],
        channel_gradient[None],
        down_gradient,
    )


def solution(mesh):
    in_specs = (
        P("dp", "seq", None),
        P(None, None, "dp", None),
        P(None, None, "dp", None),
        P(None, "dp", None),
        P(),
        P("dp", None),
        P("dp", "seq", None),
    )
    out_specs = (
        P("dp", "seq", None),
        P("dp", "seq", None),
        P(None, None, "dp", None),
        P(None, None, "dp", None),
        P(None, "dp", None),
    )
    return jax.shard_map(local, mesh=mesh, in_specs=in_specs, out_specs=out_specs, check_vma=False)
```

time: 978 us -> 614 us (0.63)
  waiting for transfers between devices: 357 us -> 176 us
  matrix products: 343 us -> 166 us
  local copies, waits for them, and re-layouts: 187 us -> 14.9 us
  Pallas kernels: 0 us -> 103 us
  starting transfers between devices: 16.2 us -> 79.9 us
    dot_general x24 -> x31, matrix products: 343 us -> 166 us  [the longest x8 57.5 us: product(): return jnp.dot(left, right, preferred_element_type=WIDE)]
    ppermute x6 -> x71, waiting for transfers between devices: 68.6 us -> 176 us  [the longest x55 82 us: moved(): return lax.ppermute(value, 'dp', pairs)]
    psum x1 -> x0, waiting for transfers between devices: 104 us -> none  [reduce_grads(): lax.psum(pieces[2].astype(jnp.bfloat16), 'seq').astype(jnp.float32)]
    pallas_call x0 -> x14, Pallas kernels: none -> 103 us  [the longest x6 56.8 us: row_call(): pl.pallas_call(kernel, out_shape=outputs, grid_spec=pltpu.PrefetchScalarG...]
    unnamed x89 -> x109, local copies, waits for them, and re-layouts: 98 us -> 9.71 us
    unnamed x11 -> x0, waiting for transfers between devices: 77.1 us -> none
    ppermute x6 -> x71, starting transfers between devices: 15.9 us -> 79.9 us  [the longest x55 39.3 us: moved(): return lax.ppermute(value, 'dp', pairs)]
    reduce_scatter x1 -> x0, waiting for transfers between devices: 56 us -> none  [reduce_grads(): lax.psum_scatter(terms[3].astype(jnp.bfloat16), 'dp', scatter_dimension=0...]
  transfers between devices with their start and end apart: 14 -> 71, of which waited for: 10 -> 14; matrix products, arithmetic and copies ran while one was open for 36% -> 23% of each run, Pallas kernels for 0% -> 14%
where the time goes in v1:
time: 614 us; the launch traced here: 606 us
  waiting for transfers between devices  176 us (29%)
  matrix products  166 us (27%)
  Pallas kernels  103 us (17%)
  starting transfers between devices  79.9 us (13%)
  other arithmetic  49.5 us (8%)
  between operations  16.6 us (3%)
  local copies, waits for them, and re-layouts  14.9 us (2%)
    ppermute x55, waiting for transfers between devices, moved(): return lax.ppermute(value, 'dp', pairs)  82 us
    ppermute x4, waiting for transfers between devices, over_seq(): received = lax.ppermute(total, 'seq', pairs)  64.6 us
    dot_general x8, matrix products, product(): return jnp.dot(left, right, preferred_element_type=WIDE)  57.5 us
    pallas_call x6, Pallas kernels, row_call(): pl.pallas_call(kernel, out_shape=outputs, grid_spec=pltpu.PrefetchScalarG...  56.8 us
    dot_general x14, matrix products, weight_gradient(): return jnp.einsum('nd,nf->df', left, right, preferred_element_type=WIDE)  39.3 us
    ppermute x55, starting transfers between devices, moved(): return lax.ppermute(value, 'dp', pairs)  39.3 us
    pallas_call x5, Pallas kernels, placed(): pl.pallas_call(place_kernel, out_shape=jax.ShapeDtypeStruct(shape, pieces...  27 us
    ppermute x8, starting transfers between devices, over_seq(): lax.ppermute(total, 'seq', pairs).astype(WIDE)  24 us
  transfers between devices with their start and end apart: 71, of which 14 were waited for; matrix products, arithmetic and copies ran while one was open for 23% of the time, Pallas kernels for 14%

profile of v1, /device:TPU:0, one launch (start us, length us, event | category | flops | bytes accessed | tf_op | source)
XLA Modules:
  0.0 605.6 jit_solution(580016158810928519)
XLA Ops:
  2.7 3.0 collective-permute-start.16
  8.0 4.3 collective-permute-done.16.refs_1_
  12.3 2.5 collective-permute-start.7
  16.7 6.8 %collective-permute-done.refs_1_ = bf16[2,128,1024]{2,1,0:T(8,128)(2,1)S(1)} collective-permute-done((bf16[2,128,1024]{2,1,0:T(8,128)(2,1)S(1)}, bf16[2,128,1024]{2,1,0:T(8,128)(2,1)S(1)}, u32[]{:S(2)}, u32[]{:S(2)}) %collective-permute-start) | collective-permute-done | bytes 524320 | tf_op jit(solution)/shard_map/ppermute | solution.py:353
  23.5 2.6 collective-permute-start.18
  26.6 8.2 %collective-permute-done.7.refs_1_ = bf16[2,128,1024]{2,1,0:T(8,128)(2,1)} collective-permute-done((bf16[2,128,1024]{2,1,0:T(8,128)(2,1)S(1)}, bf16[2,128,1024]{2,1,0:T(8,128)(2,1)}, u32[]{:S(2)}, u32[]{:S(2)}) %collective-permute-start.7) | collective-permute-done | bytes 524320 | tf_op jit(solution)/shard_map/ppermute | solution.py:353
  34.8 2.6 collective-permute-start.9
  41.1 3.8 collective-permute-done.9.refs_3_
  66.1 3.1 shard_map.169
  69.2 4.4 shard_map.165
  75.9 5.9 convolution_convert_fusion.6
  84.6 4.2 shard_map.164
  88.9 5.9 convolution_convert_fusion.5
  94.8 5.4 shard_map.167
  100.7 4.0 collective-permute-start.14
  104.8 5.9 convolution_convert_fusion.8
  110.6 8.8 %shard_map.166.part_ref = bf16[2,512,1024]{2,1,0:T(8,128)(2,1)} custom-call(s32[1]{0:T(128)} %bitcast.1.start_ref, f32[8]{0:T(128)} %bitcast.249, s32[2,4]{1,0:T(2,128)} %lengths_ref.11, bf16[2,512,1024]{2,1,0:T(8,128)(2,1)} %bitcast.212, bf16[2,512,1024]{2,1,0:T(8,128)(2,1)} %bitcast.205, bf16[2,512,1024]{2,1,0:T(8,128)(2,1)} %bitcast.209), custom_call_target="tpu_custom_call" | custom-call | flops 2147483648 | bytes 8388608 | tf_op jit(solution)/shard_map/pallas_call | solution.py:265
  120.9 4.3 collective-permute-start.15
  125.2 5.8 convolution_convert_fusion.7
  132.4 5.8 shard_map.171
  140.3 6.6 %shard_map.168 = (bf16[2,512,1024]{2,1,0:T(8,128)(2,1)}, bf16[2,512,1024]{2,1,0:T(8,128)(2,1)}) custom-call(s32[1]{0:T(128)} %bitcast.1.start_ref, f32[8]{0:T(128)} %bitcast.250, s32[2,4]{1,0:T(2,128)} %lengths_ref.11, bf16[2,512,1024]{2,1,0:T(8,128)(2,1)} %bitcast.213, bf16[2,512,1024]{2,1,0:T(8,128)(2,1)} %bitcast.219, ...), custom_call_target="tpu_custom_call" | custom-call | flops 268435456 | bytes 11010048 | tf_op jit(solution)/shard_map/pallas_call | solution.py:265
  146.9 6.4 %shard_map.176 = bf16[1024,1024]{1,0:T(8,128)(2,1)} custom-call(s32[8]{0:T(128)} %get-tuple-element.69.order_ref, bf16[1024,1024]{1,0:T(8,128)(2,1)} %bitcast.242), custom_call_target="tpu_custom_call" | custom-call | bytes 4194304 | tf_op jit(solution)/shard_map/pallas_call | solution.py:386
  153.3 4.7 multiply_reduce_fusion.1
  161.6 6.4 %shard_map.177 = bf16[1024,1024]{1,0:T(8,128)(2,1)} custom-call(s32[8]{0:T(128)} %get-tuple-element.69.order_ref, bf16[1024,1024]{1,0:T(8,128)(2,1)} %multiply_convert_fusion.in_ref), custom_call_target="tpu_custom_call" | custom-call | bytes 4194304 | tf_op jit(solution)/shard_map/pallas_call | solution.py:386
  168.0 9.5 %shard_map.170 = bf16[2,1024,2816]{2,1,0:T(8,128)(2,1)} custom-call(s32[8]{0:T(128)} %get-tuple-element.69.order_ref, bf16[2,128,2816]{2,1,0:T(8,128)(2,1)} %copy-done.13, bf16[2,128,2816]{2,1,0:T(8,128)(2,1)} %collective-permute-done.23.refs_1_, bf16[2,128,2816]{2,1,0:T(8,128)(2,1)} %collective-permute-done.24.refs_2_, ...), custom_call_target="tpu_custom_call" | custom-call | bytes 23068672 | tf_op jit(solution)/shard_map/pallas_call | solution.py:324
  177.6 9.4 %convolution_convert_fusion.1 = bf16[1024,2816]{1,0:T(8,128)(2,1)S(1)} fusion(bf16[1024,1024]{1,0:T(8,128)(2,1)} %multiply_convert_fusion.in_ref, bf16[2,1024,2816]{2,1,0:T(8,128)(2,1)} %shard_map.170), kind=kOutput, calls=%fused_computation.15 | convolution fusion | flops 5908463616 | bytes 13631488 | tf_op jit(solution)/shard_map/dot_general | solution.py:459
  187.1 8.0 %convolution_convert_fusion.2 = bf16[1024,2816]{1,0:T(8,128)(2,1)} fusion(bf16[1024,1024]{1,0:T(8,128)(2,1)S(1)} %copy-done.12, bf16[2,1024,2816]{2,1,0:T(8,128)(2,1)S(1)} %copy-done.8), kind=kOutput, calls=%fused_computation.16 | convolution fusion | flops 5908463616 | bytes 13631488 | tf_op jit(solution)/shard_map/dot_general | solution.py:459
  195.1 10.7 %convolution_convert_fusion = bf16[2816,1024]{1,0:T(8,128)(2,1)} fusion(bf16[1024,1024]{1,0:T(8,128)(2,1)S(1)} %bitcast.244, bf16[1024,2816]{1,0:T(8,128)(2,1)S(1)} %convolution_convert_fusion.1, bf16[1024,2816]{1,0:T(8,128)(2,1)} %convolution_convert_fusion.2), kind=kOutput, calls=%fused_computation.14 | convolution fusion | flops 5919997952 | bytes 19398656 | tf_op jit(solution)/shard_map/nf,nd->fd/dot_general | solution.py:561
  205.8 14.2 %fusion.2 = (bf16[1024,2816]{1,0:T(8,128)(2,1)}, bf16[1024,2816]{1,0:T(8,128)(2,1)}) fusion(bf16[1024,2816]{1,0:T(8,128)(2,1)} %copy-done.49, bf16[1024,2816]{1,0:T(8,128)(2,1)} %convolution_convert_fusion.2, bf16[1024,1024]{1,0:T(8,128)(2,1)S(1)} %bitcast.245, bf16[1,2816,1024]{2,1,0:T(8,128)(2,1)} %shard_map.171), kind=kOutput, calls=%fused_computation.5 | convolution fusion | flops 5922881536 | bytes 30932992 | tf_op jit(solution)/shard_map/nd,fd->nf/dot_general | solution.py:558
  220.0 9.6 %fusion.8 = f32[1024,1024]{1,0:T(8,128)} fusion(bf16[1024,2816]{1,0:T(8,128)(2,1)} %get-tuple-element.28, bf16[2,1024,2816]{2,1,0:T(8,128)(2,1)S(1)} %copy-done.8), kind=kOutput, calls=%fused_computation.18 | convolution fusion | flops 5905580032 | bytes 15728640 | tf_op jit(solution)/shard_map/nf,df->nd/dot_general | solution.py:567
  229.7 4.5 convolution_convert_fusion.3
  234.2 4.6 convolution_convert_fusion.4
  238.9 9.3 %multiply_reduce_fusion = (f32[1024]{0:T(1024)S(1)}, f32[1024,1024]{1,0:T(8,128)S(1)}) fusion(f32[1024,1024]{1,0:T(8,128)S(1)} %copy-done.3, f32[1024,1024]{1,0:T(8,128)} %fusion.8, bf16[1024,2816]{1,0:T(8,128)(2,1)} %get-tuple-element.27, bf16[2,1024,2816]{2,1,0:T(8,128)(2,1)S(1)} %copy-done.8), kind=kOutput, calls=%fused_computation.36 | convolution fusion | flops 5908724736 | bytes 24121344 | tf_op jit(solution)/shard_map/nf,df->nd/dot_general | solution.py:566
  250.0 3.7 fusion.25
  253.7 8.6 %shard_map.172 = (bf16[2,512,1024]{2,1,0:T(8,128)(2,1)}, bf16[2,512,1024]{2,1,0:T(8,128)(2,1)}, bf16[2,8,128,128]{3,2,1,0:T(8,128)(2,1)}) custom-call(s32[1]{0:T(128)} %bitcast.1.start_ref, f32[8]{0:T(128)} %bitcast.251, s32[2,4]{1,0:T(2,128)} %lengths_ref.11, bf16[2,512,1024]{2,1,0:T(8,128)(2,1)} %bitcast.214, bf16[2,512,1024]{2,1,0:T(8,128)(2,1)} %bitcast.220, ...), custom_call_target="tpu_custom_call" | custom-call | flops 268435456 | bytes 13107200 | tf_op jit(solution)/shard_map/pallas_call | solution.py:265
  263.8 4.9 convolution_convert_fusion.9
  271.8 19.2 %shard_map.173 = (bf16[2,512,1024]{2,1,0:T(8,128)(2,1)}, bf16[2,512,1024]{2,1,0:T(8,128)(2,1)}, bf16[2,512,1024]{2,1,0:T(8,128)(2,1)}) custom-call(s32[1]{0:T(128)} %bitcast.1.start_ref, f32[8]{0:T(128)} %bitcast.252, s32[2,4]{1,0:T(2,128)} %lengths_ref.11, bf16[2,512,1024]{2,1,0:T(8,128)(2,1)} %bitcast.215, bf16[2,512,1024]{2,1,0:T(8,128)(2,1)} %bitcast.206, ...), custom_call_target="tpu_custom_call" | custom-call | flops 6442450944 | bytes 15204352 | tf_op jit(solution)/shard_map/pallas_call | solution.py:265
  292.5 6.5 %fusion.28 = f32[1024,1024]{1,0:T(8,128)} fusion(bf16[1024,1024]{1,0:T(8,128)(2,1)} %bitcast.233, bf16[2,1024,1024]{2,1,0:T(8,128)(2,1)} %shard_map.164), kind=kOutput, calls=%fused_computation.64 | convolution fusion | flops 2147483648 | bytes 8388608 | tf_op jit(solution)/shard_map/ne,de->nd/dot_general | solution.py:603
  299.1 8.8 %collective-permute-done.38 = bf16[2,8,128,128]{3,2,1,0:T(8,128)(2,1)S(1)} collective-permute-done((bf16[2,8,128,128]{3,2,1,0:T(8,128)(2,1)S(1)}, bf16[2,8,128,128]{3,2,1,0:T(8,128)(2,1)S(1)}, u32[]{:S(2)}, u32[]{:S(2)}) %collective-permute-start.38) | collective-permute-done | bytes 524320 | tf_op jit(solution)/shard_map/ppermute | solution.py:283
  308.8 8.1 %shard_map.174 = (bf16[2,512,1024]{2,1,0:T(8,128)(2,1)}, bf16[2,512,1024]{2,1,0:T(8,128)(2,1)}) custom-call(s32[1]{0:T(128)} %bitcast.1.start_ref, f32[8]{0:T(128)} %bitcast.253, s32[2,4]{1,0:T(2,128)} %lengths_ref.11, bf16[2,512,1024]{2,1,0:T(8,128)(2,1)} %bitcast.207, bf16[2,512,1024]{2,1,0:T(8,128)(2,1)} %bitcast.211, ...), custom_call_target="tpu_custom_call" | custom-call | flops 536870912 | bytes 13107200 | tf_op jit(solution)/shard_map/pallas_call | solution.py:265
  317.0 4.7 fusion.31
  321.8 4.5 fusion.30
  327.3 5.4 fusion.14
  332.7 3.4 fusion.15
  336.2 6.8 %shard_map.175 = bf16[1024,1024]{1,0:T(8,128)(2,1)} custom-call(s32[8]{0:T(128)} %get-tuple-element.69.order_ref, bf16[1024,1024]{1,0:T(8,128)(2,1)} %get-tuple-element.43.in_ref), custom_call_target="tpu_custom_call" | custom-call | bytes 4194304 | tf_op jit(solution)/shard_map/pallas_call | solution.py:386
  343.0 3.3 convolution_convert_fusion.10
  357.6 6.5 %add_convert_fusion = bf16[512,2816]{1,0:T(8,128)(2,1)S(1)} fusion(bf16[512,2816]{1,0:T(8,128)(2,1)} %collective-permute-done.57, bf16[1024,2816]{1,0:T(8,128)(2,1)} %get-tuple-element.28, bf16[1024,1024]{1,0:T(8,128)(2,1)S(1)} %copy-done.21), kind=kOutput, calls=%fused_computation.12 | convolution fusion | flops 2957115392 | bytes 12582912 | tf_op jit(solution)/shard_map/nd,nf->df/dot_general | solution.py:422
  365.9 5.0 add_convert_fusion.1
  378.3 12.1 %collective-permute-done.59 = bf16[2,128,2816]{2,1,0:T(8,128)(2,1)S(1)} collective-permute-done((bf16[2,128,2816]{2,1,0:T(8,128)(2,1)S(1)}, bf16[2,128,2816]{2,1,0:T(8,128)(2,1)S(1)}, u32[]{:S(2)}, u32[]{:S(2)}) %collective-permute-start.59) | collective-permute-done | bytes 1441824 | tf_op jit(solution)/shard_map/ppermute | solution.py:353
  397.2 3.5 add_convert_fusion.22
  400.7 26.2 %collective-permute-done.58 = bf16[2,128,2816]{2,1,0:T(8,128)(2,1)S(1)} collective-permute-done((bf16[2,128,2816]{2,1,0:T(8,128)(2,1)S(1)}, bf16[2,128,2816]{2,1,0:T(8,128)(2,1)S(1)}, u32[]{:S(2)}, u32[]{:S(2)}) %collective-permute-start.58) | collective-permute-done | bytes 1441824 | tf_op jit(solution)/shard_map/ppermute | solution.py:353
  429.6 4.7 collective-permute-start.61
  434.3 7.4 %collective-permute-done.52 = bf16[2,128,1024]{2,1,0:T(8,128)(2,1)S(1)} collective-permute-done((bf16[2,128,1024]{2,1,0:T(8,128)(2,1)S(1)}, bf16[2,128,1024]{2,1,0:T(8,128)(2,1)S(1)}, u32[]{:S(2)}, u32[]{:S(2)}) %collective-permute-start.52) | collective-permute-done | bytes 524320 | tf_op jit(solution)/shard_map/ppermute | solution.py:353
  442.0 4.5 collective-permute-start.53
  452.3 13.1 %collective-permute-done.66 = bf16[1,352,1024]{2,1,0:T(8,128)(2,1)S(1)} collective-permute-done((bf16[1,352,1024]{2,1,0:T(8,128)(2,1)}, bf16[1,352,1024]{2,1,0:T(8,128)(2,1)S(1)}, u32[]{:S(2)}, u32[]{:S(2)}) %collective-permute-start.66) | collective-permute-done | bytes 720928 | tf_op jit(solution)/shard_map/ppermute | solution.py:353
  468.6 5.4 collective-permute-done.53
  479.2 5.8 collective-permute-start.45
  488.5 2.7 add_convert_fusion.18
  491.3 3.5 collective-permute-start.68
  494.8 8.2 %collective-permute-done.45 = bf16[3,128,1024]{2,1,0:T(8,128)(2,1)S(1)} collective-permute-done((bf16[3,128,1024]{2,1,0:T(8,128)(2,1)S(1)}, bf16[3,128,1024]{2,1,0:T(8,128)(2,1)S(1)}, u32[]{:S(2)}, u32[]{:S(2)}) %collective-permute-start.45) | collective-permute-done | bytes 786464 | tf_op jit(solution)/shard_map/ppermute | solution.py:410
  507.4 6.9 %collective-permute-done.68 = bf16[1,352,1024]{2,1,0:T(8,128)(2,1)} collective-permute-done((bf16[1,352,1024]{2,1,0:T(8,128)(2,1)}, bf16[1,352,1024]{2,1,0:T(8,128)(2,1)}, u32[]{:S(2)}, u32[]{:S(2)}) %collective-permute-start.68) | collective-permute-done | bytes 720928 | tf_op jit(solution)/shard_map/ppermute | solution.py:410
  522.6 11.9 %add_convert_fusion.2 = bf16[1024,1024]{1,0:T(8,128)(2,1)} fusion(f32[1024,1024]{1,0:T(8,128)S(1)} %copy-done.4, bf16[1,2816,1024]{2,1,0:T(8,128)(2,1)} %shard_map.171, bf16[1024,2816]{1,0:T(8,128)(2,1)} %copy-done.49, bf16[1024,2816]{1,0:T(8,128)(2,1)} %convolution_convert_fusion.2), kind=kOutput, calls=%fused_computation.37 | convolution fusion | flops 5919211520 | bytes 23592960 | tf_op jit(solution)/shard_map/dot_general | solution.py:459
  536.1 28.4 %collective-permute-done.47 = bf16[3,128,1024]{2,1,0:T(8,128)(2,1)S(1)} collective-permute-done((bf16[3,128,1024]{2,1,0:T(8,128)(2,1)S(1)}, bf16[3,128,1024]{2,1,0:T(8,128)(2,1)S(1)}, u32[]{:S(2)}, u32[]{:S(2)}) %collective-permute-start.47) | collective-permute-done | bytes 786464 | tf_op jit(solution)/shard_map/ppermute | solution.py:415
  566.3 36.1 %collective-permute-done.70 = bf16[1,352,1024]{2,1,0:T(8,128)(2,1)S(1)} collective-permute-done((bf16[1,352,1024]{2,1,0:T(8,128)(2,1)S(1)}, bf16[1,352,1024]{2,1,0:T(8,128)(2,1)S(1)}, u32[]{:S(2)}, u32[]{:S(2)}) %collective-permute-start.70) | collective-permute-done | bytes 720928 | tf_op jit(solution)/shard_map/ppermute | solution.py:415
  (296 shorter events, 107.6 us)
Async XLA Ops:
  2.7 9.6 %collective-permute-start.16 = (bf16[1,128,1024]{2,1,0:T(8,128)(2,1)S(1)}, bf16[1,128,1024]{2,1,0:T(8,128)(2,1)S(1)}, u32[]{:S(2)}, u32[]{:S(2)}) collective-permute-start(bf16[1,128,1024]{2,1,0:T(8,128)(2,1)S(1)} %get-tuple-element.45.refs_0_), channel_id=1, source_target_pairs={{0,2},{1,5},{2,0},{3,7},{4,6},{5,1},{6,4},{7,3},{8,10},{9,13},{10,... | collective-permute-start | bytes 786440 | tf_op jit(solution)/shard_map/ppermute | solution.py:353
  7.3 16.2 %collective-permute-start = (bf16[2,128,1024]{2,1,0:T(8,128)(2,1)S(1)}, bf16[2,128,1024]{2,1,0:T(8,128)(2,1)S(1)}, u32[]{:S(2)}, u32[]{:S(2)}) collective-permute-start(bf16[2,128,1024]{2,1,0:T(8,128)(2,1)S(1)} %pad_maximum_fusion.5.refs_0_), channel_id=1, source_target_pairs={{0,2},{1,5},{2,0},{3,7},{4,6},{5,1},{6,4},{7,3},{8,10},{9,13},{10,... | collective-permute-start | bytes 1572872 | tf_op jit(solution)/shard_map/ppermute | solution.py:353
  7.9 29.6 %collective-permute-start.1 = (bf16[2,128,1024]{2,1,0:T(8,128)(2,1)S(1)}, bf16[2,128,1024]{2,1,0:T(8,128)(2,1)S(1)}, u32[]{:S(2)}, u32[]{:S(2)}) collective-permute-start(bf16[2,128,1024]{2,1,0:T(8,128)(2,1)S(1)} %pad_maximum_fusion.5.refs_0_), channel_id=1, source_target_pairs={{0,4},{1,3},{2,6},{3,1},{4,0},{5,7},{6,2},{7,5},{8,12},{9,11},{10,... | collective-permute-start | bytes 1572872 | tf_op jit(solution)/shard_map/ppermute | solution.py:353
  12.3 22.6 %collective-permute-start.7 = (bf16[2,128,1024]{2,1,0:T(8,128)(2,1)S(1)}, bf16[2,128,1024]{2,1,0:T(8,128)(2,1)}, u32[]{:S(2)}, u32[]{:S(2)}) collective-permute-start(bf16[2,128,1024]{2,1,0:T(8,128)(2,1)S(1)} %slice_bitcast_fusion.30.refs_0_), channel_id=1, source_target_pairs={{0,2},{1,5},{2,0},{3,7},{4,6},{5,1},{6,4},{7,3},{8,10},{9,13},{10,... | collective-permute-start | bytes 1572872 | tf_op jit(solution)/shard_map/ppermute | solution.py:353
  14.7 22.8 %collective-permute-start.8 = (bf16[2,128,1024]{2,1,0:T(8,128)(2,1)S(1)}, bf16[2,128,1024]{2,1,0:T(8,128)(2,1)}, u32[]{:S(2)}, u32[]{:S(2)}) collective-permute-start(bf16[2,128,1024]{2,1,0:T(8,128)(2,1)S(1)} %slice_bitcast_fusion.30.refs_0_), channel_id=1, source_target_pairs={{0,4},{1,3},{2,6},{3,1},{4,0},{5,7},{6,2},{7,5},{8,12},{9,11},{10,... | collective-permute-start | bytes 1572872 | tf_op jit(solution)/shard_map/ppermute | solution.py:353
  16.5 21.5 %collective-permute-start.10 = (bf16[2,128,1024]{2,1,0:T(8,128)(2,1)S(1)}, bf16[2,128,1024]{2,1,0:T(8,128)(2,1)S(1)}, u32[]{:S(2)}, u32[]{:S(2)}) collective-permute-start(bf16[2,128,1024]{2,1,0:T(8,128)(2,1)S(1)} %slice_bitcast_fusion.30.refs_0_), channel_id=1, source_target_pairs={{0,1},{1,0},{2,3},{3,2},{4,5},{5,4},{6,7},{7,6},{8,9},{9,8},{10,11... | collective-permute-start | bytes 1572872 | tf_op jit(solution)/shard_map/ppermute | solution.py:353
  23.5 14.7 %collective-permute-start.18 = (bf16[1,128,1024]{2,1,0:T(8,128)(2,1)S(1)}, bf16[1,128,1024]{2,1,0:T(8,128)(2,1)}, u32[]{:S(2)}, u32[]{:S(2)}) collective-permute-start(bf16[1,128,1024]{2,1,0:T(8,128)(2,1)S(1)} %collective-permute-done.16.refs_1_), channel_id=1, source_target_pairs={{0,4},{1,3},{2,6},{3,1},{4,0},{5,7},{6,2},{7,5},{8,12},{9,11},{10,... | collective-permute-start | bytes 786440 | tf_op jit(solution)/shard_map/ppermute | solution.py:353
  34.8 10.1 %collective-permute-start.9 = (bf16[2,128,1024]{2,1,0:T(8,128)(2,1)}, bf16[2,128,1024]{2,1,0:T(8,128)(2,1)}, u32[]{:S(2)}, u32[]{:S(2)}) collective-permute-start(bf16[2,128,1024]{2,1,0:T(8,128)(2,1)} %collective-permute-done.7.refs_1_), channel_id=1, source_target_pairs={{0,4},{1,3},{2,6},{3,1},{4,0},{5,7},{6,2},{7,5},{8,12},{9,11},{10,... | collective-permute-start | bytes 1572872 | tf_op jit(solution)/shard_map/ppermute | solution.py:353
  37.6 10.4 %collective-permute-start.21 = (bf16[1,128,1024]{2,1,0:T(8,128)(2,1)}, bf16[1,128,1024]{2,1,0:T(8,128)(2,1)}, u32[]{:S(2)}, u32[]{:S(2)}) collective-permute-start(bf16[1,128,1024]{2,1,0:T(8,128)(2,1)} %collective-permute-done.17.refs_2_), channel_id=1, source_target_pairs={{0,1},{1,0},{2,3},{3,2},{4,5},{5,4},{6,7},{7,6},{8,9},{9,8},{10,11... | collective-permute-start | bytes 786440 | tf_op jit(solution)/shard_map/ppermute | solution.py:353
  38.1 13.5 %collective-permute-start.11 = (bf16[2,128,1024]{2,1,0:T(8,128)(2,1)}, bf16[2,128,1024]{2,1,0:T(8,128)(2,1)}, u32[]{:S(2)}, u32[]{:S(2)}) collective-permute-start(bf16[2,128,1024]{2,1,0:T(8,128)(2,1)} %collective-permute-done.7.refs_1_), channel_id=1, source_target_pairs={{0,1},{1,0},{2,3},{3,2},{4,5},{5,4},{6,7},{7,6},{8,9},{9,8},{10,11... | collective-permute-start | bytes 1572872 | tf_op jit(solution)/shard_map/ppermute | solution.py:353
  38.2 14.7 %collective-permute-start.12 = (bf16[2,128,1024]{2,1,0:T(8,128)(2,1)}, bf16[2,128,1024]{2,1,0:T(8,128)(2,1)}, u32[]{:S(2)}, u32[]{:S(2)}) collective-permute-start(bf16[2,128,1024]{2,1,0:T(8,128)(2,1)} %collective-permute-done.8.refs_2_), channel_id=1, source_target_pairs={{0,1},{1,0},{2,3},{3,2},{4,5},{5,4},{6,7},{7,6},{8,9},{9,8},{10,11... | collective-permute-start | bytes 1572872 | tf_op jit(solution)/shard_map/ppermute | solution.py:353
  41.0 10.2 %collective-permute-start.22 = (bf16[1,128,1024]{2,1,0:T(8,128)(2,1)}, bf16[1,128,1024]{2,1,0:T(8,128)(2,1)}, u32[]{:S(2)}, u32[]{:S(2)}) collective-permute-start(bf16[1,128,1024]{2,1,0:T(8,128)(2,1)} %collective-permute-done.18.refs_3_), channel_id=1, source_target_pairs={{0,1},{1,0},{2,3},{3,2},{4,5},{5,4},{6,7},{7,6},{8,9},{9,8},{10,11... | collective-permute-start | bytes 786440 | tf_op jit(solution)/shard_map/ppermute | solution.py:353
  47.9 27.3 %collective-permute-start.30 = (bf16[1,352,1024]{2,1,0:T(8,128)(2,1)}, bf16[1,352,1024]{2,1,0:T(8,128)(2,1)}, u32[]{:S(2)}, u32[]{:S(2)}) collective-permute-start(bf16[1,352,1024]{2,1,0:T(8,128)(2,1)} %convert_element_type.406.refs_0_), channel_id=1, source_target_pairs={{0,2},{1,5},{2,0},{3,7},{4,6},{5,1},{6,4},{7,3},{8,10},{9,13},{10,... | collective-permute-start | bytes 2162696 | tf_op jit(solution)/shard_map/ppermute | solution.py:353
  51.2 22.4 %collective-permute-start.3 = (bf16[2,128,1024]{2,1,0:T(8,128)(2,1)}, bf16[2,128,1024]{2,1,0:T(8,128)(2,1)}, u32[]{:S(2)}, u32[]{:S(2)}) collective-permute-start(bf16[2,128,1024]{2,1,0:T(8,128)(2,1)} %copy-done.17), channel_id=1, source_target_pairs={{0,1},{1,0},{2,3},{3,2},{4,5},{5,4},{6,7},{7,6},{8,9},{9,8},{10,11... | collective-permute-start | bytes 1572872 | tf_op jit(solution)/shard_map/ppermute | solution.py:353
  51.6 23.7 %collective-permute-start.2 = (bf16[2,128,1024]{2,1,0:T(8,128)(2,1)}, bf16[2,128,1024]{2,1,0:T(8,128)(2,1)}, u32[]{:S(2)}, u32[]{:S(2)}) collective-permute-start(bf16[2,128,1024]{2,1,0:T(8,128)(2,1)} %copy-done.35), channel_id=1, source_target_pairs={{0,4},{1,3},{2,6},{3,1},{4,0},{5,7},{6,2},{7,5},{8,12},{9,11},{10,... | collective-permute-start | bytes 1572872 | tf_op jit(solution)/shard_map/ppermute | solution.py:353
  52.9 22.9 %collective-permute-start.4 = (bf16[2,128,1024]{2,1,0:T(8,128)(2,1)}, bf16[2,128,1024]{2,1,0:T(8,128)(2,1)}, u32[]{:S(2)}, u32[]{:S(2)}) collective-permute-start(bf16[2,128,1024]{2,1,0:T(8,128)(2,1)} %copy-done.35), channel_id=1, source_target_pairs={{0,1},{1,0},{2,3},{3,2},{4,5},{5,4},{6,7},{7,6},{8,9},{9,8},{10,11... | collective-permute-start | bytes 1572872 | tf_op jit(solution)/shard_map/ppermute | solution.py:353
  53.6 46.7 %collective-permute-start.23 = (bf16[2,128,2816]{2,1,0:T(8,128)(2,1)S(1)}, bf16[2,128,2816]{2,1,0:T(8,128)(2,1)}, u32[]{:S(2)}, u32[]{:S(2)}) collective-permute-start(bf16[2,128,2816]{2,1,0:T(8,128)(2,1)S(1)} %convert_bitcast_fusion.refs_0_), channel_id=1, source_target_pairs={{0,2},{1,5},{2,0},{3,7},{4,6},{5,1},{6,4},{7,3},{8,10},{9,13},{10,... | collective-permute-start | bytes 4325384 | tf_op jit(solution)/shard_map/ppermute | solution.py:353
  73.6 26.6 %collective-permute-start.31 = (bf16[1,352,1024]{2,1,0:T(8,128)(2,1)}, bf16[1,352,1024]{2,1,0:T(8,128)(2,1)}, u32[]{:S(2)}, u32[]{:S(2)}) collective-permute-start(bf16[1,352,1024]{2,1,0:T(8,128)(2,1)} %convert_element_type.406.refs_0_), channel_id=1, source_target_pairs={{0,4},{1,3},{2,6},{3,1},{4,0},{5,7},{6,2},{7,5},{8,12},{9,11},{10,... | collective-permute-start | bytes 2162696 | tf_op jit(solution)/shard_map/ppermute | solution.py:353
  75.3 25.4 %collective-permute-start.33 = (bf16[1,352,1024]{2,1,0:T(8,128)(2,1)}, bf16[1,352,1024]{2,1,0:T(8,128)(2,1)}, u32[]{:S(2)}, u32[]{:S(2)}) collective-permute-start(bf16[1,352,1024]{2,1,0:T(8,128)(2,1)} %convert_element_type.406.refs_0_), channel_id=1, source_target_pairs={{0,1},{1,0},{2,3},{3,2},{4,5},{5,4},{6,7},{7,6},{8,9},{9,8},{10,11... | collective-permute-start | bytes 2162696 | tf_op jit(solution)/shard_map/ppermute | solution.py:353
  82.6 48.5 %collective-permute-start.24 = (bf16[2,128,2816]{2,1,0:T(8,128)(2,1)S(1)}, bf16[2,128,2816]{2,1,0:T(8,128)(2,1)}, u32[]{:S(2)}, u32[]{:S(2)}) collective-permute-start(bf16[2,128,2816]{2,1,0:T(8,128)(2,1)S(1)} %convert_bitcast_fusion.refs_0_), channel_id=1, source_target_pairs={{0,4},{1,3},{2,6},{3,1},{4,0},{5,7},{6,2},{7,5},{8,12},{9,11},{10,... | collective-permute-start | bytes 4325384 | tf_op jit(solution)/shard_map/ppermute | solution.py:353
  83.0 36.4 %collective-permute-start.32 = (bf16[1,352,1024]{2,1,0:T(8,128)(2,1)}, bf16[1,352,1024]{2,1,0:T(8,128)(2,1)}, u32[]{:S(2)}, u32[]{:S(2)}) collective-permute-start(bf16[1,352,1024]{2,1,0:T(8,128)(2,1)} %collective-permute-done.30.refs_1_), channel_id=1, source_target_pairs={{0,4},{1,3},{2,6},{3,1},{4,0},{5,7},{6,2},{7,5},{8,12},{9,11},{10,... | collective-permute-start | bytes 2162696 | tf_op jit(solution)/shard_map/ppermute | solution.py:353
  100.2 20.7 %collective-permute-start.34 = (bf16[1,352,1024]{2,1,0:T(8,128)(2,1)}, bf16[1,352,1024]{2,1,0:T(8,128)(2,1)}, u32[]{:S(2)}, u32[]{:S(2)}) collective-permute-start(bf16[1,352,1024]{2,1,0:T(8,128)(2,1)} %collective-permute-done.30.refs_1_), channel_id=1, source_target_pairs={{0,1},{1,0},{2,3},{3,2},{4,5},{5,4},{6,7},{7,6},{8,9},{9,8},{10,11... | collective-permute-start | bytes 2162696 | tf_op jit(solution)/shard_map/ppermute | solution.py:353
  100.3 37.9 %collective-permute-start.25 = (bf16[2,128,2816]{2,1,0:T(8,128)(2,1)}, bf16[2,128,2816]{2,1,0:T(8,128)(2,1)}, u32[]{:S(2)}, u32[]{:S(2)}) collective-permute-start(bf16[2,128,2816]{2,1,0:T(8,128)(2,1)} %collective-permute-done.23.refs_1_), channel_id=1, source_target_pairs={{0,4},{1,3},{2,6},{3,1},{4,0},{5,7},{6,2},{7,5},{8,12},{9,11},{10,... | collective-permute-start | bytes 4325384 | tf_op jit(solution)/shard_map/ppermute | solution.py:353
  100.7 18.7 %collective-permute-start.14 = (bf16[2,8,128,128]{3,2,1,0:T(8,128)(2,1)}, bf16[2,8,128,128]{3,2,1,0:T(8,128)(2,1)S(1)}, u32[]{:S(2)}, u32[]{:S(2)}) collective-permute-start(bf16[2,8,128,128]{3,2,1,0:T(8,128)(2,1)} %shard_map.167), channel_id=1, source_target_pairs={{0,8},{8,16},{16,24},{1,9},{9,17},{17,25},{2,10},{10,18},{18,26},{... | collective-permute-start | bytes 1572872 | tf_op jit(solution)/shard_map/ppermute | solution.py:283
  119.4 11.6 %collective-permute-start.35 = (bf16[1,352,1024]{2,1,0:T(8,128)(2,1)}, bf16[1,352,1024]{2,1,0:T(8,128)(2,1)S(1)}, u32[]{:S(2)}, u32[]{:S(2)}) collective-permute-start(bf16[1,352,1024]{2,1,0:T(8,128)(2,1)} %collective-permute-done.31.refs_2_), channel_id=1, source_target_pairs={{0,1},{1,0},{2,3},{3,2},{4,5},{5,4},{6,7},{7,6},{8,9},{9,8},{10,11... | collective-permute-start | bytes 2162696 | tf_op jit(solution)/shard_map/ppermute | solution.py:353
  119.4 12.5 %collective-permute-start.36 = (bf16[1,352,1024]{2,1,0:T(8,128)(2,1)}, bf16[1,352,1024]{2,1,0:T(8,128)(2,1)}, u32[]{:S(2)}, u32[]{:S(2)}) collective-permute-start(bf16[1,352,1024]{2,1,0:T(8,128)(2,1)} %collective-permute-done.32.refs_3_), channel_id=1, source_target_pairs={{0,1},{1,0},{2,3},{3,2},{4,5},{5,4},{6,7},{7,6},{8,9},{9,8},{10,11... | collective-permute-start | bytes 2162696 | tf_op jit(solution)/shard_map/ppermute | solution.py:353
  120.9 17.4 %collective-permute-start.15 = (bf16[2,8,128,128]{3,2,1,0:T(8,128)(2,1)}, bf16[2,8,128,128]{3,2,1,0:T(8,128)(2,1)}, u32[]{:S(2)}, u32[]{:S(2)}) collective-permute-start(bf16[2,8,128,128]{3,2,1,0:T(8,128)(2,1)} %fusion.37), channel_id=1, source_target_pairs={{0,8},{8,16},{16,24},{1,9},{9,17},{17,25},{2,10},{10,18},{18,26},{... | collective-permute-start | bytes 1572872 | tf_op jit(solution)/shard_map/ppermute | solution.py:283
  131.0 37.0 %collective-permute-start.26 = (bf16[2,128,2816]{2,1,0:T(8,128)(2,1)S(1)}, bf16[2,128,2816]{2,1,0:T(8,128)(2,1)}, u32[]{:S(2)}, u32[]{:S(2)}) collective-permute-start(bf16[2,128,2816]{2,1,0:T(8,128)(2,1)S(1)} %convert_bitcast_fusion.refs_0_), channel_id=1, source_target_pairs={{0,1},{1,0},{2,3},{3,2},{4,5},{5,4},{6,7},{7,6},{8,9},{9,8},{10,11... | collective-permute-start | bytes 4325384 | tf_op jit(solution)/shard_map/ppermute | solution.py:353
  131.9 36.1 %collective-permute-start.27 = (bf16[2,128,2816]{2,1,0:T(8,128)(2,1)}, bf16[2,128,2816]{2,1,0:T(8,128)(2,1)}, u32[]{:S(2)}, u32[]{:S(2)}) collective-permute-start(bf16[2,128,2816]{2,1,0:T(8,128)(2,1)} %collective-permute-done.23.refs_1_), channel_id=1, source_target_pairs={{0,1},{1,0},{2,3},{3,2},{4,5},{5,4},{6,7},{7,6},{8,9},{9,8},{10,11... | collective-permute-start | bytes 4325384 | tf_op jit(solution)/shard_map/ppermute | solution.py:353
  131.9 36.1 %collective-permute-start.28 = (bf16[2,128,2816]{2,1,0:T(8,128)(2,1)}, bf16[2,128,2816]{2,1,0:T(8,128)(2,1)}, u32[]{:S(2)}, u32[]{:S(2)}) collective-permute-start(bf16[2,128,2816]{2,1,0:T(8,128)(2,1)} %collective-permute-done.24.refs_2_), channel_id=1, source_target_pairs={{0,1},{1,0},{2,3},{3,2},{4,5},{5,4},{6,7},{7,6},{8,9},{9,8},{10,11... | collective-permute-start | bytes 4325384 | tf_op jit(solution)/shard_map/ppermute | solution.py:353
  138.2 29.8 %collective-permute-start.29 = (bf16[2,128,2816]{2,1,0:T(8,128)(2,1)}, bf16[2,128,2816]{2,1,0:T(8,128)(2,1)}, u32[]{:S(2)}, u32[]{:S(2)}) collective-permute-start(bf16[2,128,2816]{2,1,0:T(8,128)(2,1)} %collective-permute-done.25.refs_3_), channel_id=1, source_target_pairs={{0,1},{1,0},{2,3},{3,2},{4,5},{5,4},{6,7},{7,6},{8,9},{9,8},{10,11... | collective-permute-start | bytes 4325384 | tf_op jit(solution)/shard_map/ppermute | solution.py:353
  262.3 28.8 %collective-permute-start.37 = (bf16[2,8,128,128]{3,2,1,0:T(8,128)(2,1)}, bf16[2,8,128,128]{3,2,1,0:T(8,128)(2,1)S(1)}, u32[]{:S(2)}, u32[]{:S(2)}) collective-permute-start(bf16[2,8,128,128]{3,2,1,0:T(8,128)(2,1)} %get-tuple-element.21), channel_id=1, source_target_pairs={{8,0},{16,8},{24,16},{9,1},{17,9},{25,17},{10,2},{18,10},{26,18},{... | collective-permute-start | bytes 1572872 | tf_op jit(solution)/shard_map/ppermute | solution.py:283
  268.7 82.0 %collective-permute-start.49 = (bf16[512,1024]{1,0:T(8,128)(2,1)}, bf16[512,1024]{1,0:T(8,128)(2,1)S(1)}, u32[]{:S(2)}, u32[]{:S(2)}) collective-permute-start(bf16[512,1024]{1,0:T(8,128)(2,1)} %convolution_convert_fusion.9), channel_id=1, source_target_pairs={{0,1},{1,0},{2,3},{3,2},{4,5},{5,4},{6,7},{7,6},{8,9},{9,8},{10,11... | collective-permute-start | bytes 3145736 | tf_op jit(solution)/shard_map/ppermute | solution.py:353
  269.2 87.0 %collective-permute-start.57 = (bf16[512,2816]{1,0:T(8,128)(2,1)}, bf16[512,2816]{1,0:T(8,128)(2,1)}, u32[]{:S(2)}, u32[]{:S(2)}) collective-permute-start(bf16[512,2816]{1,0:T(8,128)(2,1)} %convolution_convert_fusion.3), channel_id=1, source_target_pairs={{0,1},{1,0},{2,3},{3,2},{4,5},{5,4},{6,7},{7,6},{8,9},{9,8},{10,11... | collective-permute-start | bytes 8650760 | tf_op jit(solution)/shard_map/ppermute | solution.py:353
  269.2 95.1 %collective-permute-start.56 = (bf16[512,2816]{1,0:T(8,128)(2,1)}, bf16[512,2816]{1,0:T(8,128)(2,1)}, u32[]{:S(2)}, u32[]{:S(2)}) collective-permute-start(bf16[512,2816]{1,0:T(8,128)(2,1)} %convolution_convert_fusion.4), channel_id=1, source_target_pairs={{0,1},{1,0},{2,3},{3,2},{4,5},{5,4},{6,7},{7,6},{8,9},{9,8},{10,11... | collective-permute-start | bytes 8650760 | tf_op jit(solution)/shard_map/ppermute | solution.py:353
  271.7 124.8 %collective-permute-start.64 = (bf16[4,352,1024]{2,1,0:T(8,128)(2,1)}, bf16[4,352,1024]{2,1,0:T(8,128)(2,1)}, u32[]{:S(2)}, u32[]{:S(2)}) collective-permute-start(bf16[4,352,1024]{2,1,0:T(8,128)(2,1)} %pad_maximum_fusion), channel_id=1, source_target_pairs={{0,1},{1,0},{2,3},{3,2},{4,5},{5,4},{6,7},{7,6},{8,9},{9,8},{10,11... | collective-permute-start | bytes 8650760 | tf_op jit(solution)/shard_map/ppermute | solution.py:353
  291.2 16.7 %collective-permute-start.38 = (bf16[2,8,128,128]{3,2,1,0:T(8,128)(2,1)S(1)}, bf16[2,8,128,128]{3,2,1,0:T(8,128)(2,1)S(1)}, u32[]{:S(2)}, u32[]{:S(2)}) collective-permute-start(bf16[2,8,128,128]{3,2,1,0:T(8,128)(2,1)S(1)} %fusion.39), channel_id=1, source_target_pairs={{8,0},{16,8},{24,16},{9,1},{17,9},{25,17},{10,2},{18,10},{26,18},{... | collective-permute-start | bytes 1572872 | tf_op jit(solution)/shard_map/ppermute | solution.py:283
  350.8 20.5 %collective-permute-start.41 = (bf16[512,1024]{1,0:T(8,128)(2,1)S(1)}, bf16[512,1024]{1,0:T(8,128)(2,1)S(1)}, u32[]{:S(2)}, u32[]{:S(2)}) collective-permute-start(bf16[512,1024]{1,0:T(8,128)(2,1)S(1)} %convolution_convert_fusion.11), channel_id=1, source_target_pairs={{0,1},{1,0},{2,3},{3,2},{4,5},{5,4},{6,7},{7,6},{8,9},{9,8},{10,11... | collective-permute-start | bytes 3145736 | tf_op jit(solution)/shard_map/ppermute | solution.py:353
  353.2 20.1 %collective-permute-start.40 = (bf16[512,1024]{1,0:T(8,128)(2,1)S(1)}, bf16[512,1024]{1,0:T(8,128)(2,1)S(1)}, u32[]{:S(2)}, u32[]{:S(2)}) collective-permute-start(bf16[512,1024]{1,0:T(8,128)(2,1)S(1)} %convolution_convert_fusion.12), channel_id=1, source_target_pairs={{0,1},{1,0},{2,3},{3,2},{4,5},{5,4},{6,7},{7,6},{8,9},{9,8},{10,11... | collective-permute-start | bytes 3145736 | tf_op jit(solution)/shard_map/ppermute | solution.py:353
  356.2 20.0 %collective-permute-start.39 = (bf16[512,1024]{1,0:T(8,128)(2,1)S(1)}, bf16[512,1024]{1,0:T(8,128)(2,1)S(1)}, u32[]{:S(2)}, u32[]{:S(2)}) collective-permute-start(bf16[512,1024]{1,0:T(8,128)(2,1)S(1)} %convolution_convert_fusion.13), channel_id=1, source_target_pairs={{0,1},{1,0},{2,3},{3,2},{4,5},{5,4},{6,7},{7,6},{8,9},{9,8},{10,11... | collective-permute-start | bytes 3145736 | tf_op jit(solution)/shard_map/ppermute | solution.py:353
  364.4 30.6 %collective-permute-start.51 = (bf16[2,128,1024]{2,1,0:T(8,128)(2,1)S(1)}, bf16[2,128,1024]{2,1,0:T(8,128)(2,1)S(1)}, u32[]{:S(2)}, u32[]{:S(2)}) collective-permute-start(bf16[2,128,1024]{2,1,0:T(8,128)(2,1)S(1)} %pad_maximum_fusion.7), channel_id=1, source_target_pairs={{0,2},{1,5},{2,0},{3,7},{4,6},{5,1},{6,4},{7,3},{8,10},{9,13},{10,... | collective-permute-start | bytes 1572872 | tf_op jit(solution)/shard_map/ppermute | solution.py:353
  371.3 19.1 %collective-permute-start.59 = (bf16[2,128,2816]{2,1,0:T(8,128)(2,1)S(1)}, bf16[2,128,2816]{2,1,0:T(8,128)(2,1)S(1)}, u32[]{:S(2)}, u32[]{:S(2)}) collective-permute-start(bf16[2,128,2816]{2,1,0:T(8,128)(2,1)S(1)} %pad_maximum_fusion.2), channel_id=1, source_target_pairs={{0,2},{1,5},{2,0},{3,7},{4,6},{5,1},{6,4},{7,3},{8,10},{9,13},{10,... | collective-permute-start | bytes 4325384 | tf_op jit(solution)/shard_map/ppermute | solution.py:353
  373.3 56.3 %collective-permute-start.50 = (bf16[2,128,1024]{2,1,0:T(8,128)(2,1)S(1)}, bf16[2,128,1024]{2,1,0:T(8,128)(2,1)S(1)}, u32[]{:S(2)}, u32[]{:S(2)}) collective-permute-start(bf16[2,128,1024]{2,1,0:T(8,128)(2,1)S(1)} %pad_maximum_fusion.6), channel_id=1, source_target_pairs={{0,2},{1,5},{2,0},{3,7},{4,6},{5,1},{6,4},{7,3},{8,10},{9,13},{10,... | collective-permute-start | bytes 1572872 | tf_op jit(solution)/shard_map/ppermute | solution.py:353
  377.7 49.2 %collective-permute-start.58 = (bf16[2,128,2816]{2,1,0:T(8,128)(2,1)S(1)}, bf16[2,128,2816]{2,1,0:T(8,128)(2,1)S(1)}, u32[]{:S(2)}, u32[]{:S(2)}) collective-permute-start(bf16[2,128,2816]{2,1,0:T(8,128)(2,1)S(1)} %pad_maximum_fusion.1), channel_id=1, source_target_pairs={{0,2},{1,5},{2,0},{3,7},{4,6},{5,1},{6,4},{7,3},{8,10},{9,13},{10,... | collective-permute-start | bytes 4325384 | tf_op jit(solution)/shard_map/ppermute | solution.py:353
  390.7 36.9 %collective-permute-start.60 = (bf16[2,128,2816]{2,1,0:T(8,128)(2,1)S(1)}, bf16[2,128,2816]{2,1,0:T(8,128)(2,1)S(1)}, u32[]{:S(2)}, u32[]{:S(2)}) collective-permute-start(bf16[2,128,2816]{2,1,0:T(8,128)(2,1)S(1)} %add_convert_fusion.6), channel_id=1, source_target_pairs={{0,4},{1,3},{2,6},{3,1},{4,0},{5,7},{6,2},{7,5},{8,12},{9,11},{10,... | collective-permute-start | bytes 4325384 | tf_op jit(solution)/shard_map/ppermute | solution.py:353
  394.9 51.6 %collective-permute-start.43 = (bf16[3,128,1024]{2,1,0:T(8,128)(2,1)S(1)}, bf16[3,128,1024]{2,1,0:T(8,128)(2,1)S(1)}, u32[]{:S(2)}, u32[]{:S(2)}) collective-permute-start(bf16[3,128,1024]{2,1,0:T(8,128)(2,1)S(1)} %pad_maximum_fusion.4), channel_id=1, source_target_pairs={{0,2},{1,5},{2,0},{3,7},{4,6},{5,1},{6,4},{7,3},{8,10},{9,13},{10,... | collective-permute-start | bytes 2359304 | tf_op jit(solution)/shard_map/ppermute | solution.py:353
  396.5 79.4 %collective-permute-start.42 = (bf16[3,128,1024]{2,1,0:T(8,128)(2,1)}, bf16[3,128,1024]{2,1,0:T(8,128)(2,1)}, u32[]{:S(2)}, u32[]{:S(2)}) collective-permute-start(bf16[3,128,1024]{2,1,0:T(8,128)(2,1)} %pad_maximum_fusion.3), channel_id=1, source_target_pairs={{0,2},{1,5},{2,0},{3,7},{4,6},{5,1},{6,4},{7,3},{8,10},{9,13},{10,... | collective-permute-start | bytes 2359304 | tf_op jit(solution)/shard_map/ppermute | solution.py:353
  426.9 14.9 %collective-permute-start.52 = (bf16[2,128,1024]{2,1,0:T(8,128)(2,1)S(1)}, bf16[2,128,1024]{2,1,0:T(8,128)(2,1)S(1)}, u32[]{:S(2)}, u32[]{:S(2)}) collective-permute-start(bf16[2,128,1024]{2,1,0:T(8,128)(2,1)S(1)} %add_convert_fusion.27), channel_id=1, source_target_pairs={{0,4},{1,3},{2,6},{3,1},{4,0},{5,7},{6,2},{7,5},{8,12},{9,11},{10,... | collective-permute-start | bytes 1572872 | tf_op jit(solution)/shard_map/ppermute | solution.py:353
  427.6 37.8 %collective-permute-start.66 = (bf16[1,352,1024]{2,1,0:T(8,128)(2,1)}, bf16[1,352,1024]{2,1,0:T(8,128)(2,1)S(1)}, u32[]{:S(2)}, u32[]{:S(2)}) collective-permute-start(bf16[1,352,1024]{2,1,0:T(8,128)(2,1)} %get-tuple-element.30), channel_id=1, source_target_pairs={{0,2},{1,5},{2,0},{3,7},{4,6},{5,1},{6,4},{7,3},{8,10},{9,13},{10,... | collective-permute-start | bytes 2162696 | tf_op jit(solution)/shard_map/ppermute | solution.py:353
  429.6 55.4 %collective-permute-start.61 = (bf16[2,128,2816]{2,1,0:T(8,128)(2,1)S(1)}, bf16[2,128,2816]{2,1,0:T(8,128)(2,1)}, u32[]{:S(2)}, u32[]{:S(2)}) collective-permute-start(bf16[2,128,2816]{2,1,0:T(8,128)(2,1)S(1)} %add_convert_fusion.5), channel_id=1, source_target_pairs={{0,8},{24,16},{1,9},{25,17},{2,10},{26,18},{3,11},{27,19},{4,12},{... | collective-permute-start | bytes 4325384 | tf_op jit(solution)/shard_map/ppermute | solution.py:410
  442.0 31.9 %collective-permute-start.53 = (bf16[2,128,1024]{2,1,0:T(8,128)(2,1)S(1)}, bf16[2,128,1024]{2,1,0:T(8,128)(2,1)}, u32[]{:S(2)}, u32[]{:S(2)}) collective-permute-start(bf16[2,128,1024]{2,1,0:T(8,128)(2,1)S(1)} %add_convert_fusion.26), channel_id=1, source_target_pairs={{0,8},{24,16},{1,9},{25,17},{2,10},{26,18},{3,11},{27,19},{4,12},{... | collective-permute-start | bytes 1572872 | tf_op jit(solution)/shard_map/ppermute | solution.py:410
  447.7 29.7 %collective-permute-start.44 = (bf16[3,128,1024]{2,1,0:T(8,128)(2,1)}, bf16[3,128,1024]{2,1,0:T(8,128)(2,1)}, u32[]{:S(2)}, u32[]{:S(2)}) collective-permute-start(bf16[3,128,1024]{2,1,0:T(8,128)(2,1)} %add_convert_fusion.15), channel_id=1, source_target_pairs={{0,4},{1,3},{2,6},{3,1},{4,0},{5,7},{6,2},{7,5},{8,12},{9,11},{10,... | collective-permute-start | bytes 2359304 | tf_op jit(solution)/shard_map/ppermute | solution.py:353
  466.3 22.2 %collective-permute-start.65 = (bf16[1,352,1024]{2,1,0:T(8,128)(2,1)}, bf16[1,352,1024]{2,1,0:T(8,128)(2,1)S(1)}, u32[]{:S(2)}, u32[]{:S(2)}) collective-permute-start(bf16[1,352,1024]{2,1,0:T(8,128)(2,1)} %get-tuple-element.29), channel_id=1, source_target_pairs={{0,2},{1,5},{2,0},{3,7},{4,6},{5,1},{6,4},{7,3},{8,10},{9,13},{10,... | collective-permute-start | bytes 2162696 | tf_op jit(solution)/shard_map/ppermute | solution.py:353
  474.0 14.5 %collective-permute-start.67 = (bf16[1,352,1024]{2,1,0:T(8,128)(2,1)S(1)}, bf16[1,352,1024]{2,1,0:T(8,128)(2,1)S(1)}, u32[]{:S(2)}, u32[]{:S(2)}) collective-permute-start(bf16[1,352,1024]{2,1,0:T(8,128)(2,1)S(1)} %add_convert_fusion.19), channel_id=1, source_target_pairs={{0,4},{1,3},{2,6},{3,1},{4,0},{5,7},{6,2},{7,5},{8,12},{9,11},{10,... | collective-permute-start | bytes 2162696 | tf_op jit(solution)/shard_map/ppermute | solution.py:353
  475.9 28.9 %collective-permute-start.54 = (bf16[2,128,1024]{2,1,0:T(8,128)(2,1)S(1)}, bf16[2,128,1024]{2,1,0:T(8,128)(2,1)}, u32[]{:S(2)}, u32[]{:S(2)}) collective-permute-start(bf16[2,128,1024]{2,1,0:T(8,128)(2,1)S(1)} %add_convert_fusion.25), channel_id=1, source_target_pairs={{8,16},{16,8},{9,17},{17,9},{10,18},{18,10},{11,19},{19,11},{12,20... | collective-permute-start | bytes 1572872 | tf_op jit(solution)/shard_map/ppermute | solution.py:412
  479.2 23.7 %collective-permute-start.45 = (bf16[3,128,1024]{2,1,0:T(8,128)(2,1)S(1)}, bf16[3,128,1024]{2,1,0:T(8,128)(2,1)S(1)}, u32[]{:S(2)}, u32[]{:S(2)}) collective-permute-start(bf16[3,128,1024]{2,1,0:T(8,128)(2,1)S(1)} %add_convert_fusion.14), channel_id=1, source_target_pairs={{0,8},{24,16},{1,9},{25,17},{2,10},{26,18},{3,11},{27,19},{4,12},{... | collective-permute-start | bytes 2359304 | tf_op jit(solution)/shard_map/ppermute | solution.py:410
  486.7 32.8 %collective-permute-start.62 = (bf16[2,128,2816]{2,1,0:T(8,128)(2,1)S(1)}, bf16[2,128,2816]{2,1,0:T(8,128)(2,1)}, u32[]{:S(2)}, u32[]{:S(2)}) collective-permute-start(bf16[2,128,2816]{2,1,0:T(8,128)(2,1)S(1)} %add_convert_fusion.4), channel_id=1, source_target_pairs={{8,16},{16,8},{9,17},{17,9},{10,18},{18,10},{11,19},{19,11},{12,20... | collective-permute-start | bytes 4325384 | tf_op jit(solution)/shard_map/ppermute | solution.py:412
  491.3 23.0 %collective-permute-start.68 = (bf16[1,352,1024]{2,1,0:T(8,128)(2,1)}, bf16[1,352,1024]{2,1,0:T(8,128)(2,1)}, u32[]{:S(2)}, u32[]{:S(2)}) collective-permute-start(bf16[1,352,1024]{2,1,0:T(8,128)(2,1)} %add_convert_fusion.18), channel_id=1, source_target_pairs={{0,8},{24,16},{1,9},{25,17},{2,10},{26,18},{3,11},{27,19},{4,12},{... | collective-permute-start | bytes 2162696 | tf_op jit(solution)/shard_map/ppermute | solution.py:410
  503.3 13.3 %collective-permute-start.46 = (bf16[3,128,1024]{2,1,0:T(8,128)(2,1)S(1)}, bf16[3,128,1024]{2,1,0:T(8,128)(2,1)}, u32[]{:S(2)}, u32[]{:S(2)}) collective-permute-start(bf16[3,128,1024]{2,1,0:T(8,128)(2,1)S(1)} %add_convert_fusion.13), channel_id=1, source_target_pairs={{8,16},{16,8},{9,17},{17,9},{10,18},{18,10},{11,19},{19,11},{12,20... | collective-permute-start | bytes 2359304 | tf_op jit(solution)/shard_map/ppermute | solution.py:412
  506.1 29.9 %collective-permute-start.55 = (bf16[2,128,1024]{2,1,0:T(8,128)(2,1)S(1)}, bf16[2,128,1024]{2,1,0:T(8,128)(2,1)S(1)}, u32[]{:S(2)}, u32[]{:S(2)}) collective-permute-start(bf16[2,128,1024]{2,1,0:T(8,128)(2,1)S(1)} %add_convert_fusion.24), channel_id=1, source_target_pairs={{8,0},{16,24},{9,1},{17,25},{10,2},{18,26},{11,3},{19,27},{12,4},{... | collective-permute-start | bytes 1572872 | tf_op jit(solution)/shard_map/ppermute | solution.py:415
  515.8 18.6 %collective-permute-start.69 = (bf16[1,352,1024]{2,1,0:T(8,128)(2,1)S(1)}, bf16[1,352,1024]{2,1,0:T(8,128)(2,1)S(1)}, u32[]{:S(2)}, u32[]{:S(2)}) collective-permute-start(bf16[1,352,1024]{2,1,0:T(8,128)(2,1)S(1)} %add_convert_fusion.17), channel_id=1, source_target_pairs={{8,16},{16,8},{9,17},{17,9},{10,18},{18,10},{11,19},{19,11},{12,20... | collective-permute-start | bytes 2162696 | tf_op jit(solution)/shard_map/ppermute | solution.py:412
  518.0 46.5 %collective-permute-start.47 = (bf16[3,128,1024]{2,1,0:T(8,128)(2,1)S(1)}, bf16[3,128,1024]{2,1,0:T(8,128)(2,1)S(1)}, u32[]{:S(2)}, u32[]{:S(2)}) collective-permute-start(bf16[3,128,1024]{2,1,0:T(8,128)(2,1)S(1)} %add_convert_fusion.12), channel_id=1, source_target_pairs={{8,0},{16,24},{9,1},{17,25},{10,2},{18,26},{11,3},{19,27},{12,4},{... | collective-permute-start | bytes 2359304 | tf_op jit(solution)/shard_map/ppermute | solution.py:415
  521.3 82.3 %collective-permute-start.63 = (bf16[2,128,2816]{2,1,0:T(8,128)(2,1)S(1)}, bf16[2,128,2816]{2,1,0:T(8,128)(2,1)S(1)}, u32[]{:S(2)}, u32[]{:S(2)}) collective-permute-start(bf16[2,128,2816]{2,1,0:T(8,128)(2,1)S(1)} %add_convert_fusion.3), channel_id=1, source_target_pairs={{8,0},{16,24},{9,1},{17,25},{10,2},{18,26},{11,3},{19,27},{12,4},{... | collective-permute-start | bytes 4325384 | tf_op jit(solution)/shard_map/ppermute | solution.py:415
  534.7 67.7 %collective-permute-start.70 = (bf16[1,352,1024]{2,1,0:T(8,128)(2,1)S(1)}, bf16[1,352,1024]{2,1,0:T(8,128)(2,1)S(1)}, u32[]{:S(2)}, u32[]{:S(2)}) collective-permute-start(bf16[1,352,1024]{2,1,0:T(8,128)(2,1)S(1)} %add_convert_fusion.16), channel_id=1, source_target_pairs={{8,0},{16,24},{9,1},{17,25},{10,2},{18,26},{11,3},{19,27},{12,4},{... | collective-permute-start | bytes 2162696 | tf_op jit(solution)/shard_map/ppermute | solution.py:415
  (61 other events, 519.9 us)

commit v2 on v1

v2 whole, which is shorter than its diff:
```python
import functools

import jax
import jax.numpy as jnp
from jax import lax
from jax.experimental import pallas as pl
from jax.experimental.pallas import tpu as pltpu
from jax.sharding import PartitionSpec as P

EPS = 1e-06
LONGEST_DOC = 1024
LOW = jnp.bfloat16
WIDE = jnp.float32
VMEM_BYTES = 60 * 1024 * 1024
ANY = pl.BlockSpec(memory_space=pl.ANY)


def dot(left, right, left_dim=1, right_dim=0):
    return lax.dot_general(
        left, right, (((left_dim,), (right_dim,)), ((), ())), preferred_element_type=WIDE
    )


def shaped(*shape, kind=LOW):
    return jax.ShapeDtypeStruct(shape, kind)


def call(kernel, scalars, grid, inputs, in_specs, outputs, out_specs, scratch, flops):
    size = sum(a.size * a.dtype.itemsize for a in (*inputs, *outputs))
    return pl.pallas_call(
        kernel,
        out_shape=outputs,
        grid_spec=pltpu.PrefetchScalarGridSpec(
            num_scalar_prefetch=len(scalars),
            grid=grid,
            in_specs=in_specs,
            out_specs=out_specs,
            scratch_shapes=scratch,
        ),
        compiler_params=pltpu.CompilerParams(vmem_limit_bytes=VMEM_BYTES),
        cost_estimate=pl.CostEstimate(
            flops=int(flops), bytes_accessed=int(size), transcendentals=0
        ),
    )(*scalars, *inputs)


def rows_spec(tile, width):
    return pl.BlockSpec((tile, width), lambda i, *_: (i, 0))


def after(value, *others):
    return lax.optimization_barrier((value, *others))[0]


def piece_copies(order_ref, pieces, layers, columns, into_ref, sems):
    copies = []
    for index, piece in enumerate(pieces):
        rows = piece.shape[1]
        at = pl.ds(pl.multiple_of(order_ref[index] * rows, rows), rows)
        copies.append(
            pltpu.make_async_copy(
                piece.at[layers, :, columns], into_ref.at[..., at, :], sems.at[index]
            )
        )
    return copies


def started(copies):
    for copy in copies:
        copy.start()


def finished(copies):
    for copy in copies:
        copy.wait()


def doc_bounds(lengths_ref, row, docs, start, count):
    last = start + count - 1
    end = jnp.int32(0)
    last_from = jnp.int32(0)
    entry_to = jnp.int32(0)
    found = jnp.int32(0)
    for index in range(docs):
        end = end + lengths_ref[row, index]
        last_from = jnp.where(end <= last, end, last_from)
        ends_later = end > start - 1
        entry_to = jnp.where(ends_later & (found == 0), end, entry_to)
        found = jnp.where(ends_later, 1, found)
    return last_from - start, entry_to - start


def doc_starts(lengths_ref, row, docs, start, places):
    end = jnp.int32(0)
    begin = jnp.full(places.shape, -start, jnp.int32)
    for index in range(docs):
        end = end + lengths_ref[row, index]
        begin = jnp.where(places >= end - start, end - start, begin)
    return begin


def column(count, first=0):
    return first + lax.broadcasted_iota(jnp.int32, (count, 1), 0)


def project_kernel(tokens, tile, count, order_ref, h_ref, table_ref, *refs):
    pieces, (left_ref, slope_ref, right_ref, w_ref, sems) = refs[:count], refs[count:]
    step, width = pl.program_id(0), left_ref.shape[1]

    def copies(at):
        columns = pl.ds(pl.multiple_of(at * width, width), width)
        return piece_copies(
            order_ref, pieces, pl.ds(0, 2), columns, w_ref.at[at], sems.at[at]
        )

    @pl.when(step == 0)
    def _():
        for at in range(w_ref.shape[0]):
            started(copies(at))

    finished(copies(step))
    for first in range(0, h_ref.shape[0], tile):
        at = slice(first, first + tile)
        h = h_ref[at, :]
        pre = dot(h, w_ref[step, 0])
        gate = jax.nn.sigmoid(pre)
        decay = table_ref[first % tokens : first % tokens + tile, :].astype(WIDE)
        left_ref[at, :] = (pre * gate * decay).astype(LOW)
        slope_ref[at, :] = (gate * (1.0 + pre * (1.0 - gate)) * decay).astype(LOW)
        right_ref[at, :] = dot(h, w_ref[step, 1]).astype(LOW)


def project(h, table, pieces, order, tokens, tile):
    count, features = h.shape
    width = min(512, features)
    steps = features // width
    out = shaped(count, features)
    block = pl.BlockSpec((count, width), lambda i, *_: (0, i))
    return call(
        functools.partial(project_kernel, tokens, tile, len(pieces)),
        [order],
        (steps,),
        [h, table, *pieces],
        [
            pl.BlockSpec((count, features), lambda i, *_: (0, 0)),
            pl.BlockSpec((tokens, width), lambda i, *_: (0, i)),
            *[ANY] * len(pieces),
        ],
        [out] * 3,
        [block] * 3,
        [
            pltpu.VMEM((steps, 2, features, width), LOW),
            pltpu.SemaphoreType.DMA((steps, len(pieces))),
        ],
        4 * count * features * features,
    )


def state_kernel(docs, start_ref, into_ref, out_ref, lengths_ref, k_ref, v_ref, state_ref):
    count, head_dim = k_ref.shape[0], state_ref.shape[-1]
    last_from, _ = doc_bounds(lengths_ref, pl.program_id(0), docs, start_ref[0], count)
    mask = jnp.broadcast_to((column(count) >= last_from).astype(WIDE), (count, head_dim))
    for head in range(state_ref.shape[1]):
        span = slice(head * head_dim, (head + 1) * head_dim)
        keys = (k_ref[:, span].astype(WIDE) * mask).astype(LOW)
        state_ref[0, head] = (dot(keys, v_ref[:, span], 0, 0) * out_ref[head]).astype(LOW)


def mixing_kernel(
    docs, tile, heads, start_ref, into_ref, out_ref, lengths_ref, q_ref, k_ref, v_ref, o_ref, mask_ref
):
    count, features = q_ref.shape
    head_dim = features // heads
    places = column(count)
    begin = doc_starts(lengths_ref, pl.program_id(0), docs, start_ref[0], places)
    across = lax.broadcasted_iota(jnp.int32, (count, count), 1)
    mask_ref[...] = ((across <= places) & (across >= begin)).astype(WIDE)
    for head in range(heads):
        span = slice(head * head_dim, (head + 1) * head_dim)
        for first in range(0, count, tile):
            upto = first + tile
            scores = dot(q_ref[first:upto, span], k_ref[:upto, span], 1, 1)
            scores = (scores * mask_ref[first:upto, :upto]).astype(LOW)
            o_ref[first:upto, span] = dot(scores, v_ref[:upto, span]).astype(LOW)


def norm_factor(value_rows):
    return lax.rsqrt(jnp.mean(value_rows * value_rows, axis=-1, keepdims=True) + EPS)


def norm_back(value_rows, upstream):
    factor = norm_factor(value_rows)
    inner = jnp.mean(upstream * value_rows, axis=-1, keepdims=True)
    return factor * upstream - (factor * factor * factor * inner) * value_rows


def finish_kernel(
    docs,
    tokens,
    heads,
    count,
    start_ref,
    into_ref,
    out_ref,
    lengths_ref,
    order_ref,
    q_ref,
    u_ref,
    part_ref,
    x_ref,
    state_ref,
    *refs,
):
    pieces = refs[:count]
    mixed_ref, gated_ref, x1_ref, h2_ref, whole_ref, w_ref, sems = refs[count:]
    tile, features = q_ref.shape
    head_dim = features // heads
    step, steps = pl.program_id(0), tokens // tile
    layer = pieces[0].shape[0] - 1
    copies = piece_copies(order_ref, pieces, layer, pl.ds(0, features), w_ref, sems)

    @pl.when(step == 0)
    def _():
        started(copies)

    row = step // steps
    _, entry_to = doc_bounds(lengths_ref, row, docs, start_ref[0], tokens)
    mask = (column(tile, (step % steps) * tile) < entry_to).astype(WIDE)
    mask = jnp.broadcast_to(mask, (tile, head_dim))
    for head in range(heads):
        span = slice(head * head_dim, (head + 1) * head_dim)
        state = (state_ref[0, head].astype(WIDE) * into_ref[head]).astype(LOW)
        whole_ref[:, span] = part_ref[:, span].astype(WIDE) + dot(q_ref[:, span], state) * mask
    mixed = whole_ref[...]
    mixed_ref[...] = mixed.astype(LOW)
    gated = (mixed * norm_factor(mixed) * u_ref[...].astype(WIDE)).astype(LOW)
    gated_ref[...] = gated

    @pl.when(step == 0)
    def _():
        finished(copies)

    x1 = x_ref[...].astype(WIDE) + dot(gated, w_ref[...])
    x1_ref[...] = x1.astype(LOW)
    h2_ref[...] = (x1 * norm_factor(x1)).astype(LOW)


def pair_kernel(tile, count, order_ref, h_ref, *refs):
    pieces, (first_ref, second_ref, turned_ref, w_ref, sems) = refs[:count], refs[count:]
    step, width = pl.program_id(0), first_ref.shape[1]

    def copies(at):
        columns = pl.ds(pl.multiple_of(at * width, 128), width)
        return piece_copies(
            order_ref, pieces, pl.ds(0, 2), columns, w_ref.at[at], sems.at[at]
        )

    @pl.when(step == 0)
    def _():
        for at in range(w_ref.shape[0]):
            started(copies(at))

    finished(copies(step))
    for begin in range(0, h_ref.shape[0], tile):
        at = slice(begin, begin + tile)
        h = h_ref[at, :]
        first = dot(h, w_ref[step, 0])
        second = dot(h, w_ref[step, 1])
        first_ref[at, :] = first.astype(LOW)
        second_ref[at, :] = second.astype(LOW)
        turned_ref[:, at] = (first * second).astype(LOW).T


def pair(h, pieces, order, tile):
    (count, features), hidden = h.shape, pieces[0].shape[-1]
    steps = 2 if hidden % 256 == 0 else 1
    width = hidden // steps
    block = pl.BlockSpec((count, width), lambda i, *_: (0, i))
    return call(
        functools.partial(pair_kernel, tile, len(pieces)),
        [order],
        (steps,),
        [h, *pieces],
        [pl.BlockSpec((count, features), lambda i, *_: (0, 0)), *[ANY] * len(pieces)],
        [shaped(count, hidden), shaped(count, hidden), shaped(hidden, count)],
        [block, block, pl.BlockSpec((width, count), lambda i, *_: (i, 0))],
        [
            pltpu.VMEM((steps, 2, features, width), LOW),
            pltpu.SemaphoreType.DMA((steps, len(pieces))),
        ],
        4 * count * features * hidden,
    )


def down_kernel(count, order_ref, first_ref, second_ref, x1_ref, dy_ref, *refs):
    pieces, (y_ref, dpair_ref, w_ref, sems) = refs[:count], refs[count:]
    copies = piece_copies(order_ref, pieces, 0, pl.ds(0, w_ref.shape[1]), w_ref, sems)

    @pl.when(pl.program_id(0) == 0)
    def _():
        started(copies)
        finished(copies)

    grad = dot(dy_ref[...], w_ref[...], 1, 1)
    dpair_ref[0] = (grad * second_ref[...].astype(WIDE)).astype(LOW)
    dpair_ref[1] = (grad * first_ref[...].astype(WIDE)).astype(LOW)
    glu = (first_ref[...].astype(WIDE) * second_ref[...].astype(WIDE)).astype(LOW)
    y_ref[...] = (x1_ref[...].astype(WIDE) + dot(glu, w_ref[...])).astype(LOW)


def down_and_back(first, second, x1, dy, pieces, order, tile):
    (count, hidden), features = first.shape, x1.shape[1]
    wide, narrow = rows_spec(tile, hidden), rows_spec(tile, features)
    return call(
        functools.partial(down_kernel, len(pieces)),
        [order],
        (count // tile,),
        [first, second, x1, dy, *pieces],
        [wide, wide, narrow, narrow, *[ANY] * len(pieces)],
        [shaped(count, features), shaped(2, count, hidden)],
        [narrow, pl.BlockSpec((2, tile, hidden), lambda i, *_: (0, i, 0))],
        [pltpu.VMEM((hidden, features), LOW), pltpu.SemaphoreType.DMA((len(pieces),))],
        4 * count * features * hidden,
    )


def pair_back_kernel(count, order_ref, dpair_ref, x1_ref, dy_ref, *refs):
    pieces, (e1_ref, w_ref, sems) = refs[:count], refs[count:]
    step = pl.program_id(0)

    def copies(layer):
        return piece_copies(
            order_ref, pieces, layer, pl.ds(0, w_ref.shape[2]), w_ref.at[layer], sems.at[layer]
        )

    @pl.when(step == 0)
    def _():
        started(copies(0))
        started(copies(1))
        finished(copies(0))

    total = dot(dpair_ref[0], w_ref[0], 1, 1)

    @pl.when(step == 0)
    def _():
        finished(copies(1))

    total = total + dot(dpair_ref[1], w_ref[1], 1, 1)
    e1 = dy_ref[...].astype(WIDE) + norm_back(x1_ref[...].astype(WIDE), total)
    e1_ref[...] = e1.astype(LOW)


def pair_back(dpair, x1, dy, pieces, order, tile):
    (_, count, hidden), features = dpair.shape, x1.shape[1]
    narrow = rows_spec(tile, features)
    return call(
        functools.partial(pair_back_kernel, len(pieces)),
        [order],
        (count // tile,),
        [dpair, x1, dy, *pieces],
        [
            pl.BlockSpec((2, tile, hidden), lambda i, *_: (0, i, 0)),
            narrow,
            narrow,
            *[ANY] * len(pieces),
        ],
        [shaped(count, features)],
        [narrow],
        [pltpu.VMEM((2, features, hidden), LOW), pltpu.SemaphoreType.DMA((2, len(pieces)))],
        4 * count * features * hidden,
    )[0]


def back_gate_kernel(
    docs,
    heads,
    count,
    start_ref,
    into_ref,
    out_ref,
    lengths_ref,
    order_ref,
    e1_ref,
    q_ref,
    u_ref,
    mixed_ref,
    *refs,
):
    pieces, (dmixed_ref, du_ref, grad_ref, w_ref, sems) = refs[:count], refs[count:]
    tokens, features = q_ref.shape
    head_dim = features // heads
    layer = pieces[0].shape[0] - 1
    copies = piece_copies(order_ref, pieces, layer, pl.ds(0, features), w_ref, sems)

    @pl.when(pl.program_id(0) == 0)
    def _():
        started(copies)
        finished(copies)

    dgated = dot(e1_ref[...], w_ref[...], 1, 1)
    mixed = mixed_ref[...].astype(WIDE)
    du_ref[...] = (dgated * (mixed * norm_factor(mixed))).astype(LOW)
    dmixed_ref[...] = norm_back(mixed, dgated * u_ref[...].astype(WIDE)).astype(LOW)
    _, entry_to = doc_bounds(lengths_ref, pl.program_id(0), docs, start_ref[0], tokens)
    mask = jnp.broadcast_to((column(tokens) < entry_to).astype(WIDE), (tokens, head_dim))
    for head in range(heads):
        span = slice(head * head_dim, (head + 1) * head_dim)
        queries = (q_ref[:, span].astype(WIDE) * mask).astype(LOW)
        grad_ref[0, head] = (dot(queries, dmixed_ref[:, span], 0, 0) * into_ref[head]).astype(LOW)


def back_mixing_kernel(
    docs,
    tile,
    heads,
    start_ref,
    into_ref,
    out_ref,
    lengths_ref,
    q_ref,
    slope_ref,
    k_ref,
    v_ref,
    dmixed_ref,
    state_ref,
    dq_ref,
    dk_ref,
    dv_ref,
    mask_ref,
    turned_ref,
):
    count, features = q_ref.shape
    head_dim = features // heads
    row, start = pl.program_id(0), start_ref[0]
    _, entry_to = doc_bounds(lengths_ref, row, docs, start, count)
    places = column(count)
    begin = doc_starts(lengths_ref, row, docs, start, places)
    across = lax.broadcasted_iota(jnp.int32, (count, count), 1)
    mask_ref[...] = ((across <= places) & (across >= begin)).astype(WIDE)
    flat = lax.broadcasted_iota(jnp.int32, (1, count), 1)
    begin = doc_starts(lengths_ref, row, docs, start, flat)
    down = lax.broadcasted_iota(jnp.int32, (count, count), 0)
    turned_ref[...] = ((down <= flat) & (down >= begin)).astype(WIDE)
    entry = jnp.broadcast_to((places < entry_to).astype(WIDE), (count, head_dim))
    for head in range(heads):
        span = slice(head * head_dim, (head + 1) * head_dim)
        state = (state_ref[0, head].astype(WIDE) * into_ref[head]).astype(LOW)
        for first in range(0, count, tile):
            upto = first + tile
            here = slice(first, upto)
            grads = dot(dmixed_ref[here, span], v_ref[:upto, span], 1, 1)
            dq = dot((grads * mask_ref[here, :upto]).astype(LOW), k_ref[:upto, span])
            dq = dq + dot(dmixed_ref[here, span], state, 1, 1) * entry[here]
            dq_ref[here, span] = (dq * slope_ref[here, span].astype(WIDE)).astype(LOW)
            turned = turned_ref[here, first:]
            grads = dot(v_ref[here, span], dmixed_ref[first:, span], 1, 1) * turned
            dk_ref[here, span] = dot(grads.astype(LOW), q_ref[first:, span]).astype(LOW)
            scores = dot(k_ref[here, span], q_ref[first:, span], 1, 1) * turned
            dv_ref[here, span] = dot(scores.astype(LOW), dmixed_ref[first:, span]).astype(LOW)


def back_finish_kernel(
    docs,
    heads,
    start_ref,
    into_ref,
    out_ref,
    lengths_ref,
    k_ref,
    slope_ref,
    v_ref,
    dk_part_ref,
    dv_part_ref,
    grad_ref,
    dk_ref,
    dv_ref,
):
    count, features = k_ref.shape
    head_dim = features // heads
    last_from, _ = doc_bounds(lengths_ref, pl.program_id(0), docs, start_ref[0], count)
    mask = jnp.broadcast_to((column(count) >= last_from).astype(WIDE), (count, head_dim))
    for head in range(heads):
        span = slice(head * head_dim, (head + 1) * head_dim)
        grad = (grad_ref[0, head].astype(WIDE) * out_ref[head]).astype(LOW)
        dk = dot(v_ref[:, span], grad, 1, 1) * mask + dk_part_ref[:, span].astype(WIDE)
        dk_ref[:, span] = (dk * slope_ref[:, span].astype(WIDE)).astype(LOW)
        dv = dot(k_ref[:, span], grad) * mask + dv_part_ref[:, span].astype(WIDE)
        dv_ref[:, span] = dv.astype(LOW)


def mixer_back_kernel(counts, order_ref, dq_ref, dk_ref, dv_ref, du_ref, x_ref, e1_ref, *refs):
    total = sum(counts)
    pieces, (out_ref, w_ref, sems) = refs[:total], refs[total:]
    groups = (pieces[: counts[0]], pieces[counts[0] :])
    grads = ((dk_ref, 0, 0), (dv_ref, 0, 1), (dq_ref, 1, 0), (du_ref, 1, 1))
    step, features = pl.program_id(0), x_ref.shape[1]

    def copies(index):
        _, group, layer = grads[index]
        return piece_copies(
            order_ref, groups[group], layer, pl.ds(0, features), w_ref.at[index], sems.at[index]
        )

    @pl.when(step == 0)
    def _():
        for index in range(4):
            started(copies(index))

    total = None
    for index in range(4):

        @pl.when(step == 0)
        def _(index=index):
            finished(copies(index))

        term = dot(grads[index][0][...], w_ref[index], 1, 1)
        total = term if total is None else total + term
    out_ref[...] = e1_ref[...].astype(WIDE) + norm_back(x_ref[...].astype(WIDE), total)


def mixer_back(grads, x, e1, key_value, rest, order, tile):
    count, features = x.shape
    spec = rows_spec(tile, features)
    pieces = [*key_value, *rest]
    return call(
        functools.partial(mixer_back_kernel, (len(key_value), len(rest))),
        [order],
        (count // tile,),
        [*grads, x, e1, *pieces],
        [spec] * 6 + [ANY] * len(pieces),
        [shaped(count, features, kind=WIDE)],
        [spec],
        [
            pltpu.VMEM((4, features, features), LOW),
            pltpu.SemaphoreType.DMA((4, len(key_value))),
        ],
        8 * count * features * features,
    )[0]


def block_grads_kernel(layers, received, order_ref, *refs):
    members = len(layers)
    left_ref, rights, refs = refs[0], refs[1 : 1 + members], refs[1 + members :]
    if received:
        add_ref, *refs = refs
    *out_refs, blocks_ref, turned_ref, right_ref, left_sems, sems = refs
    member, at = pl.program_id(0), pl.program_id(1)
    tiles, width, tile = blocks_ref.shape[0], blocks_ref.shape[2], right_ref.shape[-1]
    steps = right_ref.shape[1]

    def left_copy(index):
        columns = pl.ds(pl.multiple_of(order_ref[index] * width, width), width)
        return pltpu.make_async_copy(
            left_ref.at[:, columns], blocks_ref.at[index], left_sems.at[index]
        )

    def right_copy(index, step):
        right = rights[index] if layers[index] is None else rights[index].at[layers[index]]
        return pltpu.make_async_copy(
            right.at[:, pl.ds(pl.multiple_of(step * tile, 128), tile)],
            right_ref.at[index, step],
            sems.at[index, step],
        )

    @pl.when((member == 0) & (at == 0))
    def _():
        for index in range(tiles):
            left_copy(index).start()
        for index in range(members):
            for step in range(steps):
                right_copy(index, step).start()
        for index in range(tiles):
            left_copy(index).wait()
            turned_ref[index * width : (index + 1) * width, :] = blocks_ref[index].T

    for index in range(members):

        @pl.when(member == index)
        def _(index=index):
            right_copy(index, at).wait()

    term = dot(turned_ref[...], right_ref[member, at])
    if received:
        term = (term + add_ref[0].astype(WIDE)).astype(LOW)
        for index, out_ref in enumerate(out_refs):
            out_ref[0] = term[index * width : (index + 1) * width]
    else:
        out_refs[0][0] = term.astype(LOW)


def block_grads(left, rights, order, received=None):
    (count, features), columns = left.shape, rights[0][0].shape[-1]
    width, blocks = features // 8, order.shape[0]
    steps = 2 if columns % 256 == 0 and columns > 1024 else 1
    tile, members = columns // steps, len(rights)

    def spec(height):
        return pl.BlockSpec((1, height, tile), lambda i, j, *_: (i, 0, j))

    whole = blocks * width
    outputs, height, extra = 1, whole, []
    if received is not None:
        outputs, height, extra = blocks, width, [received]
    results = call(
        functools.partial(block_grads_kernel, [layer for _, layer in rights], bool(extra)),
        [order],
        (members, steps),
        [left, *(right for right, _ in rights), *extra],
        [ANY] * (1 + members) + [spec(whole)] * len(extra),
        [shaped(members, height, columns)] * outputs,
        [spec(height)] * outputs,
        [
            pltpu.VMEM((blocks, count, width), LOW),
            pltpu.VMEM((whole, count), LOW),
            pltpu.VMEM((members, steps, count, tile), LOW),
            pltpu.SemaphoreType.DMA((blocks,)),
            pltpu.SemaphoreType.DMA((members, steps)),
        ],
        2 * members * count * whole * columns,
    )
    return results if extra else results[0]


def row_grads_kernel(half, order_ref, turned_ref, right_ref, send_ref, keep_ref):
    step = pl.program_id(0)
    term = dot(turned_ref[...], right_ref[...]).astype(LOW)

    @pl.when(step < half)
    def _():
        send_ref[0] = term

    @pl.when(step >= half)
    def _():
        keep_ref[0] = term


def row_grads(turned, right, order):
    (hidden, count), columns = turned.shape, right.shape[1]
    blocks = order.shape[0]
    half, width = blocks // 2, hidden // blocks
    out = shaped(half, width, columns)
    return call(
        functools.partial(row_grads_kernel, half),
        [order],
        (blocks,),
        [turned, right],
        [
            pl.BlockSpec((width, count), lambda i, order: (order[(i + half) % blocks], 0)),
            pl.BlockSpec((count, columns), lambda i, *_: (0, 0)),
        ],
        [out, out],
        [
            pl.BlockSpec((1, width, columns), lambda i, *_: (jnp.minimum(i, half - 1), 0, 0)),
            pl.BlockSpec((1, width, columns), lambda i, *_: (jnp.maximum(i - half, 0), 0, 0)),
        ],
        [],
        2 * hidden * count * columns,
    )


def passed_along(value, steps):
    count = lax.axis_size("seq")
    leading, last = max(0, -steps), min(count, count - steps)
    return lax.ppermute(value, "seq", [(source, source + steps) for source in range(leading, last)])


def hops_needed(tokens):
    return min((LONGEST_DOC - 2) // tokens + 1, lax.axis_size("seq") - 1)


def carried(local_state, passing, tokens, steps, between=()):
    message, total, ran = local_state, None, []
    for hop in range(hops_needed(tokens)):
        received = passed_along(message, steps)
        if hop < len(between):
            ran.append(between[hop]())
            received = after(received, *jax.tree.leaves(ran[-1]))
        total = received.astype(WIDE) if total is None else total + received.astype(WIDE)
        message = (passing[..., None, None] * received.astype(WIDE)).astype(LOW)
    return total.astype(LOW), ran


def side_steps(device):
    return (2, 4) if device % 2 == 0 else (4, 2)


def moved(value, kind):
    count = lax.axis_size("dp")
    if kind == "core":
        pairs = [(device, device ^ 1) for device in range(count)]
    else:
        pairs = [(device, device ^ side_steps(device)[kind]) for device in range(count)]
    return lax.ppermute(value, "dp", pairs)


def block_order():
    device = lax.axis_index("dp")
    table = []
    for index in range(8):
        row = []
        for mine in (index, index ^ 1):
            first, second = side_steps(mine)
            row += [mine, mine ^ first, mine ^ second, mine ^ first ^ second]
        table.append(row)
    return jnp.asarray(table, jnp.int32)[device]


def gathered(piece):
    first, second = moved(piece, 0), moved(piece, 1)
    mine = [piece, first, second, moved(first, 1)]
    return mine + [moved(part, "core") for part in mine], (first, second)


def over_seq(value):
    count = lax.axis_size("seq")
    if count % 2:
        return lax.psum(value, "seq")
    place = lax.axis_index("seq")
    total = value
    half = count // 2
    for step in range(half - 1):
        pairs = [(step, step + 1), (count - 1 - step, count - 2 - step)]
        total = (total.astype(WIDE) + lax.ppermute(total, "seq", pairs).astype(WIDE)).astype(LOW)
    pairs = [(half - 1, half), (half, half - 1)]
    total = (total.astype(WIDE) + lax.ppermute(total, "seq", pairs).astype(WIDE)).astype(LOW)
    for step in reversed(range(half - 1)):
        pairs = [(step + 1, step), (count - 2 - step, count - 1 - step)]
        received = lax.ppermute(total, "seq", pairs)
        outside = (place == step) | (place == count - 1 - step)
        total = jnp.where(outside, received, total)
    return total


def plus(*terms):
    return sum(term.astype(WIDE) for term in terms).astype(LOW)


def scattered(own, first, second, across):
    from_across = moved(across, 0)
    from_first = moved(first, 0)
    from_second = moved(plus(second, from_across), 1)
    return over_seq(plus(own, from_first, from_second)).astype(WIDE)


def scattered_plainly(left, rights):
    terms = [
        lax.dot_general(left, right, (((0,), (0,)), ((), ())), preferred_element_type=WIDE)
        for right in rights
    ]
    part = lax.psum_scatter(jnp.stack(terms).astype(LOW), "dp", scatter_dimension=1, tiled=True)
    return over_seq(part).astype(WIDE)


def local(
    hidden_in,
    mixer_weights,
    channel_in_weights,
    channel_out_weights,
    decay_rates,
    doc_lengths,
    out_cotangent,
):
    rows, tokens, features = hidden_in.shape
    heads = decay_rates.shape[1]
    head_dim = features // heads
    docs = doc_lengths.shape[1]
    count = rows * tokens
    tile = min(256, tokens)
    by_hand = lax.axis_size("dp") == 8
    order = block_order() if by_hand else jnp.zeros((1,), jnp.int32)
    rates = decay_rates[0]
    start = lax.axis_index("seq") * jnp.asarray(tokens, jnp.int32)
    centre = tokens // 2
    into = jnp.exp(-rates * (centre + 1))
    out = jnp.exp(-rates * (tokens - 1 - centre))
    scalars = [start[None], into, out, doc_lengths]
    ends = jnp.cumsum(doc_lengths, axis=1, dtype=jnp.int32)
    doc_before = jnp.sum((ends <= start - 1).astype(jnp.int32), axis=1)
    doc_last = jnp.sum((ends <= start + tokens - 1).astype(jnp.int32), axis=1)
    passing = jnp.where(
        (doc_before == doc_last)[:, None], jnp.exp(-rates * tokens)[None, :], 0.0
    )
    centred = (jnp.arange(tokens, dtype=jnp.int32) - centre).astype(WIDE)[:, None]
    spread = jnp.repeat(rates, head_dim)[None, :] * centred
    query_table, key_table = jnp.exp(-spread), jnp.exp(spread)

    def gather(piece, *others):
        if not by_hand:
            return [lax.all_gather(piece, "dp", axis=1, tiled=True)], ()
        return gathered(after(piece, *others) if others else piece)

    mixer = mixer_weights[0]
    key_value, arrived = gather(mixer[1:3].astype(LOW))
    rest = jnp.stack([mixer[0], mixer[3], mixer[4]]).astype(LOW)
    rest, arrived = gather(rest, *arrived)
    channel, arrived = gather(channel_in_weights[0].astype(LOW), *arrived)
    down, arrived = gather(channel_out_weights.astype(LOW), *arrived)

    x = hidden_in.reshape(count, features)
    wide_x = x.astype(WIDE)
    h = (wide_x * norm_factor(wide_x)).astype(LOW)
    dy = out_cotangent.reshape(count, features)
    narrow = shaped(count, features)
    states = shaped(rows, heads, head_dim, head_dim)
    row_spec = rows_spec(tokens, features)
    state_spec = pl.BlockSpec((1, heads, head_dim, head_dim), lambda i, *_: (i, 0, 0, 0))
    square = pltpu.VMEM((tokens, tokens), WIDE)

    k, k_slope, v = project(h, key_table, key_value, order, tokens, tile)
    local_state = call(
        functools.partial(state_kernel, docs),
        scalars,
        (rows,),
        [k, v],
        [row_spec] * 2,
        [states],
        [state_spec],
        [],
        2 * count * features * head_dim,
    )[0]

    def inside():
        q, q_slope, u = project(after(h, local_state), query_table, rest, order, tokens, tile)
        part = call(
            functools.partial(mixing_kernel, docs, tile, heads),
            scalars,
            (rows,),
            [q, k, v],
            [row_spec] * 3,
            [narrow],
            [row_spec],
            [square],
            4 * count * features * tokens,
        )[0]
        return q, q_slope, u, part

    state_in, _ = carried(local_state, passing, tokens, 1)
    q, q_slope, u, part = inside()
    spec = rows_spec(tile, features)
    steps = tokens // tile
    mixed, gated, x1, h2 = call(
        functools.partial(finish_kernel, docs, tokens, heads, len(rest)),
        [*scalars, order],
        (count // tile,),
        [q, u, part, x, state_in, *rest],
        [spec] * 4
        + [
            pl.BlockSpec(
                (1, heads, head_dim, head_dim), lambda i, *_: (i // steps, 0, 0, 0)
            )
        ]
        + [ANY] * len(rest),
        [narrow] * 4,
        [spec] * 4,
        [
            pltpu.VMEM((tile, features), WIDE),
            pltpu.VMEM((features, features), LOW),
            pltpu.SemaphoreType.DMA((len(rest),)),
        ],
        2 * count * features * (features + head_dim),
    )
    first, second, turned = pair(h2, channel, order, tile)
    if by_hand:
        send_down, keep_down = row_grads(turned, dy, order)
        received_down = moved(send_down, "core")
        keep_down = [plus(keep_down[i], received_down[i])[None] for i in range(4)]
        down_gradient = scattered(*keep_down)
        first = after(first, send_down)
    else:
        down_gradient = scattered_plainly(turned.T, [dy])
    y, dpair = down_and_back(first, second, x1, dy, down, order, tile)

    if by_hand:
        sent = block_grads(h2, [(dpair, 0), (dpair, 1)], order[4:])
        received = moved(sent, "core")
        e1 = pair_back(after(dpair, sent), x1, dy, channel, order, tile)
    else:
        channel_gradient = scattered_plainly(h2, [dpair[0], dpair[1]])
        e1 = pair_back(dpair, x1, dy, channel, order, tile)
    dmixed, du, local_grad = call(
        functools.partial(back_gate_kernel, docs, heads, len(rest)),
        [*scalars, order],
        (rows,),
        [e1, q, u, mixed, *rest],
        [row_spec] * 4 + [ANY] * len(rest),
        [narrow, narrow, states],
        [row_spec, row_spec, state_spec],
        [pltpu.VMEM((features, features), LOW), pltpu.SemaphoreType.DMA((len(rest),))],
        2 * count * features * (features + head_dim),
    )

    def back_inside(*others):
        return call(
            functools.partial(back_mixing_kernel, docs, tile, heads),
            scalars,
            (rows,),
            [q, q_slope, k, v, after(dmixed, *others), state_in],
            [row_spec] * 5 + [state_spec],
            [narrow] * 3,
            [row_spec] * 3,
            [square] * 2,
            12 * count * features * tokens,
        )

    if by_hand:

        def channel_kept():
            own = after(h2, local_grad)
            return block_grads(own, [(dpair, 0), (dpair, 1)], order[:4], received)

        def inner():
            return back_inside(*kept[0])

        kept = []

        def outer():
            sent_o = block_grads(after(gated, local_grad), [(e1, None)], order[4:])
            kept.append(channel_kept())
            return sent_o, kept[0]

        state_grad, ((sent_o, _), (dq, dk_part, dv_part)) = carried(
            local_grad, passing, tokens, -1, (outer, inner)
        )
        channel_gradient = scattered(*kept[0])
        received_o = moved(sent_o, "core")
        sent_uq = block_grads(after(h, dq), [(du, None), (dq, None)], order[4:])
        received_uq = moved(sent_uq, "core")
    else:
        dq, dk_part, dv_part = back_inside()
        state_grad, _ = carried(local_grad, passing, tokens, -1)
        sent_uq = dq
    dk, dv = call(
        functools.partial(back_finish_kernel, docs, heads),
        scalars,
        (rows,),
        [k, k_slope, v, after(dk_part, sent_uq), dv_part, state_grad],
        [row_spec] * 5 + [state_spec],
        [narrow] * 2,
        [row_spec] * 2,
        [],
        4 * count * features * head_dim,
    )
    grads = [dq, dk, dv, du]
    if by_hand:
        sent_kv = block_grads(h, [(dk, None), (dv, None)], order[4:])
        received_kv = moved(sent_kv, "core")
        kept_o = block_grads(after(gated, sent_kv), [(e1, None)], order[:4], received_o)
        kept_uq = block_grads(
            after(h, sent_kv), [(du, None), (dq, None)], order[:4], received_uq
        )
        kept_kv = block_grads(
            after(h, *kept_o, *kept_uq), [(dk, None), (dv, None)], order[:4], received_kv
        )
        outer_gradient = scattered(
            *(jnp.concatenate([a, b]) for a, b in zip(kept_uq, kept_o))
        )
        inner_gradient = scattered(*kept_kv)
        mixer_gradient = jnp.stack(
            [
                outer_gradient[1],
                inner_gradient[0],
                inner_gradient[1],
                outer_gradient[0],
                outer_gradient[2],
            ]
        )
        grads[0] = after(dq, *kept_kv)
    else:
        mixer_gradient = jnp.concatenate(
            [scattered_plainly(h, grads), scattered_plainly(gated, [e1])]
        )
    upstream = mixer_back(grads, x, e1, key_value, rest, order, tile)
    by_row = (rows, tokens, features)
    return (
        y.reshape(by_row),
        upstream.reshape(by_row),
        mixer_gradient[None],
        channel_gradient[None],
        down_gradient,
    )


def solution(mesh):
    in_specs = (
        P("dp", "seq", None),
        P(None, None, "dp", None),
        P(None, None, "dp", None),
        P(None, "dp", None),
        P(),
        P("dp", None),
        P("dp", "seq", None),
    )
    out_specs = (
        P("dp", "seq", None),
        P("dp", "seq", None),
        P(None, None, "dp", None),
        P(None, None, "dp", None),
        P(None, "dp", None),
    )
    return jax.shard_map(local, mesh=mesh, in_specs=in_specs, out_specs=out_specs, check_vma=False)
```

time: 614 us -> 578 us (0.941)
  matrix products: 166 us -> 0 us
  Pallas kernels: 103 us -> 249 us
  between operations: 16.6 us -> 1.87 us
  waiting for transfers between devices: 176 us -> 188 us
  local copies, waits for them, and re-layouts: 14.9 us -> 7.13 us
    dot_general x31 -> x0, matrix products: 166 us -> none  [the longest x8 57.5 us: product(): return jnp.dot(left, right, preferred_element_type=WIDE)]
    pallas_call x14 -> x21, Pallas kernels: 103 us -> 249 us  [call(): pl.pallas_call(kernel, out_shape=outputs, grid_spec=pltpu.PrefetchScalarG...]
    ppermute x8, waiting for transfers between devices: 20.4 us -> 44.2 us  [over_seq(): lax.ppermute(total, 'seq', pairs).astype(WIDE)]
    ppermute x4, waiting for transfers between devices: 64.6 us -> 48.6 us  [over_seq(): received = lax.ppermute(total, 'seq', pairs)]
    ppermute x55 -> x45, starting transfers between devices: 39.3 us -> 34.7 us  [moved(): return lax.ppermute(value, 'dp', pairs)]
    ppermute x55 -> x45, waiting for transfers between devices: 82 us -> 86.1 us  [moved(): return lax.ppermute(value, 'dp', pairs)]
  transfers between devices with their start and end apart: 71 -> 61, of which waited for: 14 -> 19; matrix products, arithmetic and copies ran while one was open for 23% -> 8% of each run, Pallas kernels for 14% -> 38%
where the time goes in v2:
time: 578 us; the launch traced here: 570 us
  Pallas kernels  249 us (43%)
  waiting for transfers between devices  188 us (33%)
  starting transfers between devices  74.7 us (13%)
  other arithmetic  49.4 us (9%)
  local copies, waits for them, and re-layouts  7.13 us (1%)
    pallas_call x21, Pallas kernels, call(): pl.pallas_call(kernel, out_shape=outputs, grid_spec=pltpu.PrefetchScalarG...  249 us
    ppermute x45, waiting for transfers between devices, moved(): return lax.ppermute(value, 'dp', pairs)  86.1 us
    ppermute x4, waiting for transfers between devices, over_seq(): received = lax.ppermute(total, 'seq', pairs)  48.6 us
    ppermute x8, waiting for transfers between devices, over_seq(): lax.ppermute(total, 'seq', pairs).astype(WIDE)  44.2 us
    ppermute x45, starting transfers between devices, moved(): return lax.ppermute(value, 'dp', pairs)  34.7 us
    ppermute x8, starting transfers between devices, over_seq(): lax.ppermute(total, 'seq', pairs).astype(WIDE)  22.7 us
    convert_element_type x9, other arithmetic, plus(): return sum((term.astype(WIDE) for term in terms)).astype(LOW)  14 us
    ppermute x4, starting transfers between devices, passed_along(): lax.ppermute(value, 'seq', [(source, source + steps) for source in range(...  11.8 us
  transfers between devices with their start and end apart: 61, of which 19 were waited for; matrix products, arithmetic and copies ran while one was open for 8% of the time, Pallas kernels for 38%

profile of v2, /device:TPU:0, one launch (start us, length us, event | category | flops | bytes accessed | tf_op | source)
XLA Modules:
  0.0 570.1 jit_solution(17528578534329944165)
XLA Ops:
  0.6 1.9 convert.13
  3.4 2.9 collective-permute-start
  11.9 7.0 %collective-permute-done.refs_1_ = bf16[2,128,1024]{2,1,0:T(8,128)(2,1)} collective-permute-done((bf16[2,128,1024]{2,1,0:T(8,128)(2,1)}, bf16[2,128,1024]{2,1,0:T(8,128)(2,1)}, u32[]{:S(2)}, u32[]{:S(2)}) %collective-permute-start) | collective-permute-done | bytes 524320 | tf_op jit(solution)/shard_map/ppermute | solution.py:693
  18.9 2.5 collective-permute-start.7
  23.5 1.8 multiply_convert_fusion.h_ref.refs_0_
  25.3 14.5 %collective-permute-done.7.refs_1_.refs_9_ = bf16[3,128,1024]{2,1,0:T(8,128)(2,1)} collective-permute-done((bf16[3,128,1024]{2,1,0:T(8,128)(2,1)S(1)}, bf16[3,128,1024]{2,1,0:T(8,128)(2,1)}, u32[]{:S(2)}, u32[]{:S(2)}) %collective-permute-start.7) | collective-permute-done | bytes 786464 | tf_op jit(solution)/shard_map/ppermute | solution.py:693
  39.8 2.1 collective-permute-start.16
  43.5 3.1 collective-permute-done.2.refs_3_
  47.3 2.6 fusion
  51.6 11.3 %shard_map.119 = (bf16[1024,1024]{1,0:T(8,128)(2,1)}, bf16[1024,1024]{1,0:T(8,128)(2,1)}, bf16[1024,1024]{1,0:T(8,128)(2,1)}) custom-call(s32[8]{0:T(128)} %get-tuple-element.134.order_ref, bf16[1024,1024]{1,0:T(8,128)(2,1)} %multiply_convert_fusion.h_ref.refs_0_, f32[512,1024]{1,0:T(8,128)} %get-tuple-element.132.table_ref, ...), custom_call_target="tpu_custom_call" | custom-call | flops 4294967296 | bytes 14680064 | tf_op jit(solution)/shard_map/pallas_call | solution.py:30
  62.9 4.3 shard_map.120
  67.2 4.7 collective-permute-start.14
  74.7 8.9 %collective-permute-done.14 = bf16[2,8,128,128]{3,2,1,0:T(8,128)(2,1)S(1)} collective-permute-done((bf16[2,8,128,128]{3,2,1,0:T(8,128)(2,1)}, bf16[2,8,128,128]{3,2,1,0:T(8,128)(2,1)S(1)}, u32[]{:S(2)}, u32[]{:S(2)}) %collective-permute-start.14) | collective-permute-done | bytes 524320 | tf_op jit(solution)/shard_map/ppermute | solution.py:664
  86.1 4.3 collective-permute-start.15
  90.4 9.4 %collective-permute-done.17.refs_2_ = bf16[2,128,2816]{2,1,0:T(8,128)(2,1)} collective-permute-done((bf16[2,128,2816]{2,1,0:T(8,128)(2,1)}, bf16[2,128,2816]{2,1,0:T(8,128)(2,1)}, u32[]{:S(2)}, u32[]{:S(2)}) %collective-permute-start.17) | collective-permute-done | bytes 1441824 | tf_op jit(solution)/shard_map/ppermute | solution.py:693
  99.8 2.4 convert_element_type.292.refs_0_
  104.3 18.7 %collective-permute-done.18.refs_3_ = bf16[2,128,2816]{2,1,0:T(8,128)(2,1)} collective-permute-done((bf16[2,128,2816]{2,1,0:T(8,128)(2,1)}, bf16[2,128,2816]{2,1,0:T(8,128)(2,1)}, u32[]{:S(2)}, u32[]{:S(2)}) %collective-permute-start.18) | collective-permute-done | bytes 1441824 | tf_op jit(solution)/shard_map/ppermute | solution.py:693
  127.4 11.5 %shard_map.121 = (bf16[1024,1024]{1,0:T(8,128)(2,1)}, bf16[1024,1024]{1,0:T(8,128)(2,1)}, bf16[1024,1024]{1,0:T(8,128)(2,1)}) custom-call(s32[8]{0:T(128)} %get-tuple-element.134.order_ref, bf16[1024,1024]{1,0:T(8,128)(2,1)} %multiply_convert_fusion.h_ref.refs_0_, f32[512,1024]{1,0:T(8,128)} %get-tuple-element.131.table_ref, ...), custom_call_target="tpu_custom_call" | custom-call | flops 4294967296 | bytes 16777216 | tf_op jit(solution)/shard_map/pallas_call | solution.py:30
  138.9 8.6 %shard_map.122.part_ref = bf16[1024,1024]{1,0:T(8,128)(2,1)} custom-call(s32[1]{0:T(128)} %bitcast.1.start_ref, f32[8]{0:T(128)} %get-tuple-element.138.into_ref, f32[8]{0:T(128)} %get-tuple-element.137.out_ref, s32[2,4]{1,0:T(2,128)} %lengths_ref.11, bf16[1024,1024]{1,0:T(8,128)(2,1)} %get-tuple-element.67.q_ref, ...), custom_call_target="tpu_custom_call" | custom-call | flops 2147483648 | bytes 8388608 | tf_op jit(solution)/shard_map/pallas_call | solution.py:30
  147.5 11.1 %shard_map.123 = (bf16[1024,1024]{1,0:T(8,128)(2,1)}, bf16[1024,1024]{1,0:T(8,128)(2,1)}, bf16[1024,1024]{1,0:T(8,128)(2,1)}, bf16[1024,1024]{1,0:T(8,128)(2,1)}) custom-call(s32[1]{0:T(128)} %bitcast.1.start_ref, f32[8]{0:T(128)} %get-tuple-element.138.into_ref, f32[8]{0:T(128)} %get-tuple-element.137.out_ref, s32[2,4]{1,0:T(2,128)} %lengths_ref.11, ...), custom_call_target="tpu_custom_call" | custom-call | flops 2415919104 | bytes 23592960 | tf_op jit(solution)/shard_map/pallas_call | solution.py:30
  159.7 21.3 %shard_map.124 = (bf16[1024,2816]{1,0:T(8,128)(2,1)}, bf16[1024,2816]{1,0:T(8,128)(2,1)}, bf16[2816,1024]{1,0:T(8,128)(2,1)}) custom-call(s32[8]{0:T(128)} %get-tuple-element.134.order_ref, bf16[1024,1024]{1,0:T(8,128)(2,1)} %get-tuple-element.85.h_ref.refs_0_, bf16[2,128,2816]{2,1,0:T(8,128)(2,1)} %convert_bitcast_fusion.refs_0_, ...), custom_call_target="tpu_custom_call" | custom-call | flops 11811160064 | bytes 30932992 | tf_op jit(solution)/shard_map/pallas_call | solution.py:30
  181.1 13.3 %shard_map.125 = (bf16[4,352,1024]{2,1,0:T(8,128)(2,1)}, bf16[4,352,1024]{2,1,0:T(8,128)(2,1)}) custom-call(s32[8]{0:T(128)} %get-tuple-element.134.order_ref, bf16[2816,1024]{1,0:T(8,128)(2,1)} %get-tuple-element.72.turned_ref, bf16[1024,1024]{1,0:T(8,128)(2,1)} %bitcast.41), custom_call_target="tpu_custom_call" | custom-call | flops 5905580032 | bytes 13631488 | tf_op jit(solution)/shard_map/pallas_call | solution.py:30
  195.3 21.3 %shard_map.126 = (bf16[1024,1024]{1,0:T(8,128)(2,1)}, bf16[2,1024,2816]{2,1,0:T(8,128)(2,1)}) custom-call(s32[8]{0:T(128)} %get-tuple-element.134.order_ref, bf16[1024,2816]{1,0:T(8,128)(2,1)} %get-tuple-element.74.first_ref, bf16[1024,2816]{1,0:T(8,128)(2,1)} %get-tuple-element.75.second_ref, bf16[1024,1024]{1,0:T(8,128)(2,1)} %get-tuple-element.76.x1_ref, ...), custom_call_target="tpu_custom_call" | custom-call | flops 11811160064 | bytes 35127296 | tf_op jit(solution)/shard_map/pallas_call | solution.py:30
  216.5 13.2 %shard_map.127 = bf16[2,512,2816]{2,1,0:T(8,128)(2,1)} custom-call(s32[4]{0:T(128)} %get-tuple-element.136.order_ref, bf16[1024,1024]{1,0:T(8,128)(2,1)} %get-tuple-element.85.h_ref.refs_0_, bf16[2,1024,2816]{2,1,0:T(8,128)(2,1)} %get-tuple-element.81.refs_1_.refs_2_.dpair_ref, bf16[2,1024,2816]{2,1,0:T(8,128)(2,1)} %get-tuple-element.81.refs_1_.refs_2_.dpair_ref), custom_call_target="tpu_custom_call" | custom-call | flops 5905580032 | bytes 30932992 | tf_op jit(solution)/shard_map/pallas_call | solution.py:30
  230.3 12.9 %collective-permute-done.54 = bf16[4,352,1024]{2,1,0:T(8,128)(2,1)S(1)} collective-permute-done((bf16[4,352,1024]{2,1,0:T(8,128)(2,1)}, bf16[4,352,1024]{2,1,0:T(8,128)(2,1)S(1)}, u32[]{:S(2)}, u32[]{:S(2)}) %collective-permute-start.54) | collective-permute-done | bytes 2883616 | tf_op jit(solution)/shard_map/ppermute | solution.py:693
  243.3 2.1 add_convert_fusion.14
  246.9 23.3 %shard_map.128.e1_ref.refs_1_ = bf16[1024,1024]{1,0:T(8,128)(2,1)} custom-call(s32[8]{0:T(128)} %get-tuple-element.134.order_ref, bf16[2,1024,2816]{2,1,0:T(8,128)(2,1)} %get-tuple-element.81.refs_1_.refs_2_.dpair_ref, bf16[1024,1024]{1,0:T(8,128)(2,1)} %get-tuple-element.76.x1_ref, bf16[1024,1024]{1,0:T(8,128)(2,1)} %bitcast.43, ...), custom_call_target="tpu_custom_call" | custom-call | flops 11811160064 | bytes 29360128 | tf_op jit(solution)/shard_map/pallas_call | solution.py:30
  270.2 10.8 %shard_map.129 = (bf16[1024,1024]{1,0:T(8,128)(2,1)}, bf16[1024,1024]{1,0:T(8,128)(2,1)}, bf16[2,8,128,128]{3,2,1,0:T(8,128)(2,1)}) custom-call(s32[1]{0:T(128)} %bitcast.1.start_ref, f32[8]{0:T(128)} %get-tuple-element.138.into_ref, f32[8]{0:T(128)} %get-tuple-element.137.out_ref, s32[2,4]{1,0:T(2,128)} %lengths_ref.11, s32[8]{0:T(128)} %get-tuple-element.134.order_ref, ...), custom_call_target="tpu_custom_call" | custom-call | flops 2415919104 | bytes 19398656 | tf_op jit(solution)/shard_map/pallas_call | solution.py:30
  282.5 4.9 shard_map.133
  288.1 2.6 add_convert_fusion.11
  292.2 14.4 %shard_map.130 = (bf16[2,128,2816]{2,1,0:T(8,128)(2,1)}, bf16[2,128,2816]{2,1,0:T(8,128)(2,1)}, bf16[2,128,2816]{2,1,0:T(8,128)(2,1)}, bf16[2,128,2816]{2,1,0:T(8,128)(2,1)}) custom-call(s32[4]{0:T(128)} %get-tuple-element.135.order_ref, bf16[1024,1024]{1,0:T(8,128)(2,1)} %get-tuple-element.85.h_ref.refs_0_, ...), custom_call_target="tpu_custom_call" | custom-call | flops 5905580032 | bytes 36700160 | tf_op jit(solution)/shard_map/pallas_call | solution.py:30
  310.1 18.6 %shard_map.131 = (bf16[1024,1024]{1,0:T(8,128)(2,1)}, bf16[1024,1024]{1,0:T(8,128)(2,1)}, bf16[1024,1024]{1,0:T(8,128)(2,1)}) custom-call(s32[1]{0:T(128)} %bitcast.1.start_ref, f32[8]{0:T(128)} %get-tuple-element.138.into_ref, f32[8]{0:T(128)} %get-tuple-element.137.out_ref, s32[2,4]{1,0:T(2,128)} %lengths_ref.11, ...), custom_call_target="tpu_custom_call" | custom-call | flops 6442450944 | bytes 17301504 | tf_op jit(solution)/shard_map/pallas_call | solution.py:30
  328.7 6.8 %shard_map.132 = bf16[2,512,1024]{2,1,0:T(8,128)(2,1)} custom-call(s32[4]{0:T(128)} %get-tuple-element.136.order_ref, bf16[1024,1024]{1,0:T(8,128)(2,1)} %multiply_convert_fusion.h_ref.refs_0_, bf16[1024,1024]{1,0:T(8,128)(2,1)} %get-tuple-element.96.refs_1_.du_ref, bf16[1024,1024]{1,0:T(8,128)(2,1)} %get-tuple-element.119.refs_2_.dq_ref), custom_call_target="tpu_custom_call" | custom-call | flops 2147483648 | bytes 8388608 | tf_op jit(solution)/shard_map/pallas_call | solution.py:30
  335.6 2.0 fusion.4.grad_ref
  337.6 7.4 %shard_map.134 = (bf16[1024,1024]{1,0:T(8,128)(2,1)}, bf16[1024,1024]{1,0:T(8,128)(2,1)}) custom-call(s32[1]{0:T(128)} %bitcast.1.start_ref, f32[8]{0:T(128)} %get-tuple-element.138.into_ref, f32[8]{0:T(128)} %get-tuple-element.137.out_ref, s32[2,4]{1,0:T(2,128)} %lengths_ref.11, bf16[1024,1024]{1,0:T(8,128)(2,1)} %get-tuple-element.63.k_ref, ...), custom_call_target="tpu_custom_call" | custom-call | flops 536870912 | bytes 15204352 | tf_op jit(solution)/shard_map/pallas_call | solution.py:30
  345.0 6.8 %shard_map.135 = bf16[2,512,1024]{2,1,0:T(8,128)(2,1)} custom-call(s32[4]{0:T(128)} %get-tuple-element.136.order_ref, bf16[1024,1024]{1,0:T(8,128)(2,1)} %multiply_convert_fusion.h_ref.refs_0_, bf16[1024,1024]{1,0:T(8,128)(2,1)} %get-tuple-element.102.refs_1_.dk_ref, bf16[1024,1024]{1,0:T(8,128)(2,1)} %get-tuple-element.103.refs_2_.dv_ref), custom_call_target="tpu_custom_call" | custom-call | flops 2147483648 | bytes 8388608 | tf_op jit(solution)/shard_map/pallas_call | solution.py:30
  352.4 1.9 add_convert_fusion.10
  354.3 5.3 collective-permute-start.58
  361.1 1.7 add_convert_fusion.3
  362.8 12.2 %collective-permute-done.58 = bf16[1,352,1024]{2,1,0:T(8,128)(2,1)S(1)} collective-permute-done((bf16[1,352,1024]{2,1,0:T(8,128)(2,1)S(1)}, bf16[1,352,1024]{2,1,0:T(8,128)(2,1)S(1)}, u32[]{:S(2)}, u32[]{:S(2)}) %collective-permute-start.58) | collective-permute-done | bytes 720928 | tf_op jit(solution)/shard_map/ppermute | solution.py:723
  378.5 6.0 %shard_map.136 = (bf16[1,128,1024]{2,1,0:T(8,128)(2,1)}, bf16[1,128,1024]{2,1,0:T(8,128)(2,1)}, bf16[1,128,1024]{2,1,0:T(8,128)(2,1)}, bf16[1,128,1024]{2,1,0:T(8,128)(2,1)}) custom-call(s32[4]{0:T(128)} %get-tuple-element.135.order_ref, bf16[1024,1024]{1,0:T(8,128)(2,1)} %get-tuple-element.104.refs_0_, bf16[1024,1024]{1,0:T(8,128)(2,1)} %shard_map.128.e1_ref.refs_1_, ...), custom_call_target="tpu_custom_call" | custom-call | flops 1073741824 | bytes 6291456 | tf_op jit(solution)/shard_map/pallas_call | solution.py:30
  384.5 8.2 %shard_map.137 = (bf16[2,128,1024]{2,1,0:T(8,128)(2,1)}, bf16[2,128,1024]{2,1,0:T(8,128)(2,1)}, bf16[2,128,1024]{2,1,0:T(8,128)(2,1)}, bf16[2,128,1024]{2,1,0:T(8,128)(2,1)}) custom-call(s32[4]{0:T(128)} %get-tuple-element.135.order_ref, bf16[1024,1024]{1,0:T(8,128)(2,1)} %multiply_convert_fusion.h_ref.refs_0_, ...), custom_call_target="tpu_custom_call" | custom-call | flops 2147483648 | bytes 10485760 | tf_op jit(solution)/shard_map/pallas_call | solution.py:30
  392.8 2.1 pad_maximum_fusion.1
  397.8 8.1 %shard_map.138 = (bf16[2,128,1024]{2,1,0:T(8,128)(2,1)}, bf16[2,128,1024]{2,1,0:T(8,128)(2,1)}, bf16[2,128,1024]{2,1,0:T(8,128)(2,1)}, bf16[2,128,1024]{2,1,0:T(8,128)(2,1)}) custom-call(s32[4]{0:T(128)} %get-tuple-element.135.order_ref, bf16[1024,1024]{1,0:T(8,128)(2,1)} %multiply_convert_fusion.h_ref.refs_0_, ...), custom_call_target="tpu_custom_call" | custom-call | flops 2147483648 | bytes 10485760 | tf_op jit(solution)/shard_map/pallas_call | solution.py:30
  408.0 2.3 add_convert_fusion.2
  410.4 10.7 %collective-permute-done.43 = bf16[2,128,1024]{2,1,0:T(8,128)(2,1)S(1)} collective-permute-done((bf16[2,128,1024]{2,1,0:T(8,128)(2,1)}, bf16[2,128,1024]{2,1,0:T(8,128)(2,1)S(1)}, u32[]{:S(2)}, u32[]{:S(2)}) %collective-permute-start.43) | collective-permute-done | bytes 524320 | tf_op jit(solution)/shard_map/ppermute | solution.py:693
  421.1 6.8 %collective-permute-start.51 = (bf16[2,128,2816]{2,1,0:T(8,128)(2,1)S(1)}, bf16[2,128,2816]{2,1,0:T(8,128)(2,1)S(1)}, u32[]{:S(2)}, u32[]{:S(2)}) collective-permute-start(bf16[2,128,2816]{2,1,0:T(8,128)(2,1)S(1)} %add_convert_fusion.2), channel_id=1, source_target_pairs={{0,8},{24,16},{1,9},{25,17},{2,10},{26,18},{3,11},{27,19},{4,12},{... | collective-permute-start | bytes 4325384 | tf_op jit(solution)/shard_map/ppermute | solution.py:723
  430.1 1.7 collective-permute-start.38
  434.6 2.8 collective-permute-done.44
  437.7 2.7 collective-permute-start.45
  440.4 5.5 collective-permute-done.38
  448.7 11.1 %collective-permute-done.51 = bf16[2,128,2816]{2,1,0:T(8,128)(2,1)S(1)} collective-permute-done((bf16[2,128,2816]{2,1,0:T(8,128)(2,1)S(1)}, bf16[2,128,2816]{2,1,0:T(8,128)(2,1)S(1)}, u32[]{:S(2)}, u32[]{:S(2)}) %collective-permute-start.51) | collective-permute-done | bytes 1441824 | tf_op jit(solution)/shard_map/ppermute | solution.py:723
  460.2 1.9 collective-permute-start.52
  462.1 9.0 %collective-permute-done.45 = bf16[2,128,1024]{2,1,0:T(8,128)(2,1)S(1)} collective-permute-done((bf16[2,128,1024]{2,1,0:T(8,128)(2,1)S(1)}, bf16[2,128,1024]{2,1,0:T(8,128)(2,1)S(1)}, u32[]{:S(2)}, u32[]{:S(2)}) %collective-permute-start.45) | collective-permute-done | bytes 524320 | tf_op jit(solution)/shard_map/ppermute | solution.py:723
  472.8 11.9 %collective-permute-done.39 = bf16[3,128,1024]{2,1,0:T(8,128)(2,1)S(1)} collective-permute-done((bf16[3,128,1024]{2,1,0:T(8,128)(2,1)S(1)}, bf16[3,128,1024]{2,1,0:T(8,128)(2,1)S(1)}, u32[]{:S(2)}, u32[]{:S(2)}) %collective-permute-start.39) | collective-permute-done | bytes 786464 | tf_op jit(solution)/shard_map/ppermute | solution.py:723
  486.5 2.3 select_convert_fusion.1
  491.4 2.3 add_convert_fusion.4
  495.0 1.7 add_convert_fusion
  498.2 18.0 %shard_map.139 = f32[1024,1024]{1,0:T(8,128)} custom-call(s32[8]{0:T(128)} %get-tuple-element.134.order_ref, bf16[1024,1024]{1,0:T(8,128)(2,1)} %get-tuple-element.119.refs_2_.dq_ref, bf16[1024,1024]{1,0:T(8,128)(2,1)} %get-tuple-element.102.refs_1_.dk_ref, bf16[1024,1024]{1,0:T(8,128)(2,1)} %get-tuple-element.103.refs_2_.dv_ref, ...), custom_call_target="tpu_custom_call" | custom-call | flops 8589934592 | bytes 27262976 | tf_op jit(solution)/shard_map/pallas_call | solution.py:30
  516.2 7.0 %collective-permute-done.47 = bf16[2,128,1024]{2,1,0:T(8,128)(2,1)S(1)} collective-permute-done((bf16[2,128,1024]{2,1,0:T(8,128)(2,1)S(1)}, bf16[2,128,1024]{2,1,0:T(8,128)(2,1)S(1)}, u32[]{:S(2)}, u32[]{:S(2)}) %collective-permute-start.47) | collective-permute-done | bytes 524320 | tf_op jit(solution)/shard_map/ppermute | solution.py:728
  523.3 18.8 %collective-permute-done.41 = bf16[3,128,1024]{2,1,0:T(8,128)(2,1)} collective-permute-done((bf16[3,128,1024]{2,1,0:T(8,128)(2,1)}, bf16[3,128,1024]{2,1,0:T(8,128)(2,1)}, u32[]{:S(2)}, u32[]{:S(2)}) %collective-permute-start.41) | collective-permute-done | bytes 786464 | tf_op jit(solution)/shard_map/ppermute | solution.py:728
  543.5 1.7 maximum_bitcast_fusion
  545.2 22.7 %collective-permute-done.53 = bf16[2,128,2816]{2,1,0:T(8,128)(2,1)S(1)} collective-permute-done((bf16[2,128,2816]{2,1,0:T(8,128)(2,1)S(1)}, bf16[2,128,2816]{2,1,0:T(8,128)(2,1)S(1)}, u32[]{:S(2)}, u32[]{:S(2)}) %collective-permute-start.53) | collective-permute-done | bytes 1441824 | tf_op jit(solution)/shard_map/ppermute | solution.py:728
  567.9 1.8 bitcast_convert_fusion
  (193 shorter events, 64.8 us)
Async XLA Ops:
  3.4 15.5 %collective-permute-start = (bf16[2,128,1024]{2,1,0:T(8,128)(2,1)}, bf16[2,128,1024]{2,1,0:T(8,128)(2,1)}, u32[]{:S(2)}, u32[]{:S(2)}) collective-permute-start(bf16[2,128,1024]{2,1,0:T(8,128)(2,1)} %slice_bitcast_fusion.refs_0_), channel_id=1, source_target_pairs={{0,2},{1,5},{2,0},{3,7},{4,6},{5,1},{6,4},{7,3},{8,10},{9,13},{10,... | collective-permute-start | bytes 1572872 | tf_op jit(solution)/shard_map/ppermute | solution.py:693
  6.4 12.5 %collective-permute-start.1 = (bf16[2,128,1024]{2,1,0:T(8,128)(2,1)}, bf16[2,128,1024]{2,1,0:T(8,128)(2,1)}, u32[]{:S(2)}, u32[]{:S(2)}) collective-permute-start(bf16[2,128,1024]{2,1,0:T(8,128)(2,1)} %slice_bitcast_fusion.refs_0_), channel_id=1, source_target_pairs={{0,4},{1,3},{2,6},{3,1},{4,0},{5,7},{6,2},{7,5},{8,12},{9,11},{10,... | collective-permute-start | bytes 1572872 | tf_op jit(solution)/shard_map/ppermute | solution.py:693
  7.9 42.0 %collective-permute-start.3 = (bf16[2,128,1024]{2,1,0:T(8,128)(2,1)}, bf16[2,128,1024]{2,1,0:T(8,128)(2,1)}, u32[]{:S(2)}, u32[]{:S(2)}) collective-permute-start(bf16[2,128,1024]{2,1,0:T(8,128)(2,1)} %slice_bitcast_fusion.refs_0_), channel_id=1, source_target_pairs={{0,1},{1,0},{2,3},{3,2},{4,5},{5,4},{6,7},{7,6},{8,9},{9,8},{10,11... | collective-permute-start | bytes 1572872 | tf_op jit(solution)/shard_map/ppermute | solution.py:693
  10.5 39.4 %copy-start.1 = (bf16[3,128,1024]{2,1,0:T(8,128)(2,1)}, bf16[3,128,1024]{2,1,0:T(8,128)(2,1)S(1)}, u32[]{:S(2)}) copy-start(bf16[3,128,1024]{2,1,0:T(8,128)(2,1)S(1)} %pad_maximum_fusion.refs_0_.refs_8_) | copy-start | bytes 2359300
  18.9 20.9 %collective-permute-start.7 = (bf16[3,128,1024]{2,1,0:T(8,128)(2,1)S(1)}, bf16[3,128,1024]{2,1,0:T(8,128)(2,1)}, u32[]{:S(2)}, u32[]{:S(2)}) collective-permute-start(bf16[3,128,1024]{2,1,0:T(8,128)(2,1)S(1)} %pad_maximum_fusion.refs_0_.refs_8_), channel_id=1, source_target_pairs={{0,2},{1,5},{2,0},{3,7},{4,6},{5,1},{6,4},{7,3},{8,10},{9,13},{10,... | collective-permute-start | bytes 2359304 | tf_op jit(solution)/shard_map/ppermute | solution.py:693
  21.4 18.4 %collective-permute-start.8 = (bf16[3,128,1024]{2,1,0:T(8,128)(2,1)S(1)}, bf16[3,128,1024]{2,1,0:T(8,128)(2,1)}, u32[]{:S(2)}, u32[]{:S(2)}) collective-permute-start(bf16[3,128,1024]{2,1,0:T(8,128)(2,1)S(1)} %pad_maximum_fusion.refs_0_.refs_8_), channel_id=1, source_target_pairs={{0,4},{1,3},{2,6},{3,1},{4,0},{5,7},{6,2},{7,5},{8,12},{9,11},{10,... | collective-permute-start | bytes 2359304 | tf_op jit(solution)/shard_map/ppermute | solution.py:693
  22.2 24.4 %collective-permute-start.2 = (bf16[2,128,1024]{2,1,0:T(8,128)(2,1)}, bf16[2,128,1024]{2,1,0:T(8,128)(2,1)S(1)}, u32[]{:S(2)}, u32[]{:S(2)}) collective-permute-start(bf16[2,128,1024]{2,1,0:T(8,128)(2,1)} %collective-permute-done.refs_1_), channel_id=1, source_target_pairs={{0,4},{1,3},{2,6},{3,1},{4,0},{5,7},{6,2},{7,5},{8,12},{9,11},{10,... | collective-permute-start | bytes 1572872 | tf_op jit(solution)/shard_map/ppermute | solution.py:693
  39.8 34.3 %collective-permute-start.16 = (bf16[2,128,2816]{2,1,0:T(8,128)(2,1)}, bf16[2,128,2816]{2,1,0:T(8,128)(2,1)}, u32[]{:S(2)}, u32[]{:S(2)}) collective-permute-start(bf16[2,128,2816]{2,1,0:T(8,128)(2,1)} %convert_bitcast_fusion.refs_0_), channel_id=1, source_target_pairs={{0,2},{1,5},{2,0},{3,7},{4,6},{5,1},{6,4},{7,3},{8,10},{9,13},{10,... | collective-permute-start | bytes 4325384 | tf_op jit(solution)/shard_map/ppermute | solution.py:693
  43.0 7.4 %collective-permute-start.4 = (bf16[2,128,1024]{2,1,0:T(8,128)(2,1)}, bf16[2,128,1024]{2,1,0:T(8,128)(2,1)S(1)}, u32[]{:S(2)}, u32[]{:S(2)}) collective-permute-start(bf16[2,128,1024]{2,1,0:T(8,128)(2,1)} %collective-permute-done.refs_1_), channel_id=1, source_target_pairs={{0,1},{1,0},{2,3},{3,2},{4,5},{5,4},{6,7},{7,6},{8,9},{9,8},{10,11... | collective-permute-start | bytes 1572872 | tf_op jit(solution)/shard_map/ppermute | solution.py:693
  43.0 7.4 %collective-permute-start.5 = (bf16[2,128,1024]{2,1,0:T(8,128)(2,1)}, bf16[2,128,1024]{2,1,0:T(8,128)(2,1)S(1)}, u32[]{:S(2)}, u32[]{:S(2)}) collective-permute-start(bf16[2,128,1024]{2,1,0:T(8,128)(2,1)} %collective-permute-done.1.refs_2_), channel_id=1, source_target_pairs={{0,1},{1,0},{2,3},{3,2},{4,5},{5,4},{6,7},{7,6},{8,9},{9,8},{10,11... | collective-permute-start | bytes 1572872 | tf_op jit(solution)/shard_map/ppermute | solution.py:693
  46.6 3.8 collective-permute-start.6
  49.9 24.2 %collective-permute-start.10 = (bf16[3,128,1024]{2,1,0:T(8,128)(2,1)S(1)}, bf16[3,128,1024]{2,1,0:T(8,128)(2,1)S(1)}, u32[]{:S(2)}, u32[]{:S(2)}) collective-permute-start(bf16[3,128,1024]{2,1,0:T(8,128)(2,1)S(1)} %pad_maximum_fusion.refs_0_.refs_8_), channel_id=1, source_target_pairs={{0,1},{1,0},{2,3},{3,2},{4,5},{5,4},{6,7},{7,6},{8,9},{9,8},{10,11... | collective-permute-start | bytes 2359304 | tf_op jit(solution)/shard_map/ppermute | solution.py:693
  67.2 16.4 %collective-permute-start.14 = (bf16[2,8,128,128]{3,2,1,0:T(8,128)(2,1)}, bf16[2,8,128,128]{3,2,1,0:T(8,128)(2,1)S(1)}, u32[]{:S(2)}, u32[]{:S(2)}) collective-permute-start(bf16[2,8,128,128]{3,2,1,0:T(8,128)(2,1)} %shard_map.120), channel_id=1, source_target_pairs={{0,8},{8,16},{16,24},{1,9},{9,17},{17,25},{2,10},{10,18},{18,26},{... | collective-permute-start | bytes 1572872 | tf_op jit(solution)/shard_map/ppermute | solution.py:664
  72.0 12.3 %collective-permute-start.9 = (bf16[3,128,1024]{2,1,0:T(8,128)(2,1)}, bf16[3,128,1024]{2,1,0:T(8,128)(2,1)S(1)}, u32[]{:S(2)}, u32[]{:S(2)}) collective-permute-start(bf16[3,128,1024]{2,1,0:T(8,128)(2,1)} %collective-permute-done.7.refs_1_.refs_9_), channel_id=1, source_target_pairs={{0,4},{1,3},{2,6},{3,1},{4,0},{5,7},{6,2},{7,5},{8,12},{9,11},{10,... | collective-permute-start | bytes 2359304 | tf_op jit(solution)/shard_map/ppermute | solution.py:693
  72.4 27.4 %collective-permute-start.17 = (bf16[2,128,2816]{2,1,0:T(8,128)(2,1)}, bf16[2,128,2816]{2,1,0:T(8,128)(2,1)}, u32[]{:S(2)}, u32[]{:S(2)}) collective-permute-start(bf16[2,128,2816]{2,1,0:T(8,128)(2,1)} %convert_bitcast_fusion.refs_0_), channel_id=1, source_target_pairs={{0,4},{1,3},{2,6},{3,1},{4,0},{5,7},{6,2},{7,5},{8,12},{9,11},{10,... | collective-permute-start | bytes 4325384 | tf_op jit(solution)/shard_map/ppermute | solution.py:693
  74.0 29.7 %collective-permute-start.19 = (bf16[2,128,2816]{2,1,0:T(8,128)(2,1)}, bf16[2,128,2816]{2,1,0:T(8,128)(2,1)}, u32[]{:S(2)}, u32[]{:S(2)}) collective-permute-start(bf16[2,128,2816]{2,1,0:T(8,128)(2,1)} %convert_bitcast_fusion.refs_0_), channel_id=1, source_target_pairs={{0,1},{1,0},{2,3},{3,2},{4,5},{5,4},{6,7},{7,6},{8,9},{9,8},{10,11... | collective-permute-start | bytes 4325384 | tf_op jit(solution)/shard_map/ppermute | solution.py:693
  74.1 48.9 %collective-permute-start.18 = (bf16[2,128,2816]{2,1,0:T(8,128)(2,1)}, bf16[2,128,2816]{2,1,0:T(8,128)(2,1)}, u32[]{:S(2)}, u32[]{:S(2)}) collective-permute-start(bf16[2,128,2816]{2,1,0:T(8,128)(2,1)} %collective-permute-done.16.refs_1_), channel_id=1, source_target_pairs={{0,4},{1,3},{2,6},{3,1},{4,0},{5,7},{6,2},{7,5},{8,12},{9,11},{10,... | collective-permute-start | bytes 4325384 | tf_op jit(solution)/shard_map/ppermute | solution.py:693
  83.6 2.5 collective-permute-start.11
  84.2 18.0 %collective-permute-start.12 = (bf16[3,128,1024]{2,1,0:T(8,128)(2,1)}, bf16[3,128,1024]{2,1,0:T(8,128)(2,1)S(1)}, u32[]{:S(2)}, u32[]{:S(2)}) collective-permute-start(bf16[3,128,1024]{2,1,0:T(8,128)(2,1)} %collective-permute-done.8.refs_2_.refs_10_), channel_id=1, source_target_pairs={{0,1},{1,0},{2,3},{3,2},{4,5},{5,4},{6,7},{7,6},{8,9},{9,8},{10,11... | collective-permute-start | bytes 2359304 | tf_op jit(solution)/shard_map/ppermute | solution.py:693
  86.1 38.4 %copy-start.4 = (bf16[3,128,1024]{2,1,0:T(8,128)(2,1)}, bf16[3,128,1024]{2,1,0:T(8,128)(2,1)S(1)}, u32[]{:S(2)}) copy-start(bf16[3,128,1024]{2,1,0:T(8,128)(2,1)S(1)} %collective-permute-done.11.refs_5_.refs_13_) | copy-start | bytes 2359300
  86.1 17.6 %collective-permute-start.15 = (bf16[2,8,128,128]{3,2,1,0:T(8,128)(2,1)S(1)}, bf16[2,8,128,128]{3,2,1,0:T(8,128)(2,1)S(1)}, u32[]{:S(2)}, u32[]{:S(2)}) collective-permute-start(bf16[2,8,128,128]{3,2,1,0:T(8,128)(2,1)S(1)} %fusion.1), channel_id=1, source_target_pairs={{0,8},{8,16},{16,24},{1,9},{9,17},{17,25},{2,10},{10,18},{18,26},{... | collective-permute-start | bytes 1572872 | tf_op jit(solution)/shard_map/ppermute | solution.py:664
  99.8 24.7 %collective-permute-start.13 = (bf16[3,128,1024]{2,1,0:T(8,128)(2,1)S(1)}, bf16[3,128,1024]{2,1,0:T(8,128)(2,1)S(1)}, u32[]{:S(2)}, u32[]{:S(2)}) collective-permute-start(bf16[3,128,1024]{2,1,0:T(8,128)(2,1)S(1)} %collective-permute-done.9.refs_3_.refs_11_), channel_id=1, source_target_pairs={{0,1},{1,0},{2,3},{3,2},{4,5},{5,4},{6,7},{7,6},{8,9},{9,8},{10,11... | collective-permute-start | bytes 2359304 | tf_op jit(solution)/shard_map/ppermute | solution.py:693
  102.2 23.6 %collective-permute-start.23 = (bf16[1,352,1024]{2,1,0:T(8,128)(2,1)}, bf16[1,352,1024]{2,1,0:T(8,128)(2,1)S(1)}, u32[]{:S(2)}, u32[]{:S(2)}) collective-permute-start(bf16[1,352,1024]{2,1,0:T(8,128)(2,1)} %convert_element_type.292.refs_0_), channel_id=1, source_target_pairs={{0,2},{1,5},{2,0},{3,7},{4,6},{5,1},{6,4},{7,3},{8,10},{9,13},{10,... | collective-permute-start | bytes 2162696 | tf_op jit(solution)/shard_map/ppermute | solution.py:693
  103.7 55.0 %collective-permute-start.20 = (bf16[2,128,2816]{2,1,0:T(8,128)(2,1)}, bf16[2,128,2816]{2,1,0:T(8,128)(2,1)}, u32[]{:S(2)}, u32[]{:S(2)}) collective-permute-start(bf16[2,128,2816]{2,1,0:T(8,128)(2,1)} %collective-permute-done.16.refs_1_), channel_id=1, source_target_pairs={{0,1},{1,0},{2,3},{3,2},{4,5},{5,4},{6,7},{7,6},{8,9},{9,8},{10,11... | collective-permute-start | bytes 4325384 | tf_op jit(solution)/shard_map/ppermute | solution.py:693
  103.7 55.5 %collective-permute-start.21 = (bf16[2,128,2816]{2,1,0:T(8,128)(2,1)}, bf16[2,128,2816]{2,1,0:T(8,128)(2,1)}, u32[]{:S(2)}, u32[]{:S(2)}) collective-permute-start(bf16[2,128,2816]{2,1,0:T(8,128)(2,1)} %collective-permute-done.17.refs_2_), channel_id=1, source_target_pairs={{0,1},{1,0},{2,3},{3,2},{4,5},{5,4},{6,7},{7,6},{8,9},{9,8},{10,11... | collective-permute-start | bytes 4325384 | tf_op jit(solution)/shard_map/ppermute | solution.py:693
  122.9 36.8 %collective-permute-start.22 = (bf16[2,128,2816]{2,1,0:T(8,128)(2,1)}, bf16[2,128,2816]{2,1,0:T(8,128)(2,1)}, u32[]{:S(2)}, u32[]{:S(2)}) collective-permute-start(bf16[2,128,2816]{2,1,0:T(8,128)(2,1)} %collective-permute-done.18.refs_3_), channel_id=1, source_target_pairs={{0,1},{1,0},{2,3},{3,2},{4,5},{5,4},{6,7},{7,6},{8,9},{9,8},{10,11... | collective-permute-start | bytes 4325384 | tf_op jit(solution)/shard_map/ppermute | solution.py:693
  125.4 33.2 %collective-permute-start.24 = (bf16[1,352,1024]{2,1,0:T(8,128)(2,1)}, bf16[1,352,1024]{2,1,0:T(8,128)(2,1)S(1)}, u32[]{:S(2)}, u32[]{:S(2)}) collective-permute-start(bf16[1,352,1024]{2,1,0:T(8,128)(2,1)} %convert_element_type.292.refs_0_), channel_id=1, source_target_pairs={{0,4},{1,3},{2,6},{3,1},{4,0},{5,7},{6,2},{7,5},{8,12},{9,11},{10,... | collective-permute-start | bytes 2162696 | tf_op jit(solution)/shard_map/ppermute | solution.py:693
  125.8 32.9 %copy-start.24 = (bf16[1,352,1024]{2,1,0:T(8,128)(2,1)}, bf16[1,352,1024]{2,1,0:T(8,128)(2,1)S(1)}, u32[]{:S(2)}) copy-start(bf16[1,352,1024]{2,1,0:T(8,128)(2,1)S(1)} %collective-permute-done.23.refs_1_) | copy-start | bytes 2162692
  125.8 33.5 %collective-permute-start.25 = (bf16[1,352,1024]{2,1,0:T(8,128)(2,1)S(1)}, bf16[1,352,1024]{2,1,0:T(8,128)(2,1)S(1)}, u32[]{:S(2)}, u32[]{:S(2)}) collective-permute-start(bf16[1,352,1024]{2,1,0:T(8,128)(2,1)S(1)} %collective-permute-done.23.refs_1_), channel_id=1, source_target_pairs={{0,4},{1,3},{2,6},{3,1},{4,0},{5,7},{6,2},{7,5},{8,12},{9,11},{10,... | collective-permute-start | bytes 2162696 | tf_op jit(solution)/shard_map/ppermute | solution.py:693
  158.6 35.7 %collective-permute-start.26 = (bf16[1,352,1024]{2,1,0:T(8,128)(2,1)}, bf16[1,352,1024]{2,1,0:T(8,128)(2,1)S(1)}, u32[]{:S(2)}, u32[]{:S(2)}) collective-permute-start(bf16[1,352,1024]{2,1,0:T(8,128)(2,1)} %convert_element_type.292.refs_0_), channel_id=1, source_target_pairs={{0,1},{1,0},{2,3},{3,2},{4,5},{5,4},{6,7},{7,6},{8,9},{9,8},{10,11... | collective-permute-start | bytes 2162696 | tf_op jit(solution)/shard_map/ppermute | solution.py:693
  158.7 35.7 %collective-permute-start.27 = (bf16[1,352,1024]{2,1,0:T(8,128)(2,1)S(1)}, bf16[1,352,1024]{2,1,0:T(8,128)(2,1)}, u32[]{:S(2)}, u32[]{:S(2)}) collective-permute-start(bf16[1,352,1024]{2,1,0:T(8,128)(2,1)S(1)} %collective-permute-done.23.refs_1_), channel_id=1, source_target_pairs={{0,1},{1,0},{2,3},{3,2},{4,5},{5,4},{6,7},{7,6},{8,9},{9,8},{10,11... | collective-permute-start | bytes 2162696 | tf_op jit(solution)/shard_map/ppermute | solution.py:693
  159.2 35.2 %collective-permute-start.28 = (bf16[1,352,1024]{2,1,0:T(8,128)(2,1)S(1)}, bf16[1,352,1024]{2,1,0:T(8,128)(2,1)}, u32[]{:S(2)}, u32[]{:S(2)}) collective-permute-start(bf16[1,352,1024]{2,1,0:T(8,128)(2,1)S(1)} %collective-permute-done.24.refs_2_), channel_id=1, source_target_pairs={{0,1},{1,0},{2,3},{3,2},{4,5},{5,4},{6,7},{7,6},{8,9},{9,8},{10,11... | collective-permute-start | bytes 2162696 | tf_op jit(solution)/shard_map/ppermute | solution.py:693
  159.3 35.1 %collective-permute-start.29 = (bf16[1,352,1024]{2,1,0:T(8,128)(2,1)S(1)}, bf16[1,352,1024]{2,1,0:T(8,128)(2,1)}, u32[]{:S(2)}, u32[]{:S(2)}) collective-permute-start(bf16[1,352,1024]{2,1,0:T(8,128)(2,1)S(1)} %collective-permute-done.25.refs_3_), channel_id=1, source_target_pairs={{0,1},{1,0},{2,3},{3,2},{4,5},{5,4},{6,7},{7,6},{8,9},{9,8},{10,11... | collective-permute-start | bytes 2162696 | tf_op jit(solution)/shard_map/ppermute | solution.py:693
  229.8 62.4 %collective-permute-start.30 = (bf16[2,512,2816]{2,1,0:T(8,128)(2,1)}, bf16[2,512,2816]{2,1,0:T(8,128)(2,1)}, u32[]{:S(2)}, u32[]{:S(2)}) collective-permute-start(bf16[2,512,2816]{2,1,0:T(8,128)(2,1)} %shard_map.127), channel_id=1, source_target_pairs={{0,1},{1,0},{2,3},{3,2},{4,5},{5,4},{6,7},{7,6},{8,9},{9,8},{10,11... | collective-permute-start | bytes 17301512 | tf_op jit(solution)/shard_map/ppermute | solution.py:693
  229.9 13.4 %collective-permute-start.54 = (bf16[4,352,1024]{2,1,0:T(8,128)(2,1)}, bf16[4,352,1024]{2,1,0:T(8,128)(2,1)S(1)}, u32[]{:S(2)}, u32[]{:S(2)}) collective-permute-start(bf16[4,352,1024]{2,1,0:T(8,128)(2,1)} %get-tuple-element.73), channel_id=1, source_target_pairs={{0,1},{1,0},{2,3},{3,2},{4,5},{5,4},{6,7},{7,6},{8,9},{9,8},{10,11... | collective-permute-start | bytes 8650760 | tf_op jit(solution)/shard_map/ppermute | solution.py:693
  245.4 42.7 %collective-permute-start.56 = (bf16[1,352,1024]{2,1,0:T(8,128)(2,1)}, bf16[1,352,1024]{2,1,0:T(8,128)(2,1)}, u32[]{:S(2)}, u32[]{:S(2)}) collective-permute-start(bf16[1,352,1024]{2,1,0:T(8,128)(2,1)} %get-tuple-element.124), channel_id=1, source_target_pairs={{0,2},{1,5},{2,0},{3,7},{4,6},{5,1},{6,4},{7,3},{8,10},{9,13},{10,... | collective-permute-start | bytes 2162696 | tf_op jit(solution)/shard_map/ppermute | solution.py:693
  281.1 26.1 %collective-permute-start.31 = (bf16[2,8,128,128]{3,2,1,0:T(8,128)(2,1)}, bf16[2,8,128,128]{3,2,1,0:T(8,128)(2,1)S(1)}, u32[]{:S(2)}, u32[]{:S(2)}) collective-permute-start(bf16[2,8,128,128]{3,2,1,0:T(8,128)(2,1)} %get-tuple-element.84), channel_id=1, source_target_pairs={{8,0},{16,8},{24,16},{9,1},{17,9},{25,17},{10,2},{18,10},{26,18},{... | collective-permute-start | bytes 1572872 | tf_op jit(solution)/shard_map/ppermute | solution.py:664
  287.4 89.5 %collective-permute-start.33 = (bf16[1,512,1024]{2,1,0:T(8,128)(2,1)}, bf16[1,512,1024]{2,1,0:T(8,128)(2,1)}, u32[]{:S(2)}, u32[]{:S(2)}) collective-permute-start(bf16[1,512,1024]{2,1,0:T(8,128)(2,1)} %shard_map.133), channel_id=1, source_target_pairs={{0,1},{1,0},{2,3},{3,2},{4,5},{5,4},{6,7},{7,6},{8,9},{9,8},{10,11... | collective-permute-start | bytes 3145736 | tf_op jit(solution)/shard_map/ppermute | solution.py:693
  287.5 64.4 %collective-permute-start.55 = (bf16[1,352,1024]{2,1,0:T(8,128)(2,1)}, bf16[1,352,1024]{2,1,0:T(8,128)(2,1)S(1)}, u32[]{:S(2)}, u32[]{:S(2)}) collective-permute-start(bf16[1,352,1024]{2,1,0:T(8,128)(2,1)} %get-tuple-element.123), channel_id=1, source_target_pairs={{0,2},{1,5},{2,0},{3,7},{4,6},{5,1},{6,4},{7,3},{8,10},{9,13},{10,... | collective-permute-start | bytes 2162696 | tf_op jit(solution)/shard_map/ppermute | solution.py:693
  290.6 61.8 %collective-permute-start.57 = (bf16[1,352,1024]{2,1,0:T(8,128)(2,1)}, bf16[1,352,1024]{2,1,0:T(8,128)(2,1)}, u32[]{:S(2)}, u32[]{:S(2)}) collective-permute-start(bf16[1,352,1024]{2,1,0:T(8,128)(2,1)} %add_convert_fusion.11), channel_id=1, source_target_pairs={{0,4},{1,3},{2,6},{3,1},{4,0},{5,7},{6,2},{7,5},{8,12},{9,11},{10,... | collective-permute-start | bytes 2162696 | tf_op jit(solution)/shard_map/ppermute | solution.py:693
  306.6 53.1 %collective-permute-start.49 = (bf16[2,128,2816]{2,1,0:T(8,128)(2,1)}, bf16[2,128,2816]{2,1,0:T(8,128)(2,1)}, u32[]{:S(2)}, u32[]{:S(2)}) collective-permute-start(bf16[2,128,2816]{2,1,0:T(8,128)(2,1)} %get-tuple-element.89), channel_id=1, source_target_pairs={{0,2},{1,5},{2,0},{3,7},{4,6},{5,1},{6,4},{7,3},{8,10},{9,13},{10,... | collective-permute-start | bytes 4325384 | tf_op jit(solution)/shard_map/ppermute | solution.py:693
  308.8 26.7 %collective-permute-start.32 = (bf16[2,8,128,128]{3,2,1,0:T(8,128)(2,1)}, bf16[2,8,128,128]{3,2,1,0:T(8,128)(2,1)}, u32[]{:S(2)}, u32[]{:S(2)}) collective-permute-start(bf16[2,8,128,128]{3,2,1,0:T(8,128)(2,1)} %fusion.3), channel_id=1, source_target_pairs={{8,0},{16,8},{24,16},{9,1},{17,9},{25,17},{10,2},{18,10},{26,18},{... | collective-permute-start | bytes 1572872 | tf_op jit(solution)/shard_map/ppermute | solution.py:664
  335.5 49.0 %collective-permute-start.34 = (bf16[2,512,1024]{2,1,0:T(8,128)(2,1)}, bf16[2,512,1024]{2,1,0:T(8,128)(2,1)}, u32[]{:S(2)}, u32[]{:S(2)}) collective-permute-start(bf16[2,512,1024]{2,1,0:T(8,128)(2,1)} %shard_map.132), channel_id=1, source_target_pairs={{0,1},{1,0},{2,3},{3,2},{4,5},{5,4},{6,7},{7,6},{8,9},{9,8},{10,11... | collective-permute-start | bytes 6291464 | tf_op jit(solution)/shard_map/ppermute | solution.py:693
  351.9 44.4 %collective-permute-start.35 = (bf16[2,512,1024]{2,1,0:T(8,128)(2,1)}, bf16[2,512,1024]{2,1,0:T(8,128)(2,1)}, u32[]{:S(2)}, u32[]{:S(2)}) collective-permute-start(bf16[2,512,1024]{2,1,0:T(8,128)(2,1)} %shard_map.135), channel_id=1, source_target_pairs={{0,1},{1,0},{2,3},{3,2},{4,5},{5,4},{6,7},{7,6},{8,9},{9,8},{10,11... | collective-permute-start | bytes 6291464 | tf_op jit(solution)/shard_map/ppermute | solution.py:693
  354.3 20.7 %collective-permute-start.58 = (bf16[1,352,1024]{2,1,0:T(8,128)(2,1)S(1)}, bf16[1,352,1024]{2,1,0:T(8,128)(2,1)S(1)}, u32[]{:S(2)}, u32[]{:S(2)}) collective-permute-start(bf16[1,352,1024]{2,1,0:T(8,128)(2,1)S(1)} %add_convert_fusion.10), channel_id=1, source_target_pairs={{0,8},{24,16},{1,9},{25,17},{2,10},{26,18},{3,11},{27,19},{4,12},{... | collective-permute-start | bytes 2162696 | tf_op jit(solution)/shard_map/ppermute | solution.py:723
  359.7 46.2 %collective-permute-start.48 = (bf16[2,128,2816]{2,1,0:T(8,128)(2,1)}, bf16[2,128,2816]{2,1,0:T(8,128)(2,1)}, u32[]{:S(2)}, u32[]{:S(2)}) collective-permute-start(bf16[2,128,2816]{2,1,0:T(8,128)(2,1)} %get-tuple-element.87), channel_id=1, source_target_pairs={{0,2},{1,5},{2,0},{3,7},{4,6},{5,1},{6,4},{7,3},{8,10},{9,13},{10,... | collective-permute-start | bytes 4325384 | tf_op jit(solution)/shard_map/ppermute | solution.py:693
  375.1 31.4 %collective-permute-start.50 = (bf16[2,128,2816]{2,1,0:T(8,128)(2,1)S(1)}, bf16[2,128,2816]{2,1,0:T(8,128)(2,1)}, u32[]{:S(2)}, u32[]{:S(2)}) collective-permute-start(bf16[2,128,2816]{2,1,0:T(8,128)(2,1)S(1)} %add_convert_fusion.3), channel_id=1, source_target_pairs={{0,4},{1,3},{2,6},{3,1},{4,0},{5,7},{6,2},{7,5},{8,12},{9,11},{10,... | collective-permute-start | bytes 4325384 | tf_op jit(solution)/shard_map/ppermute | solution.py:693
  376.9 53.2 %collective-permute-start.59 = (bf16[1,352,1024]{2,1,0:T(8,128)(2,1)S(1)}, bf16[1,352,1024]{2,1,0:T(8,128)(2,1)}, u32[]{:S(2)}, u32[]{:S(2)}) collective-permute-start(bf16[1,352,1024]{2,1,0:T(8,128)(2,1)S(1)} %add_convert_fusion.9), channel_id=1, source_target_pairs={{8,16},{16,8},{9,17},{17,9},{10,18},{18,10},{11,19},{19,11},{12,20... | collective-permute-start | bytes 2162696 | tf_op jit(solution)/shard_map/ppermute | solution.py:725
  394.8 45.5 %collective-permute-start.36 = (bf16[3,128,1024]{2,1,0:T(8,128)(2,1)}, bf16[3,128,1024]{2,1,0:T(8,128)(2,1)}, u32[]{:S(2)}, u32[]{:S(2)}) collective-permute-start(bf16[3,128,1024]{2,1,0:T(8,128)(2,1)} %pad_maximum_fusion.1), channel_id=1, source_target_pairs={{0,2},{1,5},{2,0},{3,7},{4,6},{5,1},{6,4},{7,3},{8,10},{9,13},{10,... | collective-permute-start | bytes 2359304 | tf_op jit(solution)/shard_map/ppermute | solution.py:693
  396.3 31.9 %collective-permute-start.37 = (bf16[3,128,1024]{2,1,0:T(8,128)(2,1)}, bf16[3,128,1024]{2,1,0:T(8,128)(2,1)}, u32[]{:S(2)}, u32[]{:S(2)}) collective-permute-start(bf16[3,128,1024]{2,1,0:T(8,128)(2,1)} %pad_maximum_fusion.2), channel_id=1, source_target_pairs={{0,2},{1,5},{2,0},{3,7},{4,6},{5,1},{6,4},{7,3},{8,10},{9,13},{10,... | collective-permute-start | bytes 2359304 | tf_op jit(solution)/shard_map/ppermute | solution.py:693
  405.9 15.2 %collective-permute-start.43 = (bf16[2,128,1024]{2,1,0:T(8,128)(2,1)}, bf16[2,128,1024]{2,1,0:T(8,128)(2,1)S(1)}, u32[]{:S(2)}, u32[]{:S(2)}) collective-permute-start(bf16[2,128,1024]{2,1,0:T(8,128)(2,1)} %get-tuple-element.118), channel_id=1, source_target_pairs={{0,2},{1,5},{2,0},{3,7},{4,6},{5,1},{6,4},{7,3},{8,10},{9,13},{10,... | collective-permute-start | bytes 1572872 | tf_op jit(solution)/shard_map/ppermute | solution.py:693
  406.5 26.7 %collective-permute-start.42 = (bf16[2,128,1024]{2,1,0:T(8,128)(2,1)}, bf16[2,128,1024]{2,1,0:T(8,128)(2,1)S(1)}, u32[]{:S(2)}, u32[]{:S(2)}) collective-permute-start(bf16[2,128,1024]{2,1,0:T(8,128)(2,1)} %get-tuple-element.116), channel_id=1, source_target_pairs={{0,2},{1,5},{2,0},{3,7},{4,6},{5,1},{6,4},{7,3},{8,10},{9,13},{10,... | collective-permute-start | bytes 1572872 | tf_op jit(solution)/shard_map/ppermute | solution.py:693
  421.1 38.8 %collective-permute-start.51 = (bf16[2,128,2816]{2,1,0:T(8,128)(2,1)S(1)}, bf16[2,128,2816]{2,1,0:T(8,128)(2,1)S(1)}, u32[]{:S(2)}, u32[]{:S(2)}) collective-permute-start(bf16[2,128,2816]{2,1,0:T(8,128)(2,1)S(1)} %add_convert_fusion.2), channel_id=1, source_target_pairs={{0,8},{24,16},{1,9},{25,17},{2,10},{26,18},{3,11},{27,19},{4,12},{... | collective-permute-start | bytes 4325384 | tf_op jit(solution)/shard_map/ppermute | solution.py:723
  428.1 9.2 %collective-permute-start.44 = (bf16[2,128,1024]{2,1,0:T(8,128)(2,1)S(1)}, bf16[2,128,1024]{2,1,0:T(8,128)(2,1)S(1)}, u32[]{:S(2)}, u32[]{:S(2)}) collective-permute-start(bf16[2,128,1024]{2,1,0:T(8,128)(2,1)S(1)} %add_convert_fusion.19), channel_id=1, source_target_pairs={{0,4},{1,3},{2,6},{3,1},{4,0},{5,7},{6,2},{7,5},{8,12},{9,11},{10,... | collective-permute-start | bytes 1572872 | tf_op jit(solution)/shard_map/ppermute | solution.py:693
  430.1 15.7 %collective-permute-start.38 = (bf16[3,128,1024]{2,1,0:T(8,128)(2,1)S(1)}, bf16[3,128,1024]{2,1,0:T(8,128)(2,1)S(1)}, u32[]{:S(2)}, u32[]{:S(2)}) collective-permute-start(bf16[3,128,1024]{2,1,0:T(8,128)(2,1)S(1)} %add_convert_fusion.7), channel_id=1, source_target_pairs={{0,4},{1,3},{2,6},{3,1},{4,0},{5,7},{6,2},{7,5},{8,12},{9,11},{10,... | collective-permute-start | bytes 2359304 | tf_op jit(solution)/shard_map/ppermute | solution.py:693
  433.2 53.3 %collective-permute-start.60 = (bf16[1,352,1024]{2,1,0:T(8,128)(2,1)S(1)}, bf16[1,352,1024]{2,1,0:T(8,128)(2,1)}, u32[]{:S(2)}, u32[]{:S(2)}) collective-permute-start(bf16[1,352,1024]{2,1,0:T(8,128)(2,1)S(1)} %add_convert_fusion.8), channel_id=1, source_target_pairs={{8,0},{16,24},{9,1},{17,25},{10,2},{18,26},{11,3},{19,27},{12,4},{... | collective-permute-start | bytes 2162696 | tf_op jit(solution)/shard_map/ppermute | solution.py:728
  437.7 33.4 %collective-permute-start.45 = (bf16[2,128,1024]{2,1,0:T(8,128)(2,1)S(1)}, bf16[2,128,1024]{2,1,0:T(8,128)(2,1)S(1)}, u32[]{:S(2)}, u32[]{:S(2)}) collective-permute-start(bf16[2,128,1024]{2,1,0:T(8,128)(2,1)S(1)} %add_convert_fusion.18), channel_id=1, source_target_pairs={{0,8},{24,16},{1,9},{25,17},{2,10},{26,18},{3,11},{27,19},{4,12},{... | collective-permute-start | bytes 1572872 | tf_op jit(solution)/shard_map/ppermute | solution.py:723
  447.4 37.2 %collective-permute-start.39 = (bf16[3,128,1024]{2,1,0:T(8,128)(2,1)S(1)}, bf16[3,128,1024]{2,1,0:T(8,128)(2,1)S(1)}, u32[]{:S(2)}, u32[]{:S(2)}) collective-permute-start(bf16[3,128,1024]{2,1,0:T(8,128)(2,1)S(1)} %add_convert_fusion.6), channel_id=1, source_target_pairs={{0,8},{24,16},{1,9},{25,17},{2,10},{26,18},{3,11},{27,19},{4,12},{... | collective-permute-start | bytes 2359304 | tf_op jit(solution)/shard_map/ppermute | solution.py:723
  460.2 34.7 %collective-permute-start.52 = (bf16[2,128,2816]{2,1,0:T(8,128)(2,1)S(1)}, bf16[2,128,2816]{2,1,0:T(8,128)(2,1)}, u32[]{:S(2)}, u32[]{:S(2)}) collective-permute-start(bf16[2,128,2816]{2,1,0:T(8,128)(2,1)S(1)} %add_convert_fusion.1), channel_id=1, source_target_pairs={{8,16},{16,8},{9,17},{17,9},{10,18},{18,10},{11,19},{19,11},{12,20... | collective-permute-start | bytes 4325384 | tf_op jit(solution)/shard_map/ppermute | solution.py:725
  471.3 17.5 %collective-permute-start.46 = (bf16[2,128,1024]{2,1,0:T(8,128)(2,1)S(1)}, bf16[2,128,1024]{2,1,0:T(8,128)(2,1)}, u32[]{:S(2)}, u32[]{:S(2)}) collective-permute-start(bf16[2,128,1024]{2,1,0:T(8,128)(2,1)S(1)} %add_convert_fusion.17), channel_id=1, source_target_pairs={{8,16},{16,8},{9,17},{17,9},{10,18},{18,10},{11,19},{19,11},{12,20... | collective-permute-start | bytes 1572872 | tf_op jit(solution)/shard_map/ppermute | solution.py:725
  484.9 6.4 %collective-permute-start.40 = (bf16[3,128,1024]{2,1,0:T(8,128)(2,1)S(1)}, bf16[3,128,1024]{2,1,0:T(8,128)(2,1)}, u32[]{:S(2)}, u32[]{:S(2)}) collective-permute-start(bf16[3,128,1024]{2,1,0:T(8,128)(2,1)S(1)} %add_convert_fusion.5), channel_id=1, source_target_pairs={{8,16},{16,8},{9,17},{17,9},{10,18},{18,10},{11,19},{19,11},{12,20... | collective-permute-start | bytes 2359304 | tf_op jit(solution)/shard_map/ppermute | solution.py:725
  490.1 33.2 %collective-permute-start.47 = (bf16[2,128,1024]{2,1,0:T(8,128)(2,1)S(1)}, bf16[2,128,1024]{2,1,0:T(8,128)(2,1)S(1)}, u32[]{:S(2)}, u32[]{:S(2)}) collective-permute-start(bf16[2,128,1024]{2,1,0:T(8,128)(2,1)S(1)} %add_convert_fusion.16), channel_id=1, source_target_pairs={{8,0},{16,24},{9,1},{17,25},{10,2},{18,26},{11,3},{19,27},{12,4},{... | collective-permute-start | bytes 1572872 | tf_op jit(solution)/shard_map/ppermute | solution.py:728
  493.7 48.4 %collective-permute-start.41 = (bf16[3,128,1024]{2,1,0:T(8,128)(2,1)}, bf16[3,128,1024]{2,1,0:T(8,128)(2,1)}, u32[]{:S(2)}, u32[]{:S(2)}) collective-permute-start(bf16[3,128,1024]{2,1,0:T(8,128)(2,1)} %add_convert_fusion.4), channel_id=1, source_target_pairs={{8,0},{16,24},{9,1},{17,25},{10,2},{18,26},{11,3},{19,27},{12,4},{... | collective-permute-start | bytes 2359304 | tf_op jit(solution)/shard_map/ppermute | solution.py:728
  496.7 71.2 %collective-permute-start.53 = (bf16[2,128,2816]{2,1,0:T(8,128)(2,1)S(1)}, bf16[2,128,2816]{2,1,0:T(8,128)(2,1)S(1)}, u32[]{:S(2)}, u32[]{:S(2)}) collective-permute-start(bf16[2,128,2816]{2,1,0:T(8,128)(2,1)S(1)} %add_convert_fusion), channel_id=1, source_target_pairs={{8,0},{16,24},{9,1},{17,25},{10,2},{18,26},{11,3},{19,27},{12,4},{... | collective-permute-start | bytes 4325384 | tf_op jit(solution)/shard_map/ppermute | solution.py:728
  (29 other events, 309.3 us)

commit v3 on v2

--- a/solution.py
+++ b/solution.py
@@ -212,7 +212,7 @@
     *refs,
 ):
     pieces = refs[:count]
-    mixed_ref, gated_ref, x1_ref, h2_ref, whole_ref, w_ref, sems = refs[count:]
+    mixed_ref, gated_ref, x1_ref, h2_ref, h2_turned_ref, whole_ref, w_ref, sems = refs[count:]
     tile, features = q_ref.shape
     head_dim = features // heads
     step, steps = pl.program_id(0), tokens // tile
@@ -234,7 +234,7 @@
     mixed = whole_ref[...]
     mixed_ref[...] = mixed.astype(LOW)
     gated = (mixed * norm_factor(mixed) * u_ref[...].astype(WIDE)).astype(LOW)
-    gated_ref[...] = gated
+    gated_ref[...] = gated.T
 
     @pl.when(step == 0)
     def _():
@@ -242,58 +242,62 @@
 
     x1 = x_ref[...].astype(WIDE) + dot(gated, w_ref[...])
     x1_ref[...] = x1.astype(LOW)
-    h2_ref[...] = (x1 * norm_factor(x1)).astype(LOW)
+    h2 = (x1 * norm_factor(x1)).astype(LOW)
+    h2_ref[...] = h2
+    h2_turned_ref[...] = h2.T
 
 
 def pair_kernel(tile, count, order_ref, h_ref, *refs):
-    pieces, (first_ref, second_ref, turned_ref, w_ref, sems) = refs[:count], refs[count:]
+    groups, refs = (refs[:count], refs[count : 2 * count]), refs[2 * count :]
+    first_ref, second_ref, turned_ref, w_ref, sems = refs
     step, width = pl.program_id(0), first_ref.shape[1]
 
-    def copies(at):
+    def copies(at, layer):
         columns = pl.ds(pl.multiple_of(at * width, 128), width)
         return piece_copies(
-            order_ref, pieces, pl.ds(0, 2), columns, w_ref.at[at], sems.at[at]
+            order_ref, groups[layer], 0, columns, w_ref.at[at, layer], sems.at[at, layer]
         )
 
     @pl.when(step == 0)
     def _():
         for at in range(w_ref.shape[0]):
-            started(copies(at))
-
-    finished(copies(step))
+            for layer in range(2):
+                started(copies(at, layer))
+
+    finished(copies(step, 0))
+    first = dot(h_ref[...], w_ref[step, 0])
+    first_ref[...] = first.astype(LOW)
+    finished(copies(step, 1))
     for begin in range(0, h_ref.shape[0], tile):
         at = slice(begin, begin + tile)
-        h = h_ref[at, :]
-        first = dot(h, w_ref[step, 0])
-        second = dot(h, w_ref[step, 1])
-        first_ref[at, :] = first.astype(LOW)
+        second = dot(h_ref[at, :], w_ref[step, 1])
         second_ref[at, :] = second.astype(LOW)
-        turned_ref[:, at] = (first * second).astype(LOW).T
-
-
-def pair(h, pieces, order, tile):
-    (count, features), hidden = h.shape, pieces[0].shape[-1]
+        turned_ref[:, at] = (first_ref[at, :].astype(WIDE) * second).astype(LOW).T
+
+
+def pair(h, first_pieces, second_pieces, order, tile):
+    (count, features), hidden = h.shape, first_pieces[0].shape[-1]
     steps = 2 if hidden % 256 == 0 else 1
-    width = hidden // steps
+    width, many = hidden // steps, len(first_pieces)
     block = pl.BlockSpec((count, width), lambda i, *_: (0, i))
     return call(
-        functools.partial(pair_kernel, tile, len(pieces)),
+        functools.partial(pair_kernel, tile, many),
         [order],
         (steps,),
-        [h, *pieces],
-        [pl.BlockSpec((count, features), lambda i, *_: (0, 0)), *[ANY] * len(pieces)],
+        [h, *first_pieces, *second_pieces],
+        [pl.BlockSpec((count, features), lambda i, *_: (0, 0)), *[ANY] * (2 * many)],
         [shaped(count, hidden), shaped(count, hidden), shaped(hidden, count)],
         [block, block, pl.BlockSpec((width, count), lambda i, *_: (i, 0))],
         [
             pltpu.VMEM((steps, 2, features, width), LOW),
-            pltpu.SemaphoreType.DMA((steps, len(pieces))),
+            pltpu.SemaphoreType.DMA((steps, 2, many)),
         ],
         4 * count * features * hidden,
     )
 
 
-def down_kernel(count, order_ref, first_ref, second_ref, x1_ref, dy_ref, *refs):
-    pieces, (y_ref, dpair_ref, w_ref, sems) = refs[:count], refs[count:]
+def down_back_kernel(count, order_ref, first_ref, second_ref, dy_ref, *refs):
+    pieces, (dpair_ref, w_ref, sems) = refs[:count], refs[count:]
     copies = piece_copies(order_ref, pieces, 0, pl.ds(0, w_ref.shape[1]), w_ref, sems)
 
     @pl.when(pl.program_id(0) == 0)
@@ -304,33 +308,60 @@
     grad = dot(dy_ref[...], w_ref[...], 1, 1)
     dpair_ref[0] = (grad * second_ref[...].astype(WIDE)).astype(LOW)
     dpair_ref[1] = (grad * first_ref[...].astype(WIDE)).astype(LOW)
+
+
+def down_back(first, second, dy, pieces, order, tile):
+    (count, hidden), features = first.shape, dy.shape[1]
+    wide, narrow = rows_spec(tile, hidden), rows_spec(tile, features)
+    return call(
+        functools.partial(down_back_kernel, len(pieces)),
+        [order],
+        (count // tile,),
+        [first, second, dy, *pieces],
+        [wide, wide, narrow, *[ANY] * len(pieces)],
+        [shaped(2, count, hidden)],
+        [pl.BlockSpec((2, tile, hidden), lambda i, *_: (0, i, 0))],
+        [pltpu.VMEM((hidden, features), LOW), pltpu.SemaphoreType.DMA((len(pieces),))],
+        2 * count * features * hidden,
+    )[0]
+
+
+def down_kernel(count, order_ref, first_ref, second_ref, x1_ref, *refs):
+    pieces, (y_ref, w_ref, sems) = refs[:count], refs[count:]
+    copies = piece_copies(order_ref, pieces, 0, pl.ds(0, w_ref.shape[1]), w_ref, sems)
+
+    @pl.when(pl.program_id(0) == 0)
+    def _():
+        started(copies)
+        finished(copies)
+
     glu = (first_ref[...].astype(WIDE) * second_ref[...].astype(WIDE)).astype(LOW)
     y_ref[...] = (x1_ref[...].astype(WIDE) + dot(glu, w_ref[...])).astype(LOW)
 
 
-def down_and_back(first, second, x1, dy, pieces, order, tile):
+def down_forward(first, second, x1, pieces, order, tile):
     (count, hidden), features = first.shape, x1.shape[1]
     wide, narrow = rows_spec(tile, hidden), rows_spec(tile, features)
     return call(
         functools.partial(down_kernel, len(pieces)),
         [order],
         (count // tile,),
-        [first, second, x1, dy, *pieces],
-        [wide, wide, narrow, narrow, *[ANY] * len(pieces)],
-        [shaped(count, features), shaped(2, count, hidden)],
-        [narrow, pl.BlockSpec((2, tile, hidden), lambda i, *_: (0, i, 0))],
+        [first, second, x1, *pieces],
+        [wide, wide, narrow, *[ANY] * len(pieces)],
+        [shaped(count, features)],
+        [narrow],
         [pltpu.VMEM((hidden, features), LOW), pltpu.SemaphoreType.DMA((len(pieces),))],
-        4 * count * features * hidden,
-    )
+        2 * count * features * hidden,
+    )[0]
 
 
 def pair_back_kernel(count, order_ref, dpair_ref, x1_ref, dy_ref, *refs):
-    pieces, (e1_ref, w_ref, sems) = refs[:count], refs[count:]
+    groups, (e1_ref, w_ref, sems) = (refs[:count], refs[count : 2 * count]), refs[2 * count :]
     step = pl.program_id(0)
 
     def copies(layer):
         return piece_copies(
-            order_ref, pieces, layer, pl.ds(0, w_ref.shape[2]), w_ref.at[layer], sems.at[layer]
+            order_ref, groups[layer], 0, pl.ds(0, w_ref.shape[2]), w_ref.at[layer], sems.at[layer]
         )
 
     @pl.when(step == 0)
@@ -350,23 +381,23 @@
     e1_ref[...] = e1.astype(LOW)
 
 
-def pair_back(dpair, x1, dy, pieces, order, tile):
-    (_, count, hidden), features = dpair.shape, x1.shape[1]
+def pair_back(dpair, x1, dy, first_pieces, second_pieces, order, tile):
+    (_, count, hidden), features, many = dpair.shape, x1.shape[1], len(first_pieces)
     narrow = rows_spec(tile, features)
     return call(
-        functools.partial(pair_back_kernel, len(pieces)),
+        functools.partial(pair_back_kernel, many),
         [order],
         (count // tile,),
-        [dpair, x1, dy, *pieces],
+        [dpair, x1, dy, *first_pieces, *second_pieces],
         [
             pl.BlockSpec((2, tile, hidden), lambda i, *_: (0, i, 0)),
             narrow,
             narrow,
-            *[ANY] * len(pieces),
+            *[ANY] * (2 * many),
         ],
         [shaped(count, features)],
         [narrow],
-        [pltpu.VMEM((2, features, hidden), LOW), pltpu.SemaphoreType.DMA((2, len(pieces)))],
+        [pltpu.VMEM((2, features, hidden), LOW), pltpu.SemaphoreType.DMA((2, many))],
         4 * count * features * hidden,
     )[0]
 
@@ -538,20 +569,22 @@
     )[0]
 
 
-def block_grads_kernel(layers, received, order_ref, *refs):
+def block_grads_kernel(layers, mode, order_ref, turned_ref, *refs):
     members = len(layers)
-    left_ref, rights, refs = refs[0], refs[1 : 1 + members], refs[1 + members :]
-    if received:
+    rights, refs = refs[:members], refs[members:]
+    if mode == "keep":
         add_ref, *refs = refs
-    *out_refs, blocks_ref, turned_ref, right_ref, left_sems, sems = refs
-    member, at = pl.program_id(0), pl.program_id(1)
-    tiles, width, tile = blocks_ref.shape[0], blocks_ref.shape[2], right_ref.shape[-1]
-    steps = right_ref.shape[1]
-
-    def left_copy(index):
-        columns = pl.ds(pl.multiple_of(order_ref[index] * width, width), width)
+    *out_refs, left_ref, right_ref, left_sems, sems = refs
+    member, half, at = pl.program_id(0), pl.program_id(1), pl.program_id(2)
+    halves, whole = left_ref.shape[:2]
+    width, tile, steps = whole // 4, right_ref.shape[-1], right_ref.shape[1]
+
+    def left_copy(part, index):
+        block = order_ref[part * 4 + index] * width
         return pltpu.make_async_copy(
-            left_ref.at[:, columns], blocks_ref.at[index], left_sems.at[index]
+            turned_ref.at[pl.ds(pl.multiple_of(block, width), width), :],
+            left_ref.at[part, pl.ds(index * width, width), :],
+            left_sems.at[part, index],
         )
 
     def right_copy(index, step):
@@ -562,99 +595,89 @@
             sems.at[index, step],
         )
 
-    @pl.when((member == 0) & (at == 0))
+    @pl.when((member == 0) & (half == 0) & (at == 0))
     def _():
-        for index in range(tiles):
-            left_copy(index).start()
+        for index in range(4):
+            left_copy(0, index).start()
         for index in range(members):
             for step in range(steps):
                 right_copy(index, step).start()
-        for index in range(tiles):
-            left_copy(index).wait()
-            turned_ref[index * width : (index + 1) * width, :] = blocks_ref[index].T
+        if halves == 2:
+            for index in range(4):
+                left_copy(1, index).start()
+        for index in range(4):
+            left_copy(0, index).wait()
+
+    if halves == 2:
+
+        @pl.when((member == 0) & (half == 1) & (at == 0))
+        def _():
+            for index in range(4):
+                left_copy(1, index).wait()
 
     for index in range(members):
 
-        @pl.when(member == index)
+        @pl.when((member == index) & (half == 0))
         def _(index=index):
             right_copy(index, at).wait()
 
-    term = dot(turned_ref[...], right_ref[member, at])
-    if received:
-        term = (term + add_ref[0].astype(WIDE)).astype(LOW)
-        for index, out_ref in enumerate(out_refs):
-            out_ref[0] = term[index * width : (index + 1) * width]
+    term = dot(left_ref[half], right_ref[member, at])
+    if mode == "keep":
+        term = term + add_ref[0].astype(WIDE)
+    term = term.astype(LOW)
+
+    def keep(refs):
+        for index, ref in enumerate(refs):
+            ref[0] = term[index * width : (index + 1) * width]
+
+    if mode == "send":
+        out_refs[0][0] = term
+    elif mode == "keep":
+        keep(out_refs)
     else:
-        out_refs[0][0] = term.astype(LOW)
-
-
-def block_grads(left, rights, order, received=None):
-    (count, features), columns = left.shape, rights[0][0].shape[-1]
-    width, blocks = features // 8, order.shape[0]
-    steps = 2 if columns % 256 == 0 and columns > 1024 else 1
-    tile, members = columns // steps, len(rights)
-
-    def spec(height):
-        return pl.BlockSpec((1, height, tile), lambda i, j, *_: (i, 0, j))
-
-    whole = blocks * width
-    outputs, height, extra = 1, whole, []
-    if received is not None:
-        outputs, height, extra = blocks, width, [received]
-    results = call(
-        functools.partial(block_grads_kernel, [layer for _, layer in rights], bool(extra)),
+
+        @pl.when(half == 0)
+        def _():
+            out_refs[0][0] = term
+
+        @pl.when(half == 1)
+        def _():
+            keep(out_refs[1:])
+
+
+def block_grads(turned, rights, order, mode, received=None):
+    (features, count), columns = turned.shape, rights[0][0].shape[-1]
+    width, members = features // 8, len(rights)
+    halves = 2 if mode == "both" else 1
+    order = {"send": order[4:], "keep": order[:4], "both": jnp.roll(order, -4)}[mode]
+    steps = 2 if columns % 256 == 0 and (columns > 1024 or members == 1) else 1
+    tile, whole = columns // steps, features // 2
+
+    def sent(i, part, j, *_):
+        return i, 0, jnp.where(part == 0, j, steps - 1)
+
+    def kept(i, part, j, *_):
+        return i, 0, jnp.where(part == halves - 1, j, 0)
+
+    send = shaped(members, whole, columns), pl.BlockSpec((1, whole, tile), sent)
+    keep = shaped(members, width, columns), pl.BlockSpec((1, width, tile), kept)
+    results = {"send": [send], "keep": [keep] * 4, "both": [send] + [keep] * 4}[mode]
+    extra = [received] if mode == "keep" else []
+    return call(
+        functools.partial(block_grads_kernel, [layer for _, layer in rights], mode),
         [order],
-        (members, steps),
-        [left, *(right for right, _ in rights), *extra],
-        [ANY] * (1 + members) + [spec(whole)] * len(extra),
-        [shaped(members, height, columns)] * outputs,
-        [spec(height)] * outputs,
+        (members, halves, steps),
+        [turned, *(right for right, _ in rights), *extra],
+        [ANY] * (1 + members) + [send[1]] * len(extra),
+        [shape for shape, _ in results],
+        [spec for _, spec in results],
         [
-            pltpu.VMEM((blocks, count, width), LOW),
-            pltpu.VMEM((whole, count), LOW),
+            pltpu.VMEM((halves, whole, count), LOW),
             pltpu.VMEM((members, steps, count, tile), LOW),
-            pltpu.SemaphoreType.DMA((blocks,)),
+            pltpu.SemaphoreType.DMA((halves, 4)),
             pltpu.SemaphoreType.DMA((members, steps)),
         ],
-        2 * members * count * whole * columns,
-    )
-    return results if extra else results[0]
-
-
-def row_grads_kernel(half, order_ref, turned_ref, right_ref, send_ref, keep_ref):
-    step = pl.program_id(0)
-    term = dot(turned_ref[...], right_ref[...]).astype(LOW)
-
-    @pl.when(step < half)
-    def _():
-        send_ref[0] = term
-
-    @pl.when(step >= half)
-    def _():
-        keep_ref[0] = term
-
-
-def row_grads(turned, right, order):
-    (hidden, count), columns = turned.shape, right.shape[1]
-    blocks = order.shape[0]
-    half, width = blocks // 2, hidden // blocks
-    out = shaped(half, width, columns)
-    return call(
-        functools.partial(row_grads_kernel, half),
-        [order],
-        (blocks,),
-        [turned, right],
-        [
-            pl.BlockSpec((width, count), lambda i, order: (order[(i + half) % blocks], 0)),
-            pl.BlockSpec((count, columns), lambda i, *_: (0, 0)),
-        ],
-        [out, out],
-        [
-            pl.BlockSpec((1, width, columns), lambda i, *_: (jnp.minimum(i, half - 1), 0, 0)),
-            pl.BlockSpec((1, width, columns), lambda i, *_: (jnp.maximum(i - half, 0), 0, 0)),
-        ],
-        [],
-        2 * hidden * count * columns,
+        2 * members * halves * count * whole * columns,
     )
 
 
@@ -666,18 +689,6 @@
 
 def hops_needed(tokens):
     return min((LONGEST_DOC - 2) // tokens + 1, lax.axis_size("seq") - 1)
-
-
-def carried(local_state, passing, tokens, steps, between=()):
-    message, total, ran = local_state, None, []
-    for hop in range(hops_needed(tokens)):
-        received = passed_along(message, steps)
-        if hop < len(between):
-            ran.append(between[hop]())
-            received = after(received, *jax.tree.leaves(ran[-1]))
-        total = received.astype(WIDE) if total is None else total + received.astype(WIDE)
-        message = (passing[..., None, None] * received.astype(WIDE)).astype(LOW)
-    return total.astype(LOW), ran
 
 
 def side_steps(device):
@@ -705,50 +716,64 @@
     return jnp.asarray(table, jnp.int32)[device]
 
 
-def gathered(piece):
-    first, second = moved(piece, 0), moved(piece, 1)
-    mine = [piece, first, second, moved(first, 1)]
-    return mine + [moved(part, "core") for part in mine], (first, second)
-
-
-def over_seq(value):
-    count = lax.axis_size("seq")
-    if count % 2:
+def across_seq(value):
+    count, place = lax.axis_size("seq"), lax.axis_index("seq")
+    rows = value.shape[-2]
+    if rows % count:
         return lax.psum(value, "seq")
-    place = lax.axis_index("seq")
-    total = value
-    half = count // 2
-    for step in range(half - 1):
-        pairs = [(step, step + 1), (count - 1 - step, count - 2 - step)]
-        total = (total.astype(WIDE) + lax.ppermute(total, "seq", pairs).astype(WIDE)).astype(LOW)
-    pairs = [(half - 1, half), (half, half - 1)]
-    total = (total.astype(WIDE) + lax.ppermute(total, "seq", pairs).astype(WIDE)).astype(LOW)
-    for step in reversed(range(half - 1)):
-        pairs = [(step + 1, step), (count - 2 - step, count - 1 - step)]
-        received = lax.ppermute(total, "seq", pairs)
-        outside = (place == step) | (place == count - 1 - step)
-        total = jnp.where(outside, received, total)
-    return total
+    parts = value.reshape(*value.shape[:-2], count, rows // count, value.shape[-1])
+    axis = parts.ndim - 3
+
+    def shifted(part, step):
+        return lax.ppermute(part, "seq", [(i, (i + step) % count) for i in range(count)])
+
+    def taken(step):
+        return lax.dynamic_index_in_dim(parts, (place + step) % count, axis, keepdims=False)
+
+    total = plus(taken(0), *(shifted(taken(step), step) for step in range(1, count)))
+    result = lax.dynamic_update_index_in_dim(parts, total, place, axis)
+    for step in range(1, count):
+        result = lax.dynamic_update_index_in_dim(
+            result, shifted(total, step), (place - step) % count, axis
+        )
+    return result.reshape(value.shape)
 
 
 def plus(*terms):
     return sum(term.astype(WIDE) for term in terms).astype(LOW)
 
 
-def scattered(own, first, second, across):
-    from_across = moved(across, 0)
-    from_first = moved(first, 0)
-    from_second = moved(plus(second, from_across), 1)
-    return over_seq(plus(own, from_first, from_second)).astype(WIDE)
+class Scatter:
+    def __init__(self, kept, received=None):
+        self.kept, self.received = kept, received
+
+    def block(self, index):
+        if self.received is None:
+            return [self.kept[index]]
+        width = self.kept[index].shape[1]
+        return [self.kept[index], self.received[:, index * width : (index + 1) * width]]
+
+    def begin(self, *others):
+        across, first = after(plus(*self.block(3)), *others), plus(*self.block(1))
+        self.begun = across, first
+        self.from_across, self.from_first = moved(across, 0), moved(first, 0)
+        return self.begun
+
+    def forward(self, *others):
+        second = plus(*self.block(2), after(self.from_across, *others))
+        self.from_second = moved(second, 1)
+        return second
+
+    def finish(self, *others):
+        return plus(*self.block(0), self.from_first, after(self.from_second, *others))
 
 
 def scattered_plainly(left, rights):
     terms = [
-        lax.dot_general(left, right, (((0,), (0,)), ((), ())), preferred_element_type=WIDE)
+        lax.dot_general(left, right, (((1,), (0,)), ((), ())), preferred_element_type=WIDE)
         for right in rights
     ]
-    part = lax.psum_scatter(jnp.stack(terms).astype(LOW), "dp", scatter_dimension=1, tiled=True)
-    return over_seq(part).astype(WIDE)
+    return lax.psum_scatter(jnp.stack(terms).astype(LOW), "dp", scatter_dimension=1, tiled=True)
 
 
 def local(
@@ -784,27 +809,43 @@
     spread = jnp.repeat(rates, head_dim)[None, :] * centred
     query_table, key_table = jnp.exp(-spread), jnp.exp(spread)
 
+    big = min(512, count)
+
+    def hop(message, steps):
+        received = passed_along(message, steps).astype(WIDE)
+        return received, (passing[..., None, None] * received).astype(LOW)
+
     def gather(piece, *others):
         if not by_hand:
-            return [lax.all_gather(piece, "dp", axis=1, tiled=True)], ()
-        return gathered(after(piece, *others) if others else piece)
+            return [lax.all_gather(piece, "dp", axis=1, tiled=True)]
+        piece = after(piece, *others) if others else piece
+        return [piece, moved(piece, 0), moved(piece, 1)]
+
+    def forward(pieces, *others):
+        if not by_hand:
+            return pieces
+        mine = [*pieces, moved(after(pieces[1], *others) if others else pieces[1], 1)]
+        return mine + [moved(part, "core") for part in mine]
+
+    def arrived(pieces):
+        return pieces[1:4]
 
     mixer = mixer_weights[0]
-    key_value, arrived = gather(mixer[1:3].astype(LOW))
+    key_value = forward(gather(mixer[1:3].astype(LOW)))
     rest = jnp.stack([mixer[0], mixer[3], mixer[4]]).astype(LOW)
-    rest, arrived = gather(rest, *arrived)
-    channel, arrived = gather(channel_in_weights[0].astype(LOW), *arrived)
-    down, arrived = gather(channel_out_weights.astype(LOW), *arrived)
+    rest = gather(rest, *arrived(key_value))
 
     x = hidden_in.reshape(count, features)
     wide_x = x.astype(WIDE)
     h = (wide_x * norm_factor(wide_x)).astype(LOW)
+    h_turned = h.T
     dy = out_cotangent.reshape(count, features)
-    narrow = shaped(count, features)
+    narrow, turned_out = shaped(count, features), shaped(features, count)
     states = shaped(rows, heads, head_dim, head_dim)
     row_spec = rows_spec(tokens, features)
     state_spec = pl.BlockSpec((1, heads, head_dim, head_dim), lambda i, *_: (i, 0, 0, 0))
     square = pltpu.VMEM((tokens, tokens), WIDE)
+    hops = hops_needed(tokens)
 
     k, k_slope, v = project(h, key_table, key_value, order, tokens, tile)
     local_state = call(
@@ -818,31 +859,34 @@
         [],
         2 * count * features * head_dim,
     )[0]
-
-    def inside():
-        q, q_slope, u = project(after(h, local_state), query_table, rest, order, tokens, tile)
-        part = call(
-            functools.partial(mixing_kernel, docs, tile, heads),
-            scalars,
-            (rows,),
-            [q, k, v],
-            [row_spec] * 3,
-            [narrow],
-            [row_spec],
-            [square],
-            4 * count * features * tokens,
-        )[0]
-        return q, q_slope, u, part
-
-    state_in, _ = carried(local_state, passing, tokens, 1)
-    q, q_slope, u, part = inside()
+    rest = forward(rest, local_state)
+    first_w = gather(channel_in_weights[0, :1].astype(LOW), *arrived(rest))
+    state_in, message = hop(local_state, 1)
+    q, q_slope, u = project(after(h, message), query_table, rest, order, tokens, tile)
+    first_w = forward(first_w, q)
+    second_w = gather(channel_in_weights[0, 1:].astype(LOW), *arrived(first_w))
+    part = call(
+        functools.partial(mixing_kernel, docs, tile, heads),
+        scalars,
+        (rows,),
+        [after(q, *first_w[1:3]), k, v],
+        [row_spec] * 3,
+        [narrow],
+        [row_spec],
+        [square],
+        4 * count * features * tokens,
+    )[0]
+    for _ in range(hops - 1):
+        received, message = hop(message, 1)
+        state_in = state_in + after(received, part)
     spec = rows_spec(tile, features)
+    turned_spec = pl.BlockSpec((features, tile), lambda i, *_: (0, i))
     steps = tokens // tile
-    mixed, gated, x1, h2 = call(
+    mixed, gated_turned, x1, h2, h2_turned = call(
         functools.partial(finish_kernel, docs, tokens, heads, len(rest)),
         [*scalars, order],
         (count // tile,),
-        [q, u, part, x, state_in, *rest],
+        [q, u, part, x, state_in.astype(LOW), *rest],
         [spec] * 4
         + [
             pl.BlockSpec(
@@ -850,8 +894,8 @@
             )
         ]
         + [ANY] * len(rest),
-        [narrow] * 4,
-        [spec] * 4,
+        [narrow, turned_out, narrow, narrow, turned_out],
+        [spec, turned_spec, spec, spec, turned_spec],
         [
             pltpu.VMEM((tile, features), WIDE),
             pltpu.VMEM((features, features), LOW),
@@ -859,24 +903,34 @@
         ],
         2 * count * features * (features + head_dim),
     )
-    first, second, turned = pair(h2, channel, order, tile)
+    second_w = forward(second_w, h2)
+    down = gather(channel_out_weights.astype(LOW), *arrived(second_w))
+    first, second, turned = pair(h2, first_w, second_w, order, tile)
+    down = forward(down, first)
+
+    down_grads = channel_grads = outer_grads = inner_grads = None
     if by_hand:
-        send_down, keep_down = row_grads(turned, dy, order)
-        received_down = moved(send_down, "core")
-        keep_down = [plus(keep_down[i], received_down[i])[None] for i in range(4)]
-        down_gradient = scattered(*keep_down)
-        first = after(first, send_down)
+        sent, *kept = block_grads(turned, [(dy, None)], order, "both")
+        down_grads = Scatter(kept, moved(sent, "core"))
+        first = after(first, sent)
+    dpair = down_back(first, second, dy, down, order, big)
+    if by_hand:
+        rights = [(dpair, 0), (dpair, 1)]
+        begun = down_grads.begin(dpair)
+        [sent] = block_grads(after(h2_turned, *begun), rights, order, "send")
+        received = moved(sent, "core")
+        y = down_forward(after(first, sent), second, x1, down, order, big)
+        channel_grads = Scatter(block_grads(after(h2_turned, y), rights, order, "keep", received))
+        begun = down_grads.forward(*channel_grads.kept), *channel_grads.begin()
+        e1 = pair_back(after(dpair, *begun), x1, dy, first_w, second_w, order, big)
+        down_part = down_grads.finish(e1)
+        down_total = lax.psum(down_part, "seq")
+        e1 = after(e1, down_part)
     else:
-        down_gradient = scattered_plainly(turned.T, [dy])
-    y, dpair = down_and_back(first, second, x1, dy, down, order, tile)
-
-    if by_hand:
-        sent = block_grads(h2, [(dpair, 0), (dpair, 1)], order[4:])
-        received = moved(sent, "core")
-        e1 = pair_back(after(dpair, sent), x1, dy, channel, order, tile)
-    else:
-        channel_gradient = scattered_plainly(h2, [dpair[0], dpair[1]])
-        e1 = pair_back(dpair, x1, dy, channel, order, tile)
+        y = down_forward(first, second, x1, down, order, big)
+        down_total = lax.psum(scattered_plainly(turned, [dy]), "seq")
+        e1 = pair_back(dpair, x1, dy, first_w, second_w, order, big)
+        channel_total = lax.psum(scattered_plainly(h2_turned, [dpair[0], dpair[1]]), "seq")
     dmixed, du, local_grad = call(
         functools.partial(back_gate_kernel, docs, heads, len(rest)),
         [*scalars, order],
@@ -888,95 +942,81 @@
         [pltpu.VMEM((features, features), LOW), pltpu.SemaphoreType.DMA((len(rest),))],
         2 * count * features * (features + head_dim),
     )
-
-    def back_inside(*others):
-        return call(
-            functools.partial(back_mixing_kernel, docs, tile, heads),
-            scalars,
-            (rows,),
-            [q, q_slope, k, v, after(dmixed, *others), state_in],
-            [row_spec] * 5 + [state_spec],
-            [narrow] * 3,
-            [row_spec] * 3,
-            [square] * 2,
-            12 * count * features * tokens,
-        )
-
+    pins = []
     if by_hand:
-
-        def channel_kept():
-            own = after(h2, local_grad)
-            return block_grads(own, [(dpair, 0), (dpair, 1)], order[:4], received)
-
-        def inner():
-            return back_inside(*kept[0])
-
-        kept = []
-
-        def outer():
-            sent_o = block_grads(after(gated, local_grad), [(e1, None)], order[4:])
-            kept.append(channel_kept())
-            return sent_o, kept[0]
-
-        state_grad, ((sent_o, _), (dq, dk_part, dv_part)) = carried(
-            local_grad, passing, tokens, -1, (outer, inner)
-        )
-        channel_gradient = scattered(*kept[0])
+        second_sent = channel_grads.forward(local_grad)
+        sent_o, *kept_o = block_grads(
+            after(gated_turned, second_sent, local_grad), [(e1, None)], order, "both"
+        )
         received_o = moved(sent_o, "core")
-        sent_uq = block_grads(after(h, dq), [(du, None), (dq, None)], order[4:])
+        pins = [sent_o]
+    state_grad, message = hop(local_grad, -1)
+    message = after(message, *pins)
+    dq, dk_part, dv_part = call(
+        functools.partial(back_mixing_kernel, docs, tile, heads),
+        scalars,
+        (rows,),
+        [q, q_slope, k, v, after(dmixed, message), state_in.astype(LOW)],
+        [row_spec] * 5 + [state_spec],
+        [narrow] * 3,
+        [row_spec] * 3,
+        [square] * 2,
+        12 * count * features * tokens,
+    )
+    pins = [dq]
+    if by_hand:
+        channel_part = channel_grads.finish(dq)
+        channel_total = lax.psum(after(channel_part, down_total), "seq")
+        sent_uq, *kept_uq = block_grads(
+            after(h_turned, channel_part), [(du, None), (dq, None)], order, "both"
+        )
         received_uq = moved(sent_uq, "core")
-    else:
-        dq, dk_part, dv_part = back_inside()
-        state_grad, _ = carried(local_grad, passing, tokens, -1)
-        sent_uq = dq
+        pins = [sent_uq]
+    for _ in range(hops - 1):
+        received, message = hop(message, -1)
+        state_grad = state_grad + after(received, *pins)
     dk, dv = call(
         functools.partial(back_finish_kernel, docs, heads),
         scalars,
         (rows,),
-        [k, k_slope, v, after(dk_part, sent_uq), dv_part, state_grad],
+        [k, k_slope, v, dk_part, dv_part, state_grad.astype(LOW)],
         [row_spec] * 5 + [state_spec],
         [narrow] * 2,
         [row_spec] * 2,
         [],
         4 * count * features * head_dim,
     )
-    grads = [dq, dk, dv, du]
     if by_hand:
-        sent_kv = block_grads(h, [(dk, None), (dv, None)], order[4:])
-        received_kv = moved(sent_kv, "core")
-        kept_o = block_grads(after(gated, sent_kv), [(e1, None)], order[:4], received_o)
-        kept_uq = block_grads(
-            after(h, sent_kv), [(du, None), (dq, None)], order[:4], received_uq
-        )
-        kept_kv = block_grads(
-            after(h, *kept_o, *kept_uq), [(dk, None), (dv, None)], order[:4], received_kv
-        )
-        outer_gradient = scattered(
-            *(jnp.concatenate([a, b]) for a, b in zip(kept_uq, kept_o))
-        )
-        inner_gradient = scattered(*kept_kv)
+        outer_grads = Scatter(
+            [jnp.concatenate([a, b]) for a, b in zip(kept_uq, kept_o)],
+            jnp.concatenate([received_uq, received_o]),
+        )
+        begun = outer_grads.begin(dk)
+        sent_kv, *kept_kv = block_grads(
+            after(h_turned, *begun), [(dk, None), (dv, None)], order, "both"
+        )
+        inner_grads = Scatter(kept_kv, moved(sent_kv, "core"))
+        begun = inner_grads.begin(sent_kv)
+        dq = after(dq, *begun)
+    upstream = mixer_back([dq, dk, dv, du], x, e1, key_value, rest, order, big)
+    if by_hand:
+        outer_total = across_seq(outer_grads.finish(outer_grads.forward(upstream)))
+        inner_total = across_seq(inner_grads.finish(inner_grads.forward(upstream)))
         mixer_gradient = jnp.stack(
-            [
-                outer_gradient[1],
-                inner_gradient[0],
-                inner_gradient[1],
-                outer_gradient[0],
-                outer_gradient[2],
-            ]
-        )
-        grads[0] = after(dq, *kept_kv)
+            [outer_total[1], inner_total[0], inner_total[1], outer_total[0], outer_total[2]]
+        )
     else:
         mixer_gradient = jnp.concatenate(
-            [scattered_plainly(h, grads), scattered_plainly(gated, [e1])]
-        )
-    upstream = mixer_back(grads, x, e1, key_value, rest, order, tile)
+            [scattered_plainly(h_turned, [dq, dk, dv, du]), scattered_plainly(gated_turned, [e1])]
+        )
+        mixer_gradient = lax.psum(mixer_gradient, "seq")
     by_row = (rows, tokens, features)
     return (
         y.reshape(by_row),
         upstream.reshape(by_row),
-        mixer_gradient[None],
-        channel_gradient[None],
-        down_gradient,
+        mixer_gradient.astype(WIDE)[None],
+        channel_total.astype(WIDE)[None],
+        down_total.astype(WIDE),
     )
 
 

time: 578 us -> 622 us (1.076)
  local copies, waits for them, and re-layouts: 7.13 us -> 23.3 us
  between operations: 1.87 us -> 15.5 us
  waiting for transfers between devices: 188 us -> 197 us
    ppermute x12, waiting for transfers between devices: 92.8 us -> 21.7 us  [shifted(): lax.ppermute(part, 'seq', [(i, (i + step) % count) for i in range(count)])]
    psum x0 -> x2, waiting for transfers between devices: none -> 63.3 us  [the longest x1 53 us: local(): channel_total = lax.psum(after(channel_part, down_total), 'seq')]
    ppermute x4, waiting for transfers between devices: 8.92 us -> 30.8 us  [passed_along(): lax.ppermute(value, 'seq', [(source, source + steps) for source in range(...]
    convert_element_type x9 -> x13, other arithmetic: 14 us -> 29.2 us  [plus(): return sum((term.astype(WIDE) for term in terms)).astype(LOW)]
    convert_element_type x17 -> x9, other arithmetic: 19.9 us -> 9.01 us  [the longest x1 1.97 us: local(): state_in.astype(LOW)]
    unnamed x65 -> x112, local copies, waits for them, and re-layouts: 3.6 us -> 11.9 us
    ppermute x45 -> x52, waiting for transfers between devices: 86.1 us -> 80.7 us  [moved(): return lax.ppermute(value, 'dp', pairs)]
    ppermute x45 -> x52, starting transfers between devices: 34.7 us -> 39.5 us  [moved(): return lax.ppermute(value, 'dp', pairs)]
  transfers between devices with their start and end apart: 61 -> 70, of which waited for: 19 -> 22; matrix products, arithmetic and copies ran while one was open for 8% -> 7% of each run, Pallas kernels for 38% -> 30%
where the time goes in v3:
time: 622 us; the launch traced here: 614 us
  Pallas kernels  249 us (40%)
  waiting for transfers between devices  197 us (32%)
  starting transfers between devices  77.7 us (12%)
  other arithmetic  52 us (8%)
  local copies, waits for them, and re-layouts  23.3 us (4%)
  between operations  15.5 us (2%)
    pallas_call x19, Pallas kernels, call(): pl.pallas_call(kernel, out_shape=outputs, grid_spec=pltpu.PrefetchScalarG...  249 us
    ppermute x52, waiting for transfers between devices, moved(): return lax.ppermute(value, 'dp', pairs)  80.7 us
    psum x1, waiting for transfers between devices, local(): channel_total = lax.psum(after(channel_part, down_total), 'seq')  53 us
    ppermute x52, starting transfers between devices, moved(): return lax.ppermute(value, 'dp', pairs)  39.5 us
    ppermute x4, waiting for transfers between devices, passed_along(): lax.ppermute(value, 'seq', [(source, source + steps) for source in range(...  30.8 us
    convert_element_type x13, other arithmetic, plus(): return sum((term.astype(WIDE) for term in terms)).astype(LOW)  29.2 us
    ppermute x12, starting transfers between devices, shifted(): lax.ppermute(part, 'seq', [(i, (i + step) % count) for i in range(count)])  26.6 us
    ppermute x12, waiting for transfers between devices, shifted(): lax.ppermute(part, 'seq', [(i, (i + step) % count) for i in range(count)])  21.7 us
  transfers between devices with their start and end apart: 70, of which 22 were waited for; matrix products, arithmetic and copies ran while one was open for 7% of the time, Pallas kernels for 30%

profile of v3, /device:TPU:0, one launch (start us, length us, event | category | flops | bytes accessed | tf_op | source)
XLA Modules:
  0.0 613.9 jit_solution(172961212274967747)
XLA Ops:
  7.2 2.1 convert.19
  10.4 3.0 collective-permute-start
  16.8 8.9 %collective-permute-done.refs_1_ = bf16[2,128,1024]{2,1,0:T(8,128)(2,1)} collective-permute-done((bf16[2,128,1024]{2,1,0:T(8,128)(2,1)S(1)}, bf16[2,128,1024]{2,1,0:T(8,128)(2,1)}, u32[]{:S(2)}, u32[]{:S(2)}) %collective-permute-start) | collective-permute-done | bytes 524320 | tf_op jit(solution)/shard_map/ppermute | solution.py:704
  30.1 5.1 collective-permute-done.2.refs_3_
  35.2 2.5 collective-permute-start.8
  39.0 2.6 fusion
  43.1 11.3 %shard_map.119 = (bf16[1024,1024]{1,0:T(8,128)(2,1)}, bf16[1024,1024]{1,0:T(8,128)(2,1)}, bf16[1024,1024]{1,0:T(8,128)(2,1)}) custom-call(s32[8]{0:T(128)} %get-tuple-element.196.order_ref, bf16[1024,1024]{1,0:T(8,128)(2,1)} %multiply_convert_fusion.h_ref, f32[512,1024]{1,0:T(8,128)} %get-tuple-element.194.table_ref, bf16[2,128,1024]{2,1,0:T(8,128)(2,1)} %copy-done.33, ...), custom_call_target="tpu_custom_call" | custom-call | flops 4294967296 | bytes 14680064 | tf_op jit(solution)/shard_map/pallas_call | solution.py:30
  54.4 4.2 shard_map.120
  62.0 4.3 collective-permute-start.7
  68.2 2.5 collective-permute-done.10.refs_3_.refs_11_
  70.8 5.2 collective-permute-done.7
  82.3 11.3 %shard_map.121 = (bf16[1024,1024]{1,0:T(8,128)(2,1)}, bf16[1024,1024]{1,0:T(8,128)(2,1)}, bf16[1024,1024]{1,0:T(8,128)(2,1)}) custom-call(s32[8]{0:T(128)} %get-tuple-element.196.order_ref, bf16[1024,1024]{1,0:T(8,128)(2,1)} %multiply_convert_fusion.h_ref, f32[512,1024]{1,0:T(8,128)} %get-tuple-element.193.table_ref, bf16[3,128,1024]{2,1,0:T(8,128)(2,1)} %copy-done.4, ...), custom_call_target="tpu_custom_call" | custom-call | flops 4294967296 | bytes 16777216 | tf_op jit(solution)/shard_map/pallas_call | solution.py:30
  94.5 2.1 collective-permute-start.18
  96.6 4.6 collective-permute-start.17
  101.3 5.8 collective-permute-done.18.refs_3_
  109.3 8.6 %shard_map.122.part_ref = bf16[1024,1024]{1,0:T(8,128)(2,1)} custom-call(s32[1]{0:T(128)} %bitcast.1.start_ref, f32[8]{0:T(128)} %get-tuple-element.200.into_ref, f32[8]{0:T(128)} %get-tuple-element.199.out_ref, s32[2,4]{1,0:T(2,128)} %lengths_ref.11, bf16[1024,1024]{1,0:T(8,128)(2,1)} %get-tuple-element.95.q_ref, ...), custom_call_target="tpu_custom_call" | custom-call | flops 2147483648 | bytes 8388608 | tf_op jit(solution)/shard_map/pallas_call | solution.py:30
  117.9 2.0 fusion.2.state_ref
  119.8 12.1 %shard_map.123 = (bf16[1024,1024]{1,0:T(8,128)(2,1)}, bf16[1024,1024]{1,0:T(8,128)(2,1)}, bf16[1024,1024]{1,0:T(8,128)(2,1)}, bf16[1024,1024]{1,0:T(8,128)(2,1)}, bf16[1024,1024]{1,0:T(8,128)(2,1)}) custom-call(s32[1]{0:T(128)} %bitcast.1.start_ref, f32[8]{0:T(128)} %get-tuple-element.200.into_ref, f32[8]{0:T(128)} %get-tuple-element.199.out_ref, ...), custom_call_target="tpu_custom_call" | custom-call | flops 2415919104 | bytes 25690112 | tf_op jit(solution)/shard_map/pallas_call | solution.py:30
  131.9 2.2 collective-permute-start.24
  134.8 8.6 %collective-permute-done.24.refs_10_ = bf16[1,128,2816]{2,1,0:T(8,128)(2,1)S(1)} collective-permute-done((bf16[1,128,2816]{2,1,0:T(8,128)(2,1)S(1)}, bf16[1,128,2816]{2,1,0:T(8,128)(2,1)S(1)}, u32[]{:S(2)}, u32[]{:S(2)}) %collective-permute-start.24) | collective-permute-done | bytes 720928 | tf_op jit(solution)/shard_map/ppermute | solution.py:704
  143.4 7.7 %collective-permute-done.25.refs_11_ = bf16[1,128,2816]{2,1,0:T(8,128)(2,1)S(1)} collective-permute-done((bf16[1,128,2816]{2,1,0:T(8,128)(2,1)S(1)}, bf16[1,128,2816]{2,1,0:T(8,128)(2,1)S(1)}, u32[]{:S(2)}, u32[]{:S(2)}) %collective-permute-start.25) | collective-permute-done | bytes 720928 | tf_op jit(solution)/shard_map/ppermute | solution.py:704
  154.2 21.0 %shard_map.124 = (bf16[1024,2816]{1,0:T(8,128)(2,1)}, bf16[1024,2816]{1,0:T(8,128)(2,1)}, bf16[2816,1024]{1,0:T(8,128)(2,1)}) custom-call(s32[8]{0:T(128)} %get-tuple-element.196.order_ref, bf16[1024,1024]{1,0:T(8,128)(2,1)} %get-tuple-element.97.h_ref, bf16[1,128,2816]{2,1,0:T(8,128)(2,1)} %get-tuple-element.94.refs_0_, ...), custom_call_target="tpu_custom_call" | custom-call | flops 11811160064 | bytes 30932992 | tf_op jit(solution)/shard_map/pallas_call | solution.py:30
  175.2 12.7 %shard_map.125 = (bf16[1,1408,1024]{2,1,0:T(8,128)(2,1)}, bf16[1,352,1024]{2,1,0:T(8,128)(2,1)}, bf16[1,352,1024]{2,1,0:T(8,128)(2,1)}, bf16[1,352,1024]{2,1,0:T(8,128)(2,1)}, bf16[1,352,1024]{2,1,0:T(8,128)(2,1)}) custom-call(s32[8]{0:T(128)} %pad_add_fusion.order_ref, bf16[2816,1024]{1,0:T(8,128)(2,1)} %get-tuple-element.102.turned_ref, ...), custom_call_target="tpu_custom_call" | custom-call | flops 5905580032 | bytes 13631488 | tf_op jit(solution)/shard_map/pallas_call | solution.py:30
  192.8 15.3 %collective-permute-done.31.refs_1_ = bf16[1,352,1024]{2,1,0:T(8,128)(2,1)S(1)} collective-permute-done((bf16[1,352,1024]{2,1,0:T(8,128)(2,1)S(1)}, bf16[1,352,1024]{2,1,0:T(8,128)(2,1)S(1)}, u32[]{:S(2)}, u32[]{:S(2)}) %collective-permute-start.31) | collective-permute-done | bytes 720928 | tf_op jit(solution)/shard_map/ppermute | solution.py:704
  208.1 2.1 collective-permute-start.33
  210.8 8.7 %collective-permute-done.33.refs_3_ = bf16[1,352,1024]{2,1,0:T(8,128)(2,1)S(1)} collective-permute-done((bf16[1,352,1024]{2,1,0:T(8,128)(2,1)S(1)}, bf16[1,352,1024]{2,1,0:T(8,128)(2,1)S(1)}, u32[]{:S(2)}, u32[]{:S(2)}) %collective-permute-start.33) | collective-permute-done | bytes 720928 | tf_op jit(solution)/shard_map/ppermute | solution.py:704
  222.5 16.9 %shard_map.126.refs_0_.refs_1_.dpair_ref = bf16[2,1024,2816]{2,1,0:T(8,128)(2,1)} custom-call(s32[8]{0:T(128)} %get-tuple-element.196.order_ref, bf16[1024,2816]{1,0:T(8,128)(2,1)} %get-tuple-element.113.first_ref, bf16[1024,2816]{1,0:T(8,128)(2,1)} %get-tuple-element.107.second_ref, bf16[1024,1024]{1,0:T(8,128)(2,1)} %bitcast.115, ...), custom_call_target="tpu_custom_call" | custom-call | flops 5905580032 | bytes 30932992 | tf_op jit(solution)/shard_map/pallas_call | solution.py:30
  239.5 3.0 add_convert_fusion.8
  242.5 12.9 %shard_map.127 = bf16[2,512,2816]{2,1,0:T(8,128)(2,1)} custom-call(s32[4]{0:T(128)} %copy-done.42, bf16[1024,1024]{1,0:T(8,128)(2,1)} %get-tuple-element.117.turned_ref, bf16[2,1024,2816]{2,1,0:T(8,128)(2,1)} %shard_map.126.refs_0_.refs_1_.dpair_ref, bf16[2,1024,2816]{2,1,0:T(8,128)(2,1)} %shard_map.126.refs_0_.refs_1_.dpair_ref), custom_call_target="tpu_custom_call" | custom-call | flops 5905580032 | bytes 30932992 | tf_op jit(solution)/shard_map/pallas_call | solution.py:30
  255.6 2.0 collective-permute-start.38
  257.7 14.7 %shard_map.128 = bf16[1024,1024]{1,0:T(8,128)(2,1)} custom-call(s32[8]{0:T(128)} %get-tuple-element.196.order_ref, bf16[1024,2816]{1,0:T(8,128)(2,1)} %get-tuple-element.113.first_ref, bf16[1024,2816]{1,0:T(8,128)(2,1)} %get-tuple-element.107.second_ref, bf16[1024,1024]{1,0:T(8,128)(2,1)} %get-tuple-element.114.x1_ref, bf16[1,352,1024]{2,1,0:T(8,128)(2,1)} %copy-done.15, ...), custom_call_target="tpu_custom_call" | custom-call | flops 5905580032 | bytes 21495808 | tf_op jit(solution)/shard_map/pallas_call | solution.py:30
  272.5 15.2 %shard_map.129 = (bf16[2,128,2816]{2,1,0:T(8,128)(2,1)}, bf16[2,128,2816]{2,1,0:T(8,128)(2,1)}, bf16[2,128,2816]{2,1,0:T(8,128)(2,1)}, bf16[2,128,2816]{2,1,0:T(8,128)(2,1)}) custom-call(s32[4]{0:T(128)} %copy-done.41, bf16[1024,1024]{1,0:T(8,128)(2,1)} %get-tuple-element.117.turned_ref, bf16[2,1024,2816]{2,1,0:T(8,128)(2,1)} %shard_map.126.refs_0_.refs_1_.dpair_ref, ...), custom_call_target="tpu_custom_call" | custom-call | flops 5905580032 | bytes 36700160 | tf_op jit(solution)/shard_map/pallas_call | solution.py:30
  287.7 2.4 add_convert_fusion.7
  293.2 24.5 %shard_map.130.e1_ref.refs_0_ = bf16[1024,1024]{1,0:T(8,128)(2,1)} custom-call(s32[8]{0:T(128)} %get-tuple-element.196.order_ref, bf16[2,1024,2816]{2,1,0:T(8,128)(2,1)} %shard_map.126.refs_0_.refs_1_.dpair_ref, bf16[1024,1024]{1,0:T(8,128)(2,1)} %get-tuple-element.114.x1_ref, bf16[1024,1024]{1,0:T(8,128)(2,1)} %bitcast.116, ...), custom_call_target="tpu_custom_call" | custom-call | flops 11811160064 | bytes 29360128 | tf_op jit(solution)/shard_map/pallas_call | solution.py:30
  317.8 2.8 add_convert_fusion.6
  320.5 11.0 %shard_map.131 = (bf16[1024,1024]{1,0:T(8,128)(2,1)}, bf16[1024,1024]{1,0:T(8,128)(2,1)}, bf16[2,8,128,128]{3,2,1,0:T(8,128)(2,1)}) custom-call(s32[1]{0:T(128)} %bitcast.1.start_ref, f32[8]{0:T(128)} %get-tuple-element.200.into_ref, f32[8]{0:T(128)} %get-tuple-element.199.out_ref, s32[2,4]{1,0:T(2,128)} %lengths_ref.11, s32[8]{0:T(128)} %get-tuple-element.196.order_ref, ...), custom_call_target="tpu_custom_call" | custom-call | flops 2415919104 | bytes 19398656 | tf_op jit(solution)/shard_map/pallas_call | solution.py:30
  332.8 2.8 add_convert_fusion.1
  336.6 10.8 %collective-permute-done.42 = bf16[2,8,128,128]{3,2,1,0:T(8,128)(2,1)S(1)} collective-permute-done((bf16[2,8,128,128]{3,2,1,0:T(8,128)(2,1)}, bf16[2,8,128,128]{3,2,1,0:T(8,128)(2,1)S(1)}, u32[]{:S(2)}, u32[]{:S(2)}) %collective-permute-start.42) | collective-permute-done | bytes 524320 | tf_op jit(solution)/shard_map/ppermute | solution.py:687
  347.6 7.0 %shard_map.132 = (bf16[1,512,1024]{2,1,0:T(8,128)(2,1)}, bf16[1,128,1024]{2,1,0:T(8,128)(2,1)}, bf16[1,128,1024]{2,1,0:T(8,128)(2,1)}, bf16[1,128,1024]{2,1,0:T(8,128)(2,1)}, bf16[1,128,1024]{2,1,0:T(8,128)(2,1)}) custom-call(s32[8]{0:T(128)} %pad_add_fusion.order_ref, bf16[1024,1024]{1,0:T(8,128)(2,1)} %get-tuple-element.132.turned_ref, ...), custom_call_target="tpu_custom_call" | custom-call | flops 2147483648 | bytes 6291456 | tf_op jit(solution)/shard_map/pallas_call | solution.py:30
  354.7 18.7 %shard_map.133 = (bf16[1024,1024]{1,0:T(8,128)(2,1)}, bf16[1024,1024]{1,0:T(8,128)(2,1)}, bf16[1024,1024]{1,0:T(8,128)(2,1)}) custom-call(s32[1]{0:T(128)} %bitcast.1.start_ref, f32[8]{0:T(128)} %get-tuple-element.200.into_ref, f32[8]{0:T(128)} %get-tuple-element.199.out_ref, s32[2,4]{1,0:T(2,128)} %lengths_ref.11, ...), custom_call_target="tpu_custom_call" | custom-call | flops 6442450944 | bytes 17301504 | tf_op jit(solution)/shard_map/pallas_call | solution.py:30
  374.5 4.0 add_convert_fusion
  378.5 2.5 copy.13.turned_ref
  381.0 9.7 %shard_map.134 = (bf16[2,512,1024]{2,1,0:T(8,128)(2,1)}, bf16[2,128,1024]{2,1,0:T(8,128)(2,1)}, bf16[2,128,1024]{2,1,0:T(8,128)(2,1)}, bf16[2,128,1024]{2,1,0:T(8,128)(2,1)}, bf16[2,128,1024]{2,1,0:T(8,128)(2,1)}) custom-call(s32[8]{0:T(128)} %pad_add_fusion.order_ref, bf16[1024,1024]{1,0:T(8,128)(2,1)} %copy.13.turned_ref, ...), custom_call_target="tpu_custom_call" | custom-call | flops 4294967296 | bytes 10485760 | tf_op jit(solution)/shard_map/pallas_call | solution.py:30
  392.7 14.5 %collective-permute-done.48 = bf16[2,8,128,128]{3,2,1,0:T(8,128)(2,1)S(1)} collective-permute-done((bf16[2,8,128,128]{3,2,1,0:T(8,128)(2,1)S(1)}, bf16[2,8,128,128]{3,2,1,0:T(8,128)(2,1)S(1)}, u32[]{:S(2)}, u32[]{:S(2)}) %collective-permute-start.48) | collective-permute-done | bytes 524320 | tf_op jit(solution)/shard_map/ppermute | solution.py:687
  408.2 7.7 %shard_map.135 = (bf16[1024,1024]{1,0:T(8,128)(2,1)}, bf16[1024,1024]{1,0:T(8,128)(2,1)}) custom-call(s32[1]{0:T(128)} %bitcast.1.start_ref, f32[8]{0:T(128)} %get-tuple-element.200.into_ref, f32[8]{0:T(128)} %get-tuple-element.199.out_ref, s32[2,4]{1,0:T(2,128)} %lengths_ref.11, bf16[1024,1024]{1,0:T(8,128)(2,1)} %get-tuple-element.87.k_ref, ...), custom_call_target="tpu_custom_call" | custom-call | flops 536870912 | bytes 15204352 | tf_op jit(solution)/shard_map/pallas_call | solution.py:30
  419.3 2.0 add_convert_fusion.4
  421.3 2.5 copy.14.turned_ref
  423.8 9.8 %shard_map.136 = (bf16[2,512,1024]{2,1,0:T(8,128)(2,1)}, bf16[2,128,1024]{2,1,0:T(8,128)(2,1)}, bf16[2,128,1024]{2,1,0:T(8,128)(2,1)}, bf16[2,128,1024]{2,1,0:T(8,128)(2,1)}, bf16[2,128,1024]{2,1,0:T(8,128)(2,1)}) custom-call(s32[8]{0:T(128)} %pad_add_fusion.order_ref, bf16[1024,1024]{1,0:T(8,128)(2,1)} %copy.14.turned_ref, ...), custom_call_target="tpu_custom_call" | custom-call | flops 4294967296 | bytes 10485760 | tf_op jit(solution)/shard_map/pallas_call | solution.py:30
  434.7 3.3 collective-permute-done.49
  438.1 3.3 add_convert_fusion.12
  441.4 19.5 %shard_map.137 = f32[1024,1024]{1,0:T(8,128)} custom-call(s32[8]{0:T(128)} %get-tuple-element.196.order_ref, bf16[1024,1024]{1,0:T(8,128)(2,1)} %get-tuple-element.157.refs_1_.dq_ref, bf16[1024,1024]{1,0:T(8,128)(2,1)} %get-tuple-element.147.refs_0_.dk_ref, bf16[1024,1024]{1,0:T(8,128)(2,1)} %get-tuple-element.152.refs_1_.dv_ref, ...), custom_call_target="tpu_custom_call" | custom-call | flops 8589934592 | bytes 27262976 | tf_op jit(solution)/shard_map/pallas_call | solution.py:30
  461.0 2.4 add_convert_fusion.3
  464.6 10.3 %all-reduce.3.cloned.1.call-done = bf16[1,352,1024]{2,1,0:T(8,128)(2,1)} async-done(((bf16[1,352,1024]{2,1,0:T(8,128)(2,1)}), bf16[1,352,1024]{2,1,0:T(8,128)(2,1)}) %all-reduce.3.cloned.1.call-update) | async-done | bytes 720912 | tf_op jit(solution)/shard_map/psum | solution.py:927
  476.5 12.4 %collective-permute-done.60 = bf16[2,128,1024]{2,1,0:T(8,128)(2,1)} collective-permute-done((bf16[2,128,1024]{2,1,0:T(8,128)(2,1)}, bf16[2,128,1024]{2,1,0:T(8,128)(2,1)}, u32[]{:S(2)}, u32[]{:S(2)}) %collective-permute-start.60) | collective-permute-done | bytes 524320 | tf_op jit(solution)/shard_map/ppermute | solution.py:704
  489.0 2.3 add_convert_fusion.2
  502.0 53.0 %all-reduce.5.cloned.1.call-done = bf16[1,2,128,2816]{3,2,1,0:T(8,128)(2,1)} async-done(((bf16[1,2,128,2816]{3,2,1,0:T(8,128)(2,1)}), bf16[1,2,128,2816]{3,2,1,0:T(8,128)(2,1)}) %all-reduce.5.cloned.1.call-update) | async-done | bytes 1441808 | tf_op jit(solution)/shard_map/psum | solution.py:969
  554.9 3.1 broadcast_in_dim.82
  562.1 2.4 collective-permute-start.58
  567.2 2.0 collective-permute-done.56
  569.1 11.6 %collective-permute-start.62 = (bf16[2,32,1024]{2,1,0:T(8,128)(2,1)S(1)}, bf16[2,32,1024]{2,1,0:T(8,128)(2,1)S(1)}, u32[]{:S(2)}, u32[]{:S(2)}) collective-permute-start(bf16[2,32,1024]{2,1,0:T(8,128)(2,1)S(1)} %get-tuple-element.190), channel_id=1, source_target_pairs={{0,8},{8,16},{16,24},{24,0},{1,9},{9,17},{17,25},{25,1},{2,10},{10... | collective-permute-start | bytes 393224 | tf_op jit(solution)/shard_map/ppermute | solution.py:728
  580.9 10.6 %collective-permute-done.63 = bf16[2,32,1024]{2,1,0:T(8,128)(2,1)S(1)} collective-permute-done((bf16[2,32,1024]{2,1,0:T(8,128)(2,1)S(1)}, bf16[2,32,1024]{2,1,0:T(8,128)(2,1)S(1)}, u32[]{:S(2)}, u32[]{:S(2)}) %collective-permute-start.63) | collective-permute-done | bytes 131104 | tf_op jit(solution)/shard_map/ppermute | solution.py:728
  592.3 3.2 collective-permute-start.67
  595.5 4.4 collective-permute-done.65
  600.0 4.6 collective-permute-done.66
  (269 shorter events, 75.9 us)
Async XLA Ops:
  7.2 467.8 %all-reduce.3.cloned.1.call-start = ((), (), s32[]{:S(2)}) async-start(), calls=%async_computation | async-start | bytes 1441792 | tf_op jit(solution)/shard_map/psum | solution.py:927
  10.4 15.3 %collective-permute-start = (bf16[2,128,1024]{2,1,0:T(8,128)(2,1)S(1)}, bf16[2,128,1024]{2,1,0:T(8,128)(2,1)}, u32[]{:S(2)}, u32[]{:S(2)}) collective-permute-start(bf16[2,128,1024]{2,1,0:T(8,128)(2,1)S(1)} %slice_bitcast_fusion.2.refs_0_), channel_id=1, source_target_pairs={{0,2},{1,5},{2,0},{3,7},{4,6},{5,1},{6,4},{7,3},{8,10},{9,13},{10,... | collective-permute-start | bytes 1572872 | tf_op jit(solution)/shard_map/ppermute | solution.py:704
  13.4 16.2 %collective-permute-start.1 = (bf16[2,128,1024]{2,1,0:T(8,128)(2,1)S(1)}, bf16[2,128,1024]{2,1,0:T(8,128)(2,1)}, u32[]{:S(2)}, u32[]{:S(2)}) collective-permute-start(bf16[2,128,1024]{2,1,0:T(8,128)(2,1)S(1)} %slice_bitcast_fusion.2.refs_0_), channel_id=1, source_target_pairs={{0,4},{1,3},{2,6},{3,1},{4,0},{5,7},{6,2},{7,5},{8,12},{9,11},{10,... | collective-permute-start | bytes 1572872 | tf_op jit(solution)/shard_map/ppermute | solution.py:704
  14.9 26.7 %collective-permute-start.3 = (bf16[2,128,1024]{2,1,0:T(8,128)(2,1)S(1)}, bf16[2,128,1024]{2,1,0:T(8,128)(2,1)}, u32[]{:S(2)}, u32[]{:S(2)}) collective-permute-start(bf16[2,128,1024]{2,1,0:T(8,128)(2,1)S(1)} %slice_bitcast_fusion.2.refs_0_), channel_id=1, source_target_pairs={{0,1},{1,0},{2,3},{3,2},{4,5},{5,4},{6,7},{7,6},{8,9},{9,8},{10,11... | collective-permute-start | bytes 1572872 | tf_op jit(solution)/shard_map/ppermute | solution.py:704
  25.7 9.5 %collective-permute-start.2 = (bf16[2,128,1024]{2,1,0:T(8,128)(2,1)}, bf16[2,128,1024]{2,1,0:T(8,128)(2,1)}, u32[]{:S(2)}, u32[]{:S(2)}) collective-permute-start(bf16[2,128,1024]{2,1,0:T(8,128)(2,1)} %collective-permute-done.refs_1_), channel_id=1, source_target_pairs={{0,4},{1,3},{2,6},{3,1},{4,0},{5,7},{6,2},{7,5},{8,12},{9,11},{10,... | collective-permute-start | bytes 1572872 | tf_op jit(solution)/shard_map/ppermute | solution.py:704
  29.6 12.7 %collective-permute-start.4 = (bf16[2,128,1024]{2,1,0:T(8,128)(2,1)}, bf16[2,128,1024]{2,1,0:T(8,128)(2,1)S(1)}, u32[]{:S(2)}, u32[]{:S(2)}) collective-permute-start(bf16[2,128,1024]{2,1,0:T(8,128)(2,1)} %collective-permute-done.refs_1_), channel_id=1, source_target_pairs={{0,1},{1,0},{2,3},{3,2},{4,5},{5,4},{6,7},{7,6},{8,9},{9,8},{10,11... | collective-permute-start | bytes 1572872 | tf_op jit(solution)/shard_map/ppermute | solution.py:704
  29.6 12.7 %collective-permute-start.5 = (bf16[2,128,1024]{2,1,0:T(8,128)(2,1)}, bf16[2,128,1024]{2,1,0:T(8,128)(2,1)}, u32[]{:S(2)}, u32[]{:S(2)}) collective-permute-start(bf16[2,128,1024]{2,1,0:T(8,128)(2,1)} %collective-permute-done.1.refs_2_), channel_id=1, source_target_pairs={{0,1},{1,0},{2,3},{3,2},{4,5},{5,4},{6,7},{7,6},{8,9},{9,8},{10,11... | collective-permute-start | bytes 1572872 | tf_op jit(solution)/shard_map/ppermute | solution.py:704
  35.2 23.4 %collective-permute-start.8 = (bf16[3,128,1024]{2,1,0:T(8,128)(2,1)S(1)}, bf16[3,128,1024]{2,1,0:T(8,128)(2,1)S(1)}, u32[]{:S(2)}, u32[]{:S(2)}) collective-permute-start(bf16[3,128,1024]{2,1,0:T(8,128)(2,1)S(1)} %pad_maximum_fusion.refs_0_.refs_8_), channel_id=1, source_target_pairs={{0,2},{1,5},{2,0},{3,7},{4,6},{5,1},{6,4},{7,3},{8,10},{9,13},{10,... | collective-permute-start | bytes 2359304 | tf_op jit(solution)/shard_map/ppermute | solution.py:704
  41.6 26.5 %collective-permute-start.9 = (bf16[3,128,1024]{2,1,0:T(8,128)(2,1)S(1)}, bf16[3,128,1024]{2,1,0:T(8,128)(2,1)S(1)}, u32[]{:S(2)}, u32[]{:S(2)}) collective-permute-start(bf16[3,128,1024]{2,1,0:T(8,128)(2,1)S(1)} %pad_maximum_fusion.refs_0_.refs_8_), channel_id=1, source_target_pairs={{0,4},{1,3},{2,6},{3,1},{4,0},{5,7},{6,2},{7,5},{8,12},{9,11},{10,... | collective-permute-start | bytes 2359304 | tf_op jit(solution)/shard_map/ppermute | solution.py:704
  58.6 12.1 %collective-permute-start.10 = (bf16[3,128,1024]{2,1,0:T(8,128)(2,1)S(1)}, bf16[3,128,1024]{2,1,0:T(8,128)(2,1)S(1)}, u32[]{:S(2)}, u32[]{:S(2)}) collective-permute-start(bf16[3,128,1024]{2,1,0:T(8,128)(2,1)S(1)} %collective-permute-done.8.refs_1_.refs_9_), channel_id=1, source_target_pairs={{0,4},{1,3},{2,6},{3,1},{4,0},{5,7},{6,2},{7,5},{8,12},{9,11},{10,... | collective-permute-start | bytes 2359304 | tf_op jit(solution)/shard_map/ppermute | solution.py:704
  62.0 14.0 %collective-permute-start.7 = (bf16[2,8,128,128]{3,2,1,0:T(8,128)(2,1)}, bf16[2,8,128,128]{3,2,1,0:T(8,128)(2,1)}, u32[]{:S(2)}, u32[]{:S(2)}) collective-permute-start(bf16[2,8,128,128]{3,2,1,0:T(8,128)(2,1)} %shard_map.120), channel_id=1, source_target_pairs={{0,8},{8,16},{16,24},{1,9},{9,17},{17,25},{2,10},{10,18},{18,26},{... | collective-permute-start | bytes 1572872 | tf_op jit(solution)/shard_map/ppermute | solution.py:687
  67.6 11.2 %collective-permute-start.11 = (bf16[3,128,1024]{2,1,0:T(8,128)(2,1)S(1)}, bf16[3,128,1024]{2,1,0:T(8,128)(2,1)S(1)}, u32[]{:S(2)}, u32[]{:S(2)}) collective-permute-start(bf16[3,128,1024]{2,1,0:T(8,128)(2,1)S(1)} %pad_maximum_fusion.refs_0_.refs_8_), channel_id=1, source_target_pairs={{0,1},{1,0},{2,3},{3,2},{4,5},{5,4},{6,7},{7,6},{8,9},{9,8},{10,11... | collective-permute-start | bytes 2359304 | tf_op jit(solution)/shard_map/ppermute | solution.py:704
  67.6 12.5 %collective-permute-start.12 = (bf16[3,128,1024]{2,1,0:T(8,128)(2,1)S(1)}, bf16[3,128,1024]{2,1,0:T(8,128)(2,1)S(1)}, u32[]{:S(2)}, u32[]{:S(2)}) collective-permute-start(bf16[3,128,1024]{2,1,0:T(8,128)(2,1)S(1)} %collective-permute-done.8.refs_1_.refs_9_), channel_id=1, source_target_pairs={{0,1},{1,0},{2,3},{3,2},{4,5},{5,4},{6,7},{7,6},{8,9},{9,8},{10,11... | collective-permute-start | bytes 2359304 | tf_op jit(solution)/shard_map/ppermute | solution.py:704
  68.1 12.0 %collective-permute-start.13 = (bf16[3,128,1024]{2,1,0:T(8,128)(2,1)S(1)}, bf16[3,128,1024]{2,1,0:T(8,128)(2,1)S(1)}, u32[]{:S(2)}, u32[]{:S(2)}) collective-permute-start(bf16[3,128,1024]{2,1,0:T(8,128)(2,1)S(1)} %collective-permute-done.9.refs_2_.refs_10_), channel_id=1, source_target_pairs={{0,1},{1,0},{2,3},{3,2},{4,5},{5,4},{6,7},{7,6},{8,9},{9,8},{10,11... | collective-permute-start | bytes 2359304 | tf_op jit(solution)/shard_map/ppermute | solution.py:704
  70.7 9.5 %collective-permute-start.14 = (bf16[3,128,1024]{2,1,0:T(8,128)(2,1)S(1)}, bf16[3,128,1024]{2,1,0:T(8,128)(2,1)S(1)}, u32[]{:S(2)}, u32[]{:S(2)}) collective-permute-start(bf16[3,128,1024]{2,1,0:T(8,128)(2,1)S(1)} %collective-permute-done.10.refs_3_.refs_11_), channel_id=1, source_target_pairs={{0,1},{1,0},{2,3},{3,2},{4,5},{5,4},{6,7},{7,6},{8,9},{9,8},{10,11... | collective-permute-start | bytes 2359304 | tf_op jit(solution)/shard_map/ppermute | solution.py:704
  76.0 18.5 %collective-permute-start.15 = (bf16[1,128,2816]{2,1,0:T(8,128)(2,1)}, bf16[1,128,2816]{2,1,0:T(8,128)(2,1)}, u32[]{:S(2)}, u32[]{:S(2)}) collective-permute-start(bf16[1,128,2816]{2,1,0:T(8,128)(2,1)} %get-tuple-element.94.refs_0_), channel_id=1, source_target_pairs={{0,2},{1,5},{2,0},{3,7},{4,6},{5,1},{6,4},{7,3},{8,10},{9,13},{10,... | collective-permute-start | bytes 2162696 | tf_op jit(solution)/shard_map/ppermute | solution.py:704
  78.8 22.5 %collective-permute-start.16 = (bf16[1,128,2816]{2,1,0:T(8,128)(2,1)}, bf16[1,128,2816]{2,1,0:T(8,128)(2,1)}, u32[]{:S(2)}, u32[]{:S(2)}) collective-permute-start(bf16[1,128,2816]{2,1,0:T(8,128)(2,1)} %get-tuple-element.94.refs_0_), channel_id=1, source_target_pairs={{0,4},{1,3},{2,6},{3,1},{4,0},{5,7},{6,2},{7,5},{8,12},{9,11},{10,... | collective-permute-start | bytes 2162696 | tf_op jit(solution)/shard_map/ppermute | solution.py:704
  94.5 12.5 %collective-permute-start.18 = (bf16[1,128,2816]{2,1,0:T(8,128)(2,1)}, bf16[1,128,2816]{2,1,0:T(8,128)(2,1)S(1)}, u32[]{:S(2)}, u32[]{:S(2)}) collective-permute-start(bf16[1,128,2816]{2,1,0:T(8,128)(2,1)} %collective-permute-done.15.refs_1_), channel_id=1, source_target_pairs={{0,4},{1,3},{2,6},{3,1},{4,0},{5,7},{6,2},{7,5},{8,12},{9,11},{10,... | collective-permute-start | bytes 2162696 | tf_op jit(solution)/shard_map/ppermute | solution.py:704
  96.6 12.0 %collective-permute-start.17 = (bf16[2,8,128,128]{3,2,1,0:T(8,128)(2,1)S(1)}, bf16[2,8,128,128]{3,2,1,0:T(8,128)(2,1)S(1)}, u32[]{:S(2)}, u32[]{:S(2)}) collective-permute-start(bf16[2,8,128,128]{3,2,1,0:T(8,128)(2,1)S(1)} %fusion.1), channel_id=1, source_target_pairs={{0,8},{8,16},{16,24},{1,9},{9,17},{17,25},{2,10},{10,18},{18,26},{... | collective-permute-start | bytes 1572872 | tf_op jit(solution)/shard_map/ppermute | solution.py:687
  107.1 27.1 %collective-permute-start.23 = (bf16[1,128,2816]{2,1,0:T(8,128)(2,1)S(1)}, bf16[1,128,2816]{2,1,0:T(8,128)(2,1)S(1)}, u32[]{:S(2)}, u32[]{:S(2)}) collective-permute-start(bf16[1,128,2816]{2,1,0:T(8,128)(2,1)S(1)} %copy-done.21), channel_id=1, source_target_pairs={{0,2},{1,5},{2,0},{3,7},{4,6},{5,1},{6,4},{7,3},{8,10},{9,13},{10,... | collective-permute-start | bytes 2162696 | tf_op jit(solution)/shard_map/ppermute | solution.py:704
  108.3 26.0 %collective-permute-start.19 = (bf16[1,128,2816]{2,1,0:T(8,128)(2,1)}, bf16[1,128,2816]{2,1,0:T(8,128)(2,1)}, u32[]{:S(2)}, u32[]{:S(2)}) collective-permute-start(bf16[1,128,2816]{2,1,0:T(8,128)(2,1)} %get-tuple-element.94.refs_0_), channel_id=1, source_target_pairs={{0,1},{1,0},{2,3},{3,2},{4,5},{5,4},{6,7},{7,6},{8,9},{9,8},{10,11... | collective-permute-start | bytes 2162696 | tf_op jit(solution)/shard_map/ppermute | solution.py:704
  108.7 25.5 %collective-permute-start.20 = (bf16[1,128,2816]{2,1,0:T(8,128)(2,1)}, bf16[1,128,2816]{2,1,0:T(8,128)(2,1)}, u32[]{:S(2)}, u32[]{:S(2)}) collective-permute-start(bf16[1,128,2816]{2,1,0:T(8,128)(2,1)} %collective-permute-done.15.refs_1_), channel_id=1, source_target_pairs={{0,1},{1,0},{2,3},{3,2},{4,5},{5,4},{6,7},{7,6},{8,9},{9,8},{10,11... | collective-permute-start | bytes 2162696 | tf_op jit(solution)/shard_map/ppermute | solution.py:704
  108.9 25.8 %collective-permute-start.21 = (bf16[1,128,2816]{2,1,0:T(8,128)(2,1)}, bf16[1,128,2816]{2,1,0:T(8,128)(2,1)}, u32[]{:S(2)}, u32[]{:S(2)}) collective-permute-start(bf16[1,128,2816]{2,1,0:T(8,128)(2,1)} %collective-permute-done.16.refs_2_), channel_id=1, source_target_pairs={{0,1},{1,0},{2,3},{3,2},{4,5},{5,4},{6,7},{7,6},{8,9},{9,8},{10,11... | collective-permute-start | bytes 2162696 | tf_op jit(solution)/shard_map/ppermute | solution.py:704
  131.9 11.4 %collective-permute-start.24 = (bf16[1,128,2816]{2,1,0:T(8,128)(2,1)S(1)}, bf16[1,128,2816]{2,1,0:T(8,128)(2,1)S(1)}, u32[]{:S(2)}, u32[]{:S(2)}) collective-permute-start(bf16[1,128,2816]{2,1,0:T(8,128)(2,1)S(1)} %copy-done.21), channel_id=1, source_target_pairs={{0,4},{1,3},{2,6},{3,1},{4,0},{5,7},{6,2},{7,5},{8,12},{9,11},{10,... | collective-permute-start | bytes 2162696 | tf_op jit(solution)/shard_map/ppermute | solution.py:704
  134.1 17.0 %collective-permute-start.25 = (bf16[1,128,2816]{2,1,0:T(8,128)(2,1)S(1)}, bf16[1,128,2816]{2,1,0:T(8,128)(2,1)S(1)}, u32[]{:S(2)}, u32[]{:S(2)}) collective-permute-start(bf16[1,128,2816]{2,1,0:T(8,128)(2,1)S(1)} %collective-permute-done.23.refs_9_), channel_id=1, source_target_pairs={{0,4},{1,3},{2,6},{3,1},{4,0},{5,7},{6,2},{7,5},{8,12},{9,11},{10,... | collective-permute-start | bytes 2162696 | tf_op jit(solution)/shard_map/ppermute | solution.py:704
  134.2 17.7 %collective-permute-start.26 = (bf16[1,128,2816]{2,1,0:T(8,128)(2,1)S(1)}, bf16[1,128,2816]{2,1,0:T(8,128)(2,1)S(1)}, u32[]{:S(2)}, u32[]{:S(2)}) collective-permute-start(bf16[1,128,2816]{2,1,0:T(8,128)(2,1)S(1)} %copy-done.21), channel_id=1, source_target_pairs={{0,1},{1,0},{2,3},{3,2},{4,5},{5,4},{6,7},{7,6},{8,9},{9,8},{10,11... | collective-permute-start | bytes 2162696 | tf_op jit(solution)/shard_map/ppermute | solution.py:704
  134.2 17.7 %collective-permute-start.22 = (bf16[1,128,2816]{2,1,0:T(8,128)(2,1)S(1)}, bf16[1,128,2816]{2,1,0:T(8,128)(2,1)S(1)}, u32[]{:S(2)}, u32[]{:S(2)}) collective-permute-start(bf16[1,128,2816]{2,1,0:T(8,128)(2,1)S(1)} %collective-permute-done.18.refs_3_), channel_id=1, source_target_pairs={{0,1},{1,0},{2,3},{3,2},{4,5},{5,4},{6,7},{7,6},{8,9},{9,8},{10,11... | collective-permute-start | bytes 2162696 | tf_op jit(solution)/shard_map/ppermute | solution.py:704
  134.8 17.2 %collective-permute-start.27 = (bf16[1,128,2816]{2,1,0:T(8,128)(2,1)S(1)}, bf16[1,128,2816]{2,1,0:T(8,128)(2,1)S(1)}, u32[]{:S(2)}, u32[]{:S(2)}) collective-permute-start(bf16[1,128,2816]{2,1,0:T(8,128)(2,1)S(1)} %collective-permute-done.23.refs_9_), channel_id=1, source_target_pairs={{0,1},{1,0},{2,3},{3,2},{4,5},{5,4},{6,7},{7,6},{8,9},{9,8},{10,11... | collective-permute-start | bytes 2162696 | tf_op jit(solution)/shard_map/ppermute | solution.py:704
  187.9 51.6 %collective-permute-start.30 = (bf16[1,1408,1024]{2,1,0:T(8,128)(2,1)}, bf16[1,1408,1024]{2,1,0:T(8,128)(2,1)S(1)}, u32[]{:S(2)}, u32[]{:S(2)}) collective-permute-start(bf16[1,1408,1024]{2,1,0:T(8,128)(2,1)} %get-tuple-element.103), channel_id=1, source_target_pairs={{0,1},{1,0},{2,3},{3,2},{4,5},{5,4},{6,7},{7,6},{8,9},{9,8},{10,11... | collective-permute-start | bytes 8650760 | tf_op jit(solution)/shard_map/ppermute | solution.py:704
  189.9 18.2 %collective-permute-start.31 = (bf16[1,352,1024]{2,1,0:T(8,128)(2,1)S(1)}, bf16[1,352,1024]{2,1,0:T(8,128)(2,1)S(1)}, u32[]{:S(2)}, u32[]{:S(2)}) collective-permute-start(bf16[1,352,1024]{2,1,0:T(8,128)(2,1)S(1)} %convert_element_type.304.refs_0_), channel_id=1, source_target_pairs={{0,2},{1,5},{2,0},{3,7},{4,6},{5,1},{6,4},{7,3},{8,10},{9,13},{10,... | collective-permute-start | bytes 2162696 | tf_op jit(solution)/shard_map/ppermute | solution.py:704
  191.4 19.3 %collective-permute-start.32 = (bf16[1,352,1024]{2,1,0:T(8,128)(2,1)S(1)}, bf16[1,352,1024]{2,1,0:T(8,128)(2,1)S(1)}, u32[]{:S(2)}, u32[]{:S(2)}) collective-permute-start(bf16[1,352,1024]{2,1,0:T(8,128)(2,1)S(1)} %convert_element_type.304.refs_0_), channel_id=1, source_target_pairs={{0,4},{1,3},{2,6},{3,1},{4,0},{5,7},{6,2},{7,5},{8,12},{9,11},{10,... | collective-permute-start | bytes 2162696 | tf_op jit(solution)/shard_map/ppermute | solution.py:704
  208.1 11.4 %collective-permute-start.33 = (bf16[1,352,1024]{2,1,0:T(8,128)(2,1)S(1)}, bf16[1,352,1024]{2,1,0:T(8,128)(2,1)S(1)}, u32[]{:S(2)}, u32[]{:S(2)}) collective-permute-start(bf16[1,352,1024]{2,1,0:T(8,128)(2,1)S(1)} %collective-permute-done.31.refs_1_), channel_id=1, source_target_pairs={{0,4},{1,3},{2,6},{3,1},{4,0},{5,7},{6,2},{7,5},{8,12},{9,11},{10,... | collective-permute-start | bytes 2162696 | tf_op jit(solution)/shard_map/ppermute | solution.py:704
  210.2 9.3 %collective-permute-start.34 = (bf16[1,352,1024]{2,1,0:T(8,128)(2,1)S(1)}, bf16[1,352,1024]{2,1,0:T(8,128)(2,1)S(1)}, u32[]{:S(2)}, u32[]{:S(2)}) collective-permute-start(bf16[1,352,1024]{2,1,0:T(8,128)(2,1)S(1)} %convert_element_type.304.refs_0_), channel_id=1, source_target_pairs={{0,1},{1,0},{2,3},{3,2},{4,5},{5,4},{6,7},{7,6},{8,9},{9,8},{10,11... | collective-permute-start | bytes 2162696 | tf_op jit(solution)/shard_map/ppermute | solution.py:704
  210.2 9.3 %collective-permute-start.35 = (bf16[1,352,1024]{2,1,0:T(8,128)(2,1)S(1)}, bf16[1,352,1024]{2,1,0:T(8,128)(2,1)S(1)}, u32[]{:S(2)}, u32[]{:S(2)}) collective-permute-start(bf16[1,352,1024]{2,1,0:T(8,128)(2,1)S(1)} %collective-permute-done.31.refs_1_), channel_id=1, source_target_pairs={{0,1},{1,0},{2,3},{3,2},{4,5},{5,4},{6,7},{7,6},{8,9},{9,8},{10,11... | collective-permute-start | bytes 2162696 | tf_op jit(solution)/shard_map/ppermute | solution.py:704
  210.7 8.8 %collective-permute-start.36 = (bf16[1,352,1024]{2,1,0:T(8,128)(2,1)S(1)}, bf16[1,352,1024]{2,1,0:T(8,128)(2,1)S(1)}, u32[]{:S(2)}, u32[]{:S(2)}) collective-permute-start(bf16[1,352,1024]{2,1,0:T(8,128)(2,1)S(1)} %collective-permute-done.32.refs_2_), channel_id=1, source_target_pairs={{0,1},{1,0},{2,3},{3,2},{4,5},{5,4},{6,7},{7,6},{8,9},{9,8},{10,11... | collective-permute-start | bytes 2162696 | tf_op jit(solution)/shard_map/ppermute | solution.py:704
  255.4 17.1 %collective-permute-start.39 = (bf16[2,512,2816]{2,1,0:T(8,128)(2,1)}, bf16[2,512,2816]{2,1,0:T(8,128)(2,1)}, u32[]{:S(2)}, u32[]{:S(2)}) collective-permute-start(bf16[2,512,2816]{2,1,0:T(8,128)(2,1)} %shard_map.127), channel_id=1, source_target_pairs={{0,1},{1,0},{2,3},{3,2},{4,5},{5,4},{6,7},{7,6},{8,9},{9,8},{10,11... | collective-permute-start | bytes 17301512 | tf_op jit(solution)/shard_map/ppermute | solution.py:704
  255.6 32.1 %collective-permute-start.38 = (bf16[1,352,1024]{2,1,0:T(8,128)(2,1)}, bf16[1,352,1024]{2,1,0:T(8,128)(2,1)}, u32[]{:S(2)}, u32[]{:S(2)}) collective-permute-start(bf16[1,352,1024]{2,1,0:T(8,128)(2,1)} %get-tuple-element.110), channel_id=1, source_target_pairs={{0,2},{1,5},{2,0},{3,7},{4,6},{5,1},{6,4},{7,3},{8,10},{9,13},{10,... | collective-permute-start | bytes 2162696 | tf_op jit(solution)/shard_map/ppermute | solution.py:704
  257.6 60.1 %collective-permute-start.40 = (bf16[1,352,1024]{2,1,0:T(8,128)(2,1)}, bf16[1,352,1024]{2,1,0:T(8,128)(2,1)}, u32[]{:S(2)}, u32[]{:S(2)}) collective-permute-start(bf16[1,352,1024]{2,1,0:T(8,128)(2,1)} %get-tuple-element.173), channel_id=1, source_target_pairs={{0,2},{1,5},{2,0},{3,7},{4,6},{5,1},{6,4},{7,3},{8,10},{9,13},{10,... | collective-permute-start | bytes 2162696 | tf_op jit(solution)/shard_map/ppermute | solution.py:704
  290.1 27.6 %collective-permute-start.41 = (bf16[1,352,1024]{2,1,0:T(8,128)(2,1)}, bf16[1,352,1024]{2,1,0:T(8,128)(2,1)}, u32[]{:S(2)}, u32[]{:S(2)}) collective-permute-start(bf16[1,352,1024]{2,1,0:T(8,128)(2,1)} %add_convert_fusion.7), channel_id=1, source_target_pairs={{0,4},{1,3},{2,6},{3,1},{4,0},{5,7},{6,2},{7,5},{8,12},{9,11},{10,... | collective-permute-start | bytes 2162696 | tf_op jit(solution)/shard_map/ppermute | solution.py:704
  292.1 40.7 %collective-permute-start.43 = (bf16[2,128,2816]{2,1,0:T(8,128)(2,1)}, bf16[2,128,2816]{2,1,0:T(8,128)(2,1)}, u32[]{:S(2)}, u32[]{:S(2)}) collective-permute-start(bf16[2,128,2816]{2,1,0:T(8,128)(2,1)} %get-tuple-element.121), channel_id=1, source_target_pairs={{0,2},{1,5},{2,0},{3,7},{4,6},{5,1},{6,4},{7,3},{8,10},{9,13},{10,... | collective-permute-start | bytes 4325384 | tf_op jit(solution)/shard_map/ppermute | solution.py:704
  331.5 15.9 %collective-permute-start.42 = (bf16[2,8,128,128]{3,2,1,0:T(8,128)(2,1)}, bf16[2,8,128,128]{3,2,1,0:T(8,128)(2,1)S(1)}, u32[]{:S(2)}, u32[]{:S(2)}) collective-permute-start(bf16[2,8,128,128]{3,2,1,0:T(8,128)(2,1)} %get-tuple-element.129), channel_id=1, source_target_pairs={{8,0},{16,8},{24,16},{9,1},{17,9},{25,17},{10,2},{18,10},{26,18},{... | collective-permute-start | bytes 1572872 | tf_op jit(solution)/shard_map/ppermute | solution.py:687
  335.6 37.8 %collective-permute-start.45 = (bf16[2,128,2816]{2,1,0:T(8,128)(2,1)}, bf16[2,128,2816]{2,1,0:T(8,128)(2,1)S(1)}, u32[]{:S(2)}, u32[]{:S(2)}) collective-permute-start(bf16[2,128,2816]{2,1,0:T(8,128)(2,1)} %add_convert_fusion.1), channel_id=1, source_target_pairs={{0,4},{1,3},{2,6},{3,1},{4,0},{5,7},{6,2},{7,5},{8,12},{9,11},{10,... | collective-permute-start | bytes 4325384 | tf_op jit(solution)/shard_map/ppermute | solution.py:704
  336.5 37.9 %collective-permute-start.44 = (bf16[2,128,2816]{2,1,0:T(8,128)(2,1)}, bf16[2,128,2816]{2,1,0:T(8,128)(2,1)}, u32[]{:S(2)}, u32[]{:S(2)}) collective-permute-start(bf16[2,128,2816]{2,1,0:T(8,128)(2,1)} %get-tuple-element.119), channel_id=1, source_target_pairs={{0,2},{1,5},{2,0},{3,7},{4,6},{5,1},{6,4},{7,3},{8,10},{9,13},{10,... | collective-permute-start | bytes 4325384 | tf_op jit(solution)/shard_map/ppermute | solution.py:704
  390.8 25.1 %collective-permute-start.46 = (bf16[2,512,1024]{2,1,0:T(8,128)(2,1)}, bf16[2,512,1024]{2,1,0:T(8,128)(2,1)}, u32[]{:S(2)}, u32[]{:S(2)}) collective-permute-start(bf16[2,512,1024]{2,1,0:T(8,128)(2,1)} %get-tuple-element.142), channel_id=1, source_target_pairs={{0,1},{1,0},{2,3},{3,2},{4,5},{5,4},{6,7},{7,6},{8,9},{9,8},{10,11... | collective-permute-start | bytes 6291464 | tf_op jit(solution)/shard_map/ppermute | solution.py:704
  390.9 26.8 %collective-permute-start.47 = (bf16[1,512,1024]{2,1,0:T(8,128)(2,1)}, bf16[1,512,1024]{2,1,0:T(8,128)(2,1)}, u32[]{:S(2)}, u32[]{:S(2)}) collective-permute-start(bf16[1,512,1024]{2,1,0:T(8,128)(2,1)} %get-tuple-element.133), channel_id=1, source_target_pairs={{0,1},{1,0},{2,3},{3,2},{4,5},{5,4},{6,7},{7,6},{8,9},{9,8},{10,11... | collective-permute-start | bytes 3145736 | tf_op jit(solution)/shard_map/ppermute | solution.py:704
  391.4 15.8 %collective-permute-start.48 = (bf16[2,8,128,128]{3,2,1,0:T(8,128)(2,1)S(1)}, bf16[2,8,128,128]{3,2,1,0:T(8,128)(2,1)S(1)}, u32[]{:S(2)}, u32[]{:S(2)}) collective-permute-start(bf16[2,8,128,128]{3,2,1,0:T(8,128)(2,1)S(1)} %fusion.3), channel_id=1, source_target_pairs={{8,0},{16,8},{24,16},{9,1},{17,9},{25,17},{10,2},{18,10},{26,18},{... | collective-permute-start | bytes 1572872 | tf_op jit(solution)/shard_map/ppermute | solution.py:687
  433.7 121.2 %all-reduce.5.cloned.1.call-start = ((), (), s32[]{:S(2)}) async-start(), calls=%async_computation.1 | async-start | bytes 2883584 | tf_op jit(solution)/shard_map/psum | solution.py:969
  433.8 27.2 %collective-permute-start.51 = (bf16[3,128,1024]{2,1,0:T(8,128)(2,1)}, bf16[3,128,1024]{2,1,0:T(8,128)(2,1)}, u32[]{:S(2)}, u32[]{:S(2)}) collective-permute-start(bf16[3,128,1024]{2,1,0:T(8,128)(2,1)} %get-tuple-element.148), channel_id=1, source_target_pairs={{0,2},{1,5},{2,0},{3,7},{4,6},{5,1},{6,4},{7,3},{8,10},{9,13},{10,... | collective-permute-start | bytes 2359304 | tf_op jit(solution)/shard_map/ppermute | solution.py:704
  463.4 25.6 %collective-permute-start.52 = (bf16[3,128,1024]{2,1,0:T(8,128)(2,1)}, bf16[3,128,1024]{2,1,0:T(8,128)(2,1)}, u32[]{:S(2)}, u32[]{:S(2)}) collective-permute-start(bf16[3,128,1024]{2,1,0:T(8,128)(2,1)} %add_convert_fusion.3), channel_id=1, source_target_pairs={{0,4},{1,3},{2,6},{3,1},{4,0},{5,7},{6,2},{7,5},{8,12},{9,11},{10,... | collective-permute-start | bytes 2359304 | tf_op jit(solution)/shard_map/ppermute | solution.py:704
  464.4 24.6 %collective-permute-start.50 = (bf16[3,128,1024]{2,1,0:T(8,128)(2,1)}, bf16[3,128,1024]{2,1,0:T(8,128)(2,1)}, u32[]{:S(2)}, u32[]{:S(2)}) collective-permute-start(bf16[3,128,1024]{2,1,0:T(8,128)(2,1)} %get-tuple-element.171), channel_id=1, source_target_pairs={{0,2},{1,5},{2,0},{3,7},{4,6},{5,1},{6,4},{7,3},{8,10},{9,13},{10,... | collective-permute-start | bytes 2359304 | tf_op jit(solution)/shard_map/ppermute | solution.py:704
  475.0 14.0 %collective-permute-start.60 = (bf16[2,128,1024]{2,1,0:T(8,128)(2,1)}, bf16[2,128,1024]{2,1,0:T(8,128)(2,1)}, u32[]{:S(2)}, u32[]{:S(2)}) collective-permute-start(bf16[2,128,1024]{2,1,0:T(8,128)(2,1)} %get-tuple-element.155), channel_id=1, source_target_pairs={{0,2},{1,5},{2,0},{3,7},{4,6},{5,1},{6,4},{7,3},{8,10},{9,13},{10,... | collective-permute-start | bytes 1572872 | tf_op jit(solution)/shard_map/ppermute | solution.py:704
  493.0 65.1 %collective-permute-start.55 = (bf16[3,32,1024]{2,1,0:T(8,128)(2,1)}, bf16[3,32,1024]{2,1,0:T(8,128)(2,1)}, u32[]{:S(2)}, u32[]{:S(2)}) collective-permute-start(bf16[3,32,1024]{2,1,0:T(8,128)(2,1)} %get-tuple-element.186), channel_id=1, source_target_pairs={{0,24},{8,0},{16,8},{24,16},{1,25},{9,1},{17,9},{25,17},{2,26},{10... | collective-permute-start | bytes 589832 | tf_op jit(solution)/shard_map/ppermute | solution.py:728
  494.8 63.3 %collective-permute-start.54 = (bf16[3,32,1024]{2,1,0:T(8,128)(2,1)}, bf16[3,32,1024]{2,1,0:T(8,128)(2,1)}, u32[]{:S(2)}, u32[]{:S(2)}) collective-permute-start(bf16[3,32,1024]{2,1,0:T(8,128)(2,1)} %get-tuple-element.187), channel_id=1, source_target_pairs={{0,16},{8,24},{16,0},{24,8},{1,17},{9,25},{17,1},{25,9},{2,18},{10... | collective-permute-start | bytes 589832 | tf_op jit(solution)/shard_map/ppermute | solution.py:728
  496.2 61.9 %collective-permute-start.53 = (bf16[3,32,1024]{2,1,0:T(8,128)(2,1)}, bf16[3,32,1024]{2,1,0:T(8,128)(2,1)}, u32[]{:S(2)}, u32[]{:S(2)}) collective-permute-start(bf16[3,32,1024]{2,1,0:T(8,128)(2,1)} %get-tuple-element.185), channel_id=1, source_target_pairs={{0,8},{8,16},{16,24},{24,0},{1,9},{9,17},{17,25},{25,1},{2,10},{10... | collective-permute-start | bytes 589832 | tf_op jit(solution)/shard_map/ppermute | solution.py:728
  499.3 65.2 %collective-permute-start.61 = (bf16[2,128,1024]{2,1,0:T(8,128)(2,1)S(1)}, bf16[2,128,1024]{2,1,0:T(8,128)(2,1)S(1)}, u32[]{:S(2)}, u32[]{:S(2)}) collective-permute-start(bf16[2,128,1024]{2,1,0:T(8,128)(2,1)S(1)} %add_convert_fusion.11), channel_id=1, source_target_pairs={{0,4},{1,3},{2,6},{3,1},{4,0},{5,7},{6,2},{7,5},{8,12},{9,11},{10,... | collective-permute-start | bytes 1572872 | tf_op jit(solution)/shard_map/ppermute | solution.py:704
  500.5 64.1 %collective-permute-start.59 = (bf16[2,128,1024]{2,1,0:T(8,128)(2,1)S(1)}, bf16[2,128,1024]{2,1,0:T(8,128)(2,1)S(1)}, u32[]{:S(2)}, u32[]{:S(2)}) collective-permute-start(bf16[2,128,1024]{2,1,0:T(8,128)(2,1)S(1)} %copy-done.34), channel_id=1, source_target_pairs={{0,2},{1,5},{2,0},{3,7},{4,6},{5,1},{6,4},{7,3},{8,10},{9,13},{10,... | collective-permute-start | bytes 1572872 | tf_op jit(solution)/shard_map/ppermute | solution.py:704
  559.3 9.8 %collective-permute-start.56 = (bf16[3,32,1024]{2,1,0:T(8,128)(2,1)S(1)}, bf16[3,32,1024]{2,1,0:T(8,128)(2,1)S(1)}, u32[]{:S(2)}, u32[]{:S(2)}) collective-permute-start(bf16[3,32,1024]{2,1,0:T(8,128)(2,1)S(1)} %fusion.7), channel_id=1, source_target_pairs={{0,8},{8,16},{16,24},{24,0},{1,9},{9,17},{17,25},{25,1},{2,10},{10... | collective-permute-start | bytes 589832 | tf_op jit(solution)/shard_map/ppermute | solution.py:728
  560.8 19.9 %collective-permute-start.57 = (bf16[3,32,1024]{2,1,0:T(8,128)(2,1)S(1)}, bf16[3,32,1024]{2,1,0:T(8,128)(2,1)S(1)}, u32[]{:S(2)}, u32[]{:S(2)}) collective-permute-start(bf16[3,32,1024]{2,1,0:T(8,128)(2,1)S(1)} %fusion.7), channel_id=1, source_target_pairs={{0,16},{8,24},{16,0},{24,8},{1,17},{9,25},{17,1},{25,9},{2,18},{10... | collective-permute-start | bytes 589832 | tf_op jit(solution)/shard_map/ppermute | solution.py:728
  562.1 18.7 %collective-permute-start.58 = (bf16[3,32,1024]{2,1,0:T(8,128)(2,1)S(1)}, bf16[3,32,1024]{2,1,0:T(8,128)(2,1)S(1)}, u32[]{:S(2)}, u32[]{:S(2)}) collective-permute-start(bf16[3,32,1024]{2,1,0:T(8,128)(2,1)S(1)} %fusion.7), channel_id=1, source_target_pairs={{0,24},{8,0},{16,8},{24,16},{1,25},{9,1},{17,9},{25,17},{2,26},{10... | collective-permute-start | bytes 589832 | tf_op jit(solution)/shard_map/ppermute | solution.py:728
  566.0 14.9 %collective-permute-start.64 = (bf16[2,32,1024]{2,1,0:T(8,128)(2,1)S(1)}, bf16[2,32,1024]{2,1,0:T(8,128)(2,1)S(1)}, u32[]{:S(2)}, u32[]{:S(2)}) collective-permute-start(bf16[2,32,1024]{2,1,0:T(8,128)(2,1)S(1)} %get-tuple-element.191), channel_id=1, source_target_pairs={{0,24},{8,0},{16,8},{24,16},{1,25},{9,1},{17,9},{25,17},{2,26},{10... | collective-permute-start | bytes 393224 | tf_op jit(solution)/shard_map/ppermute | solution.py:728
  566.8 24.8 %collective-permute-start.63 = (bf16[2,32,1024]{2,1,0:T(8,128)(2,1)S(1)}, bf16[2,32,1024]{2,1,0:T(8,128)(2,1)S(1)}, u32[]{:S(2)}, u32[]{:S(2)}) collective-permute-start(bf16[2,32,1024]{2,1,0:T(8,128)(2,1)S(1)} %get-tuple-element.192), channel_id=1, source_target_pairs={{0,16},{8,24},{16,0},{24,8},{1,17},{9,25},{17,1},{25,9},{2,18},{10... | collective-permute-start | bytes 393224 | tf_op jit(solution)/shard_map/ppermute | solution.py:728
  569.1 22.4 %collective-permute-start.62 = (bf16[2,32,1024]{2,1,0:T(8,128)(2,1)S(1)}, bf16[2,32,1024]{2,1,0:T(8,128)(2,1)S(1)}, u32[]{:S(2)}, u32[]{:S(2)}) collective-permute-start(bf16[2,32,1024]{2,1,0:T(8,128)(2,1)S(1)} %get-tuple-element.190), channel_id=1, source_target_pairs={{0,8},{8,16},{16,24},{24,0},{1,9},{9,17},{17,25},{25,1},{2,10},{10... | collective-permute-start | bytes 393224 | tf_op jit(solution)/shard_map/ppermute | solution.py:728
  591.7 12.9 %collective-permute-start.66 = (bf16[2,32,1024]{2,1,0:T(8,128)(2,1)S(1)}, bf16[2,32,1024]{2,1,0:T(8,128)(2,1)S(1)}, u32[]{:S(2)}, u32[]{:S(2)}) collective-permute-start(bf16[2,32,1024]{2,1,0:T(8,128)(2,1)S(1)} %fusion.10), channel_id=1, source_target_pairs={{0,16},{8,24},{16,0},{24,8},{1,17},{9,25},{17,1},{25,9},{2,18},{10... | collective-permute-start | bytes 393224 | tf_op jit(solution)/shard_map/ppermute | solution.py:728
  592.3 12.3 %collective-permute-start.67 = (bf16[2,32,1024]{2,1,0:T(8,128)(2,1)S(1)}, bf16[2,32,1024]{2,1,0:T(8,128)(2,1)S(1)}, u32[]{:S(2)}, u32[]{:S(2)}) collective-permute-start(bf16[2,32,1024]{2,1,0:T(8,128)(2,1)S(1)} %fusion.10), channel_id=1, source_target_pairs={{0,24},{8,0},{16,8},{24,16},{1,25},{9,1},{17,9},{25,17},{2,26},{10... | collective-permute-start | bytes 393224 | tf_op jit(solution)/shard_map/ppermute | solution.py:728
  (59 other events, 620.5 us)
Sparse Core Ops, SparseCore 0:
  433.8 41.1 all-reduce.2
  477.4 77.5 all-reduce.4

commit v4 on v3

--- a/solution.py
+++ b/solution.py
@@ -1,4 +1,5 @@
 import functools
+import math
 
 import jax
 import jax.numpy as jnp
@@ -12,6 +13,7 @@
 LOW = jnp.bfloat16
 WIDE = jnp.float32
 VMEM_BYTES = 60 * 1024 * 1024
+WEIGH = 50
 ANY = pl.BlockSpec(memory_space=pl.ANY)
 
 
@@ -25,8 +27,20 @@
     return jax.ShapeDtypeStruct(shape, kind)
 
 
-def call(kernel, scalars, grid, inputs, in_specs, outputs, out_specs, scratch, flops):
+def vmem_needed(arrays, specs, scratch, spare):
+    total = spare
+    for array, spec in zip(arrays, specs):
+        if spec.block_shape is not None:
+            total += 2 * math.prod(spec.block_shape) * array.dtype.itemsize
+    for ref in scratch:
+        if ref.memory_space == pltpu.VMEM:
+            total += math.prod(ref.shape) * jnp.dtype(ref.dtype).itemsize
+    return min(total, VMEM_BYTES)
+
+
+def call(kernel, scalars, grid, inputs, in_specs, outputs, out_specs, scratch, flops, spare=8):
     size = sum(a.size * a.dtype.itemsize for a in (*inputs, *outputs))
+    limit = vmem_needed((*inputs, *outputs), (*in_specs, *out_specs), scratch, spare << 20)
     return pl.pallas_call(
         kernel,
         out_shape=outputs,
@@ -37,9 +51,9 @@
             out_specs=out_specs,
             scratch_shapes=scratch,
         ),
-        compiler_params=pltpu.CompilerParams(vmem_limit_bytes=VMEM_BYTES),
+        compiler_params=pltpu.CompilerParams(vmem_limit_bytes=limit),
         cost_estimate=pl.CostEstimate(
-            flops=int(flops), bytes_accessed=int(size), transcendentals=0
+            flops=int(flops) * WEIGH, bytes_accessed=int(size) * WEIGH, transcendentals=0
         ),
     )(*scalars, *inputs)
 
@@ -716,27 +730,36 @@
     return jnp.asarray(table, jnp.int32)[device]
 
 
-def across_seq(value):
-    count, place = lax.axis_size("seq"), lax.axis_index("seq")
-    rows = value.shape[-2]
-    if rows % count:
-        return lax.psum(value, "seq")
-    parts = value.reshape(*value.shape[:-2], count, rows // count, value.shape[-1])
-    axis = parts.ndim - 3
-
-    def shifted(part, step):
-        return lax.ppermute(part, "seq", [(i, (i + step) % count) for i in range(count)])
-
-    def taken(step):
-        return lax.dynamic_index_in_dim(parts, (place + step) % count, axis, keepdims=False)
-
-    total = plus(taken(0), *(shifted(taken(step), step) for step in range(1, count)))
-    result = lax.dynamic_update_index_in_dim(parts, total, place, axis)
-    for step in range(1, count):
-        result = lax.dynamic_update_index_in_dim(
-            result, shifted(total, step), (place - step) % count, axis
-        )
-    return result.reshape(value.shape)
+class SeqSum:
+    def __init__(self, value):
+        members, rows, columns = value.shape
+        self.count, self.place = lax.axis_size("seq"), lax.axis_index("seq")
+        self.shape = value.shape
+        self.parts = value.reshape(members, self.count, rows // self.count, columns)
+        self.received = [
+            self.shifted(self.taken(step), step) for step in range(1, self.count)
+        ]
+
+    def shifted(self, part, step):
+        pairs = [(i, (i + step) % self.count) for i in range(self.count)]
+        return lax.ppermute(part, "seq", pairs)
+
+    def taken(self, step):
+        index = (self.place + step) % self.count
+        return lax.dynamic_index_in_dim(self.parts, index, 1, keepdims=False)
+
+    def share(self, *others):
+        total = plus(self.taken(0), *after(tuple(self.received), *others))
+        self.totals = [total] + [self.shifted(total, step) for step in range(1, self.count)]
+        return total
+
+    def finish(self, *others):
+        totals = [total.astype(WIDE) for total in after(tuple(self.totals), *others)]
+        parts = [
+            lax.select_n((self.place - index) % self.count, *totals)
+            for index in range(self.count)
+        ]
+        return jnp.stack(parts, axis=1).reshape(self.shape)
 
 
 def plus(*terms):
@@ -760,7 +783,7 @@
         return self.begun
 
     def forward(self, *others):
-        second = plus(*self.block(2), after(self.from_across, *others))
+        second = plus(*self.block(2), after(self.from_across, self.from_first, *others))
         self.from_second = moved(second, 1)
         return second
 
@@ -811,8 +834,8 @@
 
     big = min(512, count)
 
-    def hop(message, steps):
-        received = passed_along(message, steps).astype(WIDE)
+    def hop(message, steps, *others):
+        received = after(passed_along(message, steps), *others).astype(WIDE)
         return received, (passing[..., None, None] * received).astype(LOW)
 
     def gather(piece, *others):
@@ -903,14 +926,14 @@
         ],
         2 * count * features * (features + head_dim),
     )
-    second_w = forward(second_w, h2)
+    second_w = forward(second_w, part)
     down = gather(channel_out_weights.astype(LOW), *arrived(second_w))
     first, second, turned = pair(h2, first_w, second_w, order, tile)
     down = forward(down, first)
 
     down_grads = channel_grads = outer_grads = inner_grads = None
     if by_hand:
-        sent, *kept = block_grads(turned, [(dy, None)], order, "both")
+        sent, *kept = block_grads(turned, [(after(dy, *down[1:3]), None)], order, "both")
         down_grads = Scatter(kept, moved(sent, "core"))
         first = after(first, sent)
     dpair = down_back(first, second, dy, down, order, big)
@@ -919,13 +942,15 @@
         begun = down_grads.begin(dpair)
         [sent] = block_grads(after(h2_turned, *begun), rights, order, "send")
         received = moved(sent, "core")
-        y = down_forward(after(first, sent), second, x1, down, order, big)
-        channel_grads = Scatter(block_grads(after(h2_turned, y), rights, order, "keep", received))
-        begun = down_grads.forward(*channel_grads.kept), *channel_grads.begin()
-        e1 = pair_back(after(dpair, *begun), x1, dy, first_w, second_w, order, big)
-        down_part = down_grads.finish(e1)
-        down_total = lax.psum(down_part, "seq")
-        e1 = after(e1, down_part)
+        e1 = pair_back(after(dpair, sent), x1, dy, first_w, second_w, order, big)
+        begun = down_grads.forward(e1)
+        channel_grads = Scatter(
+            block_grads(after(h2_turned, begun), rights, order, "keep", received)
+        )
+        begun = channel_grads.begin()
+        down_part = down_grads.finish(*channel_grads.kept)
+        down_sum = SeqSum(down_part)
+        e1 = after(e1, down_part, *begun)
     else:
         y = down_forward(first, second, x1, down, order, big)
         down_total = lax.psum(scattered_plainly(turned, [dy]), "seq")
@@ -944,14 +969,13 @@
     )
     pins = []
     if by_hand:
-        second_sent = channel_grads.forward(local_grad)
+        second_sent = channel_grads.forward(local_grad), down_sum.share(local_grad)
         sent_o, *kept_o = block_grads(
-            after(gated_turned, second_sent, local_grad), [(e1, None)], order, "both"
+            after(gated_turned, *second_sent), [(e1, None)], order, "both"
         )
         received_o = moved(sent_o, "core")
         pins = [sent_o]
-    state_grad, message = hop(local_grad, -1)
-    message = after(message, *pins)
+    state_grad, message = hop(local_grad, -1, *pins)
     dq, dk_part, dv_part = call(
         functools.partial(back_mixing_kernel, docs, tile, heads),
         scalars,
@@ -966,7 +990,8 @@
     pins = [dq]
     if by_hand:
         channel_part = channel_grads.finish(dq)
-        channel_total = lax.psum(after(channel_part, down_total), "seq")
+        channel_sum = SeqSum(channel_part)
+        down_total = down_sum.finish(dq)
         sent_uq, *kept_uq = block_grads(
             after(h_turned, channel_part), [(du, None), (dq, None)], order, "both"
         )
@@ -996,12 +1021,22 @@
             after(h_turned, *begun), [(dk, None), (dv, None)], order, "both"
         )
         inner_grads = Scatter(kept_kv, moved(sent_kv, "core"))
-        begun = inner_grads.begin(sent_kv)
+        begun = outer_grads.forward(sent_kv), *inner_grads.begin(sent_kv)
+        begun = *begun, channel_sum.share(sent_kv)
         dq = after(dq, *begun)
     upstream = mixer_back([dq, dk, dv, du], x, e1, key_value, rest, order, big)
     if by_hand:
-        outer_total = across_seq(outer_grads.finish(outer_grads.forward(upstream)))
-        inner_total = across_seq(inner_grads.finish(inner_grads.forward(upstream)))
+        outer_part = outer_grads.finish(upstream)
+        outer_sum = SeqSum(outer_part)
+        begun = inner_grads.forward(upstream), outer_part
+        y = down_forward(after(first, *begun), second, x1, down, order, big)
+        inner_part = inner_grads.finish(y)
+        inner_sum = SeqSum(inner_part)
+        outer_total = outer_sum.share(inner_part)
+        channel_total = channel_sum.finish(outer_total)
+        inner_total = inner_sum.share(outer_total)
+        outer_total = outer_sum.finish(inner_total)
+        inner_total = inner_sum.finish(inner_total)
         mixer_gradient = jnp.stack(
             [outer_total[1], inner_total[0], inner_total[1], outer_total[0], outer_total[2]]
         )
@@ -1015,8 +1050,8 @@
         y.reshape(by_row),
         upstream.reshape(by_row),
         mixer_gradient.astype(WIDE)[None],
-        channel_total.astype(WIDE)[None],
-        down_total.astype(WIDE),
+        channel_total.astype(WIDE).reshape(channel_in_weights.shape),
+        down_total.astype(WIDE).reshape(channel_out_weights.shape),
     )
 
 

time: 622 us -> 569 us (0.915)
  waiting for transfers between devices: 197 us -> 123 us
  Pallas kernels: 249 us -> 190 us
  local copies, waits for them, and re-layouts: 23.3 us -> 76.5 us
  starting transfers between devices: 77.7 us -> 114 us
  between operations: 15.5 us -> 3 us
    psum x2 -> x0, waiting for transfers between devices: 63.3 us -> none  [the longest x1 53 us: local(): channel_total = lax.psum(after(channel_part, down_total), 'seq')]
    pallas_call x19, Pallas kernels: 249 us -> 190 us  [call(): pl.pallas_call(kernel, out_shape=outputs, grid_spec=pltpu.PrefetchScalarG...]
    unnamed x112 -> x328, local copies, waits for them, and re-layouts: 11.9 us -> 60.1 us
    ppermute x12 -> x24, starting transfers between devices: 26.6 us -> 64.6 us  [shifted(): return lax.ppermute(part, 'seq', pairs)]
    ppermute x4, waiting for transfers between devices: 30.8 us -> 6.86 us  [passed_along(): lax.ppermute(value, 'seq', [(source, source + steps) for source in range(...]
    ppermute x12 -> x24, waiting for transfers between devices: 21.7 us -> 40.7 us  [shifted(): return lax.ppermute(part, 'seq', pairs)]
    another operation x2 -> x10, other arithmetic: 4.03 us -> 10.4 us  [the longest x8 5.27 us: finish(): return jnp.stack(parts, axis=1).reshape(self.shape)]
    convert_element_type x13 -> x15, other arithmetic: 29.2 us -> 30.9 us  [plus(): return sum((term.astype(WIDE) for term in terms)).astype(LOW)]
  transfers between devices with their start and end apart: 70 -> 80, of which waited for: 22 -> 23; matrix products, arithmetic and copies ran while one was open for 7% -> 10% of each run, Pallas kernels for 30% -> 33%
where the time goes in v4:
time: 569 us; the launch traced here: 560 us
  Pallas kernels  190 us (33%)
  waiting for transfers between devices  123 us (22%)
  starting transfers between devices  114 us (20%)
  local copies, waits for them, and re-layouts  76.5 us (13%)
  other arithmetic  53.1 us (9%)
    pallas_call x19, Pallas kernels, call(): pl.pallas_call(kernel, out_shape=outputs, grid_spec=pltpu.PrefetchScalarG...  190 us
    ppermute x52, waiting for transfers between devices, moved(): return lax.ppermute(value, 'dp', pairs)  75.6 us
    ppermute x24, starting transfers between devices, shifted(): return lax.ppermute(part, 'seq', pairs)  64.6 us
    unnamed x328, local copies, waits for them, and re-layouts  60.1 us
    ppermute x24, waiting for transfers between devices, shifted(): return lax.ppermute(part, 'seq', pairs)  40.7 us
    ppermute x52, starting transfers between devices, moved(): return lax.ppermute(value, 'dp', pairs)  38.4 us
    convert_element_type x15, other arithmetic, plus(): return sum((term.astype(WIDE) for term in terms)).astype(LOW)  30.9 us
  transfers between devices with their start and end apart: 80, of which 23 were waited for; matrix products, arithmetic and copies ran while one was open for 10% of the time, Pallas kernels for 33%

profile of v4, /device:TPU:0, one launch (start us, length us, event | category | flops | bytes accessed | tf_op | source)
XLA Modules:
  0.0 559.8 jit_solution(11469415353767640898)
XLA Ops:
  0.6 3.1 convert.20
  4.9 3.0 collective-permute-start
  13.4 6.7 %collective-permute-done.refs_1_ = bf16[2,128,1024]{2,1,0:T(8,128)(2,1)S(1)} collective-permute-done((bf16[2,128,1024]{2,1,0:T(8,128)(2,1)S(1)}, bf16[2,128,1024]{2,1,0:T(8,128)(2,1)S(1)}, u32[]{:S(2)}, u32[]{:S(2)}) %collective-permute-start) | collective-permute-done | bytes 524320 | tf_op jit(solution)/shard_map/ppermute | solution.py:718
  24.3 5.0 collective-permute-done.2.refs_3_
  34.5 7.8 %shard_map.119 = (bf16[1024,1024]{1,0:T(8,128)(2,1)S(1)}, bf16[1024,1024]{1,0:T(8,128)(2,1)S(1)}, bf16[1024,1024]{1,0:T(8,128)(2,1)S(1)}) custom-call(s32[8]{0:T(128)S(1)} %get-tuple-element.274.order_ref, bf16[1024,1024]{1,0:T(8,128)(2,1)S(1)} %multiply_convert_fusion.h_ref, f32[512,1024]{1,0:T(8,128)S(1)} %get-tuple-element.272.table_ref, ...), custom_call_target="tpu_custom_call" | custom-call | flops 214748364800 | bytes 734003200 | tf_op jit(solution)/shard_map/pallas_call | solution.py:44
  45.1 7.1 %collective-permute-done.8.refs_1_.refs_9_ = bf16[3,128,1024]{2,1,0:T(8,128)(2,1)} collective-permute-done((bf16[3,128,1024]{2,1,0:T(8,128)(2,1)}, bf16[3,128,1024]{2,1,0:T(8,128)(2,1)}, u32[]{:S(2)}, u32[]{:S(2)}) %collective-permute-start.8) | collective-permute-done | bytes 786464 | tf_op jit(solution)/shard_map/ppermute | solution.py:718
  55.8 3.5 collective-permute-start.7
  59.9 4.5 collective-permute-done.10.refs_3_.refs_11_
  65.7 5.3 collective-permute-done.7
  75.3 8.9 %shard_map.121 = (bf16[1024,1024]{1,0:T(8,128)(2,1)S(1)}, bf16[1024,1024]{1,0:T(8,128)(2,1)S(1)}, bf16[1024,1024]{1,0:T(8,128)(2,1)S(1)}) custom-call(s32[8]{0:T(128)S(1)} %get-tuple-element.274.order_ref, bf16[1024,1024]{1,0:T(8,128)(2,1)S(1)} %multiply_convert_fusion.h_ref, f32[512,1024]{1,0:T(8,128)S(1)} %copy-done.5, ...), custom_call_target="tpu_custom_call" | custom-call | flops 214748364800 | bytes 838860800 | tf_op jit(solution)/shard_map/pallas_call | solution.py:44
  85.5 5.7 %collective-permute-done.15.refs_1_ = bf16[1,128,2816]{2,1,0:T(8,128)(2,1)} collective-permute-done((bf16[1,128,2816]{2,1,0:T(8,128)(2,1)}, bf16[1,128,2816]{2,1,0:T(8,128)(2,1)}, u32[]{:S(2)}, u32[]{:S(2)}) %collective-permute-start.15) | collective-permute-done | bytes 720928 | tf_op jit(solution)/shard_map/ppermute | solution.py:718
  91.7 4.6 collective-permute-start.17
  97.0 6.7 %collective-permute-done.18.refs_3_ = bf16[1,128,2816]{2,1,0:T(8,128)(2,1)S(1)} collective-permute-done((bf16[1,128,2816]{2,1,0:T(8,128)(2,1)}, bf16[1,128,2816]{2,1,0:T(8,128)(2,1)S(1)}, u32[]{:S(2)}, u32[]{:S(2)}) %collective-permute-start.18) | collective-permute-done | bytes 720928 | tf_op jit(solution)/shard_map/ppermute | solution.py:718
  105.2 5.6 %shard_map.122.part_ref = bf16[1024,1024]{1,0:T(8,128)(2,1)S(1)} custom-call(s32[1]{0:T(128)} %bitcast.1.start_ref, f32[8]{0:T(128)S(1)} %copy-done.80, f32[8]{0:T(128)S(1)} %copy-done.76, s32[2,4]{1,0:T(2,128)S(1)} %copy-done.20, bf16[1024,1024]{1,0:T(8,128)(2,1)S(1)} %get-tuple-element.123.q_ref, bf16[1024,1024]{1,0:T(8,128)(2,1)S(1)} %copy-done.87, ...), custom_call_target="tpu_custom_call" | custom-call | flops 107374182400 | bytes 419430400 | tf_op jit(solution)/shard_map/pallas_call | solution.py:44
  110.9 6.0 %collective-permute-done.23.refs_9_ = bf16[1,128,2816]{2,1,0:T(8,128)(2,1)S(1)} collective-permute-done((bf16[1,128,2816]{2,1,0:T(8,128)(2,1)S(1)}, bf16[1,128,2816]{2,1,0:T(8,128)(2,1)S(1)}, u32[]{:S(2)}, u32[]{:S(2)}) %collective-permute-start.23) | collective-permute-done | bytes 720928 | tf_op jit(solution)/shard_map/ppermute | solution.py:718
  120.8 7.3 %collective-permute-done.24.refs_10_ = bf16[1,128,2816]{2,1,0:T(8,128)(2,1)S(1)} collective-permute-done((bf16[1,128,2816]{2,1,0:T(8,128)(2,1)S(1)}, bf16[1,128,2816]{2,1,0:T(8,128)(2,1)S(1)}, u32[]{:S(2)}, u32[]{:S(2)}) %collective-permute-start.24) | collective-permute-done | bytes 720928 | tf_op jit(solution)/shard_map/ppermute | solution.py:718
  128.1 7.7 %collective-permute-done.25.refs_11_ = bf16[1,128,2816]{2,1,0:T(8,128)(2,1)S(1)} collective-permute-done((bf16[1,128,2816]{2,1,0:T(8,128)(2,1)S(1)}, bf16[1,128,2816]{2,1,0:T(8,128)(2,1)S(1)}, u32[]{:S(2)}, u32[]{:S(2)}) %collective-permute-start.25) | collective-permute-done | bytes 720928 | tf_op jit(solution)/shard_map/ppermute | solution.py:718
  135.9 8.2 %shard_map.123 = (bf16[1024,1024]{1,0:T(8,128)(2,1)S(1)}, bf16[1024,1024]{1,0:T(8,128)(2,1)S(1)}, bf16[1024,1024]{1,0:T(8,128)(2,1)S(1)}, bf16[1024,1024]{1,0:T(8,128)(2,1)S(1)}, bf16[1024,1024]{1,0:T(8,128)(2,1)S(1)}) custom-call(s32[1]{0:T(128)} %bitcast.1.start_ref, f32[8]{0:T(128)S(1)} %copy-done.80, f32[8]{0:T(128)S(1)} %copy-done.76, ...), custom_call_target="tpu_custom_call" | custom-call | flops 120795955200 | bytes 1284505600 | tf_op jit(solution)/shard_map/pallas_call | solution.py:44
  153.5 18.5 %shard_map.124 = (bf16[1024,2816]{1,0:T(8,128)(2,1)}, bf16[1024,2816]{1,0:T(8,128)(2,1)}, bf16[2816,1024]{1,0:T(8,128)(2,1)}) custom-call(s32[8]{0:T(128)S(1)} %get-tuple-element.274.order_ref, bf16[1024,1024]{1,0:T(8,128)(2,1)S(1)} %copy-done.123, bf16[1,128,2816]{2,1,0:T(8,128)(2,1)} %get-tuple-element.122.refs_0_, ...), custom_call_target="tpu_custom_call" | custom-call | flops 590558003200 | bytes 1546649600 | tf_op jit(solution)/shard_map/pallas_call | solution.py:44
  174.7 9.0 %collective-permute-done.33.refs_3_ = bf16[1,352,1024]{2,1,0:T(8,128)(2,1)} collective-permute-done((bf16[1,352,1024]{2,1,0:T(8,128)(2,1)}, bf16[1,352,1024]{2,1,0:T(8,128)(2,1)}, u32[]{:S(2)}, u32[]{:S(2)}) %collective-permute-start.33) | collective-permute-done | bytes 720928 | tf_op jit(solution)/shard_map/ppermute | solution.py:718
  185.3 2.6 copy-done.132
  188.0 12.2 %shard_map.125 = (bf16[1,1408,1024]{2,1,0:T(8,128)(2,1)}, bf16[1,352,1024]{2,1,0:T(8,128)(2,1)S(1)}, bf16[1,352,1024]{2,1,0:T(8,128)(2,1)S(1)}, bf16[1,352,1024]...) custom-call(s32[8]{0:T(128)S(1)} %pad_add_fusion.order_ref, bf16[2816,1024]{1,0:T(8,128)(2,1)S(1)} %copy-done.132, ...), custom_call_target="tpu_custom_call" | custom-call | flops 295279001600 | bytes 681574400 | tf_op jit(solution)/shard_map/pallas_call | solution.py:44
  200.8 14.6 %shard_map.126.refs_0_.refs_1_.dpair_ref = bf16[2,1024,2816]{2,1,0:T(8,128)(2,1)} custom-call(s32[8]{0:T(128)S(1)} %get-tuple-element.274.order_ref, bf16[1024,2816]{1,0:T(8,128)(2,1)S(1)} %copy-done.129, bf16[1024,2816]{1,0:T(8,128)(2,1)} %get-tuple-element.138.second_ref, bf16[1024,1024]{1,0:T(8,128)(2,1)S(1)} %bitcast.120, ...), custom_call_target="tpu_custom_call" | custom-call | flops 295279001600 | bytes 1546649600 | tf_op jit(solution)/shard_map/pallas_call | solution.py:44
  215.4 3.2 add_convert_fusion.8
  220.6 4.3 copy-done.127
  225.0 10.0 %shard_map.127 = bf16[2,512,2816]{2,1,0:T(8,128)(2,1)} custom-call(s32[4]{0:T(128)S(1)} %get-tuple-element.275.order_ref, bf16[1024,1024]{1,0:T(8,128)(2,1)S(1)} %copy-done.120, bf16[2,1024,2816]{2,1,0:T(8,128)(2,1)S(1)} %copy-done.127, bf16[2,1024,2816]{2,1,0:T(8,128)(2,1)S(1)} %copy-done.127), custom_call_target="tpu_custom_call" | custom-call | flops 295279001600 | bytes 1546649600 | tf_op jit(solution)/shard_map/pallas_call | solution.py:44
  235.3 22.1 %shard_map.128.e1_ref.refs_0_ = bf16[1024,1024]{1,0:T(8,128)(2,1)S(1)} custom-call(s32[8]{0:T(128)S(1)} %get-tuple-element.274.order_ref, bf16[2,1024,2816]{2,1,0:T(8,128)(2,1)} %shard_map.126.refs_0_.refs_1_.dpair_ref, bf16[1024,1024]{1,0:T(8,128)(2,1)S(1)} %copy-done.113, bf16[1024,1024]{1,0:T(8,128)(2,1)S(1)} %bitcast.121, ...), custom_call_target="tpu_custom_call" | custom-call | flops 590558003200 | bytes 1468006400 | tf_op jit(solution)/shard_map/pallas_call | solution.py:44
  257.4 3.4 add_convert_fusion.7
  262.6 4.3 copy-done.128
  266.9 10.6 %shard_map.129 = (bf16[2,128,2816]{2,1,0:T(8,128)(2,1)S(1)}, bf16[2,128,2816]{2,1,0:T(8,128)(2,1)S(1)}, bf16[2,128,2816]{2,1,0:T(8,128)(2,1)S(1)}, bf16[2,128,2816]{2,1,0:T(8,128)(2,1)S(1)}) custom-call(s32[4]{0:T(128)S(1)} %get-tuple-element.276.order_ref, bf16[1024,1024]{1,0:T(8,128)(2,1)S(1)} %copy-done.121, bf16[2,1024,2816]{2,1,0:T(8,128)(2,1)S(1)} %copy-done.128, ...), custom_call_target="tpu_custom_call" | custom-call | flops 295279001600 | bytes 1835008000 | tf_op jit(solution)/shard_map/pallas_call | solution.py:44
  282.0 2.5 collective-permute-start.46
  284.5 2.6 collective-permute-start.47
  293.3 6.9 %shard_map.130 = (bf16[1024,1024]{1,0:T(8,128)(2,1)S(1)}, bf16[1024,1024]{1,0:T(8,128)(2,1)S(1)}, bf16[2,8,128,128]{3,2,1,0:T(8,128)(2,1)S(1)}) custom-call(s32[1]{0:T(128)} %bitcast.1.start_ref, f32[8]{0:T(128)S(1)} %copy-done.81, f32[8]{0:T(128)S(1)} %copy-done.77, s32[2,4]{1,0:T(2,128)S(1)} %copy-done.20, s32[8]{0:T(128)S(1)} %get-tuple-element.274.order_ref, ...), custom_call_target="tpu_custom_call" | custom-call | flops 120795955200 | bytes 969932800 | tf_op jit(solution)/shard_map/pallas_call | solution.py:44
  302.3 9.8 %collective-permute-done.41 = bf16[2,128,2816]{2,1,0:T(8,128)(2,1)S(1)} collective-permute-done((bf16[2,128,2816]{2,1,0:T(8,128)(2,1)S(1)}, bf16[2,128,2816]{2,1,0:T(8,128)(2,1)S(1)}, u32[]{:S(2)}, u32[]{:S(2)}) %collective-permute-start.41) | collective-permute-done | bytes 1441824 | tf_op jit(solution)/shard_map/ppermute | solution.py:718
  313.9 5.6 shard_map.131
  323.9 14.3 %shard_map.132 = (bf16[1024,1024]{1,0:T(8,128)(2,1)S(1)}, bf16[1024,1024]{1,0:T(8,128)(2,1)S(1)}, bf16[1024,1024]{1,0:T(8,128)(2,1)S(1)}) custom-call(s32[1]{0:T(128)} %bitcast.1.start_ref, f32[8]{0:T(128)S(1)} %copy-done.81, f32[8]{0:T(128)S(1)} %copy-done.77, s32[2,4]{1,0:T(2,128)S(1)} %copy-done.20, bf16[1024,1024]{1,0:T(8,128)(2,1)S(1)} %copy-done.108, ...), custom_call_target="tpu_custom_call" | custom-call | flops 322122547200 | bytes 865075200 | tf_op jit(solution)/shard_map/pallas_call | solution.py:44
  342.4 3.0 add_convert_fusion
  345.4 2.6 copy.13.turned_ref
  352.8 6.6 %shard_map.133 = (bf16[2,512,1024]{2,1,0:T(8,128)(2,1)S(1)}, bf16[2,128,1024]{2,1,0:T(8,128)(2,1)S(1)}, bf16[2,128,1024]{2,1,0:T(8,128)(2,1)S(1)}, bf16[2,128,10...) custom-call(s32[8]{0:T(128)S(1)} %copy-done.85, bf16[1024,1024]{1,0:T(8,128)(2,1)S(1)} %copy-done.7, ...), custom_call_target="tpu_custom_call" | custom-call | flops 214748364800 | bytes 524288000 | tf_op jit(solution)/shard_map/pallas_call | solution.py:44
  367.3 3.0 shard_map.134
  376.1 2.7 copy.14.turned_ref
  383.6 7.6 %shard_map.135 = (bf16[2,512,1024]{2,1,0:T(8,128)(2,1)}, bf16[2,128,1024]{2,1,0:T(8,128)(2,1)S(1)}, bf16[2,128,1024]{2,1,0:T(8,128)(2,1)S(1)}, bf16[2,128,1024]{...) custom-call(s32[8]{0:T(128)S(1)} %copy-done.85, bf16[1024,1024]{1,0:T(8,128)(2,1)S(1)} %copy-done.6, ...), custom_call_target="tpu_custom_call" | custom-call | flops 214748364800 | bytes 524288000 | tf_op jit(solution)/shard_map/pallas_call | solution.py:44
  393.9 3.5 collective-permute-start.78
  402.6 7.7 %collective-permute-done.78 = bf16[1,88,1024]{2,1,0:T(8,128)(2,1)} collective-permute-done((bf16[1,88,1024]{2,1,0:T(8,128)(2,1)}, bf16[1,88,1024]{2,1,0:T(8,128)(2,1)}, u32[]{:S(2)}, u32[]{:S(2)}) %collective-permute-start.78) | collective-permute-done | bytes 180256 | tf_op jit(solution)/shard_map/ppermute | solution.py:745
  410.3 10.7 %collective-permute-start.58 = (bf16[2,32,2816]{2,1,0:T(8,128)(2,1)}, bf16[2,32,2816]{2,1,0:T(8,128)(2,1)S(1)}, u32[]{:S(2)}, u32[]{:S(2)}) collective-permute-start(bf16[2,32,2816]{2,1,0:T(8,128)(2,1)} %get-tuple-element.241), channel_id=1, source_target_pairs={{0,16},{8,24},{16,0},{24,8},{1,17},{9,25},{17,1},{25,9},{2,18},{10... | collective-permute-start | bytes 1081352 | tf_op jit(solution)/shard_map/ppermute | solution.py:745
  421.0 3.4 collective-permute-start.59
  429.4 8.8 %collective-permute-done.58 = bf16[2,32,2816]{2,1,0:T(8,128)(2,1)S(1)} collective-permute-done((bf16[2,32,2816]{2,1,0:T(8,128)(2,1)}, bf16[2,32,2816]{2,1,0:T(8,128)(2,1)S(1)}, u32[]{:S(2)}, u32[]{:S(2)}) %collective-permute-start.58) | collective-permute-done | bytes 360480 | tf_op jit(solution)/shard_map/ppermute | solution.py:745
  440.4 7.8 %collective-permute-start.74 = (bf16[2,32,2816]{2,1,0:T(8,128)(2,1)}, bf16[2,32,2816]{2,1,0:T(8,128)(2,1)}, u32[]{:S(2)}, u32[]{:S(2)}) collective-permute-start(bf16[2,32,2816]{2,1,0:T(8,128)(2,1)} %fusion.15), channel_id=1, source_target_pairs={{0,8},{8,16},{16,24},{24,0},{1,9},{9,17},{17,25},{25,1},{2,10},{10... | collective-permute-start | bytes 1081352 | tf_op jit(solution)/shard_map/ppermute | solution.py:745
  448.2 3.3 collective-permute-start.75
  451.5 2.8 add_convert_fusion.3
  456.1 2.6 add_convert_fusion.12
  465.6 15.4 %shard_map.136 = f32[1024,1024]{1,0:T(8,128)} custom-call(s32[8]{0:T(128)S(1)} %copy-done.23, bf16[1024,1024]{1,0:T(8,128)(2,1)S(1)} %copy-done.137, bf16[1024,1024]{1,0:T(8,128)(2,1)S(1)} %copy-done.98, bf16[1024,1024]{1,0:T(8,128)(2,1)S(1)} %copy-done.101, bf16[1024,1024]{1,0:T(8,128)(2,1)S(1)} %copy-done.126, bf16[1024,1024]{1,0:T(8,128)(2,1)S(1)} %bitcast.118, ...), custom_call_target="tpu_custom_call" | custom-call | flops 429496729600 | bytes 1363148800 | tf_op jit(solution)/shard_map/pallas_call | solution.py:44
  486.8 2.6 copy-done.130
  489.5 2.6 copy-done.131
  492.1 10.8 %shard_map.137 = bf16[1024,1024]{1,0:T(8,128)(2,1)} custom-call(s32[8]{0:T(128)S(1)} %copy-done.23, bf16[1024,2816]{1,0:T(8,128)(2,1)S(1)} %copy-done.130, bf16[1024,2816]{1,0:T(8,128)(2,1)S(1)} %copy-done.131, bf16[1024,1024]{1,0:T(8,128)(2,1)S(1)} %copy-done.114, bf16[1,352,1024]{2,1,0:T(8,128)(2,1)} %convert_element_type.379.refs_0_, ...), custom_call_target="tpu_custom_call" | custom-call | flops 295279001600 | bytes 1074790400 | tf_op jit(solution)/shard_map/pallas_call | solution.py:44
  502.9 3.6 collective-permute-start.63
  508.9 3.9 collective-permute-done.63
  519.3 4.4 collective-permute-done.76
  527.5 5.0 collective-permute-done.68
  532.6 8.3 %collective-permute-start.67 = (bf16[3,32,1024]{2,1,0:T(8,128)(2,1)S(1)}, bf16[3,32,1024]{2,1,0:T(8,128)(2,1)S(1)}, u32[]{:S(2)}, u32[]{:S(2)}) collective-permute-start(bf16[3,32,1024]{2,1,0:T(8,128)(2,1)S(1)} %fusion.26), channel_id=1, source_target_pairs={{0,24},{8,0},{16,8},{24,16},{1,25},{9,1},{17,9},{25,17},{2,26},{10... | collective-permute-start | bytes 589832 | tf_op jit(solution)/shard_map/ppermute | solution.py:745
  543.0 3.7 collective-permute-start.71
  546.7 3.5 collective-permute-start.72
  550.9 3.4 collective-permute-done.71
  554.3 3.2 collective-permute-done.72
  (505 shorter events, 147.3 us)
Async XLA Ops:
  4.9 15.2 %collective-permute-start = (bf16[2,128,1024]{2,1,0:T(8,128)(2,1)S(1)}, bf16[2,128,1024]{2,1,0:T(8,128)(2,1)S(1)}, u32[]{:S(2)}, u32[]{:S(2)}) collective-permute-start(bf16[2,128,1024]{2,1,0:T(8,128)(2,1)S(1)} %slice_bitcast_fusion.2.refs_0_), channel_id=1, source_target_pairs={{0,2},{1,5},{2,0},{3,7},{4,6},{5,1},{6,4},{7,3},{8,10},{9,13},{10,... | collective-permute-start | bytes 1572872 | tf_op jit(solution)/shard_map/ppermute | solution.py:718
  7.9 15.9 %collective-permute-start.1 = (bf16[2,128,1024]{2,1,0:T(8,128)(2,1)S(1)}, bf16[2,128,1024]{2,1,0:T(8,128)(2,1)}, u32[]{:S(2)}, u32[]{:S(2)}) collective-permute-start(bf16[2,128,1024]{2,1,0:T(8,128)(2,1)S(1)} %slice_bitcast_fusion.2.refs_0_), channel_id=1, source_target_pairs={{0,4},{1,3},{2,6},{3,1},{4,0},{5,7},{6,2},{7,5},{8,12},{9,11},{10,... | collective-permute-start | bytes 1572872 | tf_op jit(solution)/shard_map/ppermute | solution.py:718
  9.4 24.3 %collective-permute-start.3 = (bf16[2,128,1024]{2,1,0:T(8,128)(2,1)S(1)}, bf16[2,128,1024]{2,1,0:T(8,128)(2,1)}, u32[]{:S(2)}, u32[]{:S(2)}) collective-permute-start(bf16[2,128,1024]{2,1,0:T(8,128)(2,1)S(1)} %slice_bitcast_fusion.2.refs_0_), channel_id=1, source_target_pairs={{0,1},{1,0},{2,3},{3,2},{4,5},{5,4},{6,7},{7,6},{8,9},{9,8},{10,11... | collective-permute-start | bytes 1572872 | tf_op jit(solution)/shard_map/ppermute | solution.py:718
  31.2 20.9 %collective-permute-start.8 = (bf16[3,128,1024]{2,1,0:T(8,128)(2,1)}, bf16[3,128,1024]{2,1,0:T(8,128)(2,1)}, u32[]{:S(2)}, u32[]{:S(2)}) collective-permute-start(bf16[3,128,1024]{2,1,0:T(8,128)(2,1)} %pad_maximum_fusion.4.refs_0_.refs_8_), channel_id=1, source_target_pairs={{0,2},{1,5},{2,0},{3,7},{4,6},{5,1},{6,4},{7,3},{8,10},{9,13},{10,... | collective-permute-start | bytes 2359304 | tf_op jit(solution)/shard_map/ppermute | solution.py:718
  33.7 25.7 %collective-permute-start.9 = (bf16[3,128,1024]{2,1,0:T(8,128)(2,1)}, bf16[3,128,1024]{2,1,0:T(8,128)(2,1)}, u32[]{:S(2)}, u32[]{:S(2)}) collective-permute-start(bf16[3,128,1024]{2,1,0:T(8,128)(2,1)} %pad_maximum_fusion.4.refs_0_.refs_8_), channel_id=1, source_target_pairs={{0,4},{1,3},{2,6},{3,1},{4,0},{5,7},{6,2},{7,5},{8,12},{9,11},{10,... | collective-permute-start | bytes 2359304 | tf_op jit(solution)/shard_map/ppermute | solution.py:718
  55.6 17.9 %collective-permute-start.11 = (bf16[3,128,1024]{2,1,0:T(8,128)(2,1)}, bf16[3,128,1024]{2,1,0:T(8,128)(2,1)S(1)}, u32[]{:S(2)}, u32[]{:S(2)}) collective-permute-start(bf16[3,128,1024]{2,1,0:T(8,128)(2,1)} %pad_maximum_fusion.4.refs_0_.refs_8_), channel_id=1, source_target_pairs={{0,1},{1,0},{2,3},{3,2},{4,5},{5,4},{6,7},{7,6},{8,9},{9,8},{10,11... | collective-permute-start | bytes 2359304 | tf_op jit(solution)/shard_map/ppermute | solution.py:718
  55.8 15.1 %collective-permute-start.7 = (bf16[2,8,128,128]{3,2,1,0:T(8,128)(2,1)S(1)}, bf16[2,8,128,128]{3,2,1,0:T(8,128)(2,1)S(1)}, u32[]{:S(2)}, u32[]{:S(2)}) collective-permute-start(bf16[2,8,128,128]{3,2,1,0:T(8,128)(2,1)S(1)} %shard_map.120), channel_id=1, source_target_pairs={{0,8},{8,16},{16,24},{1,9},{9,17},{17,25},{2,10},{10,18},{18,26},{... | collective-permute-start | bytes 1572872 | tf_op jit(solution)/shard_map/ppermute | solution.py:701
  59.3 15.9 %collective-permute-start.12 = (bf16[3,128,1024]{2,1,0:T(8,128)(2,1)}, bf16[3,128,1024]{2,1,0:T(8,128)(2,1)S(1)}, u32[]{:S(2)}, u32[]{:S(2)}) collective-permute-start(bf16[3,128,1024]{2,1,0:T(8,128)(2,1)} %collective-permute-done.8.refs_1_.refs_9_), channel_id=1, source_target_pairs={{0,1},{1,0},{2,3},{3,2},{4,5},{5,4},{6,7},{7,6},{8,9},{9,8},{10,11... | collective-permute-start | bytes 2359304 | tf_op jit(solution)/shard_map/ppermute | solution.py:718
  59.5 15.8 %collective-permute-start.13 = (bf16[3,128,1024]{2,1,0:T(8,128)(2,1)}, bf16[3,128,1024]{2,1,0:T(8,128)(2,1)S(1)}, u32[]{:S(2)}, u32[]{:S(2)}) collective-permute-start(bf16[3,128,1024]{2,1,0:T(8,128)(2,1)} %collective-permute-done.9.refs_2_.refs_10_), channel_id=1, source_target_pairs={{0,1},{1,0},{2,3},{3,2},{4,5},{5,4},{6,7},{7,6},{8,9},{9,8},{10,11... | collective-permute-start | bytes 2359304 | tf_op jit(solution)/shard_map/ppermute | solution.py:718
  72.0 19.3 %collective-permute-start.15 = (bf16[1,128,2816]{2,1,0:T(8,128)(2,1)}, bf16[1,128,2816]{2,1,0:T(8,128)(2,1)}, u32[]{:S(2)}, u32[]{:S(2)}) collective-permute-start(bf16[1,128,2816]{2,1,0:T(8,128)(2,1)} %get-tuple-element.122.refs_0_), channel_id=1, source_target_pairs={{0,2},{1,5},{2,0},{3,7},{4,6},{5,1},{6,4},{7,3},{8,10},{9,13},{10,... | collective-permute-start | bytes 2162696 | tf_op jit(solution)/shard_map/ppermute | solution.py:718
  73.4 23.5 %collective-permute-start.16 = (bf16[1,128,2816]{2,1,0:T(8,128)(2,1)}, bf16[1,128,2816]{2,1,0:T(8,128)(2,1)}, u32[]{:S(2)}, u32[]{:S(2)}) collective-permute-start(bf16[1,128,2816]{2,1,0:T(8,128)(2,1)} %get-tuple-element.122.refs_0_), channel_id=1, source_target_pairs={{0,4},{1,3},{2,6},{3,1},{4,0},{5,7},{6,2},{7,5},{8,12},{9,11},{10,... | collective-permute-start | bytes 2162696 | tf_op jit(solution)/shard_map/ppermute | solution.py:718
  91.7 25.1 %collective-permute-start.17 = (bf16[2,8,128,128]{3,2,1,0:T(8,128)(2,1)S(1)}, bf16[2,8,128,128]{3,2,1,0:T(8,128)(2,1)S(1)}, u32[]{:S(2)}, u32[]{:S(2)}) collective-permute-start(bf16[2,8,128,128]{3,2,1,0:T(8,128)(2,1)S(1)} %copy-done.153), channel_id=1, source_target_pairs={{0,8},{8,16},{16,24},{1,9},{9,17},{17,25},{2,10},{10,18},{18,26},{... | collective-permute-start | bytes 1572872 | tf_op jit(solution)/shard_map/ppermute | solution.py:701
  96.3 23.8 %collective-permute-start.19 = (bf16[1,128,2816]{2,1,0:T(8,128)(2,1)}, bf16[1,128,2816]{2,1,0:T(8,128)(2,1)S(1)}, u32[]{:S(2)}, u32[]{:S(2)}) collective-permute-start(bf16[1,128,2816]{2,1,0:T(8,128)(2,1)} %get-tuple-element.122.refs_0_), channel_id=1, source_target_pairs={{0,1},{1,0},{2,3},{3,2},{4,5},{5,4},{6,7},{7,6},{8,9},{9,8},{10,11... | collective-permute-start | bytes 2162696 | tf_op jit(solution)/shard_map/ppermute | solution.py:718
  96.4 23.8 %collective-permute-start.20 = (bf16[1,128,2816]{2,1,0:T(8,128)(2,1)}, bf16[1,128,2816]{2,1,0:T(8,128)(2,1)S(1)}, u32[]{:S(2)}, u32[]{:S(2)}) collective-permute-start(bf16[1,128,2816]{2,1,0:T(8,128)(2,1)} %collective-permute-done.15.refs_1_), channel_id=1, source_target_pairs={{0,1},{1,0},{2,3},{3,2},{4,5},{5,4},{6,7},{7,6},{8,9},{9,8},{10,11... | collective-permute-start | bytes 2162696 | tf_op jit(solution)/shard_map/ppermute | solution.py:718
  96.9 23.8 %collective-permute-start.21 = (bf16[1,128,2816]{2,1,0:T(8,128)(2,1)}, bf16[1,128,2816]{2,1,0:T(8,128)(2,1)S(1)}, u32[]{:S(2)}, u32[]{:S(2)}) collective-permute-start(bf16[1,128,2816]{2,1,0:T(8,128)(2,1)} %collective-permute-done.16.refs_2_), channel_id=1, source_target_pairs={{0,1},{1,0},{2,3},{3,2},{4,5},{5,4},{6,7},{7,6},{8,9},{9,8},{10,11... | collective-permute-start | bytes 2162696 | tf_op jit(solution)/shard_map/ppermute | solution.py:718
  103.7 13.1 %collective-permute-start.23 = (bf16[1,128,2816]{2,1,0:T(8,128)(2,1)S(1)}, bf16[1,128,2816]{2,1,0:T(8,128)(2,1)S(1)}, u32[]{:S(2)}, u32[]{:S(2)}) collective-permute-start(bf16[1,128,2816]{2,1,0:T(8,128)(2,1)S(1)} %copy-done.8), channel_id=1, source_target_pairs={{0,2},{1,5},{2,0},{3,7},{4,6},{5,1},{6,4},{7,3},{8,10},{9,13},{10,... | collective-permute-start | bytes 2162696 | tf_op jit(solution)/shard_map/ppermute | solution.py:718
  116.8 19.0 %collective-permute-start.25 = (bf16[1,128,2816]{2,1,0:T(8,128)(2,1)S(1)}, bf16[1,128,2816]{2,1,0:T(8,128)(2,1)S(1)}, u32[]{:S(2)}, u32[]{:S(2)}) collective-permute-start(bf16[1,128,2816]{2,1,0:T(8,128)(2,1)S(1)} %collective-permute-done.23.refs_9_), channel_id=1, source_target_pairs={{0,4},{1,3},{2,6},{3,1},{4,0},{5,7},{6,2},{7,5},{8,12},{9,11},{10,... | collective-permute-start | bytes 2162696 | tf_op jit(solution)/shard_map/ppermute | solution.py:718
  120.2 30.7 %collective-permute-start.26 = (bf16[1,128,2816]{2,1,0:T(8,128)(2,1)S(1)}, bf16[1,128,2816]{2,1,0:T(8,128)(2,1)S(1)}, u32[]{:S(2)}, u32[]{:S(2)}) collective-permute-start(bf16[1,128,2816]{2,1,0:T(8,128)(2,1)S(1)} %copy-done.8), channel_id=1, source_target_pairs={{0,1},{1,0},{2,3},{3,2},{4,5},{5,4},{6,7},{7,6},{8,9},{9,8},{10,11... | collective-permute-start | bytes 2162696 | tf_op jit(solution)/shard_map/ppermute | solution.py:718
  120.3 29.1 %collective-permute-start.22 = (bf16[1,128,2816]{2,1,0:T(8,128)(2,1)S(1)}, bf16[1,128,2816]{2,1,0:T(8,128)(2,1)S(1)}, u32[]{:S(2)}, u32[]{:S(2)}) collective-permute-start(bf16[1,128,2816]{2,1,0:T(8,128)(2,1)S(1)} %collective-permute-done.18.refs_3_), channel_id=1, source_target_pairs={{0,1},{1,0},{2,3},{3,2},{4,5},{5,4},{6,7},{7,6},{8,9},{9,8},{10,11... | collective-permute-start | bytes 2162696 | tf_op jit(solution)/shard_map/ppermute | solution.py:718
  120.7 30.1 %collective-permute-start.27 = (bf16[1,128,2816]{2,1,0:T(8,128)(2,1)S(1)}, bf16[1,128,2816]{2,1,0:T(8,128)(2,1)S(1)}, u32[]{:S(2)}, u32[]{:S(2)}) collective-permute-start(bf16[1,128,2816]{2,1,0:T(8,128)(2,1)S(1)} %collective-permute-done.23.refs_9_), channel_id=1, source_target_pairs={{0,1},{1,0},{2,3},{3,2},{4,5},{5,4},{6,7},{7,6},{8,9},{9,8},{10,11... | collective-permute-start | bytes 2162696 | tf_op jit(solution)/shard_map/ppermute | solution.py:718
  128.1 22.8 %collective-permute-start.28 = (bf16[1,128,2816]{2,1,0:T(8,128)(2,1)S(1)}, bf16[1,128,2816]{2,1,0:T(8,128)(2,1)S(1)}, u32[]{:S(2)}, u32[]{:S(2)}) collective-permute-start(bf16[1,128,2816]{2,1,0:T(8,128)(2,1)S(1)} %collective-permute-done.24.refs_10_), channel_id=1, source_target_pairs={{0,1},{1,0},{2,3},{3,2},{4,5},{5,4},{6,7},{7,6},{8,9},{9,8},{10,11... | collective-permute-start | bytes 2162696 | tf_op jit(solution)/shard_map/ppermute | solution.py:718
  135.9 15.1 %collective-permute-start.29 = (bf16[1,128,2816]{2,1,0:T(8,128)(2,1)S(1)}, bf16[1,128,2816]{2,1,0:T(8,128)(2,1)S(1)}, u32[]{:S(2)}, u32[]{:S(2)}) collective-permute-start(bf16[1,128,2816]{2,1,0:T(8,128)(2,1)S(1)} %collective-permute-done.25.refs_11_), channel_id=1, source_target_pairs={{0,1},{1,0},{2,3},{3,2},{4,5},{5,4},{6,7},{7,6},{8,9},{9,8},{10,11... | collective-permute-start | bytes 2162696 | tf_op jit(solution)/shard_map/ppermute | solution.py:718
  149.4 22.7 %collective-permute-start.30 = (bf16[1,352,1024]{2,1,0:T(8,128)(2,1)}, bf16[1,352,1024]{2,1,0:T(8,128)(2,1)}, u32[]{:S(2)}, u32[]{:S(2)}) collective-permute-start(bf16[1,352,1024]{2,1,0:T(8,128)(2,1)} %convert_element_type.379.refs_0_), channel_id=1, source_target_pairs={{0,2},{1,5},{2,0},{3,7},{4,6},{5,1},{6,4},{7,3},{8,10},{9,13},{10,... | collective-permute-start | bytes 2162696 | tf_op jit(solution)/shard_map/ppermute | solution.py:718
  150.9 23.3 %collective-permute-start.31 = (bf16[1,352,1024]{2,1,0:T(8,128)(2,1)}, bf16[1,352,1024]{2,1,0:T(8,128)(2,1)}, u32[]{:S(2)}, u32[]{:S(2)}) collective-permute-start(bf16[1,352,1024]{2,1,0:T(8,128)(2,1)} %convert_element_type.379.refs_0_), channel_id=1, source_target_pairs={{0,4},{1,3},{2,6},{3,1},{4,0},{5,7},{6,2},{7,5},{8,12},{9,11},{10,... | collective-permute-start | bytes 2162696 | tf_op jit(solution)/shard_map/ppermute | solution.py:718
  174.1 26.7 %collective-permute-start.34 = (bf16[1,352,1024]{2,1,0:T(8,128)(2,1)}, bf16[1,352,1024]{2,1,0:T(8,128)(2,1)}, u32[]{:S(2)}, u32[]{:S(2)}) collective-permute-start(bf16[1,352,1024]{2,1,0:T(8,128)(2,1)} %convert_element_type.379.refs_0_), channel_id=1, source_target_pairs={{0,1},{1,0},{2,3},{3,2},{4,5},{5,4},{6,7},{7,6},{8,9},{9,8},{10,11... | collective-permute-start | bytes 2162696 | tf_op jit(solution)/shard_map/ppermute | solution.py:718
  174.1 26.6 %collective-permute-start.35 = (bf16[1,352,1024]{2,1,0:T(8,128)(2,1)}, bf16[1,352,1024]{2,1,0:T(8,128)(2,1)}, u32[]{:S(2)}, u32[]{:S(2)}) collective-permute-start(bf16[1,352,1024]{2,1,0:T(8,128)(2,1)} %collective-permute-done.30.refs_1_), channel_id=1, source_target_pairs={{0,1},{1,0},{2,3},{3,2},{4,5},{5,4},{6,7},{7,6},{8,9},{9,8},{10,11... | collective-permute-start | bytes 2162696 | tf_op jit(solution)/shard_map/ppermute | solution.py:718
  174.6 26.2 %collective-permute-start.36 = (bf16[1,352,1024]{2,1,0:T(8,128)(2,1)}, bf16[1,352,1024]{2,1,0:T(8,128)(2,1)}, u32[]{:S(2)}, u32[]{:S(2)}) collective-permute-start(bf16[1,352,1024]{2,1,0:T(8,128)(2,1)} %collective-permute-done.31.refs_2_), channel_id=1, source_target_pairs={{0,1},{1,0},{2,3},{3,2},{4,5},{5,4},{6,7},{7,6},{8,9},{9,8},{10,11... | collective-permute-start | bytes 2162696 | tf_op jit(solution)/shard_map/ppermute | solution.py:718
  183.7 17.1 %collective-permute-start.37 = (bf16[1,352,1024]{2,1,0:T(8,128)(2,1)}, bf16[1,352,1024]{2,1,0:T(8,128)(2,1)}, u32[]{:S(2)}, u32[]{:S(2)}) collective-permute-start(bf16[1,352,1024]{2,1,0:T(8,128)(2,1)} %collective-permute-done.33.refs_3_), channel_id=1, source_target_pairs={{0,1},{1,0},{2,3},{3,2},{4,5},{5,4},{6,7},{7,6},{8,9},{9,8},{10,11... | collective-permute-start | bytes 2162696 | tf_op jit(solution)/shard_map/ppermute | solution.py:718
  200.2 15.2 %collective-permute-start.32 = (bf16[1,1408,1024]{2,1,0:T(8,128)(2,1)}, bf16[1,1408,1024]{2,1,0:T(8,128)(2,1)}, u32[]{:S(2)}, u32[]{:S(2)}) collective-permute-start(bf16[1,1408,1024]{2,1,0:T(8,128)(2,1)} %get-tuple-element.133), channel_id=1, source_target_pairs={{0,1},{1,0},{2,3},{3,2},{4,5},{5,4},{6,7},{7,6},{8,9},{9,8},{10,11... | collective-permute-start | bytes 8650760 | tf_op jit(solution)/shard_map/ppermute | solution.py:718
  218.6 38.8 %collective-permute-start.38 = (bf16[1,352,1024]{2,1,0:T(8,128)(2,1)}, bf16[1,352,1024]{2,1,0:T(8,128)(2,1)}, u32[]{:S(2)}, u32[]{:S(2)}) collective-permute-start(bf16[1,352,1024]{2,1,0:T(8,128)(2,1)} %get-tuple-element.140), channel_id=1, source_target_pairs={{0,2},{1,5},{2,0},{3,7},{4,6},{5,1},{6,4},{7,3},{8,10},{9,13},{10,... | collective-permute-start | bytes 2162696 | tf_op jit(solution)/shard_map/ppermute | solution.py:718
  219.6 37.9 %collective-permute-start.39 = (bf16[1,352,1024]{2,1,0:T(8,128)(2,1)}, bf16[1,352,1024]{2,1,0:T(8,128)(2,1)}, u32[]{:S(2)}, u32[]{:S(2)}) collective-permute-start(bf16[1,352,1024]{2,1,0:T(8,128)(2,1)} %get-tuple-element.229), channel_id=1, source_target_pairs={{0,2},{1,5},{2,0},{3,7},{4,6},{5,1},{6,4},{7,3},{8,10},{9,13},{10,... | collective-permute-start | bytes 2162696 | tf_op jit(solution)/shard_map/ppermute | solution.py:718
  235.1 27.5 %collective-permute-start.40 = (bf16[2,512,2816]{2,1,0:T(8,128)(2,1)}, bf16[2,512,2816]{2,1,0:T(8,128)(2,1)}, u32[]{:S(2)}, u32[]{:S(2)}) collective-permute-start(bf16[2,512,2816]{2,1,0:T(8,128)(2,1)} %shard_map.127), channel_id=1, source_target_pairs={{0,1},{1,0},{2,3},{3,2},{4,5},{5,4},{6,7},{7,6},{8,9},{9,8},{10,11... | collective-permute-start | bytes 17301512 | tf_op jit(solution)/shard_map/ppermute | solution.py:718
  260.8 18.9 %collective-permute-start.43 = (bf16[1,352,1024]{2,1,0:T(8,128)(2,1)}, bf16[1,352,1024]{2,1,0:T(8,128)(2,1)}, u32[]{:S(2)}, u32[]{:S(2)}) collective-permute-start(bf16[1,352,1024]{2,1,0:T(8,128)(2,1)} %add_convert_fusion.7), channel_id=1, source_target_pairs={{0,4},{1,3},{2,6},{3,1},{4,0},{5,7},{6,2},{7,5},{8,12},{9,11},{10,... | collective-permute-start | bytes 2162696 | tf_op jit(solution)/shard_map/ppermute | solution.py:718
  277.6 24.7 %collective-permute-start.42 = (bf16[2,128,2816]{2,1,0:T(8,128)(2,1)S(1)}, bf16[2,128,2816]{2,1,0:T(8,128)(2,1)S(1)}, u32[]{:S(2)}, u32[]{:S(2)}) collective-permute-start(bf16[2,128,2816]{2,1,0:T(8,128)(2,1)S(1)} %get-tuple-element.150), channel_id=1, source_target_pairs={{0,2},{1,5},{2,0},{3,7},{4,6},{5,1},{6,4},{7,3},{8,10},{9,13},{10,... | collective-permute-start | bytes 4325384 | tf_op jit(solution)/shard_map/ppermute | solution.py:718
  278.2 33.9 %collective-permute-start.41 = (bf16[2,128,2816]{2,1,0:T(8,128)(2,1)S(1)}, bf16[2,128,2816]{2,1,0:T(8,128)(2,1)S(1)}, u32[]{:S(2)}, u32[]{:S(2)}) collective-permute-start(bf16[2,128,2816]{2,1,0:T(8,128)(2,1)S(1)} %get-tuple-element.148), channel_id=1, source_target_pairs={{0,2},{1,5},{2,0},{3,7},{4,6},{5,1},{6,4},{7,3},{8,10},{9,13},{10,... | collective-permute-start | bytes 4325384 | tf_op jit(solution)/shard_map/ppermute | solution.py:718
  282.0 18.2 %collective-permute-start.46 = (bf16[1,88,1024]{2,1,0:T(8,128)(2,1)S(1)}, bf16[1,88,1024]{2,1,0:T(8,128)(2,1)S(1)}, u32[]{:S(2)}, u32[]{:S(2)}) collective-permute-start(bf16[1,88,1024]{2,1,0:T(8,128)(2,1)S(1)} %get-tuple-element.263), channel_id=1, source_target_pairs={{0,8},{8,16},{16,24},{24,0},{1,9},{9,17},{17,25},{25,1},{2,10},{10... | collective-permute-start | bytes 540680 | tf_op jit(solution)/shard_map/ppermute | solution.py:745
  284.5 17.0 %collective-permute-start.47 = (bf16[1,88,1024]{2,1,0:T(8,128)(2,1)S(1)}, bf16[1,88,1024]{2,1,0:T(8,128)(2,1)S(1)}, u32[]{:S(2)}, u32[]{:S(2)}) collective-permute-start(bf16[1,88,1024]{2,1,0:T(8,128)(2,1)S(1)} %get-tuple-element.262), channel_id=1, source_target_pairs={{0,16},{8,24},{16,0},{24,8},{1,17},{9,25},{17,1},{25,9},{2,18},{10... | collective-permute-start | bytes 540680 | tf_op jit(solution)/shard_map/ppermute | solution.py:745
  287.1 14.4 %collective-permute-start.48 = (bf16[1,88,1024]{2,1,0:T(8,128)(2,1)S(1)}, bf16[1,88,1024]{2,1,0:T(8,128)(2,1)S(1)}, u32[]{:S(2)}, u32[]{:S(2)}) collective-permute-start(bf16[1,88,1024]{2,1,0:T(8,128)(2,1)S(1)} %get-tuple-element.261), channel_id=1, source_target_pairs={{0,24},{8,0},{16,8},{24,16},{1,25},{9,1},{17,9},{25,17},{2,26},{10... | collective-permute-start | bytes 540680 | tf_op jit(solution)/shard_map/ppermute | solution.py:745
  300.2 21.4 %collective-permute-start.45 = (bf16[2,8,128,128]{3,2,1,0:T(8,128)(2,1)S(1)}, bf16[2,8,128,128]{3,2,1,0:T(8,128)(2,1)S(1)}, u32[]{:S(2)}, u32[]{:S(2)}) collective-permute-start(bf16[2,8,128,128]{3,2,1,0:T(8,128)(2,1)S(1)} %get-tuple-element.155), channel_id=1, source_target_pairs={{8,0},{16,8},{24,16},{9,1},{17,9},{25,17},{10,2},{18,10},{26,18},{... | collective-permute-start | bytes 1572872 | tf_op jit(solution)/shard_map/ppermute | solution.py:701
  313.7 28.7 %collective-permute-start.44 = (bf16[2,128,2816]{2,1,0:T(8,128)(2,1)}, bf16[2,128,2816]{2,1,0:T(8,128)(2,1)}, u32[]{:S(2)}, u32[]{:S(2)}) collective-permute-start(bf16[2,128,2816]{2,1,0:T(8,128)(2,1)} %add_convert_fusion.1), channel_id=1, source_target_pairs={{0,4},{1,3},{2,6},{3,1},{4,0},{5,7},{6,2},{7,5},{8,12},{9,11},{10,... | collective-permute-start | bytes 4325384 | tf_op jit(solution)/shard_map/ppermute | solution.py:718
  321.6 49.0 %collective-permute-start.50 = (bf16[1,512,1024]{2,1,0:T(8,128)(2,1)}, bf16[1,512,1024]{2,1,0:T(8,128)(2,1)}, u32[]{:S(2)}, u32[]{:S(2)}) collective-permute-start(bf16[1,512,1024]{2,1,0:T(8,128)(2,1)} %get-tuple-element.164), channel_id=1, source_target_pairs={{0,1},{1,0},{2,3},{3,2},{4,5},{5,4},{6,7},{7,6},{8,9},{9,8},{10,11... | collective-permute-start | bytes 3145736 | tf_op jit(solution)/shard_map/ppermute | solution.py:718
  322.6 17.3 %collective-permute-start.51 = (bf16[2,8,128,128]{3,2,1,0:T(8,128)(2,1)}, bf16[2,8,128,128]{3,2,1,0:T(8,128)(2,1)}, u32[]{:S(2)}, u32[]{:S(2)}) collective-permute-start(bf16[2,8,128,128]{3,2,1,0:T(8,128)(2,1)} %fusion.3), channel_id=1, source_target_pairs={{8,0},{16,8},{24,16},{9,1},{17,9},{25,17},{10,2},{18,10},{26,18},{... | collective-permute-start | bytes 1572872 | tf_op jit(solution)/shard_map/ppermute | solution.py:701
  391.2 64.9 %collective-permute-start.52 = (bf16[2,512,1024]{2,1,0:T(8,128)(2,1)}, bf16[2,512,1024]{2,1,0:T(8,128)(2,1)}, u32[]{:S(2)}, u32[]{:S(2)}) collective-permute-start(bf16[2,512,1024]{2,1,0:T(8,128)(2,1)} %get-tuple-element.185), channel_id=1, source_target_pairs={{0,1},{1,0},{2,3},{3,2},{4,5},{5,4},{6,7},{7,6},{8,9},{9,8},{10,11... | collective-permute-start | bytes 6291464 | tf_op jit(solution)/shard_map/ppermute | solution.py:718
  393.9 16.4 %collective-permute-start.78 = (bf16[1,88,1024]{2,1,0:T(8,128)(2,1)}, bf16[1,88,1024]{2,1,0:T(8,128)(2,1)}, u32[]{:S(2)}, u32[]{:S(2)}) collective-permute-start(bf16[1,88,1024]{2,1,0:T(8,128)(2,1)} %fusion.37), channel_id=1, source_target_pairs={{0,16},{8,24},{16,0},{24,8},{1,17},{9,25},{17,1},{25,9},{2,18},{10... | collective-permute-start | bytes 540680 | tf_op jit(solution)/shard_map/ppermute | solution.py:745
  399.0 28.0 %collective-permute-start.57 = (bf16[2,32,2816]{2,1,0:T(8,128)(2,1)}, bf16[2,32,2816]{2,1,0:T(8,128)(2,1)}, u32[]{:S(2)}, u32[]{:S(2)}) collective-permute-start(bf16[2,32,2816]{2,1,0:T(8,128)(2,1)} %get-tuple-element.242), channel_id=1, source_target_pairs={{0,8},{8,16},{16,24},{24,0},{1,9},{9,17},{17,25},{25,1},{2,10},{10... | collective-permute-start | bytes 1081352 | tf_op jit(solution)/shard_map/ppermute | solution.py:745
  410.3 27.9 %collective-permute-start.58 = (bf16[2,32,2816]{2,1,0:T(8,128)(2,1)}, bf16[2,32,2816]{2,1,0:T(8,128)(2,1)S(1)}, u32[]{:S(2)}, u32[]{:S(2)}) collective-permute-start(bf16[2,32,2816]{2,1,0:T(8,128)(2,1)} %get-tuple-element.241), channel_id=1, source_target_pairs={{0,16},{8,24},{16,0},{24,8},{1,17},{9,25},{17,1},{25,9},{2,18},{10... | collective-permute-start | bytes 1081352 | tf_op jit(solution)/shard_map/ppermute | solution.py:745
  421.0 17.2 %collective-permute-start.59 = (bf16[2,32,2816]{2,1,0:T(8,128)(2,1)}, bf16[2,32,2816]{2,1,0:T(8,128)(2,1)S(1)}, u32[]{:S(2)}, u32[]{:S(2)}) collective-permute-start(bf16[2,32,2816]{2,1,0:T(8,128)(2,1)} %get-tuple-element.240), channel_id=1, source_target_pairs={{0,24},{8,0},{16,8},{24,16},{1,25},{9,1},{17,9},{25,17},{2,26},{10... | collective-permute-start | bytes 1081352 | tf_op jit(solution)/shard_map/ppermute | solution.py:745
  426.0 25.4 %collective-permute-start.55 = (bf16[3,128,1024]{2,1,0:T(8,128)(2,1)S(1)}, bf16[3,128,1024]{2,1,0:T(8,128)(2,1)S(1)}, u32[]{:S(2)}, u32[]{:S(2)}) collective-permute-start(bf16[3,128,1024]{2,1,0:T(8,128)(2,1)S(1)} %copy-done.150), channel_id=1, source_target_pairs={{0,2},{1,5},{2,0},{3,7},{4,6},{5,1},{6,4},{7,3},{8,10},{9,13},{10,... | collective-permute-start | bytes 2359304 | tf_op jit(solution)/shard_map/ppermute | solution.py:718
  427.0 24.4 %collective-permute-start.56 = (bf16[3,128,1024]{2,1,0:T(8,128)(2,1)S(1)}, bf16[3,128,1024]{2,1,0:T(8,128)(2,1)S(1)}, u32[]{:S(2)}, u32[]{:S(2)}) collective-permute-start(bf16[3,128,1024]{2,1,0:T(8,128)(2,1)S(1)} %copy-done.149), channel_id=1, source_target_pairs={{0,2},{1,5},{2,0},{3,7},{4,6},{5,1},{6,4},{7,3},{8,10},{9,13},{10,... | collective-permute-start | bytes 2359304 | tf_op jit(solution)/shard_map/ppermute | solution.py:718
  440.4 77.8 %collective-permute-start.74 = (bf16[2,32,2816]{2,1,0:T(8,128)(2,1)}, bf16[2,32,2816]{2,1,0:T(8,128)(2,1)}, u32[]{:S(2)}, u32[]{:S(2)}) collective-permute-start(bf16[2,32,2816]{2,1,0:T(8,128)(2,1)} %fusion.15), channel_id=1, source_target_pairs={{0,8},{8,16},{16,24},{24,0},{1,9},{9,17},{17,25},{25,1},{2,10},{10... | collective-permute-start | bytes 1081352 | tf_op jit(solution)/shard_map/ppermute | solution.py:745
  448.2 70.4 %collective-permute-start.75 = (bf16[2,32,2816]{2,1,0:T(8,128)(2,1)}, bf16[2,32,2816]{2,1,0:T(8,128)(2,1)}, u32[]{:S(2)}, u32[]{:S(2)}) collective-permute-start(bf16[2,32,2816]{2,1,0:T(8,128)(2,1)} %fusion.15), channel_id=1, source_target_pairs={{0,16},{8,24},{16,0},{24,8},{1,17},{9,25},{17,1},{25,9},{2,18},{10... | collective-permute-start | bytes 1081352 | tf_op jit(solution)/shard_map/ppermute | solution.py:745
  454.2 26.8 %collective-permute-start.60 = (bf16[3,128,1024]{2,1,0:T(8,128)(2,1)}, bf16[3,128,1024]{2,1,0:T(8,128)(2,1)}, u32[]{:S(2)}, u32[]{:S(2)}) collective-permute-start(bf16[3,128,1024]{2,1,0:T(8,128)(2,1)} %add_convert_fusion.3), channel_id=1, source_target_pairs={{0,4},{1,3},{2,6},{3,1},{4,0},{5,7},{6,2},{7,5},{8,12},{9,11},{10,... | collective-permute-start | bytes 2359304 | tf_op jit(solution)/shard_map/ppermute | solution.py:718
  458.7 25.2 %collective-permute-start.53 = (bf16[2,128,1024]{2,1,0:T(8,128)(2,1)}, bf16[2,128,1024]{2,1,0:T(8,128)(2,1)}, u32[]{:S(2)}, u32[]{:S(2)}) collective-permute-start(bf16[2,128,1024]{2,1,0:T(8,128)(2,1)} %get-tuple-element.187), channel_id=1, source_target_pairs={{0,2},{1,5},{2,0},{3,7},{4,6},{5,1},{6,4},{7,3},{8,10},{9,13},{10,... | collective-permute-start | bytes 1572872 | tf_op jit(solution)/shard_map/ppermute | solution.py:718
  459.2 24.7 %collective-permute-start.54 = (bf16[2,128,1024]{2,1,0:T(8,128)(2,1)}, bf16[2,128,1024]{2,1,0:T(8,128)(2,1)}, u32[]{:S(2)}, u32[]{:S(2)}) collective-permute-start(bf16[2,128,1024]{2,1,0:T(8,128)(2,1)} %get-tuple-element.231), channel_id=1, source_target_pairs={{0,2},{1,5},{2,0},{3,7},{4,6},{5,1},{6,4},{7,3},{8,10},{9,13},{10,... | collective-permute-start | bytes 1572872 | tf_op jit(solution)/shard_map/ppermute | solution.py:718
  483.9 24.3 %collective-permute-start.61 = (bf16[3,32,1024]{2,1,0:T(8,128)(2,1)}, bf16[3,32,1024]{2,1,0:T(8,128)(2,1)}, u32[]{:S(2)}, u32[]{:S(2)}) collective-permute-start(bf16[3,32,1024]{2,1,0:T(8,128)(2,1)} %get-tuple-element.256), channel_id=1, source_target_pairs={{0,8},{8,16},{16,24},{24,0},{1,9},{9,17},{17,25},{25,1},{2,10},{10... | collective-permute-start | bytes 589832 | tf_op jit(solution)/shard_map/ppermute | solution.py:745
  483.9 25.0 %collective-permute-start.62 = (bf16[3,32,1024]{2,1,0:T(8,128)(2,1)}, bf16[3,32,1024]{2,1,0:T(8,128)(2,1)}, u32[]{:S(2)}, u32[]{:S(2)}) collective-permute-start(bf16[3,32,1024]{2,1,0:T(8,128)(2,1)} %get-tuple-element.255), channel_id=1, source_target_pairs={{0,16},{8,24},{16,0},{24,8},{1,17},{9,25},{17,1},{25,9},{2,18},{10... | collective-permute-start | bytes 589832 | tf_op jit(solution)/shard_map/ppermute | solution.py:745
  486.5 16.4 %collective-permute-start.64 = (bf16[2,128,1024]{2,1,0:T(8,128)(2,1)}, bf16[2,128,1024]{2,1,0:T(8,128)(2,1)}, u32[]{:S(2)}, u32[]{:S(2)}) collective-permute-start(bf16[2,128,1024]{2,1,0:T(8,128)(2,1)} %add_convert_fusion.11), channel_id=1, source_target_pairs={{0,4},{1,3},{2,6},{3,1},{4,0},{5,7},{6,2},{7,5},{8,12},{9,11},{10,... | collective-permute-start | bytes 1572872 | tf_op jit(solution)/shard_map/ppermute | solution.py:718
  508.3 15.5 %collective-permute-start.76 = (bf16[2,32,2816]{2,1,0:T(8,128)(2,1)}, bf16[2,32,2816]{2,1,0:T(8,128)(2,1)S(1)}, u32[]{:S(2)}, u32[]{:S(2)}) collective-permute-start(bf16[2,32,2816]{2,1,0:T(8,128)(2,1)} %fusion.15), channel_id=1, source_target_pairs={{0,24},{8,0},{16,8},{24,16},{1,25},{9,1},{17,9},{25,17},{2,26},{10... | collective-permute-start | bytes 1081352 | tf_op jit(solution)/shard_map/ppermute | solution.py:745
  514.0 36.2 %collective-permute-start.65 = (bf16[3,32,1024]{2,1,0:T(8,128)(2,1)S(1)}, bf16[3,32,1024]{2,1,0:T(8,128)(2,1)S(1)}, u32[]{:S(2)}, u32[]{:S(2)}) collective-permute-start(bf16[3,32,1024]{2,1,0:T(8,128)(2,1)S(1)} %fusion.26), channel_id=1, source_target_pairs={{0,8},{8,16},{16,24},{24,0},{1,9},{9,17},{17,25},{25,1},{2,10},{10... | collective-permute-start | bytes 589832 | tf_op jit(solution)/shard_map/ppermute | solution.py:745
  516.2 34.0 %collective-permute-start.66 = (bf16[3,32,1024]{2,1,0:T(8,128)(2,1)S(1)}, bf16[3,32,1024]{2,1,0:T(8,128)(2,1)S(1)}, u32[]{:S(2)}, u32[]{:S(2)}) collective-permute-start(bf16[3,32,1024]{2,1,0:T(8,128)(2,1)S(1)} %fusion.26), channel_id=1, source_target_pairs={{0,16},{8,24},{16,0},{24,8},{1,17},{9,25},{17,1},{25,9},{2,18},{10... | collective-permute-start | bytes 589832 | tf_op jit(solution)/shard_map/ppermute | solution.py:745
  518.2 14.4 %collective-permute-start.68 = (bf16[2,32,1024]{2,1,0:T(8,128)(2,1)S(1)}, bf16[2,32,1024]{2,1,0:T(8,128)(2,1)S(1)}, u32[]{:S(2)}, u32[]{:S(2)}) collective-permute-start(bf16[2,32,1024]{2,1,0:T(8,128)(2,1)S(1)} %get-tuple-element.270), channel_id=1, source_target_pairs={{0,8},{8,16},{16,24},{24,0},{1,9},{9,17},{17,25},{25,1},{2,10},{10... | collective-permute-start | bytes 393224 | tf_op jit(solution)/shard_map/ppermute | solution.py:745
  518.6 22.6 %collective-permute-start.69 = (bf16[2,32,1024]{2,1,0:T(8,128)(2,1)S(1)}, bf16[2,32,1024]{2,1,0:T(8,128)(2,1)S(1)}, u32[]{:S(2)}, u32[]{:S(2)}) collective-permute-start(bf16[2,32,1024]{2,1,0:T(8,128)(2,1)S(1)} %get-tuple-element.269), channel_id=1, source_target_pairs={{0,16},{8,24},{16,0},{24,8},{1,17},{9,25},{17,1},{25,9},{2,18},{10... | collective-permute-start | bytes 393224 | tf_op jit(solution)/shard_map/ppermute | solution.py:745
  523.7 19.2 %collective-permute-start.70 = (bf16[2,32,1024]{2,1,0:T(8,128)(2,1)S(1)}, bf16[2,32,1024]{2,1,0:T(8,128)(2,1)S(1)}, u32[]{:S(2)}, u32[]{:S(2)}) collective-permute-start(bf16[2,32,1024]{2,1,0:T(8,128)(2,1)S(1)} %get-tuple-element.268), channel_id=1, source_target_pairs={{0,24},{8,0},{16,8},{24,16},{1,25},{9,1},{17,9},{25,17},{2,26},{10... | collective-permute-start | bytes 393224 | tf_op jit(solution)/shard_map/ppermute | solution.py:745
  532.6 17.6 %collective-permute-start.67 = (bf16[3,32,1024]{2,1,0:T(8,128)(2,1)S(1)}, bf16[3,32,1024]{2,1,0:T(8,128)(2,1)S(1)}, u32[]{:S(2)}, u32[]{:S(2)}) collective-permute-start(bf16[3,32,1024]{2,1,0:T(8,128)(2,1)S(1)} %fusion.26), channel_id=1, source_target_pairs={{0,24},{8,0},{16,8},{24,16},{1,25},{9,1},{17,9},{25,17},{2,26},{10... | collective-permute-start | bytes 589832 | tf_op jit(solution)/shard_map/ppermute | solution.py:745
  (177 other events, 3044.1 us)

commit v5 on v4

--- a/solution.py
+++ b/solution.py
@@ -13,7 +13,7 @@
 LOW = jnp.bfloat16
 WIDE = jnp.float32
 VMEM_BYTES = 60 * 1024 * 1024
-WEIGH = 50
+WEIGH = 4
 ANY = pl.BlockSpec(memory_space=pl.ANY)
 
 
@@ -67,16 +67,24 @@
 
 
 def piece_copies(order_ref, pieces, layers, columns, into_ref, sems):
+    parts = []
+    for piece in pieces:
+        stacked = len(piece.shape) == 4
+        parts += [piece.at[i] for i in range(piece.shape[0])] if stacked else [piece]
     copies = []
-    for index, piece in enumerate(pieces):
-        rows = piece.shape[1]
+    for index, part in enumerate(parts):
+        rows = part.shape[1]
         at = pl.ds(pl.multiple_of(order_ref[index] * rows, rows), rows)
         copies.append(
             pltpu.make_async_copy(
-                piece.at[layers, :, columns], into_ref.at[..., at, :], sems.at[index]
+                part.at[layers, :, columns], into_ref.at[..., at, :], sems.at[index]
             )
         )
     return copies
+
+
+def piece_count(pieces):
+    return sum(piece.shape[0] if piece.ndim == 4 else 1 for piece in pieces)
 
 
 def started(copies):
@@ -164,7 +172,7 @@
         [block] * 3,
         [
             pltpu.VMEM((steps, 2, features, width), LOW),
-            pltpu.SemaphoreType.DMA((steps, len(pieces))),
+            pltpu.SemaphoreType.DMA((steps, piece_count(pieces))),
         ],
         4 * count * features * features,
     )
@@ -230,7 +238,7 @@
     tile, features = q_ref.shape
     head_dim = features // heads
     step, steps = pl.program_id(0), tokens // tile
-    layer = pieces[0].shape[0] - 1
+    layer = pieces[0].shape[-3] - 1
     copies = piece_copies(order_ref, pieces, layer, pl.ds(0, features), w_ref, sems)
 
     @pl.when(step == 0)
@@ -262,14 +270,13 @@
 
 
 def pair_kernel(tile, count, order_ref, h_ref, *refs):
-    groups, refs = (refs[:count], refs[count : 2 * count]), refs[2 * count :]
-    first_ref, second_ref, turned_ref, w_ref, sems = refs
+    pieces, (first_ref, second_ref, turned_ref, w_ref, sems) = refs[:count], refs[count:]
     step, width = pl.program_id(0), first_ref.shape[1]
 
     def copies(at, layer):
         columns = pl.ds(pl.multiple_of(at * width, 128), width)
         return piece_copies(
-            order_ref, groups[layer], 0, columns, w_ref.at[at, layer], sems.at[at, layer]
+            order_ref, pieces, layer, columns, w_ref.at[at, layer], sems.at[at, layer]
         )
 
     @pl.when(step == 0)
@@ -289,17 +296,17 @@
         turned_ref[:, at] = (first_ref[at, :].astype(WIDE) * second).astype(LOW).T
 
 
-def pair(h, first_pieces, second_pieces, order, tile):
-    (count, features), hidden = h.shape, first_pieces[0].shape[-1]
+def pair(h, pieces, order, tile):
+    (count, features), hidden = h.shape, pieces[0].shape[-1]
     steps = 2 if hidden % 256 == 0 else 1
-    width, many = hidden // steps, len(first_pieces)
+    width, many = hidden // steps, len(pieces)
     block = pl.BlockSpec((count, width), lambda i, *_: (0, i))
     return call(
         functools.partial(pair_kernel, tile, many),
         [order],
         (steps,),
-        [h, *first_pieces, *second_pieces],
-        [pl.BlockSpec((count, features), lambda i, *_: (0, 0)), *[ANY] * (2 * many)],
+        [h, *pieces],
+        [pl.BlockSpec((count, features), lambda i, *_: (0, 0)), *[ANY] * many],
         [shaped(count, hidden), shaped(count, hidden), shaped(hidden, count)],
         [block, block, pl.BlockSpec((width, count), lambda i, *_: (i, 0))],
         [
@@ -370,12 +377,12 @@
 
 
 def pair_back_kernel(count, order_ref, dpair_ref, x1_ref, dy_ref, *refs):
-    groups, (e1_ref, w_ref, sems) = (refs[:count], refs[count : 2 * count]), refs[2 * count :]
+    pieces, (e1_ref, w_ref, sems) = refs[:count], refs[count:]
     step = pl.program_id(0)
 
     def copies(layer):
         return piece_copies(
-            order_ref, groups[layer], 0, pl.ds(0, w_ref.shape[2]), w_ref.at[layer], sems.at[layer]
+            order_ref, pieces, layer, pl.ds(0, w_ref.shape[2]), w_ref.at[layer], sems.at[layer]
         )
 
     @pl.when(step == 0)
@@ -395,19 +402,19 @@
     e1_ref[...] = e1.astype(LOW)
 
 
-def pair_back(dpair, x1, dy, first_pieces, second_pieces, order, tile):
-    (_, count, hidden), features, many = dpair.shape, x1.shape[1], len(first_pieces)
+def pair_back(dpair, x1, dy, pieces, order, tile):
+    (_, count, hidden), features, many = dpair.shape, x1.shape[1], len(pieces)
     narrow = rows_spec(tile, features)
     return call(
         functools.partial(pair_back_kernel, many),
         [order],
         (count // tile,),
-        [dpair, x1, dy, *first_pieces, *second_pieces],
+        [dpair, x1, dy, *pieces],
         [
             pl.BlockSpec((2, tile, hidden), lambda i, *_: (0, i, 0)),
             narrow,
             narrow,
-            *[ANY] * (2 * many),
+            *[ANY] * many,
         ],
         [shaped(count, features)],
         [narrow],
@@ -434,7 +441,7 @@
     pieces, (dmixed_ref, du_ref, grad_ref, w_ref, sems) = refs[:count], refs[count:]
     tokens, features = q_ref.shape
     head_dim = features // heads
-    layer = pieces[0].shape[0] - 1
+    layer = pieces[0].shape[-3] - 1
     copies = piece_copies(order_ref, pieces, layer, pl.ds(0, features), w_ref, sems)
 
     @pl.when(pl.program_id(0) == 0)
@@ -533,53 +540,95 @@
         dv_ref[:, span] = dv.astype(LOW)
 
 
-def mixer_back_kernel(counts, order_ref, dq_ref, dk_ref, dv_ref, du_ref, x_ref, e1_ref, *refs):
-    total = sum(counts)
-    pieces, (out_ref, w_ref, sems) = refs[:total], refs[total:]
-    groups = (pieces[: counts[0]], pieces[counts[0] :])
-    grads = ((dk_ref, 0, 0), (dv_ref, 0, 1), (dq_ref, 1, 0), (du_ref, 1, 1))
-    step, features = pl.program_id(0), x_ref.shape[1]
+def mixer_back_kernel(count, last, order_ref, *refs):
+    grads, refs = refs[:2], refs[2:]
+    if last:
+        (back_ref, x_ref, e1_ref), refs = refs[:3], refs[3:]
+    pieces, (out_ref, w_ref, sems) = refs[:count], refs[count:]
+    step, features = pl.program_id(0), out_ref.shape[1]
 
     def copies(index):
-        _, group, layer = grads[index]
         return piece_copies(
-            order_ref, groups[group], layer, pl.ds(0, features), w_ref.at[index], sems.at[index]
+            order_ref, pieces, index, pl.ds(0, features), w_ref.at[index], sems.at[index]
         )
 
     @pl.when(step == 0)
     def _():
-        for index in range(4):
-            started(copies(index))
-
-    total = None
-    for index in range(4):
-
-        @pl.when(step == 0)
-        def _(index=index):
-            finished(copies(index))
-
-        term = dot(grads[index][0][...], w_ref[index], 1, 1)
-        total = term if total is None else total + term
-    out_ref[...] = e1_ref[...].astype(WIDE) + norm_back(x_ref[...].astype(WIDE), total)
-
-
-def mixer_back(grads, x, e1, key_value, rest, order, tile):
-    count, features = x.shape
+        started(copies(0))
+        started(copies(1))
+        finished(copies(0))
+
+    total = dot(grads[0][...], w_ref[0], 1, 1)
+
+    @pl.when(step == 0)
+    def _():
+        finished(copies(1))
+
+    total = total + dot(grads[1][...], w_ref[1], 1, 1)
+    if last:
+        total = total + back_ref[...]
+        total = e1_ref[...].astype(WIDE) + norm_back(x_ref[...].astype(WIDE), total)
+    out_ref[...] = total
+
+
+def mixer_back(grads, pieces, order, tile, *others):
+    count, features = grads[0].shape
     spec = rows_spec(tile, features)
-    pieces = [*key_value, *rest]
     return call(
-        functools.partial(mixer_back_kernel, (len(key_value), len(rest))),
+        functools.partial(mixer_back_kernel, len(pieces), bool(others)),
         [order],
         (count // tile,),
-        [*grads, x, e1, *pieces],
-        [spec] * 6 + [ANY] * len(pieces),
+        [*grads, *others, *pieces],
+        [spec] * (2 + len(others)) + [ANY] * len(pieces),
         [shaped(count, features, kind=WIDE)],
         [spec],
         [
-            pltpu.VMEM((4, features, features), LOW),
-            pltpu.SemaphoreType.DMA((4, len(key_value))),
+            pltpu.VMEM((2, features, features), LOW),
+            pltpu.SemaphoreType.DMA((2, piece_count(pieces))),
         ],
-        8 * count * features * features,
+        4 * count * features * features,
+    )[0]
+
+
+def norm_kernel(x_ref, h_ref, turned_ref):
+    x = x_ref[...].astype(WIDE)
+    h = (x * norm_factor(x)).astype(LOW)
+    h_ref[...] = h
+    turned_ref[...] = h.T
+
+
+def normed(x, tile):
+    count, features = x.shape
+    spec = rows_spec(tile, features)
+    return call(
+        norm_kernel,
+        [],
+        (count // tile,),
+        [x],
+        [spec],
+        [shaped(count, features), shaped(features, count)],
+        [spec, pl.BlockSpec((features, tile), lambda i, *_: (0, i))],
+        [],
+        0,
+    )
+
+
+def cast_kernel(layers_ref, in_ref, out_ref):
+    out_ref[...] = in_ref[...].astype(LOW)
+
+
+def cast(array, layers):
+    block = (1, *array.shape[1:])
+    return call(
+        cast_kernel,
+        [jnp.asarray(layers, jnp.int32)],
+        (len(layers),),
+        [array],
+        [pl.BlockSpec(block, lambda i, layers: (layers[i], 0, 0))],
+        [shaped(len(layers), *array.shape[1:])],
+        [pl.BlockSpec(block, lambda i, *_: (i, 0, 0))],
+        [],
+        0,
     )[0]
 
 
@@ -731,35 +780,51 @@
 
 
 class SeqSum:
+    def __init__(self, *values):
+        self.totals, self.step = list(values), 0
+        self.send()
+
+    def send(self):
+        pairs = [[(0, 1), (3, 2)], [(1, 2), (2, 1)], [(1, 0), (2, 3)]][self.step]
+        self.received = [lax.ppermute(total, "seq", pairs) for total in self.totals]
+
+    def on(self, *others):
+        received = after(tuple(self.received), *others)
+        self.totals = [plus(a, b) for a, b in zip(self.totals, received)]
+        self.step += 1
+        self.send()
+        return tuple(self.totals)
+
+    def finish(self, *others):
+        place = lax.axis_index("seq")
+        outside = (place == 0) | (place == 3)
+        received = after(tuple(self.received), *others)
+        return [
+            jnp.where(outside, a, b).astype(WIDE) for a, b in zip(received, self.totals)
+        ]
+
+
+class SeqHalves:
     def __init__(self, value):
-        members, rows, columns = value.shape
-        self.count, self.place = lax.axis_size("seq"), lax.axis_index("seq")
+        self.odd = lax.axis_index("seq") % 2
         self.shape = value.shape
-        self.parts = value.reshape(members, self.count, rows // self.count, columns)
-        self.received = [
-            self.shifted(self.taken(step), step) for step in range(1, self.count)
-        ]
-
-    def shifted(self, part, step):
-        pairs = [(i, (i + step) % self.count) for i in range(self.count)]
-        return lax.ppermute(part, "seq", pairs)
-
-    def taken(self, step):
-        index = (self.place + step) % self.count
-        return lax.dynamic_index_in_dim(self.parts, index, 1, keepdims=False)
-
-    def share(self, *others):
-        total = plus(self.taken(0), *after(tuple(self.received), *others))
-        self.totals = [total] + [self.shifted(total, step) for step in range(1, self.count)]
-        return total
+        halves = value.reshape(value.shape[0], 2, value.shape[1] // 2, value.shape[2])
+        self.total = lax.dynamic_index_in_dim(halves, self.odd, 1, keepdims=False)
+        self.received = self.swapped(lax.dynamic_index_in_dim(halves, 1 - self.odd, 1, False), 1)
+
+    def swapped(self, value, step):
+        return lax.ppermute(value, "seq", [(i, i ^ step) for i in range(4)])
+
+    def on(self, step, *others):
+        self.total = plus(self.total, after(self.received, *others))
+        self.received = self.swapped(self.total, step)
+        return self.total
 
     def finish(self, *others):
-        totals = [total.astype(WIDE) for total in after(tuple(self.totals), *others)]
-        parts = [
-            lax.select_n((self.place - index) % self.count, *totals)
-            for index in range(self.count)
-        ]
-        return jnp.stack(parts, axis=1).reshape(self.shape)
+        received = after(self.received, *others)
+        pair = [self.total.astype(WIDE), received.astype(WIDE)]
+        halves = [lax.select_n(self.odd, *pair), lax.select_n(self.odd, *pair[::-1])]
+        return jnp.stack(halves, axis=1).reshape(self.shape)
 
 
 def plus(*terms):
@@ -777,18 +842,21 @@
         return [self.kept[index], self.received[:, index * width : (index + 1) * width]]
 
     def begin(self, *others):
-        across, first = after(plus(*self.block(3)), *others), plus(*self.block(1))
-        self.begun = across, first
-        self.from_across, self.from_first = moved(across, 0), moved(first, 0)
-        return self.begun
+        received = self.received
+        if received is not None:
+            self.received = after(received, *others)
+        message = jnp.stack([plus(*self.block(3)), plus(*self.block(1))])
+        self.from_side = moved(message, 0)
+        return message
 
     def forward(self, *others):
-        second = plus(*self.block(2), after(self.from_across, self.from_first, *others))
+        self.from_side = after(self.from_side, *others)
+        second = plus(*self.block(2), self.from_side[0])
         self.from_second = moved(second, 1)
         return second
 
     def finish(self, *others):
-        return plus(*self.block(0), self.from_first, after(self.from_second, *others))
+        return plus(*self.block(0), self.from_side[1], after(self.from_second, *others))
 
 
 def scattered_plainly(left, rights):
@@ -814,7 +882,7 @@
     docs = doc_lengths.shape[1]
     count = rows * tokens
     tile = min(256, tokens)
-    by_hand = lax.axis_size("dp") == 8
+    by_hand = lax.axis_size("dp") == 8 and lax.axis_size("seq") == 4
     order = block_order() if by_hand else jnp.zeros((1,), jnp.int32)
     rates = decay_rates[0]
     start = lax.axis_index("seq") * jnp.asarray(tokens, jnp.int32)
@@ -847,21 +915,21 @@
     def forward(pieces, *others):
         if not by_hand:
             return pieces
-        mine = [*pieces, moved(after(pieces[1], *others) if others else pieces[1], 1)]
-        return mine + [moved(part, "core") for part in mine]
-
-    def arrived(pieces):
-        return pieces[1:4]
-
+        mine = [*pieces, moved(pieces[1], 1)]
+        return mine + [moved(jnp.stack(after(tuple(mine), *others)), "core")]
+
+    def gathered(piece):
+        return [lax.all_gather(piece, "dp", axis=1, tiled=True)]
+
+    first_order = jnp.zeros((1,), jnp.int32)
     mixer = mixer_weights[0]
-    key_value = forward(gather(mixer[1:3].astype(LOW)))
-    rest = jnp.stack([mixer[0], mixer[3], mixer[4]]).astype(LOW)
-    rest = gather(rest, *arrived(key_value))
+    key_value = forward(gather(cast(mixer, (1, 2))))
+    channel = gathered(channel_in_weights[0].astype(LOW))
+    down = gathered(channel_out_weights.astype(LOW))
+    rest = gather(cast(mixer, (0, 3, 4)), *key_value[1:4])
 
     x = hidden_in.reshape(count, features)
-    wide_x = x.astype(WIDE)
-    h = (wide_x * norm_factor(wide_x)).astype(LOW)
-    h_turned = h.T
+    h, h_turned = normed(x, tile)
     dy = out_cotangent.reshape(count, features)
     narrow, turned_out = shaped(count, features), shaped(features, count)
     states = shaped(rows, heads, head_dim, head_dim)
@@ -871,11 +939,13 @@
     hops = hops_needed(tokens)
 
     k, k_slope, v = project(h, key_table, key_value, order, tokens, tile)
+    if by_hand:
+        rest[1] = after(rest[1], k)
     local_state = call(
         functools.partial(state_kernel, docs),
         scalars,
         (rows,),
-        [k, v],
+        [after(k, *rest[1:2]) if by_hand else k, v],
         [row_spec] * 2,
         [states],
         [state_spec],
@@ -883,16 +953,13 @@
         2 * count * features * head_dim,
     )[0]
     rest = forward(rest, local_state)
-    first_w = gather(channel_in_weights[0, :1].astype(LOW), *arrived(rest))
     state_in, message = hop(local_state, 1)
     q, q_slope, u = project(after(h, message), query_table, rest, order, tokens, tile)
-    first_w = forward(first_w, q)
-    second_w = gather(channel_in_weights[0, 1:].astype(LOW), *arrived(first_w))
     part = call(
         functools.partial(mixing_kernel, docs, tile, heads),
         scalars,
         (rows,),
-        [after(q, *first_w[1:3]), k, v],
+        [q, k, v],
         [row_spec] * 3,
         [narrow],
         [row_spec],
@@ -922,27 +989,24 @@
         [
             pltpu.VMEM((tile, features), WIDE),
             pltpu.VMEM((features, features), LOW),
-            pltpu.SemaphoreType.DMA((len(rest),)),
+            pltpu.SemaphoreType.DMA((piece_count(rest),)),
         ],
         2 * count * features * (features + head_dim),
     )
-    second_w = forward(second_w, part)
-    down = gather(channel_out_weights.astype(LOW), *arrived(second_w))
-    first, second, turned = pair(h2, first_w, second_w, order, tile)
-    down = forward(down, first)
+    first, second, turned = pair(h2, channel, first_order, tile)
 
     down_grads = channel_grads = outer_grads = inner_grads = None
     if by_hand:
-        sent, *kept = block_grads(turned, [(after(dy, *down[1:3]), None)], order, "both")
+        sent, *kept = block_grads(turned, [(dy, None)], order, "both")
         down_grads = Scatter(kept, moved(sent, "core"))
         first = after(first, sent)
-    dpair = down_back(first, second, dy, down, order, big)
+    dpair = down_back(first, second, dy, down, first_order, big)
     if by_hand:
         rights = [(dpair, 0), (dpair, 1)]
         begun = down_grads.begin(dpair)
-        [sent] = block_grads(after(h2_turned, *begun), rights, order, "send")
+        [sent] = block_grads(after(h2_turned, begun), rights, order, "send")
         received = moved(sent, "core")
-        e1 = pair_back(after(dpair, sent), x1, dy, first_w, second_w, order, big)
+        e1 = pair_back(after(dpair, sent), x1, dy, channel, first_order, big)
         begun = down_grads.forward(e1)
         channel_grads = Scatter(
             block_grads(after(h2_turned, begun), rights, order, "keep", received)
@@ -950,11 +1014,11 @@
         begun = channel_grads.begin()
         down_part = down_grads.finish(*channel_grads.kept)
         down_sum = SeqSum(down_part)
-        e1 = after(e1, down_part, *begun)
+        e1 = after(e1, down_part, begun)
     else:
-        y = down_forward(first, second, x1, down, order, big)
+        y = down_forward(first, second, x1, down, first_order, big)
         down_total = lax.psum(scattered_plainly(turned, [dy]), "seq")
-        e1 = pair_back(dpair, x1, dy, first_w, second_w, order, big)
+        e1 = pair_back(dpair, x1, dy, channel, first_order, big)
         channel_total = lax.psum(scattered_plainly(h2_turned, [dpair[0], dpair[1]]), "seq")
     dmixed, du, local_grad = call(
         functools.partial(back_gate_kernel, docs, heads, len(rest)),
@@ -964,12 +1028,12 @@
         [row_spec] * 4 + [ANY] * len(rest),
         [narrow, narrow, states],
         [row_spec, row_spec, state_spec],
-        [pltpu.VMEM((features, features), LOW), pltpu.SemaphoreType.DMA((len(rest),))],
+        [pltpu.VMEM((features, features), LOW), pltpu.SemaphoreType.DMA((piece_count(rest),))],
         2 * count * features * (features + head_dim),
     )
     pins = []
     if by_hand:
-        second_sent = channel_grads.forward(local_grad), down_sum.share(local_grad)
+        second_sent = down_sum.on(local_grad)
         sent_o, *kept_o = block_grads(
             after(gated_turned, *second_sent), [(e1, None)], order, "both"
         )
@@ -989,11 +1053,9 @@
     )
     pins = [dq]
     if by_hand:
-        channel_part = channel_grads.finish(dq)
-        channel_sum = SeqSum(channel_part)
-        down_total = down_sum.finish(dq)
+        channel_part = channel_grads.forward(dq), *down_sum.on(dq)
         sent_uq, *kept_uq = block_grads(
-            after(h_turned, channel_part), [(du, None), (dq, None)], order, "both"
+            after(h_turned, *channel_part), [(du, None), (dq, None)], order, "both"
         )
         received_uq = moved(sent_uq, "core")
         pins = [sent_uq]
@@ -1016,27 +1078,33 @@
             [jnp.concatenate([a, b]) for a, b in zip(kept_uq, kept_o)],
             jnp.concatenate([received_uq, received_o]),
         )
-        begun = outer_grads.begin(dk)
+        channel_part = channel_grads.finish(dk)
+        channel_sum = SeqSum(channel_part[:1], channel_part[1:])
+        begun = outer_grads.begin(dk), channel_part
         sent_kv, *kept_kv = block_grads(
             after(h_turned, *begun), [(dk, None), (dv, None)], order, "both"
         )
         inner_grads = Scatter(kept_kv, moved(sent_kv, "core"))
-        begun = outer_grads.forward(sent_kv), *inner_grads.begin(sent_kv)
-        begun = *begun, channel_sum.share(sent_kv)
-        dq = after(dq, *begun)
-    upstream = mixer_back([dq, dk, dv, du], x, e1, key_value, rest, order, big)
+        du = after(du, sent_kv)
+    back = mixer_back([dq, du], rest, order, big)
+    if by_hand:
+        begun = inner_grads.begin(back), outer_grads.forward(back), *channel_sum.on(back)
+        dk = after(dk, *begun)
+    upstream = mixer_back([dk, dv], key_value, order, big, back, x, e1)
     if by_hand:
         outer_part = outer_grads.finish(upstream)
-        outer_sum = SeqSum(outer_part)
-        begun = inner_grads.forward(upstream), outer_part
-        y = down_forward(after(first, *begun), second, x1, down, order, big)
+        outer_sum = SeqHalves(outer_part)
+        begun = inner_grads.forward(upstream), outer_part, *channel_sum.on(upstream)
+        y = down_forward(after(first, *begun), second, x1, down, first_order, big)
         inner_part = inner_grads.finish(y)
-        inner_sum = SeqSum(inner_part)
-        outer_total = outer_sum.share(inner_part)
-        channel_total = channel_sum.finish(outer_total)
-        inner_total = inner_sum.share(outer_total)
-        outer_total = outer_sum.finish(inner_total)
-        inner_total = inner_sum.finish(inner_total)
+        inner_sum = SeqHalves(inner_part)
+        down_total = down_sum.finish(y)[0]
+        outer_sum.on(2, inner_part)
+        inner_sum.on(2, inner_part)
+        outer_sum.on(1)
+        inner_sum.on(1)
+        channel_total = jnp.concatenate(channel_sum.finish(y))
+        outer_total, inner_total = outer_sum.finish(), inner_sum.finish()
         mixer_gradient = jnp.stack(
             [outer_total[1], inner_total[0], inner_total[1], outer_total[0], outer_total[2]]
         )

time: 569 us -> 556 us (0.977)
  starting transfers between devices: 114 us -> 77.6 us
  waiting for transfers between devices: 123 us -> 156 us
  local copies, waits for them, and re-layouts: 76.5 us -> 62.6 us
  between operations: 3 us -> 15.8 us
    ppermute x24 -> x15, waiting for transfers between devices: 40.7 us -> 65.2 us  [the longest x6 35.6 us: swapped(): return lax.ppermute(value, 'seq', [(i, i ^ step) for i in range(4)])]
    ppermute x52 -> x21, starting transfers between devices: 38.4 us -> 19 us  [moved(): return lax.ppermute(value, 'dp', pairs)]
    ppermute x24 -> x15, starting transfers between devices: 64.6 us -> 47.8 us  [the longest x6 26.5 us: swapped(): return lax.ppermute(value, 'seq', [(i, i ^ step) for i in range(4)])]
    ppermute x4, waiting for transfers between devices: 6.86 us -> 23.3 us  [passed_along(): lax.ppermute(value, 'seq', [(source, source + steps) for source in range(...]
    convert_element_type x15 -> x17, other arithmetic: 30.9 us -> 19.3 us  [plus(): return sum((term.astype(WIDE) for term in terms)).astype(LOW)]
    ppermute x52 -> x21, waiting for transfers between devices: 75.6 us -> 67.3 us  [moved(): return lax.ppermute(value, 'dp', pairs)]
    pallas_call x19 -> x23, Pallas kernels: 190 us -> 189 us  [call(): pl.pallas_call(kernel, out_shape=outputs, grid_spec=pltpu.PrefetchScalarG...]
    unnamed x328 -> x242, local copies, waits for them, and re-layouts: 60.1 us -> 61.5 us
  transfers between devices with their start and end apart: 80 -> 42, of which waited for: 23 -> 18; matrix products, arithmetic and copies ran while one was open for 10% -> 8% of each run, Pallas kernels for 33% -> 33%
where the time goes in v5:
time: 556 us; the launch traced here: 549 us
  Pallas kernels  189 us (34%)
  waiting for transfers between devices  156 us (28%)
  starting transfers between devices  77.6 us (14%)
  local copies, waits for them, and re-layouts  62.6 us (11%)
  other arithmetic  48.9 us (9%)
  between operations  15.8 us (3%)
    pallas_call x23, Pallas kernels, call(): pl.pallas_call(kernel, out_shape=outputs, grid_spec=pltpu.PrefetchScalarG...  189 us
    ppermute x21, waiting for transfers between devices, moved(): return lax.ppermute(value, 'dp', pairs)  67.3 us
    unnamed x242, local copies, waits for them, and re-layouts  61.5 us
    ppermute x6, waiting for transfers between devices, swapped(): return lax.ppermute(value, 'seq', [(i, i ^ step) for i in range(4)])  35.6 us
    ppermute x9, waiting for transfers between devices, send(): self.received = [lax.ppermute(total, 'seq', pairs) for total in self.totals]  29.6 us
    ppermute x6, starting transfers between devices, swapped(): return lax.ppermute(value, 'seq', [(i, i ^ step) for i in range(4)])  26.5 us
    ppermute x4, waiting for transfers between devices, passed_along(): lax.ppermute(value, 'seq', [(source, source + steps) for source in range(...  23.3 us
    ppermute x9, starting transfers between devices, send(): self.received = [lax.ppermute(total, 'seq', pairs) for total in self.totals]  21.3 us
  transfers between devices with their start and end apart: 42, of which 18 were waited for; matrix products, arithmetic and copies ran while one was open for 8% of the time, Pallas kernels for 33%

profile of v5, /device:TPU:0, one launch (start us, length us, event | category | flops | bytes accessed | tf_op | source)
XLA Modules:
  0.0 549.4 jit_solution(10773687415784345744)
XLA Ops:
  7.2 3.2 convert_element_type.367
  11.2 3.0 collective-permute-start
  15.7 14.9 %collective-permute-done.refs_1_.refs_6_ = bf16[2,128,1024]{2,1,0:T(8,128)(2,1)S(1)} collective-permute-done((bf16[2,128,1024]{2,1,0:T(8,128)(2,1)S(1)}, bf16[2,128,1024]{2,1,0:T(8,128)(2,1)S(1)}, u32[]{:S(2)}, u32[]{:S(2)}) %collective-permute-start) | collective-permute-done | bytes 524320 | tf_op jit(solution)/shard_map/ppermute | solution.py:767
  32.1 15.1 %collective-permute-done.2.refs_3_.refs_8_ = bf16[2,128,1024]{2,1,0:T(8,128)(2,1)S(1)} collective-permute-done((bf16[2,128,1024]{2,1,0:T(8,128)(2,1)S(1)}, bf16[2,128,1024]{2,1,0:T(8,128)(2,1)S(1)}, u32[]{:S(2)}, u32[]{:S(2)}) %collective-permute-start.2) | collective-permute-done | bytes 524320 | tf_op jit(solution)/shard_map/ppermute | solution.py:767
  56.8 1.9 fusion.3
  58.8 2.5 collective-permute-start.4
  61.5 8.2 %shard_map.139 = (bf16[1024,1024]{1,0:T(8,128)(2,1)S(1)}, bf16[1024,1024]{1,0:T(8,128)(2,1)S(1)}, bf16[1024,1024]{1,0:T(8,128)(2,1)S(1)}) custom-call(s32[8]{0:T(128)S(1)} %get-tuple-element.223.order_ref, bf16[1024,1024]{1,0:T(8,128)(2,1)S(1)} %copy-done.64, f32[512,1024]{1,0:T(8,128)S(1)} %get-tuple-element.221.table_ref, ...), custom_call_target="tpu_custom_call" | custom-call | flops 17179869184 | bytes 58720256 | tf_op jit(solution)/shard_map/pallas_call | solution.py:44
  72.4 24.1 %collective-permute-done.4.refs_1_.refs_3_ = bf16[3,128,1024]{2,1,0:T(8,128)(2,1)} collective-permute-done((bf16[3,128,1024]{2,1,0:T(8,128)(2,1)S(1)}, bf16[3,128,1024]{2,1,0:T(8,128)(2,1)}, u32[]{:S(2)}, u32[]{:S(2)}) %collective-permute-start.4) | collective-permute-done | bytes 786464 | tf_op jit(solution)/shard_map/ppermute | solution.py:767
  97.1 1.7 copy-done.2
  98.9 1.9 shard_map.141
  100.8 12.1 %collective-permute-done.7.refs_3_.refs_5_ = bf16[3,128,1024]{2,1,0:T(8,128)(2,1)} collective-permute-done((bf16[3,128,1024]{2,1,0:T(8,128)(2,1)}, bf16[3,128,1024]{2,1,0:T(8,128)(2,1)}, u32[]{:S(2)}, u32[]{:S(2)}) %collective-permute-start.7) | collective-permute-done | bytes 786464 | tf_op jit(solution)/shard_map/ppermute | solution.py:767
  112.9 3.1 pad_maximum_fusion
  116.3 3.4 collective-permute-start.5
  120.0 11.4 %collective-permute-done.5 = bf16[2,8,128,128]{3,2,1,0:T(8,128)(2,1)S(1)} collective-permute-done((bf16[2,8,128,128]{3,2,1,0:T(8,128)(2,1)S(1)}, bf16[2,8,128,128]{3,2,1,0:T(8,128)(2,1)S(1)}, u32[]{:S(2)}, u32[]{:S(2)}) %collective-permute-start.5) | collective-permute-done | bytes 524320 | tf_op jit(solution)/shard_map/ppermute | solution.py:750
  133.1 4.4 collective-permute-start.9
  137.6 2.3 convert_element_type.370
  140.1 8.7 %collective-permute-done.9 = bf16[2,8,128,128]{3,2,1,0:T(8,128)(2,1)S(1)} collective-permute-done((bf16[2,8,128,128]{3,2,1,0:T(8,128)(2,1)}, bf16[2,8,128,128]{3,2,1,0:T(8,128)(2,1)S(1)}, u32[]{:S(2)}, u32[]{:S(2)}) %collective-permute-start.9) | collective-permute-done | bytes 524320 | tf_op jit(solution)/shard_map/ppermute | solution.py:750
  152.0 8.7 %shard_map.142 = (bf16[1024,1024]{1,0:T(8,128)(2,1)S(1)}, bf16[1024,1024]{1,0:T(8,128)(2,1)S(1)}, bf16[1024,1024]{1,0:T(8,128)(2,1)S(1)}) custom-call(s32[8]{0:T(128)S(1)} %get-tuple-element.223.order_ref, bf16[1024,1024]{1,0:T(8,128)(2,1)S(1)} %copy-done.65, f32[512,1024]{1,0:T(8,128)S(1)} %copy-done.9, ...), custom_call_target="tpu_custom_call" | custom-call | flops 17179869184 | bytes 67108864 | tf_op jit(solution)/shard_map/pallas_call | solution.py:44
  160.8 5.7 %shard_map.143.part_ref = bf16[1024,1024]{1,0:T(8,128)(2,1)S(1)} custom-call(s32[1]{0:T(128)} %bitcast.start_ref, f32[8]{0:T(128)S(1)} %get-tuple-element.227.into_ref, f32[8]{0:T(128)S(1)} %get-tuple-element.226.out_ref, s32[2,4]{1,0:T(2,128)S(1)} %copy-done.54, bf16[1024,1024]{1,0:T(8,128)(2,1)S(1)} %get-tuple-element.117.q_ref, ...), custom_call_target="tpu_custom_call" | custom-call | flops 8589934592 | bytes 33554432 | tf_op jit(solution)/shard_map/pallas_call | solution.py:44
  168.1 8.5 %shard_map.144 = (bf16[1024,1024]{1,0:T(8,128)(2,1)S(1)}, bf16[1024,1024]{1,0:T(8,128)(2,1)S(1)}, bf16[1024,1024]{1,0:T(8,128)(2,1)S(1)}, bf16[1024,1024]{1,0:T(8,128)(2,1)S(1)}, bf16[1024,1024]{1,0:T(8,128)(2,1)S(1)}) custom-call(s32[1]{0:T(128)} %bitcast.start_ref, f32[8]{0:T(128)S(1)} %get-tuple-element.227.into_ref, f32[8]{0:T(128)S(1)} %get-tuple-element.226.out_ref, ...), custom_call_target="tpu_custom_call" | custom-call | flops 9663676416 | bytes 102760448 | tf_op jit(solution)/shard_map/pallas_call | solution.py:44
  185.6 18.6 %shard_map.145 = (bf16[1024,2816]{1,0:T(8,128)(2,1)S(1)}, bf16[1024,2816]{1,0:T(8,128)(2,1)S(1)}, bf16[2816,1024]{1,0:T(8,128)(2,1)}) custom-call(s32[1]{0:T(128)} %constant.59.clone.1.order_ref, bf16[1024,1024]{1,0:T(8,128)(2,1)S(1)} %copy-done.82, bf16[2,1024,2816]{2,1,0:T(8,128)(2,1)} %bitcast.129), custom_call_target="tpu_custom_call" | custom-call | flops 47244640256 | bytes 123731968 | tf_op jit(solution)/shard_map/pallas_call | solution.py:44
  204.2 6.6 %copy-done.93 = bf16[2816,1024]{1,0:T(8,128)(2,1)S(1)} copy-done((bf16[2816,1024]{1,0:T(8,128)(2,1)S(1)}, bf16[2816,1024]{1,0:T(8,128)(2,1)}, u32[]{:S(2)}) %copy-start.93) | copy-done | bytes 5767192
  210.8 12.3 %shard_map.146 = (bf16[1,1408,1024]{2,1,0:T(8,128)(2,1)}, bf16[1,352,1024]{2,1,0:T(8,128)(2,1)S(1)}, bf16[1,352,1024]{2,1,0:T(8,128)(2,1)S(1)}, bf16[1,352,1024]...) custom-call(s32[8]{0:T(128)S(1)} %pad_add_fusion.order_ref, bf16[2816,1024]{1,0:T(8,128)(2,1)S(1)} %copy-done.93, ...), custom_call_target="tpu_custom_call" | custom-call | flops 23622320128 | bytes 54525952 | tf_op jit(solution)/shard_map/pallas_call | solution.py:44
  228.3 2.6 copy-done.90
  231.0 2.6 copy-done.92
  233.6 12.3 %shard_map.147.refs_0_.refs_1_.dpair_ref = bf16[2,1024,2816]{2,1,0:T(8,128)(2,1)} custom-call(s32[1]{0:T(128)} %constant.59.clone.1.order_ref, bf16[1024,2816]{1,0:T(8,128)(2,1)S(1)} %copy-done.90, bf16[1024,2816]{1,0:T(8,128)(2,1)S(1)} %copy-done.92, bf16[1024,1024]{1,0:T(8,128)(2,1)S(1)} %bitcast.112, ...), custom_call_target="tpu_custom_call" | custom-call | flops 23622320128 | bytes 123731968 | tf_op jit(solution)/shard_map/pallas_call | solution.py:44
  245.9 2.0 fusion.23
  250.0 4.3 copy-done.87
  254.2 10.0 %shard_map.148 = bf16[2,512,2816]{2,1,0:T(8,128)(2,1)} custom-call(s32[4]{0:T(128)S(1)} %get-tuple-element.224.order_ref, bf16[1024,1024]{1,0:T(8,128)(2,1)S(1)} %copy-done.79, bf16[2,1024,2816]{2,1,0:T(8,128)(2,1)S(1)} %copy-done.87, bf16[2,1024,2816]{2,1,0:T(8,128)(2,1)S(1)} %copy-done.87), custom_call_target="tpu_custom_call" | custom-call | flops 23622320128 | bytes 123731968 | tf_op jit(solution)/shard_map/pallas_call | solution.py:44
  268.1 19.0 %shard_map.149.e1_ref.refs_0_.refs_4_ = bf16[1024,1024]{1,0:T(8,128)(2,1)S(1)} custom-call(s32[1]{0:T(128)} %constant.59.clone.1.order_ref, bf16[2,1024,2816]{2,1,0:T(8,128)(2,1)S(1)} %copy-done.88, bf16[1024,1024]{1,0:T(8,128)(2,1)S(1)} %copy-done.68, bf16[1024,1024]{1,0:T(8,128)(2,1)S(1)} %bitcast.113, bf16[2,1024,2816]{2,1,0:T(8,128)(2,1)} %bitcast.130), custom_call_target="tpu_custom_call" | custom-call | flops 47244640256 | bytes 117440512 | tf_op jit(solution)/shard_map/pallas_call | solution.py:44
  287.1 2.5 fusion.10
  290.2 9.8 %shard_map.150 = (bf16[2,128,2816]{2,1,0:T(8,128)(2,1)S(1)}, bf16[2,128,2816]{2,1,0:T(8,128)(2,1)S(1)}, bf16[2,128,2816]{2,1,0:T(8,128)(2,1)S(1)}, bf16[2,128,2816]{2,1,0:T(8,128)(2,1)S(1)}) custom-call(s32[4]{0:T(128)S(1)} %get-tuple-element.225.order_ref, bf16[1024,1024]{1,0:T(8,128)(2,1)S(1)} %copy-done.80, bf16[2,1024,2816]{2,1,0:T(8,128)(2,1)S(1)} %copy-done.88, ...), custom_call_target="tpu_custom_call" | custom-call | flops 23622320128 | bytes 146800640 | tf_op jit(solution)/shard_map/pallas_call | solution.py:44
  301.0 2.0 fusion.9
  303.1 4.4 collective-permute-start.16
  309.6 7.4 %shard_map.151 = (bf16[1024,1024]{1,0:T(8,128)(2,1)S(1)}, bf16[1024,1024]{1,0:T(8,128)(2,1)S(1)}, bf16[2,8,128,128]{3,2,1,0:T(8,128)(2,1)S(1)}) custom-call(s32[1]{0:T(128)} %bitcast.start_ref, f32[8]{0:T(128)S(1)} %get-tuple-element.227.into_ref, f32[8]{0:T(128)S(1)} %get-tuple-element.226.out_ref, s32[2,4]{1,0:T(2,128)S(1)} %copy-done.54, ...), custom_call_target="tpu_custom_call" | custom-call | flops 9663676416 | bytes 77594624 | tf_op jit(solution)/shard_map/pallas_call | solution.py:44
  318.7 3.2 collective-permute-done.16
  322.9 4.7 shard_map.152
  328.6 3.2 collective-permute-done.15
  334.1 14.8 %shard_map.153 = (bf16[1024,1024]{1,0:T(8,128)(2,1)S(1)}, bf16[1024,1024]{1,0:T(8,128)(2,1)S(1)}, bf16[1024,1024]{1,0:T(8,128)(2,1)S(1)}) custom-call(s32[1]{0:T(128)} %bitcast.start_ref, f32[8]{0:T(128)S(1)} %get-tuple-element.227.into_ref, f32[8]{0:T(128)S(1)} %get-tuple-element.226.out_ref, s32[2,4]{1,0:T(2,128)S(1)} %copy-done.54, ...), custom_call_target="tpu_custom_call" | custom-call | flops 25769803776 | bytes 69206016 | tf_op jit(solution)/shard_map/pallas_call | solution.py:44
  353.5 7.6 %shard_map.154 = (bf16[2,512,1024]{2,1,0:T(8,128)(2,1)}, bf16[2,128,1024]{2,1,0:T(8,128)(2,1)S(1)}, bf16[2,128,1024]{2,1,0:T(8,128)(2,1)S(1)}, bf16[2,128,1024]{...) custom-call(s32[8]{0:T(128)S(1)} %pad_add_fusion.order_ref, bf16[1024,1024]{1,0:T(8,128)(2,1)S(1)} %copy-done.61, ...), custom_call_target="tpu_custom_call" | custom-call | flops 17179869184 | bytes 41943040 | tf_op jit(solution)/shard_map/pallas_call | solution.py:44
  372.6 3.6 shard_map.155
  376.3 1.9 fusion.1
  378.3 7.7 %collective-permute-start.25 = (bf16[1,128,2816]{2,1,0:T(8,128)(2,1)S(1)}, bf16[1,128,2816]{2,1,0:T(8,128)(2,1)S(1)}, u32[]{:S(2)}, u32[]{:S(2)}) collective-permute-start(bf16[1,128,2816]{2,1,0:T(8,128)(2,1)S(1)} %get-tuple-element.213), channel_id=1, source_target_pairs={{0,8},{24,16},{1,9},{25,17},{2,10},{26,18},{3,11},{27,19},{4,12},{... | collective-permute-start | bytes 2162696 | tf_op jit(solution)/shard_map/ppermute | solution.py:789
  387.5 1.9 pad_maximum_fusion.1
  390.3 1.7 copy-done.62
  392.1 6.6 %shard_map.156 = (bf16[2,512,1024]{2,1,0:T(8,128)(2,1)S(1)}, bf16[2,128,1024]{2,1,0:T(8,128)(2,1)S(1)}, bf16[2,128,1024]{2,1,0:T(8,128)(2,1)S(1)}, bf16[2,128,10...) custom-call(s32[8]{0:T(128)S(1)} %pad_add_fusion.order_ref, bf16[1024,1024]{1,0:T(8,128)(2,1)S(1)} %copy-done.62, ...), custom_call_target="tpu_custom_call" | custom-call | flops 17179869184 | bytes 41943040 | tf_op jit(solution)/shard_map/pallas_call | solution.py:44
  399.3 7.7 %shard_map.157.refs_2_ = f32[1024,1024]{1,0:T(8,128)S(1)} custom-call(s32[8]{0:T(128)S(1)} %get-tuple-element.223.order_ref, bf16[1024,1024]{1,0:T(8,128)(2,1)S(1)} %copy-done.95, bf16[1024,1024]{1,0:T(8,128)(2,1)S(1)} %copy-done.86, bf16[3,128,1024]{2,1,0:T(8,128)(2,1)S(1)} %shard_map.140.refs_0_.refs_2_, ...), custom_call_target="tpu_custom_call" | custom-call | flops 17179869184 | bytes 58720256 | tf_op jit(solution)/shard_map/pallas_call | solution.py:44
  407.1 9.9 %collective-permute-done.26 = bf16[1,128,2816]{2,1,0:T(8,128)(2,1)S(1)} collective-permute-done((bf16[1,128,2816]{2,1,0:T(8,128)(2,1)S(1)}, bf16[1,128,2816]{2,1,0:T(8,128)(2,1)S(1)}, u32[]{:S(2)}, u32[]{:S(2)}) %collective-permute-start.26) | collective-permute-done | bytes 720928 | tf_op jit(solution)/shard_map/ppermute | solution.py:789
  426.1 10.7 %shard_map.158 = f32[1024,1024]{1,0:T(8,128)} custom-call(s32[8]{0:T(128)S(1)} %get-tuple-element.223.order_ref, bf16[1024,1024]{1,0:T(8,128)(2,1)S(1)} %get-tuple-element.184.refs_0_, bf16[1024,1024]{1,0:T(8,128)(2,1)S(1)} %get-tuple-element.172.refs_1_, f32[1024,1024]{1,0:T(8,128)S(1)} %shard_map.157.refs_2_, bf16[1024,1024]{1,0:T(8,128)(2,1)S(1)} %bitcast.102, ...), custom_call_target="tpu_custom_call" | custom-call | flops 17179869184 | bytes 83886080 | tf_op jit(solution)/shard_map/pallas_call | solution.py:44
  442.5 2.2 fusion.5
  444.7 19.8 %collective-permute-start.30 = (bf16[3,64,1024]{2,1,0:T(8,128)(2,1)S(1)}, bf16[3,64,1024]{2,1,0:T(8,128)(2,1)S(1)}, u32[]{:S(2)}, u32[]{:S(2)}) collective-permute-start(bf16[3,64,1024]{2,1,0:T(8,128)(2,1)S(1)} %dynamic-slice_bitcast_fusion), channel_id=1, source_target_pairs={{0,8},{8,0},{16,24},{24,16},{1,9},{9,1},{17,25},{25,17},{2,10},{10... | collective-permute-start | bytes 1179656 | tf_op jit(solution)/shard_map/ppermute | solution.py:816
  465.8 1.6 collective-permute-start.31
  467.5 7.8 %shard_map.159 = bf16[1024,1024]{1,0:T(8,128)(2,1)} custom-call(s32[1]{0:T(128)} %constant.59.clone.1.order_ref, bf16[1024,2816]{1,0:T(8,128)(2,1)S(1)} %bitcast.115, bf16[1024,2816]{1,0:T(8,128)(2,1)S(1)} %bitcast.117, bf16[1024,1024]{1,0:T(8,128)(2,1)S(1)} %copy-done.69, bf16[1,2816,1024]{2,1,0:T(8,128)(2,1)S(1)} %bitcast.110), custom_call_target="tpu_custom_call" | custom-call | flops 23622320128 | bytes 85983232 | tf_op jit(solution)/shard_map/pallas_call | solution.py:44
  476.3 15.4 %collective-permute-done.38 = bf16[1,128,2816]{2,1,0:T(8,128)(2,1)S(1)} collective-permute-done((bf16[1,128,2816]{2,1,0:T(8,128)(2,1)S(1)}, bf16[1,128,2816]{2,1,0:T(8,128)(2,1)S(1)}, u32[]{:S(2)}, u32[]{:S(2)}) %collective-permute-start.38) | collective-permute-done | bytes 720928 | tf_op jit(solution)/shard_map/ppermute | solution.py:789
  493.3 4.3 collective-permute-done.30
  498.3 2.5 collective-permute-start.34
  500.9 1.8 fusion.7
  502.6 7.3 %collective-permute-done.34 = bf16[2,64,1024]{2,1,0:T(8,128)(2,1)S(1)} collective-permute-done((bf16[2,64,1024]{2,1,0:T(8,128)(2,1)S(1)}, bf16[2,64,1024]{2,1,0:T(8,128)(2,1)S(1)}, u32[]{:S(2)}, u32[]{:S(2)}) %collective-permute-start.34) | collective-permute-done | bytes 262176 | tf_op jit(solution)/shard_map/ppermute | solution.py:816
  510.0 3.5 collective-permute-start.35
  513.5 7.4 %collective-permute-done.32 = bf16[3,64,1024]{2,1,0:T(8,128)(2,1)S(1)} collective-permute-done((bf16[3,64,1024]{2,1,0:T(8,128)(2,1)S(1)}, bf16[3,64,1024]{2,1,0:T(8,128)(2,1)S(1)}, u32[]{:S(2)}, u32[]{:S(2)}) %collective-permute-start.32) | collective-permute-done | bytes 393248 | tf_op jit(solution)/shard_map/ppermute | solution.py:816
  521.2 2.3 select_convert_fusion
  523.5 3.1 collective-permute-done.35
  526.7 8.3 %collective-permute-done.33 = bf16[3,64,1024]{2,1,0:T(8,128)(2,1)S(1)} collective-permute-done((bf16[3,64,1024]{2,1,0:T(8,128)(2,1)S(1)}, bf16[3,64,1024]{2,1,0:T(8,128)(2,1)S(1)}, u32[]{:S(2)}, u32[]{:S(2)}) %collective-permute-start.33) | collective-permute-done | bytes 393248 | tf_op jit(solution)/shard_map/ppermute | solution.py:816
  535.3 5.2 collective-permute-done.36
  (348 shorter events, 94.4 us)
Async XLA Ops:
  7.2 176.8 %all-gather.6.cloned.1.call-start = ((), (), s32[]{:S(2)}) async-start(), calls=%async_computation.1 | async-start | bytes 12976128 | tf_op jit(solution)/shard_map/all_gather | solution.py:922
  10.5 216.3 %all-gather.4.cloned.1.call-start = ((), (), s32[]{:S(2)}) async-start(), calls=%async_computation | async-start | bytes 6488064 | tf_op jit(solution)/shard_map/all_gather | solution.py:922
  11.2 37.6 %copy-start.16 = (bf16[2,128,1024]{2,1,0:T(8,128)(2,1)}, bf16[2,128,1024]{2,1,0:T(8,128)(2,1)S(1)}, u32[]{:S(2)}) copy-start(bf16[2,128,1024]{2,1,0:T(8,128)(2,1)S(1)} %shard_map.138.refs_0_.refs_5_) | copy-start | bytes 1572868
  11.2 19.4 %collective-permute-start = (bf16[2,128,1024]{2,1,0:T(8,128)(2,1)S(1)}, bf16[2,128,1024]{2,1,0:T(8,128)(2,1)S(1)}, u32[]{:S(2)}, u32[]{:S(2)}) collective-permute-start(bf16[2,128,1024]{2,1,0:T(8,128)(2,1)S(1)} %shard_map.138.refs_0_.refs_5_), channel_id=1, source_target_pairs={{0,2},{1,5},{2,0},{3,7},{4,6},{5,1},{6,4},{7,3},{8,10},{9,13},{10,... | collective-permute-start | bytes 1572872 | tf_op jit(solution)/shard_map/ppermute | solution.py:767
  14.2 17.9 %collective-permute-start.1 = (bf16[2,128,1024]{2,1,0:T(8,128)(2,1)S(1)}, bf16[2,128,1024]{2,1,0:T(8,128)(2,1)S(1)}, u32[]{:S(2)}, u32[]{:S(2)}) collective-permute-start(bf16[2,128,1024]{2,1,0:T(8,128)(2,1)S(1)} %shard_map.138.refs_0_.refs_5_), channel_id=1, source_target_pairs={{0,4},{1,3},{2,6},{3,1},{4,0},{5,7},{6,2},{7,5},{8,12},{9,11},{10,... | collective-permute-start | bytes 1572872 | tf_op jit(solution)/shard_map/ppermute | solution.py:767
  30.6 18.2 %copy-start.37 = (bf16[2,128,1024]{2,1,0:T(8,128)(2,1)}, bf16[2,128,1024]{2,1,0:T(8,128)(2,1)S(1)}, u32[]{:S(2)}) copy-start(bf16[2,128,1024]{2,1,0:T(8,128)(2,1)S(1)} %collective-permute-done.refs_1_.refs_6_) | copy-start | bytes 1572868
  30.6 16.6 %collective-permute-start.2 = (bf16[2,128,1024]{2,1,0:T(8,128)(2,1)S(1)}, bf16[2,128,1024]{2,1,0:T(8,128)(2,1)S(1)}, u32[]{:S(2)}, u32[]{:S(2)}) collective-permute-start(bf16[2,128,1024]{2,1,0:T(8,128)(2,1)S(1)} %collective-permute-done.refs_1_.refs_6_), channel_id=1, source_target_pairs={{0,4},{1,3},{2,6},{3,1},{4,0},{5,7},{6,2},{7,5},{8,12},{9,11},{10,... | collective-permute-start | bytes 1572872 | tf_op jit(solution)/shard_map/ppermute | solution.py:767
  32.1 16.7 %copy-start.40 = (bf16[2,128,1024]{2,1,0:T(8,128)(2,1)}, bf16[2,128,1024]{2,1,0:T(8,128)(2,1)S(1)}, u32[]{:S(2)}) copy-start(bf16[2,128,1024]{2,1,0:T(8,128)(2,1)S(1)} %collective-permute-done.1.refs_2_.refs_7_) | copy-start | bytes 1572868
  48.8 12.6 %collective-permute-start.3 = (bf16[4,2,128,1024]{3,2,1,0:T(8,128)(2,1)}, bf16[4,2,128,1024]{3,2,1,0:T(8,128)(2,1)}, u32[]{:S(2)}, u32[]{:S(2)}) collective-permute-start(bf16[4,2,128,1024]{3,2,1,0:T(8,128)(2,1)} %pad_maximum_fusion.3), channel_id=1, source_target_pairs={{0,1},{1,0},{2,3},{3,2},{4,5},{5,4},{6,7},{7,6},{8,9},{9,8},{10,11... | collective-permute-start | bytes 6291464 | tf_op jit(solution)/shard_map/ppermute | solution.py:767
  58.8 37.8 %collective-permute-start.4 = (bf16[3,128,1024]{2,1,0:T(8,128)(2,1)S(1)}, bf16[3,128,1024]{2,1,0:T(8,128)(2,1)}, u32[]{:S(2)}, u32[]{:S(2)}) collective-permute-start(bf16[3,128,1024]{2,1,0:T(8,128)(2,1)S(1)} %shard_map.140.refs_0_.refs_2_), channel_id=1, source_target_pairs={{0,2},{1,5},{2,0},{3,7},{4,6},{5,1},{6,4},{7,3},{8,10},{9,13},{10,... | collective-permute-start | bytes 2359304 | tf_op jit(solution)/shard_map/ppermute | solution.py:767
  61.3 39.5 %collective-permute-start.6 = (bf16[3,128,1024]{2,1,0:T(8,128)(2,1)S(1)}, bf16[3,128,1024]{2,1,0:T(8,128)(2,1)}, u32[]{:S(2)}, u32[]{:S(2)}) collective-permute-start(bf16[3,128,1024]{2,1,0:T(8,128)(2,1)S(1)} %shard_map.140.refs_0_.refs_2_), channel_id=1, source_target_pairs={{0,4},{1,3},{2,6},{3,1},{4,0},{5,7},{6,2},{7,5},{8,12},{9,11},{10,... | collective-permute-start | bytes 2359304 | tf_op jit(solution)/shard_map/ppermute | solution.py:767
  61.4 35.7 %copy-start.54 = (s32[2,4]{1,0:T(2,128)S(1)}, s32[2,4]{1,0:T(2,128)}, u32[]{:S(2)}) copy-start(s32[2,4]{1,0:T(2,128)} %lengths_ref.11) | copy-start | bytes 100
  96.6 16.3 %collective-permute-start.7 = (bf16[3,128,1024]{2,1,0:T(8,128)(2,1)}, bf16[3,128,1024]{2,1,0:T(8,128)(2,1)}, u32[]{:S(2)}, u32[]{:S(2)}) collective-permute-start(bf16[3,128,1024]{2,1,0:T(8,128)(2,1)} %collective-permute-done.4.refs_1_.refs_3_), channel_id=1, source_target_pairs={{0,4},{1,3},{2,6},{3,1},{4,0},{5,7},{6,2},{7,5},{8,12},{9,11},{10,... | collective-permute-start | bytes 2359304 | tf_op jit(solution)/shard_map/ppermute | solution.py:767
  116.0 32.9 %collective-permute-start.8 = (bf16[4,3,128,1024]{3,2,1,0:T(8,128)(2,1)}, bf16[4,3,128,1024]{3,2,1,0:T(8,128)(2,1)}, u32[]{:S(2)}, u32[]{:S(2)}) collective-permute-start(bf16[4,3,128,1024]{3,2,1,0:T(8,128)(2,1)} %pad_maximum_fusion), channel_id=1, source_target_pairs={{0,1},{1,0},{2,3},{3,2},{4,5},{5,4},{6,7},{7,6},{8,9},{9,8},{10,11... | collective-permute-start | bytes 9437192 | tf_op jit(solution)/shard_map/ppermute | solution.py:767
  116.3 15.1 %collective-permute-start.5 = (bf16[2,8,128,128]{3,2,1,0:T(8,128)(2,1)S(1)}, bf16[2,8,128,128]{3,2,1,0:T(8,128)(2,1)S(1)}, u32[]{:S(2)}, u32[]{:S(2)}) collective-permute-start(bf16[2,8,128,128]{3,2,1,0:T(8,128)(2,1)S(1)} %shard_map.141), channel_id=1, source_target_pairs={{0,8},{8,16},{16,24},{1,9},{9,17},{17,25},{2,10},{10,18},{18,26},{... | collective-permute-start | bytes 1572872 | tf_op jit(solution)/shard_map/ppermute | solution.py:750
  133.1 15.6 %collective-permute-start.9 = (bf16[2,8,128,128]{3,2,1,0:T(8,128)(2,1)}, bf16[2,8,128,128]{3,2,1,0:T(8,128)(2,1)S(1)}, u32[]{:S(2)}, u32[]{:S(2)}) collective-permute-start(bf16[2,8,128,128]{3,2,1,0:T(8,128)(2,1)} %fusion.11), channel_id=1, source_target_pairs={{0,8},{8,16},{16,24},{1,9},{9,17},{17,25},{2,10},{10,18},{18,26},{... | collective-permute-start | bytes 1572872 | tf_op jit(solution)/shard_map/ppermute | solution.py:750
  185.6 18.6 %copy-start.57 = (bf16[2,512,1024]{2,1,0:T(8,128)(2,1)S(1)}, bf16[2,512,1024]{2,1,0:T(8,128)(2,1)}, u32[]{:S(2)}) copy-start(bf16[2,512,1024]{2,1,0:T(8,128)(2,1)} %param.16) | copy-start | bytes 6291460
  204.2 19.0 %copy-start.89 = (bf16[1024,2816]{1,0:T(8,128)(2,1)}, bf16[1024,2816]{1,0:T(8,128)(2,1)S(1)}, u32[]{:S(2)}) copy-start(bf16[1024,2816]{1,0:T(8,128)(2,1)S(1)} %get-tuple-element.191.first_ref) | copy-start | bytes 17301508
  204.2 19.0 %copy-start.91 = (bf16[1024,2816]{1,0:T(8,128)(2,1)}, bf16[1024,2816]{1,0:T(8,128)(2,1)S(1)}, u32[]{:S(2)}) copy-start(bf16[1024,2816]{1,0:T(8,128)(2,1)S(1)} %get-tuple-element.128.second_ref) | copy-start | bytes 17301508
  226.7 19.1 %collective-permute-start.10 = (bf16[1,1408,1024]{2,1,0:T(8,128)(2,1)}, bf16[1,1408,1024]{2,1,0:T(8,128)(2,1)}, u32[]{:S(2)}, u32[]{:S(2)}) collective-permute-start(bf16[1,1408,1024]{2,1,0:T(8,128)(2,1)} %get-tuple-element.123), channel_id=1, source_target_pairs={{0,1},{1,0},{2,3},{3,2},{4,5},{5,4},{6,7},{7,6},{8,9},{9,8},{10,11... | collective-permute-start | bytes 8650760 | tf_op jit(solution)/shard_map/ppermute | solution.py:767
  264.3 25.9 %collective-permute-start.12 = (bf16[2,512,2816]{2,1,0:T(8,128)(2,1)}, bf16[2,512,2816]{2,1,0:T(8,128)(2,1)S(1)}, u32[]{:S(2)}, u32[]{:S(2)}) collective-permute-start(bf16[2,512,2816]{2,1,0:T(8,128)(2,1)} %shard_map.148), channel_id=1, source_target_pairs={{0,1},{1,0},{2,3},{3,2},{4,5},{5,4},{6,7},{7,6},{8,9},{9,8},{10,11... | collective-permute-start | bytes 17301512 | tf_op jit(solution)/shard_map/ppermute | solution.py:767
  264.9 22.3 %collective-permute-start.11 = (bf16[2,1,352,1024]{3,2,1,0:T(8,128)(2,1)}, bf16[2,1,352,1024]{3,2,1,0:T(8,128)(2,1)}, u32[]{:S(2)}, u32[]{:S(2)}) collective-permute-start(bf16[2,1,352,1024]{3,2,1,0:T(8,128)(2,1)} %pad_maximum_fusion.5), channel_id=1, source_target_pairs={{0,2},{1,5},{2,0},{3,7},{4,6},{5,1},{6,4},{7,3},{8,10},{9,13},{10,... | collective-permute-start | bytes 4325384 | tf_op jit(solution)/shard_map/ppermute | solution.py:767
  268.1 19.1 %copy-start.24 = (bf16[1,352,1024]{2,1,0:T(8,128)(2,1)S(1)}, bf16[1,352,1024]{2,1,0:T(8,128)(2,1)}, u32[]{:S(2)}) copy-start(bf16[1,352,1024]{2,1,0:T(8,128)(2,1)} %copy-done.23) | copy-start | bytes 2162692
  287.1 35.8 %copy-start.83 = (bf16[1024,1024]{1,0:T(8,128)(2,1)}, bf16[1024,1024]{1,0:T(8,128)(2,1)S(1)}, u32[]{:S(2)}) copy-start(bf16[1024,1024]{1,0:T(8,128)(2,1)S(1)} %shard_map.149.e1_ref.refs_0_.refs_4_) | copy-start | bytes 6291460
  289.7 11.4 %collective-permute-start.14 = (bf16[1,352,1024]{2,1,0:T(8,128)(2,1)S(1)}, bf16[1,352,1024]{2,1,0:T(8,128)(2,1)S(1)}, u32[]{:S(2)}, u32[]{:S(2)}) collective-permute-start(bf16[1,352,1024]{2,1,0:T(8,128)(2,1)S(1)} %fusion.10), channel_id=1, source_target_pairs={{0,4},{1,3},{2,6},{3,1},{4,0},{5,7},{6,2},{7,5},{8,12},{9,11},{10,... | collective-permute-start | bytes 2162696 | tf_op jit(solution)/shard_map/ppermute | solution.py:767
  303.1 18.8 %collective-permute-start.16 = (bf16[1,352,1024]{2,1,0:T(8,128)(2,1)S(1)}, bf16[1,352,1024]{2,1,0:T(8,128)(2,1)S(1)}, u32[]{:S(2)}, u32[]{:S(2)}) collective-permute-start(bf16[1,352,1024]{2,1,0:T(8,128)(2,1)S(1)} %fusion.9), channel_id=1, source_target_pairs={{0,8},{24,16},{1,9},{25,17},{2,10},{26,18},{3,11},{27,19},{4,12},{... | collective-permute-start | bytes 2162696 | tf_op jit(solution)/shard_map/ppermute | solution.py:789
  307.7 42.7 %collective-permute-start.13 = (bf16[2,2,128,2816]{3,2,1,0:T(8,128)(2,1)S(1)}, bf16[2,2,128,2816]{3,2,1,0:T(8,128)(2,1)S(1)}, u32[]{:S(2)}, u32[]{:S(2)}) collective-permute-start(bf16[2,2,128,2816]{3,2,1,0:T(8,128)(2,1)S(1)} %pad_maximum_fusion.2), channel_id=1, source_target_pairs={{0,2},{1,5},{2,0},{3,7},{4,6},{5,1},{6,4},{7,3},{8,10},{9,13},{10,... | collective-permute-start | bytes 8650760 | tf_op jit(solution)/shard_map/ppermute | solution.py:767
  317.1 36.3 %copy-start.85 = (bf16[1024,1024]{1,0:T(8,128)(2,1)}, bf16[1024,1024]{1,0:T(8,128)(2,1)S(1)}, u32[]{:S(2)}) copy-start(bf16[1024,1024]{1,0:T(8,128)(2,1)S(1)} %get-tuple-element.175.refs_0_.refs_1_) | copy-start | bytes 6291460
  317.1 14.7 %collective-permute-start.15 = (bf16[2,8,128,128]{3,2,1,0:T(8,128)(2,1)S(1)}, bf16[2,8,128,128]{3,2,1,0:T(8,128)(2,1)S(1)}, u32[]{:S(2)}, u32[]{:S(2)}) collective-permute-start(bf16[2,8,128,128]{3,2,1,0:T(8,128)(2,1)S(1)} %get-tuple-element.147), channel_id=1, source_target_pairs={{8,0},{16,8},{24,16},{9,1},{17,9},{25,17},{10,2},{18,10},{26,18},{... | collective-permute-start | bytes 1572872 | tf_op jit(solution)/shard_map/ppermute | solution.py:750
  322.2 26.8 %collective-permute-start.17 = (bf16[1,352,1024]{2,1,0:T(8,128)(2,1)S(1)}, bf16[1,352,1024]{2,1,0:T(8,128)(2,1)S(1)}, u32[]{:S(2)}, u32[]{:S(2)}) collective-permute-start(bf16[1,352,1024]{2,1,0:T(8,128)(2,1)S(1)} %add_convert_fusion.7), channel_id=1, source_target_pairs={{8,16},{16,8},{9,17},{17,9},{10,18},{18,10},{11,19},{19,11},{12,20... | collective-permute-start | bytes 2162696 | tf_op jit(solution)/shard_map/ppermute | solution.py:789
  328.6 20.3 %copy-start.50 = (bf16[1,128,1024]{2,1,0:T(8,128)(2,1)}, bf16[1,128,1024]{2,1,0:T(8,128)(2,1)S(1)}, u32[]{:S(2)}) copy-start(bf16[1,128,1024]{2,1,0:T(8,128)(2,1)S(1)} %get-tuple-element.160) | copy-start | bytes 786436
  332.8 31.3 %collective-permute-start.20 = (bf16[2,8,128,128]{3,2,1,0:T(8,128)(2,1)}, bf16[2,8,128,128]{3,2,1,0:T(8,128)(2,1)}, u32[]{:S(2)}, u32[]{:S(2)}) collective-permute-start(bf16[2,8,128,128]{3,2,1,0:T(8,128)(2,1)} %fusion.13), channel_id=1, source_target_pairs={{8,0},{16,8},{24,16},{9,1},{17,9},{25,17},{10,2},{18,10},{26,18},{... | collective-permute-start | bytes 1572872 | tf_op jit(solution)/shard_map/ppermute | solution.py:750
  351.9 24.4 %collective-permute-start.21 = (bf16[2,128,2816]{2,1,0:T(8,128)(2,1)}, bf16[2,128,2816]{2,1,0:T(8,128)(2,1)}, u32[]{:S(2)}, u32[]{:S(2)}) collective-permute-start(bf16[2,128,2816]{2,1,0:T(8,128)(2,1)} %fusion.2), channel_id=1, source_target_pairs={{0,4},{1,3},{2,6},{3,1},{4,0},{5,7},{6,2},{7,5},{8,12},{9,11},{10,... | collective-permute-start | bytes 4325384 | tf_op jit(solution)/shard_map/ppermute | solution.py:767
  363.5 24.0 %collective-permute-start.18 = (bf16[2,512,1024]{2,1,0:T(8,128)(2,1)}, bf16[2,512,1024]{2,1,0:T(8,128)(2,1)}, u32[]{:S(2)}, u32[]{:S(2)}) collective-permute-start(bf16[2,512,1024]{2,1,0:T(8,128)(2,1)} %get-tuple-element.161), channel_id=1, source_target_pairs={{0,1},{1,0},{2,3},{3,2},{4,5},{5,4},{6,7},{7,6},{8,9},{9,8},{10,11... | collective-permute-start | bytes 6291464 | tf_op jit(solution)/shard_map/ppermute | solution.py:767
  363.5 24.0 %collective-permute-start.19 = (bf16[1,512,1024]{2,1,0:T(8,128)(2,1)}, bf16[1,512,1024]{2,1,0:T(8,128)(2,1)S(1)}, u32[]{:S(2)}, u32[]{:S(2)}) collective-permute-start(bf16[1,512,1024]{2,1,0:T(8,128)(2,1)} %copy-done.66), channel_id=1, source_target_pairs={{0,1},{1,0},{2,3},{3,2},{4,5},{5,4},{6,7},{7,6},{8,9},{9,8},{10,11... | collective-permute-start | bytes 3145736 | tf_op jit(solution)/shard_map/ppermute | solution.py:767
  365.3 137.3 %collective-permute-start.39 = (bf16[1,352,1024]{2,1,0:T(8,128)(2,1)}, bf16[1,352,1024]{2,1,0:T(8,128)(2,1)}, u32[]{:S(2)}, u32[]{:S(2)}) collective-permute-start(bf16[1,352,1024]{2,1,0:T(8,128)(2,1)} %add_convert_fusion.6), channel_id=1, source_target_pairs={{8,0},{16,24},{9,1},{17,25},{10,2},{18,26},{11,3},{19,27},{12,4},{... | collective-permute-start | bytes 2162696 | tf_op jit(solution)/shard_map/ppermute | solution.py:789
  378.3 28.7 %collective-permute-start.25 = (bf16[1,128,2816]{2,1,0:T(8,128)(2,1)S(1)}, bf16[1,128,2816]{2,1,0:T(8,128)(2,1)S(1)}, u32[]{:S(2)}, u32[]{:S(2)}) collective-permute-start(bf16[1,128,2816]{2,1,0:T(8,128)(2,1)S(1)} %get-tuple-element.213), channel_id=1, source_target_pairs={{0,8},{24,16},{1,9},{25,17},{2,10},{26,18},{3,11},{27,19},{4,12},{... | collective-permute-start | bytes 2162696 | tf_op jit(solution)/shard_map/ppermute | solution.py:789
  386.0 30.9 %collective-permute-start.26 = (bf16[1,128,2816]{2,1,0:T(8,128)(2,1)S(1)}, bf16[1,128,2816]{2,1,0:T(8,128)(2,1)S(1)}, u32[]{:S(2)}, u32[]{:S(2)}) collective-permute-start(bf16[1,128,2816]{2,1,0:T(8,128)(2,1)S(1)} %get-tuple-element.212), channel_id=1, source_target_pairs={{0,8},{24,16},{1,9},{25,17},{2,10},{26,18},{3,11},{27,19},{4,12},{... | collective-permute-start | bytes 2162696 | tf_op jit(solution)/shard_map/ppermute | solution.py:789
  389.4 31.0 %copy-start.98 = (bf16[3,512,1024]{2,1,0:T(8,128)(2,1)}, bf16[3,512,1024]{2,1,0:T(8,128)(2,1)S(1)}, u32[]{:S(2)}) copy-start(bf16[3,512,1024]{2,1,0:T(8,128)(2,1)S(1)} %pad_maximum_fusion.1) | copy-start | bytes 9437188
  398.7 24.1 %collective-permute-start.22 = (bf16[2,512,1024]{2,1,0:T(8,128)(2,1)S(1)}, bf16[2,512,1024]{2,1,0:T(8,128)(2,1)S(1)}, u32[]{:S(2)}, u32[]{:S(2)}) collective-permute-start(bf16[2,512,1024]{2,1,0:T(8,128)(2,1)S(1)} %get-tuple-element.174), channel_id=1, source_target_pairs={{0,1},{1,0},{2,3},{3,2},{4,5},{5,4},{6,7},{7,6},{8,9},{9,8},{10,11... | collective-permute-start | bytes 6291464 | tf_op jit(solution)/shard_map/ppermute | solution.py:767
  398.8 21.6 %collective-permute-start.24 = (bf16[2,3,128,1024]{3,2,1,0:T(8,128)(2,1)S(1)}, bf16[2,3,128,1024]{3,2,1,0:T(8,128)(2,1)S(1)}, u32[]{:S(2)}, u32[]{:S(2)}) collective-permute-start(bf16[2,3,128,1024]{3,2,1,0:T(8,128)(2,1)S(1)} %pad_maximum_fusion.4), channel_id=1, source_target_pairs={{0,2},{1,5},{2,0},{3,7},{4,6},{5,1},{6,4},{7,3},{8,10},{9,13},{10,... | collective-permute-start | bytes 4718600 | tf_op jit(solution)/shard_map/ppermute | solution.py:767
  407.0 13.4 %copy-start.34 = (bf16[2,128,1024]{2,1,0:T(8,128)(2,1)S(1)}, bf16[2,128,1024]{2,1,0:T(8,128)(2,1)}, u32[]{:S(2)}) copy-start(bf16[2,128,1024]{2,1,0:T(8,128)(2,1)} %copy-done.33) | copy-start | bytes 1572868
  417.3 19.6 %collective-permute-start.28 = (bf16[1,128,2816]{2,1,0:T(8,128)(2,1)S(1)}, bf16[1,128,2816]{2,1,0:T(8,128)(2,1)}, u32[]{:S(2)}, u32[]{:S(2)}) collective-permute-start(bf16[1,128,2816]{2,1,0:T(8,128)(2,1)S(1)} %get-tuple-element.211), channel_id=1, source_target_pairs={{8,16},{16,8},{9,17},{17,9},{10,18},{18,10},{11,19},{19,11},{12,20... | collective-permute-start | bytes 2162696 | tf_op jit(solution)/shard_map/ppermute | solution.py:789
  418.9 18.0 %collective-permute-start.29 = (bf16[1,128,2816]{2,1,0:T(8,128)(2,1)S(1)}, bf16[1,128,2816]{2,1,0:T(8,128)(2,1)}, u32[]{:S(2)}, u32[]{:S(2)}) collective-permute-start(bf16[1,128,2816]{2,1,0:T(8,128)(2,1)S(1)} %get-tuple-element.210), channel_id=1, source_target_pairs={{8,16},{16,8},{9,17},{17,9},{10,18},{18,10},{11,19},{19,11},{12,20... | collective-permute-start | bytes 2162696 | tf_op jit(solution)/shard_map/ppermute | solution.py:789
  421.8 20.6 %collective-permute-start.27 = (bf16[3,128,1024]{2,1,0:T(8,128)(2,1)}, bf16[3,128,1024]{2,1,0:T(8,128)(2,1)}, u32[]{:S(2)}, u32[]{:S(2)}) collective-permute-start(bf16[3,128,1024]{2,1,0:T(8,128)(2,1)} %fusion.6), channel_id=1, source_target_pairs={{0,4},{1,3},{2,6},{3,1},{4,0},{5,7},{6,2},{7,5},{8,12},{9,11},{10,... | collective-permute-start | bytes 2359304 | tf_op jit(solution)/shard_map/ppermute | solution.py:767
  422.9 44.6 %slice-start = ((s8[5767168]{0:T(1024)(128)(4,1)}), s8[4194304]{0:T(1024)(128)(4,1)S(1)}, s32[]{:S(2)}) async-start(s8[5767168]{0:T(1024)(128)(4,1)} %bitcast.109), calls=%async_computation.2 | async-start | bytes 8388608
  422.9 44.6 %slice-start.2 = ((s8[5767168]{0:T(1024)(128)(4,1)}), s8[4194304]{0:T(1024)(128)(4,1)S(1)}, s32[]{:S(2)}) async-start(s8[5767168]{0:T(1024)(128)(4,1)} %bitcast.114), calls=%async_computation.4 | async-start | bytes 8388608
  422.9 44.5 %slice-start.4 = ((s8[5767168]{0:T(1024)(128)(4,1)}), s8[4194304]{0:T(1024)(128)(4,1)S(1)}, s32[]{:S(2)}) async-start(s8[5767168]{0:T(1024)(128)(4,1)} %bitcast.116), calls=%async_computation.6 | async-start | bytes 8388608
  424.5 42.9 %slice-start.1 = ((s8[5767168]{0:T(1024)(128)(4,1)}), s8[1572864]{0:T(1024)(128)(4,1)S(1)}, s32[]{:S(2)}) async-start(s8[5767168]{0:T(1024)(128)(4,1)} %bitcast.109), calls=%async_computation.3 | async-start | bytes 3145728
  424.5 42.9 %slice-start.3 = ((s8[5767168]{0:T(1024)(128)(4,1)}), s8[1572864]{0:T(1024)(128)(4,1)S(1)}, s32[]{:S(2)}) async-start(s8[5767168]{0:T(1024)(128)(4,1)} %bitcast.114), calls=%async_computation.5 | async-start | bytes 3145728
  424.5 43.0 %slice-start.5 = ((s8[5767168]{0:T(1024)(128)(4,1)}), s8[1572864]{0:T(1024)(128)(4,1)S(1)}, s32[]{:S(2)}) async-start(s8[5767168]{0:T(1024)(128)(4,1)} %bitcast.116), calls=%async_computation.7 | async-start | bytes 3145728
  424.5 40.0 %collective-permute-start.23 = (bf16[2,2,128,1024]{3,2,1,0:T(8,128)(2,1)}, bf16[2,2,128,1024]{3,2,1,0:T(8,128)(2,1)}, u32[]{:S(2)}, u32[]{:S(2)}) collective-permute-start(bf16[2,2,128,1024]{3,2,1,0:T(8,128)(2,1)} %pad_maximum_fusion.6), channel_id=1, source_target_pairs={{0,2},{1,5},{2,0},{3,7},{4,6},{5,1},{6,4},{7,3},{8,10},{9,13},{10,... | collective-permute-start | bytes 3145736 | tf_op jit(solution)/shard_map/ppermute | solution.py:767
  438.4 38.0 %collective-permute-start.37 = (bf16[1,128,2816]{2,1,0:T(8,128)(2,1)S(1)}, bf16[1,128,2816]{2,1,0:T(8,128)(2,1)S(1)}, u32[]{:S(2)}, u32[]{:S(2)}) collective-permute-start(bf16[1,128,2816]{2,1,0:T(8,128)(2,1)S(1)} %add_convert_fusion.3), channel_id=1, source_target_pairs={{8,0},{16,24},{9,1},{17,25},{10,2},{18,26},{11,3},{19,27},{12,4},{... | collective-permute-start | bytes 2162696 | tf_op jit(solution)/shard_map/ppermute | solution.py:789
  441.1 50.6 %collective-permute-start.38 = (bf16[1,128,2816]{2,1,0:T(8,128)(2,1)S(1)}, bf16[1,128,2816]{2,1,0:T(8,128)(2,1)S(1)}, u32[]{:S(2)}, u32[]{:S(2)}) collective-permute-start(bf16[1,128,2816]{2,1,0:T(8,128)(2,1)S(1)} %add_convert_fusion.2), channel_id=1, source_target_pairs={{8,0},{16,24},{9,1},{17,25},{10,2},{18,26},{11,3},{19,27},{12,4},{... | collective-permute-start | bytes 2162696 | tf_op jit(solution)/shard_map/ppermute | solution.py:789
  442.5 22.0 %copy-start.103 = (bf16[2,512,1024]{2,1,0:T(8,128)(2,1)S(1)}, bf16[2,512,1024]{2,1,0:T(8,128)(2,1)}, u32[]{:S(2)}) copy-start(bf16[2,512,1024]{2,1,0:T(8,128)(2,1)} %copy-done.102) | copy-start | bytes 6291460
  444.6 22.8 %copy-start.69 = (bf16[1024,1024]{1,0:T(8,128)(2,1)S(1)}, bf16[1024,1024]{1,0:T(8,128)(2,1)}, u32[]{:S(2)}) copy-start(bf16[1024,1024]{1,0:T(8,128)(2,1)} %copy-done.67) | copy-start | bytes 6291460
  444.7 53.0 %collective-permute-start.30 = (bf16[3,64,1024]{2,1,0:T(8,128)(2,1)S(1)}, bf16[3,64,1024]{2,1,0:T(8,128)(2,1)S(1)}, u32[]{:S(2)}, u32[]{:S(2)}) collective-permute-start(bf16[3,64,1024]{2,1,0:T(8,128)(2,1)S(1)} %dynamic-slice_bitcast_fusion), channel_id=1, source_target_pairs={{0,8},{8,0},{16,24},{24,16},{1,9},{9,1},{17,25},{25,17},{2,10},{10... | collective-permute-start | bytes 1179656 | tf_op jit(solution)/shard_map/ppermute | solution.py:816
  465.8 26.1 %collective-permute-start.31 = (bf16[2,128,1024]{2,1,0:T(8,128)(2,1)S(1)}, bf16[2,128,1024]{2,1,0:T(8,128)(2,1)S(1)}, u32[]{:S(2)}, u32[]{:S(2)}) collective-permute-start(bf16[2,128,1024]{2,1,0:T(8,128)(2,1)S(1)} %fusion.17), channel_id=1, source_target_pairs={{0,4},{1,3},{2,6},{3,1},{4,0},{5,7},{6,2},{7,5},{8,12},{9,11},{10,... | collective-permute-start | bytes 1572872 | tf_op jit(solution)/shard_map/ppermute | solution.py:767
  497.8 23.1 %collective-permute-start.32 = (bf16[3,64,1024]{2,1,0:T(8,128)(2,1)S(1)}, bf16[3,64,1024]{2,1,0:T(8,128)(2,1)S(1)}, u32[]{:S(2)}, u32[]{:S(2)}) collective-permute-start(bf16[3,64,1024]{2,1,0:T(8,128)(2,1)S(1)} %fusion.22), channel_id=1, source_target_pairs={{0,16},{8,24},{16,0},{24,8},{1,17},{9,25},{17,1},{25,9},{2,18},{10... | collective-permute-start | bytes 1179656 | tf_op jit(solution)/shard_map/ppermute | solution.py:816
  498.3 11.6 %collective-permute-start.34 = (bf16[2,64,1024]{2,1,0:T(8,128)(2,1)S(1)}, bf16[2,64,1024]{2,1,0:T(8,128)(2,1)S(1)}, u32[]{:S(2)}, u32[]{:S(2)}) collective-permute-start(bf16[2,64,1024]{2,1,0:T(8,128)(2,1)S(1)} %dynamic-slice_bitcast_fusion.1), channel_id=1, source_target_pairs={{0,8},{8,0},{16,24},{24,16},{1,9},{9,1},{17,25},{25,17},{2,10},{10... | collective-permute-start | bytes 786440 | tf_op jit(solution)/shard_map/ppermute | solution.py:816
  500.9 20.3 %copy-start.101 = (bf16[1,352,1024]{2,1,0:T(8,128)(2,1)S(1)}, bf16[1,352,1024]{2,1,0:T(8,128)(2,1)}, u32[]{:S(2)}) copy-start(bf16[1,352,1024]{2,1,0:T(8,128)(2,1)} %add_convert_fusion.6) | copy-start | bytes 2162692
  510.0 16.6 %collective-permute-start.35 = (bf16[2,64,1024]{2,1,0:T(8,128)(2,1)S(1)}, bf16[2,64,1024]{2,1,0:T(8,128)(2,1)S(1)}, u32[]{:S(2)}, u32[]{:S(2)}) collective-permute-start(bf16[2,64,1024]{2,1,0:T(8,128)(2,1)S(1)} %fusion.32), channel_id=1, source_target_pairs={{0,16},{8,24},{16,0},{24,8},{1,17},{9,25},{17,1},{25,9},{2,18},{10... | collective-permute-start | bytes 786440 | tf_op jit(solution)/shard_map/ppermute | solution.py:816
  521.1 13.9 %collective-permute-start.33 = (bf16[3,64,1024]{2,1,0:T(8,128)(2,1)S(1)}, bf16[3,64,1024]{2,1,0:T(8,128)(2,1)S(1)}, u32[]{:S(2)}, u32[]{:S(2)}) collective-permute-start(bf16[3,64,1024]{2,1,0:T(8,128)(2,1)S(1)} %add_convert_fusion.12), channel_id=1, source_target_pairs={{0,8},{8,0},{16,24},{24,16},{1,9},{9,1},{17,25},{25,17},{2,10},{10... | collective-permute-start | bytes 1179656 | tf_op jit(solution)/shard_map/ppermute | solution.py:816
  526.6 13.9 %collective-permute-start.36 = (bf16[2,64,1024]{2,1,0:T(8,128)(2,1)S(1)}, bf16[2,64,1024]{2,1,0:T(8,128)(2,1)S(1)}, u32[]{:S(2)}, u32[]{:S(2)}) collective-permute-start(bf16[2,64,1024]{2,1,0:T(8,128)(2,1)S(1)} %add_convert_fusion.13), channel_id=1, source_target_pairs={{0,8},{8,0},{16,24},{24,16},{1,9},{9,1},{17,25},{25,17},{2,10},{10... | collective-permute-start | bytes 786440 | tf_op jit(solution)/shard_map/ppermute | solution.py:816
  (97 other events, 406.0 us)
Sparse Core Ops, SparseCore 0:
  10.6 98.4 all-gather.5
  140.0 42.3 all-gather.3
